TPU v7x, 128 devices: a whole 4x4x4 slice. The times are simulated.
128 devices in a mesh: seq: 16 (over y, x_hi, core), head: 8 (over z, x_lo).
Axes of the slice: x: 4 (x_hi: 2, x_lo: 2; x = x_hi * 2 + x_lo), y: 4, z: 4, core: 2. Of those that a mesh axis runs over, the one named last changes fastest.
Arguments:
- queries: bfloat16 [2048, 8192], P('seq', 'head'), may hold values from -24 to 24
- key_rows: bfloat16 [2048, 1024], P('seq', 'head'), may hold values from -6 to 6
- value_rows: bfloat16 [2048, 1024], P('seq', 'head'), may hold values from -6 to 6
- out_weight: bfloat16 [8192, 8192], P('head'), may hold values from -0.5 to 0.5
- residual: bfloat16 [2048, 8192], P('seq', 'head'), may hold values from -54 to 54
- norm_gain: float32 [8192], replicated, may hold values from 0.1 to 1.9
- gate_weight: bfloat16 [8192, 28672], P(None, ('seq', 'head')), may hold values from -0.0625 to 0.0625
- up_weight: bfloat16 [8192, 28672], P(None, ('seq', 'head')), may hold values from -0.0625 to 0.0625
Outputs:
- edit_keys: bfloat16 [2048, 28672], P(None, ('seq', 'head'))
- hidden_state: bfloat16 [2048, 8192], P('seq', 'head')
All inputs are finite; a program needn't handle non-finite values.
Results may differ from a plain program's by a relative error of at most 0.019.
Values may be sent and summed in bfloat16 or wider, within the bound.
No kernel may reach another device: no remote copies, remote signals or barrier semaphores. Data moves between devices by JAX's collectives and lax.ppermute only.
A program may use at most 128 MiB of HBM per device.

v0:
```python
import functools
import math

import jax
import jax.numpy as jnp
from jax import lax
from jax.experimental import pallas as pl
from jax.experimental.pallas import tpu as pltpu
from jax.sharding import Mesh, PartitionSpec as P


HD = 128
LOW = -1e30
EPS = 1e-5
SEQ = ("y", "xh", "c")
HEAD = ("z", "xl")
MESH = ("y", "xh", "c", "z", "xl")
MAIN = ("yzx", "zxy")
SIDE = ("xyz", "xyz")
OFFSETS = (0, -1, 1, 2)
MROWS, MCOLS = 224, 384
BF = jnp.bfloat16
F32 = jnp.float32


def shift(x, axes, by):
    pairs = []
    for core in range(2):
        for n in range(64):
            at = {"x": n // 16, "y": n // 4 % 4, "z": n % 4}
            to = dict(at)
            to[axes[core]] = (to[axes[core]] + by) % 4
            pairs.append(tuple(
                (((p["y"] * 2 + p["x"] // 2) * 2 + core) * 4 + p["z"]) * 2 + p["x"] % 2
                for p in (at, to)
            ))
    return lax.ppermute(x, MESH, pairs)


def swap_core(x):
    return lax.ppermute(x, "c", [(0, 1), (1, 0)])


def attend_kernel(pos_ref, q_ref, own_ref, oth_ref, w_hbm, out_ref, w_buf, qs, acc, att, sems):
    blocks = w_buf.shape[0]
    width = w_buf.shape[2]
    for b in range(blocks):
        pltpu.make_async_copy(w_hbm.at[:, pl.ds(b * width, width)], w_buf.at[b], sems.at[b]).start()
    heads = q_ref.shape[1] // HD
    rows = q_ref.shape[0]
    cols = heads * rows
    for h in range(heads):
        qs[pl.ds(h * rows, rows), :] = q_ref[:, h * HD:(h + 1) * HD]
    group = pos_ref[0]
    core = pos_ref[1]
    factor = math.log2(math.e) / math.sqrt(HD)
    qv = qs[...]

    def scores(ref, g):
        return lax.dot_general(
            ref[g, :, :HD], qv, (((1,), (1,)), ((), ())), preferred_element_type=F32
        ) * factor

    def weigh(ref, g, p):
        return lax.dot_general(
            ref[g, :, HD:], p.astype(BF), (((0,), (0,)), ((), ())), preferred_element_type=F32
        )

    key_at = lax.broadcasted_iota(jnp.int32, (rows, cols), 0)
    row_at = lax.broadcasted_iota(jnp.int32, (rows, cols), 1) % rows
    s1 = jnp.where(key_at <= row_at, scores(own_ref, group), LOW)
    s2 = jnp.where(core == 1, scores(oth_ref, group), LOW)
    top = jnp.maximum(jnp.max(s1, axis=0, keepdims=True), jnp.max(s2, axis=0, keepdims=True))
    p1 = jnp.exp2(s1 - top)
    p2 = jnp.where(core == 1, jnp.exp2(s2 - top), 0.0)
    total = jnp.sum(p1, axis=0, keepdims=True) + jnp.sum(p2, axis=0, keepdims=True)
    acc[...] = weigh(own_ref, group, p1) + weigh(oth_ref, group, p2)

    def step(g, carry):
        top, total = carry
        s1 = scores(own_ref, g)
        s2 = scores(oth_ref, g)
        new = jnp.maximum(
            top, jnp.maximum(jnp.max(s1, axis=0, keepdims=True), jnp.max(s2, axis=0, keepdims=True))
        )
        alpha = jnp.exp2(top - new)
        p1 = jnp.exp2(s1 - new)
        p2 = jnp.exp2(s2 - new)
        total = total * alpha + jnp.sum(p1, axis=0, keepdims=True) + jnp.sum(p2, axis=0, keepdims=True)
        acc[...] = acc[...] * alpha + weigh(own_ref, g, p1) + weigh(oth_ref, g, p2)
        return new, total

    top, total = lax.fori_loop(0, group, step, (top, total))
    final = acc[...] / total
    for h in range(heads):
        att[:, h * HD:(h + 1) * HD] = final[:, h * rows:(h + 1) * rows].T.astype(BF)

    def project(b, _):
        pltpu.make_async_copy(w_hbm.at[:, pl.ds(0, width)], w_buf.at[b], sems.at[b]).wait()
        out_ref[b] = jnp.dot(att[...], w_buf[b], preferred_element_type=F32).astype(BF)
        return 0

    lax.fori_loop(0, blocks, project, 0)


def attend_project(pos, q, own, oth, w, blocks):
    rows, cols = q.shape
    depth, wide = w.shape
    width = wide // blocks
    vm = pl.BlockSpec(memory_space=pltpu.VMEM)
    return pl.pallas_call(
        attend_kernel,
        out_shape=jax.ShapeDtypeStruct((blocks, rows, width), BF),
        in_specs=[pl.BlockSpec(memory_space=pltpu.SMEM), vm, vm, vm, pl.BlockSpec(memory_space=pl.ANY)],
        out_specs=vm,
        scratch_shapes=[
            pltpu.VMEM((blocks, depth, width), BF),
            pltpu.VMEM((rows * cols // HD, HD), BF),
            pltpu.VMEM((HD, rows * cols // HD), F32),
            pltpu.VMEM((rows, cols), BF),
            pltpu.SemaphoreType.DMA((blocks,)),
        ],
        compiler_params=pltpu.CompilerParams(vmem_limit_bytes=48 << 20),
        cost_estimate=pl.CostEstimate(flops=4 << 30, bytes_accessed=20 << 20, transcendentals=2 << 20),
        name="attend_project",
    )(pos, q, own, oth, w)


def gate_kernel(pos_ref, *refs):
    main, side, weights = refs[:8], refs[8:16], refs[16:20]
    own_ref, own_ss, par_ref = refs[20:23]
    hid, wsc, sems, wsem = refs[23:]
    i = pl.program_id(0)
    core = pos_ref[3]
    n = weights[0].shape[0]
    kb = 512
    blocks = wsc.shape[1] // kb

    def place(order, slots):
        at = {}
        for m, axis in enumerate("xyz"):
            off0 = OFFSETS[slots[order[0].index(axis)]]
            off1 = OFFSETS[slots[order[1].index(axis)]]
            off = off0 if off0 == off1 else jnp.where(core == 0, off0, off1)
            at[axis] = (pos_ref[m] + off + 4) & 3
        col = pl.multiple_of((at["z"] * 2 + (at["x"] & 1)) * kb, kb)
        return at["y"] * 2 + at["x"] // 2, col

    def source(names, slots):
        a, b, c = slots
        half = b // 2
        return names[((0, 1), (2, 3), (5, 4), (6, 7))[c][half]].at[(b % 2) * 4 + a]

    @pl.when(i == 0)
    def _():
        for t in range(blocks):
            for j, ref in enumerate(weights):
                pltpu.make_async_copy(
                    ref.at[:, pl.ds(pl.multiple_of(t * 2 * kb + core * kb, kb), kb)],
                    wsc.at[pl.ds(j * n, n), pl.ds(t * kb, kb)],
                    wsem,
                ).start()
        for c in range(4):
            for b in range(4):
                for a in range(4):
                    slots = (a, b, c)
                    src = source(main, slots)
                    g, col = place(MAIN, slots)
                    pltpu.make_async_copy(
                        src, hid.at[g, pl.ds(0, MROWS), pl.ds(col, MCOLS)], sems.at[g]
                    ).start()
                    src = source(side, slots)
                    g, col = place(SIDE, slots)
                    pltpu.make_async_copy(
                        src.at[pl.ds(0, 256)], hid.at[g, :, pl.ds(col + MCOLS, 128)], sems.at[g]
                    ).start()
                    for j in range(3):
                        pltpu.make_async_copy(
                            src.at[pl.ds(256 + 32 * j, 32)],
                            hid.at[g, pl.ds(MROWS, 32), pl.ds(col + 128 * j, 128)],
                            sems.at[g],
                        ).start()
        pltpu.make_async_copy(wsc, wsc, wsem).wait()

    pltpu.make_async_copy(hid.at[i], hid.at[i], sems.at[i]).wait()
    block = hid[i]
    prod = lax.dot_general(wsc[...], block, (((1,), (1,)), ((), ())), preferred_element_type=F32)
    own_ref[...] = prod[:2 * n]
    par_ref[:2 * n, :] = prod[2 * n:].astype(BF)
    part = jnp.zeros((block.shape[0], 128), F32)
    for j in range(block.shape[1] // 128):
        wide = hid[i, :, j * 128:(j + 1) * 128].astype(F32)
        part = part + wide * wide
    sums = lax.dot_general(
        jnp.ones((8, 128), F32), part, (((1,), (1,)), ((), ())),
        preferred_element_type=F32, precision=lax.Precision.HIGHEST,
    )
    own_ss[...] = sums
    first = sums.astype(BF)
    par_ref[2 * n:, :] = jnp.concatenate(
        [first.astype(F32), sums - first.astype(F32)], axis=0
    ).astype(BF)


def gate_up(pos, main, side, weights):
    n, depth = weights[0].shape
    groups, piece, tokens = 8, 256, 2048
    any_spec = pl.BlockSpec(memory_space=pl.ANY)
    ospec = lambda r: pl.BlockSpec((r, piece), lambda i, pos: (0, i))
    return pl.pallas_call(
        gate_kernel,
        out_shape=[
            jax.ShapeDtypeStruct((2 * n, tokens), F32),
            jax.ShapeDtypeStruct((8, tokens), F32),
            jax.ShapeDtypeStruct((2 * n + 16, tokens), BF),
        ],
        grid_spec=pltpu.PrefetchScalarGridSpec(
            num_scalar_prefetch=1,
            grid=(groups,),
            in_specs=[any_spec] * 20,
            out_specs=[ospec(2 * n), ospec(8), ospec(2 * n + 16)],
            scratch_shapes=[
                pltpu.VMEM((groups, piece, depth // 2), BF),
                pltpu.VMEM((4 * n, depth // 2), BF),
                pltpu.SemaphoreType.DMA((groups,)),
                pltpu.SemaphoreType.DMA,
            ],
        ),
        compiler_params=pltpu.CompilerParams(
            vmem_limit_bytes=48 << 20, dimension_semantics=("arbitrary",)
        ),
        cost_estimate=pl.CostEstimate(
            flops=4 * n * tokens * depth, bytes_accessed=32 << 20, transcendentals=0
        ),
        name="gate_up",
    )(pos, *main, *side, *weights)


def finish_kernel(own_ref, ss_ref, got_ref, out_ref, *, depth):
    n = out_ref.shape[0]
    got = got_ref[...].astype(F32)
    total = ss_ref[:1] + got[2 * n:2 * n + 1] + got[2 * n + 8:2 * n + 9]
    scale = lax.rsqrt(total / depth + EPS)
    gate = (own_ref[:n] + got[:n]) * scale
    up = (own_ref[n:] + got[n:2 * n]) * scale
    out_ref[...] = (gate / (1.0 + jnp.exp(-gate)) * up).astype(BF)


def finish(own, ss, got, depth):
    rows, tokens = own.shape
    n = rows // 2
    piece = 512
    spec = lambda r: pl.BlockSpec((r, piece), lambda i: (0, i))
    return pl.pallas_call(
        functools.partial(finish_kernel, depth=depth),
        out_shape=jax.ShapeDtypeStruct((n, tokens), BF),
        grid=(tokens // piece,),
        in_specs=[spec(rows), spec(8), spec(rows + 16)],
        out_specs=spec(n),
        cost_estimate=pl.CostEstimate(flops=8 << 20, bytes_accessed=7 << 20, transcendentals=1 << 20),
        name="finish",
    )(own, ss, got)


def gather(blocks, orders):
    axes = [[(o[0][p], o[1][p]) for p in range(3)] for o in orders]
    near = lax.optimization_barrier(
        [[b] + [shift(b, a[0], by) for by in (1, -1, 2)] for b, a in zip(blocks, axes)]
    )
    cur = [jnp.stack(p) for p in near]
    near = lax.optimization_barrier(
        [[b] + [shift(b, a[1], by) for by in (1, -1, 2)] for b, a in zip(cur, axes)]
    )
    out = []
    lows = [jnp.concatenate(p[:2], 0) for p in near]
    highs = [jnp.concatenate(p[2:], 0) for p in near]
    lows, highs = lax.optimization_barrier((lows, highs))
    for low, high, a in zip(lows, highs, axes):
        c = a[2]
        l1 = shift(low, c, 1)
        r1 = shift(high, c, -1)
        l2 = shift(high, c, 1)
        r2 = shift(low, c, -1)
        o1 = shift(l1, c, 1)
        o2 = shift(r1, c, -1)
        out.append((low, high, l1, l2, r1, r2, o1, o2))
    return out


def per_device(queries, key_rows, value_rows, out_weight, residual, norm_gain, gate_weight, up_weight):
    y_at, xh, core = lax.axis_index("y"), lax.axis_index("xh"), lax.axis_index("c")
    z_at, xl = lax.axis_index("z"), lax.axis_index("xl")
    x_at = xh * 2 + xl
    group = y_at * 2 + xh

    pair = jnp.concatenate([key_rows, value_rows], axis=1)
    spread = jnp.broadcast_to(pair[None], (8,) + pair.shape)
    own = lax.all_to_all(spread, ("y", "xh"), 0, 0, tiled=True)
    oth = swap_core(own)

    pos = jnp.stack([group, core]).astype(jnp.int32)
    partial = attend_project(pos, queries, own, oth, out_weight, 8)
    partial, gate_raw, up_raw = lax.optimization_barrier((partial, gate_weight.T, up_weight.T))
    terms = lax.all_to_all(partial, HEAD, 0, 0, tiled=True)
    gain = norm_gain[None, :]
    gate_t = (gate_raw.astype(F32) * gain).astype(BF)
    up_t = (up_raw.astype(F32) * gain).astype(BF)
    terms, weights = lax.optimization_barrier(
        (terms, (gate_t, up_t, swap_core(gate_t), swap_core(up_t)))
    )
    hidden = (residual.astype(F32) + jnp.sum(terms.astype(F32), axis=0)).astype(BF)

    keep = jnp.where(core == 0, hidden[:, :512], hidden[:, 512:])
    got = swap_core(jnp.where(core == 0, hidden[:, 512:], hidden[:, :512]))
    chip = jnp.where(
        core == 0, jnp.concatenate([keep, got], 0), jnp.concatenate([got, keep], 0)
    )
    main_part = chip[:MROWS, :MCOLS]
    side_part = jnp.concatenate(
        [chip[:, MCOLS:]] + [chip[MROWS:, 128 * j:128 * (j + 1)] for j in range(3)], 0
    )
    main, side = gather((main_part, side_part), (MAIN, SIDE))
    pos2 = jnp.stack([x_at, y_at, z_at, core]).astype(jnp.int32)
    own_sums, own_ss, theirs = gate_up(pos2, main, side, weights)
    out = finish(own_sums, own_ss, swap_core(theirs), norm_gain.shape[0])
    return out.T, hidden


def solution(mesh):
    devices = mesh.devices.reshape(4, 2, 2, 4, 2)
    fine = Mesh(devices, MESH)
    both = P(SEQ, HEAD)
    cols = P(None, SEQ + HEAD)
    return jax.shard_map(
        per_device,
        mesh=fine,
        in_specs=(both, both, both, P(HEAD, None), both, P(), cols, cols),
        out_specs=(cols, both),
        check_vma=False,
    )
```

profile of v0, /device:TPU:1, one launch (start us, length us, event | category | flops | bytes accessed | tf_op | source)
XLA Modules:
  0.0 214.1 jit_solution(3531809607737507801)
XLA Ops:
  0.6 0.8 pad_maximum_fusion.7
  1.5 18.0 %all_to_all.10.own_ref = bf16[8,128,256]{2,1,0:T(8,128)(2,1)S(1)} all-to-all(bf16[8,128,256]{2,1,0:T(8,128)(2,1)S(1)} %broadcast_in_dim.2), channel_id=1, replica_groups=mesh['y'=4,'xh'=2,'c'=2,'z'=4,'xl'=2] {'y','xh'}, dimensions={0} | all-to-all | bytes 1048576 | tf_op jit(solution)/shard_map/all_to_all | solution.py:298
  19.4 1.8 collective-permute-start
  21.3 1.5 collective-permute-done.oth_ref
  22.8 0.9 copy-done
  23.8 9.2 %attend_project.1 = bf16[8,128,1024]{2,1,0:T(8,128)(2,1)} custom-call(s32[2]{0:T(128)S(1)} %pad_add_fusion.1.pos_ref, bf16[128,1024]{1,0:T(8,128)(2,1)S(1)} %copy-done, bf16[8,128,256]{2,1,0:T(8,128)(2,1)S(1)} %all_to_all.10.own_ref, bf16[8,128,256]{2,1,0:T(8,128)(2,1)S(1)} %collective-permute-done.oth_ref, bf16[1024,8192]{1,0:T(8,128)(2,1)} %w_hbm.1), custom_call_target="tpu_custom_call" | custom-call | flops 4294967296 | bytes 20971520 | tf_op jit(solution)/shard_map/attend_project/pallas_call | solution.py:111
  33.0 4.7 %multiply_convert_fusion = (bf16[224,8192]{1,0:T(8,128)(2,1)}, bf16[224,8192]{1,0:T(8,128)(2,1)}) fusion(bf16[224,8192]{1,0:T(8,128)(2,1)S(1)} %bitcast.16, f32[8192]{0:T(1024)S(1)} %copy-done.10, bf16[224,8192]{1,0:T(8,128)(2,1)S(1)} %bitcast.17), kind=kLoop, calls=%fused_computation | loop fusion | flops 11010048 | bytes 14712832 | tf_op jit(solution)/shard_map/convert_element_type | solution.py:307
  38.2 5.1 %all-to-all-start.1 = ((bf16[8,128,1024]{2,1,0:T(8,128)(2,1)}), bf16[8,128,1024]{2,1,0:T(8,128)(2,1)S(1)}, u32[]{:S(2)}, u32[]{:S(2)}) async-start(bf16[8,128,1024]{2,1,0:T(8,128)(2,1)} %attend_project.1), calls=%async_computation.1 | async-start | bytes 4194304 | tf_op jit(solution)/shard_map/all_to_all | solution.py:304
  43.3 26.4 %all-to-all-done.1 = bf16[8,128,1024]{2,1,0:T(8,128)(2,1)S(1)} async-done(((bf16[8,128,1024]{2,1,0:T(8,128)(2,1)}), bf16[8,128,1024]{2,1,0:T(8,128)(2,1)S(1)}, u32[]{:S(2)}, u32[]{:S(2)}) %all-to-all-start.1) | async-done | bytes 2097184 | tf_op jit(solution)/shard_map/all_to_all | solution.py:304
  70.2 1.6 collective-permute-start.3
  71.7 1.0 collective-permute-done.3
  72.8 1.3 collective-permute-start.9
  74.1 0.7 collective-permute-start.6
  74.8 1.8 collective-permute-start.5
  76.6 2.1 collective-permute-start.8
  78.8 1.5 collective-permute-done.8
  80.2 3.3 %collective-permute-done.7 = bf16[352,128]{1,0:T(8,128)(2,1)S(1)} collective-permute-done((bf16[352,128]{1,0:T(8,128)(2,1)S(1)}, bf16[352,128]{1,0:T(8,128)(2,1)S(1)}, u32[]{:S(2)}, u32[]{:S(2)}) %collective-permute-start.7) | collective-permute-done | bytes 90144 | tf_op jit(solution)/shard_map/ppermute | solution.py:37
  83.6 0.8 collective-permute-start.15
  84.5 0.7 collective-permute-start.12
  85.2 1.1 collective-permute-start.11
  86.7 2.0 collective-permute-start.14
  88.7 4.0 %collective-permute-done.15 = bf16[4,352,128]{2,1,0:T(8,128)(2,1)S(1)} collective-permute-done((bf16[4,352,128]{2,1,0:T(8,128)(2,1)S(1)}, bf16[4,352,128]{2,1,0:T(8,128)(2,1)S(1)}, u32[]{:S(2)}, u32[]{:S(2)}) %collective-permute-start.15) | collective-permute-done | bytes 360480 | tf_op jit(solution)/shard_map/ppermute | solution.py:37
  92.7 7.6 %collective-permute-done.14 = bf16[4,352,128]{2,1,0:T(8,128)(2,1)S(1)} collective-permute-done((bf16[4,352,128]{2,1,0:T(8,128)(2,1)S(1)}, bf16[4,352,128]{2,1,0:T(8,128)(2,1)S(1)}, u32[]{:S(2)}, u32[]{:S(2)}) %collective-permute-start.14) | collective-permute-done | bytes 360480 | tf_op jit(solution)/shard_map/ppermute | solution.py:37
  100.4 1.6 collective-permute-done.11
  102.1 1.5 collective-permute-done.10
  103.6 1.4 pad_maximum_fusion
  105.1 3.5 %collective-permute-start.25 = (bf16[8,352,128]{2,1,0:T(8,128)(2,1)S(1)}, bf16[8,352,128]{2,1,0:T(8,128)(2,1)S(1)}, u32[]{:S(2)}, u32[]{:S(2)}) collective-permute-start(bf16[8,352,128]{2,1,0:T(8,128)(2,1)S(1)} %get-tuple-element.55.refs_8_), channel_id=1, source_target_pairs={{0,6},{2,0},{4,2},{6,4},{32,38},{34,32},{36,34},{38,36},{64,70},{6... | collective-permute-start | bytes 2162696 | tf_op jit(solution)/shard_map/ppermute | solution.py:37
  108.6 1.7 collective-permute-start.16
  110.3 0.9 collective-permute-start.18
  111.2 2.7 %collective-permute-start.24 = (bf16[8,352,128]{2,1,0:T(8,128)(2,1)S(1)}, bf16[8,352,128]{2,1,0:T(8,128)(2,1)}, u32[]{:S(2)}, u32[]{:S(2)}) collective-permute-start(bf16[8,352,128]{2,1,0:T(8,128)(2,1)S(1)} %get-tuple-element.56.refs_9_), channel_id=1, source_target_pairs={{0,6},{2,0},{4,2},{6,4},{32,38},{34,32},{36,34},{38,36},{64,70},{6... | collective-permute-start | bytes 2162696 | tf_op jit(solution)/shard_map/ppermute | solution.py:37
  113.9 7.3 %collective-permute-done.25.refs_13_ = bf16[8,352,128]{2,1,0:T(8,128)(2,1)S(1)} collective-permute-done((bf16[8,352,128]{2,1,0:T(8,128)(2,1)S(1)}, bf16[8,352,128]{2,1,0:T(8,128)(2,1)S(1)}, u32[]{:S(2)}, u32[]{:S(2)}) %collective-permute-start.25) | collective-permute-done | bytes 720928 | tf_op jit(solution)/shard_map/ppermute | solution.py:37
  121.2 0.8 collective-permute-start.19
  121.9 4.6 %collective-permute-done.22.refs_10_ = bf16[8,352,128]{2,1,0:T(8,128)(2,1)S(1)} collective-permute-done((bf16[8,352,128]{2,1,0:T(8,128)(2,1)S(1)}, bf16[8,352,128]{2,1,0:T(8,128)(2,1)S(1)}, u32[]{:S(2)}, u32[]{:S(2)}) %collective-permute-start.22) | collective-permute-done | bytes 720928 | tf_op jit(solution)/shard_map/ppermute | solution.py:37
  126.5 10.1 %collective-permute-done.24.refs_12_ = bf16[8,352,128]{2,1,0:T(8,128)(2,1)} collective-permute-done((bf16[8,352,128]{2,1,0:T(8,128)(2,1)S(1)}, bf16[8,352,128]{2,1,0:T(8,128)(2,1)}, u32[]{:S(2)}, u32[]{:S(2)}) %collective-permute-start.24) | collective-permute-done | bytes 720928 | tf_op jit(solution)/shard_map/ppermute | solution.py:37
  136.6 2.5 %collective-permute-start.17 = (bf16[8,224,384]{2,1,0:T(8,128)(2,1)}, bf16[8,224,384]{2,1,0:T(8,128)(2,1)}, u32[]{:S(2)}, u32[]{:S(2)}) collective-permute-start(bf16[8,224,384]{2,1,0:T(8,128)(2,1)} %get-tuple-element.54.refs_1_), channel_id=1, source_target_pairs={{0,1},{2,3},{4,5},{6,7},{32,33},{34,35},{36,37},{38,39},{64,65},{6... | collective-permute-start | bytes 4128776 | tf_op jit(solution)/shard_map/ppermute | solution.py:37
  139.5 2.3 %collective-permute-start.21 = (bf16[8,224,384]{2,1,0:T(8,128)(2,1)}, bf16[8,224,384]{2,1,0:T(8,128)(2,1)}, u32[]{:S(2)}, u32[]{:S(2)}) collective-permute-start(bf16[8,224,384]{2,1,0:T(8,128)(2,1)} %collective-permute-done.18.refs_4_), channel_id=1, source_target_pairs={{0,17},{2,19},{4,21},{6,23},{32,49},{34,51},{36,53},{38,55},{64,81... | collective-permute-start | bytes 4128776 | tf_op jit(solution)/shard_map/ppermute | solution.py:37
  141.8 0.9 copy-done.2
  142.7 1.1 copy-done.11
  143.8 3.5 %collective-permute-start.27 = (bf16[8,352,128]{2,1,0:T(8,128)(2,1)}, bf16[8,352,128]{2,1,0:T(8,128)(2,1)}, u32[]{:S(2)}, u32[]{:S(2)}) collective-permute-start(bf16[8,352,128]{2,1,0:T(8,128)(2,1)} %collective-permute-done.24.refs_12_), channel_id=1, source_target_pairs={{0,6},{2,0},{4,2},{6,4},{32,38},{34,32},{36,34},{38,36},{64,70},{6... | collective-permute-start | bytes 2162696 | tf_op jit(solution)/shard_map/ppermute | solution.py:37
  147.4 8.2 %collective-permute-done.17.refs_3_ = bf16[8,224,384]{2,1,0:T(8,128)(2,1)} collective-permute-done((bf16[8,224,384]{2,1,0:T(8,128)(2,1)}, bf16[8,224,384]{2,1,0:T(8,128)(2,1)}, u32[]{:S(2)}, u32[]{:S(2)}) %collective-permute-start.17) | collective-permute-done | bytes 1376288 | tf_op jit(solution)/shard_map/ppermute | solution.py:37
  155.6 3.2 %collective-permute-done.26.refs_14_ = bf16[8,352,128]{2,1,0:T(8,128)(2,1)} collective-permute-done((bf16[8,352,128]{2,1,0:T(8,128)(2,1)S(1)}, bf16[8,352,128]{2,1,0:T(8,128)(2,1)}, u32[]{:S(2)}, u32[]{:S(2)}) %collective-permute-start.26) | collective-permute-done | bytes 720928 | tf_op jit(solution)/shard_map/ppermute | solution.py:37
  159.0 11.3 %collective-permute-done.20.refs_6_ = bf16[8,224,384]{2,1,0:T(8,128)(2,1)} collective-permute-done((bf16[8,224,384]{2,1,0:T(8,128)(2,1)}, bf16[8,224,384]{2,1,0:T(8,128)(2,1)}, u32[]{:S(2)}, u32[]{:S(2)}) %collective-permute-start.20) | collective-permute-done | bytes 1376288 | tf_op jit(solution)/shard_map/ppermute | solution.py:37
  170.4 1.1 copy-done.3
  171.5 27.8 %gate_up.1 = (f32[448,2048]{1,0:T(8,128)}, f32[8,2048]{1,0:T(8,128)S(1)}, bf16[464,2048]{1,0:T(8,128)(2,1)}) custom-call(s32[4]{0:T(128)S(1)} %pad_add_fusion.pos_ref, bf16[8,224,384]{2,1,0:T(8,128)(2,1)} %copy-done.7, bf16[8,224,384]{2,1,0:T(8,128)(2,1)} %get-tuple-element.54.refs_1_, bf16[8,224,384]{2,1,0:T(8,128)(2,1)} %collective-permute-done.16.refs_2_, ...), custom_call_target="tpu_custom_call" | custom-call | flops 15032385536 | bytes 33554432 | tf_op jit(solution)/shard_map/gate_up/pallas_call | solution.py:210
  199.9 4.6 %collective-permute-start.28 = (bf16[464,2048]{1,0:T(8,128)(2,1)}, bf16[464,2048]{1,0:T(8,128)(2,1)S(1)}, u32[]{:S(2)}, u32[]{:S(2)}) collective-permute-start(bf16[464,2048]{1,0:T(8,128)(2,1)} %get-tuple-element.63), channel_id=1, source_target_pairs={{0,8},{8,0},{1,9},{9,1},{2,10},{10,2},{3,11},{11,3},{4,12},{12,4},... | collective-permute-start | bytes 5701640 | tf_op jit(solution)/shard_map/ppermute | solution.py:41
  204.5 3.7 %collective-permute-done.28.got_ref = bf16[464,2048]{1,0:T(8,128)(2,1)S(1)} collective-permute-done((bf16[464,2048]{1,0:T(8,128)(2,1)}, bf16[464,2048]{1,0:T(8,128)(2,1)S(1)}, u32[]{:S(2)}, u32[]{:S(2)}) %collective-permute-start.28) | collective-permute-done | bytes 1900576 | tf_op jit(solution)/shard_map/ppermute | solution.py:41
  208.3 1.3 copy-done.6
  209.5 4.6 %finish.1 = bf16[224,2048]{1,0:T(8,128)(2,1)} custom-call(f32[448,2048]{1,0:T(8,128)} %get-tuple-element.61.own_ref, f32[8,2048]{1,0:T(8,128)} %copy-done.1, bf16[464,2048]{1,0:T(8,128)(2,1)} %copy-done.6), custom_call_target="tpu_custom_call" | custom-call | flops 8388608 | bytes 7340032 | tf_op jit(solution)/shard_map/finish/pallas_call | solution.py:254
  (57 shorter events, 3.6 us)
Async XLA Ops:
  19.4 3.3 %collective-permute-start = (bf16[8,128,256]{2,1,0:T(8,128)(2,1)S(1)}, bf16[8,128,256]{2,1,0:T(8,128)(2,1)S(1)}, u32[]{:S(2)}, u32[]{:S(2)}) collective-permute-start(bf16[8,128,256]{2,1,0:T(8,128)(2,1)S(1)} %all_to_all.10.own_ref), channel_id=1, source_target_pairs={{0,8},{8,0},{1,9},{9,1},{2,10},{10,2},{3,11},{11,3},{4,12},{12,4},... | collective-permute-start | bytes 1572872 | tf_op jit(solution)/shard_map/ppermute | solution.py:41
  22.8 0.9 copy-start
  23.7 9.2 %copy-start.4 = (bf16[8192,224]{0,1:T(8,128)(2,1)S(1)}, bf16[8192,224]{0,1:T(8,128)(2,1)}, u32[]{:S(2)}) copy-start(bf16[8192,224]{0,1:T(8,128)(2,1)} %param.15) | copy-start | bytes 11010052
  23.7 9.2 %copy-start.5 = (bf16[8192,224]{0,1:T(8,128)(2,1)S(1)}, bf16[8192,224]{0,1:T(8,128)(2,1)}, u32[]{:S(2)}) copy-start(bf16[8192,224]{0,1:T(8,128)(2,1)} %param.14) | copy-start | bytes 11010052
  23.8 9.2 %copy-start.10 = (f32[8192]{0:T(1024)S(1)}, f32[8192]{0:T(1024)}, u32[]{:S(2)}) copy-start(f32[8192]{0:T(1024)} %param.13) | copy-start | bytes 98308
  37.7 32.0 %collective-permute-start.2 = (bf16[224,8192]{1,0:T(8,128)(2,1)}, bf16[224,8192]{1,0:T(8,128)(2,1)}, u32[]{:S(2)}, u32[]{:S(2)}) collective-permute-start(bf16[224,8192]{1,0:T(8,128)(2,1)} %get-tuple-element.58.refs_17_), channel_id=1, source_target_pairs={{0,8},{8,0},{1,9},{9,1},{2,10},{10,2},{3,11},{11,3},{4,12},{12,4},... | collective-permute-start | bytes 11010056 | tf_op jit(solution)/shard_map/ppermute | solution.py:41
  38.0 31.6 %collective-permute-start.1 = (bf16[224,8192]{1,0:T(8,128)(2,1)}, bf16[224,8192]{1,0:T(8,128)(2,1)}, u32[]{:S(2)}, u32[]{:S(2)}) collective-permute-start(bf16[224,8192]{1,0:T(8,128)(2,1)} %get-tuple-element.57.refs_16_), channel_id=1, source_target_pairs={{0,8},{8,0},{1,9},{9,1},{2,10},{10,2},{3,11},{11,3},{4,12},{12,4},... | collective-permute-start | bytes 11010056 | tf_op jit(solution)/shard_map/ppermute | solution.py:41
  38.2 31.5 %all-to-all-start.1 = ((bf16[8,128,1024]{2,1,0:T(8,128)(2,1)}), bf16[8,128,1024]{2,1,0:T(8,128)(2,1)S(1)}, u32[]{:S(2)}, u32[]{:S(2)}) async-start(bf16[8,128,1024]{2,1,0:T(8,128)(2,1)} %attend_project.1), calls=%async_computation.1 | async-start | bytes 4194304 | tf_op jit(solution)/shard_map/all_to_all | solution.py:304
  43.2 26.8 %copy-start.9 = (bf16[128,1024]{1,0:T(8,128)(2,1)S(1)}, bf16[128,1024]{1,0:T(8,128)(2,1)}, u32[]{:S(2)}) copy-start(bf16[128,1024]{1,0:T(8,128)(2,1)} %param.12) | copy-start | bytes 786436
  70.1 34.9 %copy-start.8 = (bf16[128,1024]{1,0:T(8,128)(2,1)}, bf16[128,1024]{1,0:T(8,128)(2,1)S(1)}, u32[]{:S(2)}) copy-start(bf16[128,1024]{1,0:T(8,128)(2,1)S(1)} %add_convert_fusion) | copy-start | bytes 786436
  70.2 2.6 %collective-permute-start.3 = (bf16[128,512]{1,0:T(8,128)(2,1)S(1)}, bf16[128,512]{1,0:T(8,128)(2,1)S(1)}, u32[]{:S(2)}, u32[]{:S(2)}) collective-permute-start(bf16[128,512]{1,0:T(8,128)(2,1)S(1)} %get-tuple-element.68), channel_id=1, source_target_pairs={{0,8},{8,0},{1,9},{9,1},{2,10},{10,2},{3,11},{11,3},{4,12},{12,4},... | collective-permute-start | bytes 393224 | tf_op jit(solution)/shard_map/ppermute | solution.py:41
  72.8 5.8 %collective-permute-start.9 = (bf16[352,128]{1,0:T(8,128)(2,1)S(1)}, bf16[352,128]{1,0:T(8,128)(2,1)S(1)}, u32[]{:S(2)}, u32[]{:S(2)}) collective-permute-start(bf16[352,128]{1,0:T(8,128)(2,1)S(1)} %pad_maximum_fusion.6), channel_id=1, source_target_pairs={{0,16},{2,18},{4,20},{6,22},{32,48},{34,50},{36,52},{38,54},{64,80... | collective-permute-start | bytes 270344 | tf_op jit(solution)/shard_map/ppermute | solution.py:37
  74.1 9.4 %collective-permute-start.6 = (bf16[224,384]{1,0:T(8,128)(2,1)S(1)}, bf16[224,384]{1,0:T(8,128)(2,1)S(1)}, u32[]{:S(2)}, u32[]{:S(2)}) collective-permute-start(bf16[224,384]{1,0:T(8,128)(2,1)S(1)} %slice.32), channel_id=1, source_target_pairs={{0,64},{2,66},{4,68},{6,70},{32,96},{34,98},{36,100},{38,102},{64,... | collective-permute-start | bytes 516104 | tf_op jit(solution)/shard_map/ppermute | solution.py:37
  74.8 8.7 %collective-permute-start.5 = (bf16[224,384]{1,0:T(8,128)(2,1)S(1)}, bf16[224,384]{1,0:T(8,128)(2,1)S(1)}, u32[]{:S(2)}, u32[]{:S(2)}) collective-permute-start(bf16[224,384]{1,0:T(8,128)(2,1)S(1)} %slice.32), channel_id=1, source_target_pairs={{0,96},{2,98},{4,100},{6,102},{32,0},{34,2},{36,4},{38,6},{64,32},... | collective-permute-start | bytes 516104 | tf_op jit(solution)/shard_map/ppermute | solution.py:37
  76.6 7.0 %collective-permute-start.4 = (bf16[224,384]{1,0:T(8,128)(2,1)S(1)}, bf16[224,384]{1,0:T(8,128)(2,1)S(1)}, u32[]{:S(2)}, u32[]{:S(2)}) collective-permute-start(bf16[224,384]{1,0:T(8,128)(2,1)S(1)} %slice.32), channel_id=1, source_target_pairs={{0,32},{2,34},{4,36},{6,38},{32,64},{34,66},{36,68},{38,70},{64,96... | collective-permute-start | bytes 516104 | tf_op jit(solution)/shard_map/ppermute | solution.py:37
  76.6 3.7 %collective-permute-start.8 = (bf16[352,128]{1,0:T(8,128)(2,1)S(1)}, bf16[352,128]{1,0:T(8,128)(2,1)S(1)}, u32[]{:S(2)}, u32[]{:S(2)}) collective-permute-start(bf16[352,128]{1,0:T(8,128)(2,1)S(1)} %pad_maximum_fusion.6), channel_id=1, source_target_pairs={{0,17},{2,19},{4,21},{6,23},{32,49},{34,51},{36,53},{38,55},{64,81... | collective-permute-start | bytes 270344 | tf_op jit(solution)/shard_map/ppermute | solution.py:37
  78.6 4.9 %collective-permute-start.7 = (bf16[352,128]{1,0:T(8,128)(2,1)S(1)}, bf16[352,128]{1,0:T(8,128)(2,1)S(1)}, u32[]{:S(2)}, u32[]{:S(2)}) collective-permute-start(bf16[352,128]{1,0:T(8,128)(2,1)S(1)} %pad_maximum_fusion.6), channel_id=1, source_target_pairs={{0,1},{2,3},{4,5},{6,7},{32,33},{34,35},{36,37},{38,39},{64,65},{6... | collective-permute-start | bytes 270344 | tf_op jit(solution)/shard_map/ppermute | solution.py:37
  83.6 9.1 %collective-permute-start.15 = (bf16[4,352,128]{2,1,0:T(8,128)(2,1)S(1)}, bf16[4,352,128]{2,1,0:T(8,128)(2,1)S(1)}, u32[]{:S(2)}, u32[]{:S(2)}) collective-permute-start(bf16[4,352,128]{2,1,0:T(8,128)(2,1)S(1)} %pad_maximum_fusion.5), channel_id=1, source_target_pairs={{0,64},{2,66},{4,68},{6,70},{32,96},{34,98},{36,100},{38,102},{64,... | collective-permute-start | bytes 1081352 | tf_op jit(solution)/shard_map/ppermute | solution.py:37
  84.5 15.9 %collective-permute-start.12 = (bf16[4,224,384]{2,1,0:T(8,128)(2,1)S(1)}, bf16[4,224,384]{2,1,0:T(8,128)(2,1)S(1)}, u32[]{:S(2)}, u32[]{:S(2)}) collective-permute-start(bf16[4,224,384]{2,1,0:T(8,128)(2,1)S(1)} %pad_maximum_fusion.4), channel_id=1, source_target_pairs={{0,4},{2,6},{4,0},{6,2},{32,36},{34,38},{36,32},{38,34},{64,68},{6... | collective-permute-start | bytes 2064392 | tf_op jit(solution)/shard_map/ppermute | solution.py:37
  85.2 16.9 %collective-permute-start.11 = (bf16[4,224,384]{2,1,0:T(8,128)(2,1)S(1)}, bf16[4,224,384]{2,1,0:T(8,128)(2,1)S(1)}, u32[]{:S(2)}, u32[]{:S(2)}) collective-permute-start(bf16[4,224,384]{2,1,0:T(8,128)(2,1)S(1)} %pad_maximum_fusion.4), channel_id=1, source_target_pairs={{0,6},{2,0},{4,2},{6,4},{32,38},{34,32},{36,34},{38,36},{64,70},{6... | collective-permute-start | bytes 2064392 | tf_op jit(solution)/shard_map/ppermute | solution.py:37
  86.3 17.3 %collective-permute-start.10 = (bf16[4,224,384]{2,1,0:T(8,128)(2,1)S(1)}, bf16[4,224,384]{2,1,0:T(8,128)(2,1)S(1)}, u32[]{:S(2)}, u32[]{:S(2)}) collective-permute-start(bf16[4,224,384]{2,1,0:T(8,128)(2,1)S(1)} %pad_maximum_fusion.4), channel_id=1, source_target_pairs={{0,2},{2,4},{4,6},{6,0},{32,34},{34,36},{36,38},{38,32},{64,66},{6... | collective-permute-start | bytes 2064392 | tf_op jit(solution)/shard_map/ppermute | solution.py:37
  86.7 13.6 %collective-permute-start.14 = (bf16[4,352,128]{2,1,0:T(8,128)(2,1)S(1)}, bf16[4,352,128]{2,1,0:T(8,128)(2,1)S(1)}, u32[]{:S(2)}, u32[]{:S(2)}) collective-permute-start(bf16[4,352,128]{2,1,0:T(8,128)(2,1)S(1)} %pad_maximum_fusion.5), channel_id=1, source_target_pairs={{0,96},{2,98},{4,100},{6,102},{32,0},{34,2},{36,4},{38,6},{64,32},... | collective-permute-start | bytes 1081352 | tf_op jit(solution)/shard_map/ppermute | solution.py:37
  92.7 7.8 %collective-permute-start.13 = (bf16[4,352,128]{2,1,0:T(8,128)(2,1)S(1)}, bf16[4,352,128]{2,1,0:T(8,128)(2,1)S(1)}, u32[]{:S(2)}, u32[]{:S(2)}) collective-permute-start(bf16[4,352,128]{2,1,0:T(8,128)(2,1)S(1)} %pad_maximum_fusion.5), channel_id=1, source_target_pairs={{0,32},{2,34},{4,36},{6,38},{32,64},{34,66},{36,68},{38,70},{64,96... | collective-permute-start | bytes 1081352 | tf_op jit(solution)/shard_map/ppermute | solution.py:37
  105.0 36.9 %copy-start.7 = (bf16[8,224,384]{2,1,0:T(8,128)(2,1)}, bf16[8,224,384]{2,1,0:T(8,128)(2,1)S(1)}, u32[]{:S(2)}) copy-start(bf16[8,224,384]{2,1,0:T(8,128)(2,1)S(1)} %get-tuple-element.53.refs_0_) | copy-start | bytes 4128772
  105.1 16.1 %collective-permute-start.25 = (bf16[8,352,128]{2,1,0:T(8,128)(2,1)S(1)}, bf16[8,352,128]{2,1,0:T(8,128)(2,1)S(1)}, u32[]{:S(2)}, u32[]{:S(2)}) collective-permute-start(bf16[8,352,128]{2,1,0:T(8,128)(2,1)S(1)} %get-tuple-element.55.refs_8_), channel_id=1, source_target_pairs={{0,6},{2,0},{4,2},{6,4},{32,38},{34,32},{36,34},{38,36},{64,70},{6... | collective-permute-start | bytes 2162696 | tf_op jit(solution)/shard_map/ppermute | solution.py:37
  108.6 30.6 %collective-permute-start.16 = (bf16[8,224,384]{2,1,0:T(8,128)(2,1)S(1)}, bf16[8,224,384]{2,1,0:T(8,128)(2,1)}, u32[]{:S(2)}, u32[]{:S(2)}) collective-permute-start(bf16[8,224,384]{2,1,0:T(8,128)(2,1)S(1)} %get-tuple-element.53.refs_0_), channel_id=1, source_target_pairs={{0,1},{2,3},{4,5},{6,7},{32,33},{34,35},{36,37},{38,39},{64,65},{6... | collective-permute-start | bytes 4128776 | tf_op jit(solution)/shard_map/ppermute | solution.py:37
  110.3 29.2 %collective-permute-start.18 = (bf16[8,224,384]{2,1,0:T(8,128)(2,1)}, bf16[8,224,384]{2,1,0:T(8,128)(2,1)}, u32[]{:S(2)}, u32[]{:S(2)}) collective-permute-start(bf16[8,224,384]{2,1,0:T(8,128)(2,1)} %get-tuple-element.54.refs_1_), channel_id=1, source_target_pairs={{0,17},{2,19},{4,21},{6,23},{32,49},{34,51},{36,53},{38,55},{64,81... | collective-permute-start | bytes 4128776 | tf_op jit(solution)/shard_map/ppermute | solution.py:37
  111.2 15.3 %collective-permute-start.22 = (bf16[8,352,128]{2,1,0:T(8,128)(2,1)S(1)}, bf16[8,352,128]{2,1,0:T(8,128)(2,1)S(1)}, u32[]{:S(2)}, u32[]{:S(2)}) collective-permute-start(bf16[8,352,128]{2,1,0:T(8,128)(2,1)S(1)} %get-tuple-element.55.refs_8_), channel_id=1, source_target_pairs={{0,2},{2,4},{4,6},{6,0},{32,34},{34,36},{36,38},{38,32},{64,66},{6... | collective-permute-start | bytes 2162696 | tf_op jit(solution)/shard_map/ppermute | solution.py:37
  111.2 25.4 %collective-permute-start.24 = (bf16[8,352,128]{2,1,0:T(8,128)(2,1)S(1)}, bf16[8,352,128]{2,1,0:T(8,128)(2,1)}, u32[]{:S(2)}, u32[]{:S(2)}) collective-permute-start(bf16[8,352,128]{2,1,0:T(8,128)(2,1)S(1)} %get-tuple-element.56.refs_9_), channel_id=1, source_target_pairs={{0,6},{2,0},{4,2},{6,4},{32,38},{34,32},{36,34},{38,36},{64,70},{6... | collective-permute-start | bytes 2162696 | tf_op jit(solution)/shard_map/ppermute | solution.py:37
  121.2 21.5 %collective-permute-start.19 = (bf16[8,224,384]{2,1,0:T(8,128)(2,1)S(1)}, bf16[8,224,384]{2,1,0:T(8,128)(2,1)S(1)}, u32[]{:S(2)}, u32[]{:S(2)}) collective-permute-start(bf16[8,224,384]{2,1,0:T(8,128)(2,1)S(1)} %get-tuple-element.53.refs_0_), channel_id=1, source_target_pairs={{0,17},{2,19},{4,21},{6,23},{32,49},{34,51},{36,53},{38,55},{64,81... | collective-permute-start | bytes 4128776 | tf_op jit(solution)/shard_map/ppermute | solution.py:37
  126.5 15.3 %collective-permute-start.23 = (bf16[8,352,128]{2,1,0:T(8,128)(2,1)S(1)}, bf16[8,352,128]{2,1,0:T(8,128)(2,1)S(1)}, u32[]{:S(2)}, u32[]{:S(2)}) collective-permute-start(bf16[8,352,128]{2,1,0:T(8,128)(2,1)S(1)} %get-tuple-element.56.refs_9_), channel_id=1, source_target_pairs={{0,2},{2,4},{4,6},{6,0},{32,34},{34,36},{36,38},{38,32},{64,66},{6... | collective-permute-start | bytes 2162696 | tf_op jit(solution)/shard_map/ppermute | solution.py:37
  136.6 19.0 %collective-permute-start.17 = (bf16[8,224,384]{2,1,0:T(8,128)(2,1)}, bf16[8,224,384]{2,1,0:T(8,128)(2,1)}, u32[]{:S(2)}, u32[]{:S(2)}) collective-permute-start(bf16[8,224,384]{2,1,0:T(8,128)(2,1)} %get-tuple-element.54.refs_1_), channel_id=1, source_target_pairs={{0,1},{2,3},{4,5},{6,7},{32,33},{34,35},{36,37},{38,39},{64,65},{6... | collective-permute-start | bytes 4128776 | tf_op jit(solution)/shard_map/ppermute | solution.py:37
  139.1 31.2 %collective-permute-start.20 = (bf16[8,224,384]{2,1,0:T(8,128)(2,1)}, bf16[8,224,384]{2,1,0:T(8,128)(2,1)}, u32[]{:S(2)}, u32[]{:S(2)}) collective-permute-start(bf16[8,224,384]{2,1,0:T(8,128)(2,1)} %collective-permute-done.16.refs_2_), channel_id=1, source_target_pairs={{0,1},{2,3},{4,5},{6,7},{32,33},{34,35},{36,37},{38,39},{64,65},{6... | collective-permute-start | bytes 4128776 | tf_op jit(solution)/shard_map/ppermute | solution.py:37
  139.5 30.8 %collective-permute-start.21 = (bf16[8,224,384]{2,1,0:T(8,128)(2,1)}, bf16[8,224,384]{2,1,0:T(8,128)(2,1)}, u32[]{:S(2)}, u32[]{:S(2)}) collective-permute-start(bf16[8,224,384]{2,1,0:T(8,128)(2,1)} %collective-permute-done.18.refs_4_), channel_id=1, source_target_pairs={{0,17},{2,19},{4,21},{6,23},{32,49},{34,51},{36,53},{38,55},{64,81... | collective-permute-start | bytes 4128776 | tf_op jit(solution)/shard_map/ppermute | solution.py:37
  141.8 0.9 copy-start.2
  142.7 16.1 %collective-permute-start.26 = (bf16[8,352,128]{2,1,0:T(8,128)(2,1)S(1)}, bf16[8,352,128]{2,1,0:T(8,128)(2,1)}, u32[]{:S(2)}, u32[]{:S(2)}) collective-permute-start(bf16[8,352,128]{2,1,0:T(8,128)(2,1)S(1)} %collective-permute-done.22.refs_10_), channel_id=1, source_target_pairs={{0,2},{2,4},{4,6},{6,0},{32,34},{34,36},{36,38},{38,32},{64,66},{6... | collective-permute-start | bytes 2162696 | tf_op jit(solution)/shard_map/ppermute | solution.py:37
  142.7 1.1 copy-start.11
  143.8 15.3 %collective-permute-start.27 = (bf16[8,352,128]{2,1,0:T(8,128)(2,1)}, bf16[8,352,128]{2,1,0:T(8,128)(2,1)}, u32[]{:S(2)}, u32[]{:S(2)}) collective-permute-start(bf16[8,352,128]{2,1,0:T(8,128)(2,1)} %collective-permute-done.24.refs_12_), channel_id=1, source_target_pairs={{0,6},{2,0},{4,2},{6,4},{32,38},{34,32},{36,34},{38,36},{64,70},{6... | collective-permute-start | bytes 2162696 | tf_op jit(solution)/shard_map/ppermute | solution.py:37
  170.4 1.1 copy-start.3
  199.3 0.6 copy-start.1
  199.9 8.3 %collective-permute-start.28 = (bf16[464,2048]{1,0:T(8,128)(2,1)}, bf16[464,2048]{1,0:T(8,128)(2,1)S(1)}, u32[]{:S(2)}, u32[]{:S(2)}) collective-permute-start(bf16[464,2048]{1,0:T(8,128)(2,1)} %get-tuple-element.63), channel_id=1, source_target_pairs={{0,8},{8,0},{1,9},{9,1},{2,10},{10,2},{3,11},{11,3},{4,12},{12,4},... | collective-permute-start | bytes 5701640 | tf_op jit(solution)/shard_map/ppermute | solution.py:41
  208.2 1.3 copy-start.6
where the time goes:
time: 215 us; the launch traced here: 214 us
  waiting for transfers between devices  97.2 us (45%)
  starting transfers between devices  42.7 us (20%)
  Pallas kernels  41.6 us (19%)
  blocking collectives  18 us (8%)
  other arithmetic  7.78 us (4%)
  local copies, waits for them, and re-layouts  5.99 us (3%)
    ppermute x24, waiting for transfers between devices, shift(): return lax.ppermute(x, MESH, pairs)  64.6 us
    ppermute x24, starting transfers between devices, shift(): return lax.ppermute(x, MESH, pairs)  29.2 us
    pallas_call x1, Pallas kernels, gate_up(): pl.pallas_call(gate_kernel, out_shape=[jax.ShapeDtypeStruct((2 * n, token...  27.8 us
    all_to_all x1, waiting for transfers between devices, per_device(): terms = lax.all_to_all(partial, HEAD, 0, 0, tiled=True)  26.4 us
    all_to_all x1, blocking collectives, per_device(): own = lax.all_to_all(spread, ('y', 'xh'), 0, 0, tiled=True)  18 us
    pallas_call x1, Pallas kernels, attend_project(): pl.pallas_call(attend_kernel, out_shape=jax.ShapeDtypeStruct((blocks, row...  9.2 us
    ppermute x5, starting transfers between devices, swap_core(): return lax.ppermute(x, 'c', [(0, 1), (1, 0)])  8.49 us
    ppermute x5, waiting for transfers between devices, swap_core(): return lax.ppermute(x, 'c', [(0, 1), (1, 0)])  6.17 us
  transfers between devices with their start and end apart: 30, of which 18 were waited for; matrix products, arithmetic and copies ran while one was open for 0% of the time, Pallas kernels for 0%

commit v1 on v0

--- a/solution.py
+++ b/solution.py
@@ -18,7 +18,7 @@
 MAIN = ("yzx", "zxy")
 SIDE = ("xyz", "xyz")
 OFFSETS = (0, -1, 1, 2)
-MROWS, MCOLS = 224, 384
+MCOLS, SCOLS = 384, 128
 BF = jnp.bfloat16
 F32 = jnp.float32
 
@@ -126,114 +126,197 @@
     )(pos, q, own, oth, w)
 
 
-def gate_kernel(pos_ref, *refs):
-    main, side, weights = refs[:8], refs[8:16], refs[16:20]
-    own_ref, own_ss, par_ref = refs[20:23]
-    hid, wsc, sems, wsem = refs[23:]
-    i = pl.program_id(0)
-    core = pos_ref[3]
-    n = weights[0].shape[0]
-    kb = 512
-    blocks = wsc.shape[1] // kb
-
-    def place(order, slots):
-        at = {}
-        for m, axis in enumerate("xyz"):
-            off0 = OFFSETS[slots[order[0].index(axis)]]
-            off1 = OFFSETS[slots[order[1].index(axis)]]
-            off = off0 if off0 == off1 else jnp.where(core == 0, off0, off1)
-            at[axis] = (pos_ref[m] + off + 4) & 3
-        col = pl.multiple_of((at["z"] * 2 + (at["x"] & 1)) * kb, kb)
-        return at["y"] * 2 + at["x"] // 2, col
-
-    def source(names, slots):
-        a, b, c = slots
-        half = b // 2
-        return names[((0, 1), (2, 3), (5, 4), (6, 7))[c][half]].at[(b % 2) * 4 + a]
-
-    @pl.when(i == 0)
-    def _():
-        for t in range(blocks):
-            for j, ref in enumerate(weights):
-                pltpu.make_async_copy(
-                    ref.at[:, pl.ds(pl.multiple_of(t * 2 * kb + core * kb, kb), kb)],
-                    wsc.at[pl.ds(j * n, n), pl.ds(t * kb, kb)],
-                    wsem,
-                ).start()
-        for c in range(4):
-            for b in range(4):
-                for a in range(4):
-                    slots = (a, b, c)
-                    src = source(main, slots)
-                    g, col = place(MAIN, slots)
-                    pltpu.make_async_copy(
-                        src, hid.at[g, pl.ds(0, MROWS), pl.ds(col, MCOLS)], sems.at[g]
-                    ).start()
-                    src = source(side, slots)
-                    g, col = place(SIDE, slots)
-                    pltpu.make_async_copy(
-                        src.at[pl.ds(0, 256)], hid.at[g, :, pl.ds(col + MCOLS, 128)], sems.at[g]
-                    ).start()
-                    for j in range(3):
-                        pltpu.make_async_copy(
-                            src.at[pl.ds(256 + 32 * j, 32)],
-                            hid.at[g, pl.ds(MROWS, 32), pl.ds(col + 128 * j, 128)],
-                            sems.at[g],
-                        ).start()
-        pltpu.make_async_copy(wsc, wsc, wsem).wait()
-
-    pltpu.make_async_copy(hid.at[i], hid.at[i], sems.at[i]).wait()
-    block = hid[i]
-    prod = lax.dot_general(wsc[...], block, (((1,), (1,)), ((), ())), preferred_element_type=F32)
-    own_ref[...] = prod[:2 * n]
-    par_ref[:2 * n, :] = prod[2 * n:].astype(BF)
-    part = jnp.zeros((block.shape[0], 128), F32)
-    for j in range(block.shape[1] // 128):
-        wide = hid[i, :, j * 128:(j + 1) * 128].astype(F32)
-        part = part + wide * wide
-    sums = lax.dot_general(
-        jnp.ones((8, 128), F32), part, (((1,), (1,)), ((), ())),
-        preferred_element_type=F32, precision=lax.Precision.HIGHEST,
-    )
-    own_ss[...] = sums
-    first = sums.astype(BF)
-    par_ref[2 * n:, :] = jnp.concatenate(
-        [first.astype(F32), sums - first.astype(F32)], axis=0
-    ).astype(BF)
-
-
-def gate_up(pos, main, side, weights):
-    n, depth = weights[0].shape
-    groups, piece, tokens = 8, 256, 2048
-    any_spec = pl.BlockSpec(memory_space=pl.ANY)
-    ospec = lambda r: pl.BlockSpec((r, piece), lambda i, pos: (0, i))
+def prep_kernel(pos_ref, g_ref, u_ref, gain_ref, km_ref, ks_ref, sm_ref, ss_ref):
+    first = pos_ref[3] == 0
+    n = g_ref.shape[0]
+    gain = gain_ref[...]
+    for j, ref in enumerate((g_ref, u_ref)):
+        scaled = (ref[...].astype(F32) * gain).astype(BF)
+        low, high = scaled[:, :512], scaled[:, 512:]
+        keep = jnp.where(first, low, high)
+        send = jnp.where(first, high, low)
+        rows = pl.ds(j * n, n)
+        km_ref[0, rows, :] = keep[:, :MCOLS]
+        ks_ref[0, rows, :] = keep[:, MCOLS:]
+        sm_ref[0, rows, :] = send[:, :MCOLS]
+        ss_ref[0, rows, :] = send[:, MCOLS:]
+
+
+def prepare(pos, gate_t, up_t, gain):
+    n, depth = gate_t.shape
+    wspec = pl.BlockSpec((n, 1024), lambda i, pos: (0, i))
+    mspec = pl.BlockSpec((1, 2 * n, MCOLS), lambda i, pos: (i % 2, 0, i // 2))
+    sspec = pl.BlockSpec((1, 2 * n, SCOLS), lambda i, pos: (i // 2, 0, i % 2))
+    mshape = jax.ShapeDtypeStruct((2, 2 * n, 4 * MCOLS), BF)
+    sshape = jax.ShapeDtypeStruct((4, 2 * n, 2 * SCOLS), BF)
     return pl.pallas_call(
-        gate_kernel,
-        out_shape=[
-            jax.ShapeDtypeStruct((2 * n, tokens), F32),
-            jax.ShapeDtypeStruct((8, tokens), F32),
-            jax.ShapeDtypeStruct((2 * n + 16, tokens), BF),
-        ],
+        prep_kernel,
+        out_shape=[mshape, sshape, mshape, sshape],
         grid_spec=pltpu.PrefetchScalarGridSpec(
             num_scalar_prefetch=1,
-            grid=(groups,),
-            in_specs=[any_spec] * 20,
-            out_specs=[ospec(2 * n), ospec(8), ospec(2 * n + 16)],
-            scratch_shapes=[
-                pltpu.VMEM((groups, piece, depth // 2), BF),
-                pltpu.VMEM((4 * n, depth // 2), BF),
-                pltpu.SemaphoreType.DMA((groups,)),
-                pltpu.SemaphoreType.DMA,
-            ],
+            grid=(depth // 1024,),
+            in_specs=[wspec, wspec, pl.BlockSpec((1, 1024), lambda i, pos: (0, i))],
+            out_specs=[mspec, sspec, mspec, sspec],
         ),
-        compiler_params=pltpu.CompilerParams(
-            vmem_limit_bytes=48 << 20, dimension_semantics=("arbitrary",)
-        ),
+        compiler_params=pltpu.CompilerParams(vmem_limit_bytes=16 << 20),
+        cost_estimate=pl.CostEstimate(flops=8 << 20, bytes_accessed=15 << 20, transcendentals=0),
+        name="prepare",
+    )(pos, gate_t, up_t, gain)
+
+
+def gate_kernel(which, first, last, pos_ref, *refs):
+    count = len(which)
+    refs = list(refs)
+    main = {c: (refs.pop(0), refs.pop(0)) for c in which}
+    side = {c: (refs.pop(0), refs.pop(0)) for c in which}
+    km, ks, gm, gs = (refs.pop(0) for _ in range(4))
+    before = None if first else refs.pop(0)
+    if last:
+        own_ref, own_ss, par_ref = (refs.pop(0) for _ in range(3))
+    else:
+        after = refs.pop(0)
+    acc, wm, ws, hm, hs, table, wsem, asem, msem, ssem, osem = refs
+    x_at, y_at, z_at, core = (pos_ref[m] for m in range(4))
+    n2 = km.shape[1]
+    rows = 2 * n2
+
+    def at(base, slot):
+        return (base + OFFSETS[slot] + 4) & 3
+
+    if not first:
+        pltpu.make_async_copy(before, acc, asem).start()
+    for src, dst, half, sem in ((km, wm, 0, 0), (gm, wm, 1, 0), (ks, ws, 0, 1), (gs, ws, 1, 1)):
+        pltpu.make_async_copy(src, dst.at[:, pl.ds(half * n2, n2), :], wsem.at[sem]).start()
+
+    def fetch(u, c, j, on):
+        for k in range(4):
+            a, b = (j, k) if on == 0 else (k, j)
+            col = pl.multiple_of(at(z_at, k) * MCOLS, MCOLS)
+            pltpu.make_async_copy(
+                main[c][b // 2].at[(b % 2) * 4 + a], hm.at[u, :, pl.ds(col, MCOLS)], msem.at[u]
+            ).start()
+
+    for m, c in enumerate(which):
+        for j in range(4):
+            u = m * 4 + j
+            x = jnp.where(core == 0, at(x_at, c), at(x_at, j))
+            y = jnp.where(core == 0, at(y_at, j), at(y_at, c))
+            table[2 * u] = y * 2 + x // 2
+            table[2 * u + 1] = x & 1
+            pl.when(core == 0)(functools.partial(fetch, u, c, j, 0))
+            pl.when(core != 0)(functools.partial(fetch, u, c, j, 1))
+    for m, c in enumerate(which):
+        for b in range(4):
+            for a in range(4):
+                x = at(x_at, a)
+                row = pl.multiple_of((at(y_at, b) * 2 + x // 2) * 256, 256)
+                col = pl.multiple_of((x & 1) * SCOLS, SCOLS)
+                pltpu.make_async_copy(
+                    side[c][b // 2].at[(b % 2) * 4 + a],
+                    hs.at[m, pl.ds(row, 256), pl.ds(col, SCOLS)],
+                    ssem.at[m],
+                ).start()
+    if first:
+        acc[...] = jnp.zeros_like(acc)
+    else:
+        pltpu.make_async_copy(before, acc, asem).wait()
+    ones = jnp.ones((8, 128), F32)
+
+    def squares(block):
+        part = jnp.zeros((block.shape[0], 128), F32)
+        for j in range(block.shape[1] // 128):
+            wide = block[:, j * 128:(j + 1) * 128].astype(F32)
+            part = part + wide * wide
+        return lax.dot_general(
+            ones, part, (((1,), (1,)), ((), ())),
+            preferred_element_type=F32, precision=lax.Precision.HIGHEST,
+        )
+
+    def unit(u, _):
+        pltpu.make_async_copy(hm.at[u], hm.at[u], msem.at[u]).wait()
+        cols = pl.ds(pl.multiple_of(table[2 * u] * 256, 256), 256)
+        block = hm[u]
+        acc[:rows, cols] += lax.dot_general(
+            wm[table[2 * u + 1]], block, (((1,), (1,)), ((), ())), preferred_element_type=F32
+        )
+        acc[rows:, cols] += squares(block)
+        return 0
+
+    pltpu.make_async_copy(wm, wm, wsem.at[0]).wait()
+    lax.fori_loop(0, 4 * count, unit, 0)
+    pltpu.make_async_copy(ws, ws, wsem.at[1]).wait()
+    for m in range(count):
+        pltpu.make_async_copy(hs.at[m], hs.at[m], ssem.at[m]).wait()
+    piece = 512
+
+    def tail(p, _):
+        cols = pl.ds(pl.multiple_of(p * piece, piece), piece)
+        total = acc[:rows, cols]
+        sq = acc[rows:, cols]
+        for m, c in enumerate(which):
+            block = hs[m, cols, :]
+            total = total + lax.dot_general(
+                ws[at(z_at, c)], block, (((1,), (1,)), ((), ())), preferred_element_type=F32
+            )
+            sq = sq + squares(block)
+        if last:
+            own_ref[:, cols] = total[:n2]
+            par_ref[:n2, cols] = total[n2:].astype(BF)
+            own_ss[:, cols] = sq
+            big = sq.astype(BF)
+            par_ref[n2:, cols] = jnp.concatenate(
+                [big.astype(F32), sq - big.astype(F32)], axis=0
+            ).astype(BF)
+        else:
+            acc[:rows, cols] = total
+            acc[rows:, cols] = sq
+            pltpu.make_async_copy(acc.at[:, cols], after.at[:, cols], osem).start()
+        return 0
+
+    lax.fori_loop(0, acc.shape[1] // piece, tail, 0)
+    if not last:
+        pltpu.make_async_copy(acc, after, osem).wait()
+
+
+def gate_up(pos, which, main, side, weights, before, last):
+    n2 = weights[0].shape[1]
+    tokens = 2048
+    count = len(which)
+    first = before is None
+    any_spec = pl.BlockSpec(memory_space=pl.ANY)
+    vm = pl.BlockSpec(memory_space=pltpu.VMEM)
+    pieces = [p for part in (main, side) for c in which for p in part[c]]
+    operands = pieces + list(weights) + ([] if first else [before])
+    partial = jax.ShapeDtypeStruct((2 * n2 + 8, tokens), F32)
+    out_shape = [
+        jax.ShapeDtypeStruct((n2, tokens), F32),
+        jax.ShapeDtypeStruct((8, tokens), F32),
+        jax.ShapeDtypeStruct((n2 + 16, tokens), BF),
+    ] if last else partial
+    return pl.pallas_call(
+        functools.partial(gate_kernel, which, first, last),
+        out_shape=out_shape,
+        in_specs=[pl.BlockSpec(memory_space=pltpu.SMEM)] + [any_spec] * len(operands),
+        out_specs=[vm] * 3 if last else any_spec,
+        scratch_shapes=[
+            pltpu.VMEM(partial.shape, F32),
+            pltpu.VMEM((2, 2 * n2, 4 * MCOLS), BF),
+            pltpu.VMEM((4, 2 * n2, 2 * SCOLS), BF),
+            pltpu.VMEM((4 * count, 256, 4 * MCOLS), BF),
+            pltpu.VMEM((count, tokens, 2 * SCOLS), BF),
+            pltpu.SMEM((8 * count,), jnp.int32),
+            pltpu.SemaphoreType.DMA((2,)),
+            pltpu.SemaphoreType.DMA,
+            pltpu.SemaphoreType.DMA((4 * count,)),
+            pltpu.SemaphoreType.DMA((count,)),
+            pltpu.SemaphoreType.DMA,
+        ],
+        compiler_params=pltpu.CompilerParams(vmem_limit_bytes=48 << 20),
         cost_estimate=pl.CostEstimate(
-            flops=4 * n * tokens * depth, bytes_accessed=32 << 20, transcendentals=0
+            flops=count * n2 * tokens * 4096, bytes_accessed=20 << 20, transcendentals=0
         ),
         name="gate_up",
-    )(pos, *main, *side, *weights)
+    )(pos, *operands)
 
 
 def finish_kernel(own_ref, ss_ref, got_ref, out_ref, *, depth):
@@ -271,20 +354,17 @@
     near = lax.optimization_barrier(
         [[b] + [shift(b, a[1], by) for by in (1, -1, 2)] for b, a in zip(cur, axes)]
     )
-    out = []
     lows = [jnp.concatenate(p[:2], 0) for p in near]
     highs = [jnp.concatenate(p[2:], 0) for p in near]
     lows, highs = lax.optimization_barrier((lows, highs))
-    for low, high, a in zip(lows, highs, axes):
-        c = a[2]
-        l1 = shift(low, c, 1)
-        r1 = shift(high, c, -1)
-        l2 = shift(high, c, 1)
-        r2 = shift(low, c, -1)
-        o1 = shift(l1, c, 1)
-        o2 = shift(r1, c, -1)
-        out.append((low, high, l1, l2, r1, r2, o1, o2))
-    return out
+    near = [
+        (shift(low, a[2], 1), shift(high, a[2], 1), shift(low, a[2], -1), shift(high, a[2], -1))
+        for low, high, a in zip(lows, highs, axes)
+    ]
+    far = [(shift(t[0], a[2], 1), shift(t[3], a[2], -1)) for t, a in zip(near, axes)]
+    return [
+        {0: own, 1: t[:2], 2: t[2:], 3: o} for own, t, o in zip(zip(lows, highs), near, far)
+    ]
 
 
 def per_device(queries, key_rows, value_rows, out_weight, residual, norm_gain, gate_weight, up_weight):
@@ -300,28 +380,20 @@
 
     pos = jnp.stack([group, core]).astype(jnp.int32)
     partial = attend_project(pos, queries, own, oth, out_weight, 8)
+    pos2 = jnp.stack([x_at, y_at, z_at, core]).astype(jnp.int32)
     partial, gate_raw, up_raw = lax.optimization_barrier((partial, gate_weight.T, up_weight.T))
     terms = lax.all_to_all(partial, HEAD, 0, 0, tiled=True)
-    gain = norm_gain[None, :]
-    gate_t = (gate_raw.astype(F32) * gain).astype(BF)
-    up_t = (up_raw.astype(F32) * gain).astype(BF)
-    terms, weights = lax.optimization_barrier(
-        (terms, (gate_t, up_t, swap_core(gate_t), swap_core(up_t)))
-    )
+    km, ks, sm, ss = prepare(pos2, gate_raw, up_raw, norm_gain[None, :])
+    terms, weights = lax.optimization_barrier((terms, (km, ks, swap_core(sm), swap_core(ss))))
     hidden = (residual.astype(F32) + jnp.sum(terms.astype(F32), axis=0)).astype(BF)
 
     keep = jnp.where(core == 0, hidden[:, :512], hidden[:, 512:])
     got = swap_core(jnp.where(core == 0, hidden[:, 512:], hidden[:, :512]))
-    chip = jnp.where(
-        core == 0, jnp.concatenate([keep, got], 0), jnp.concatenate([got, keep], 0)
-    )
-    main_part = chip[:MROWS, :MCOLS]
-    side_part = jnp.concatenate(
-        [chip[:, MCOLS:]] + [chip[MROWS:, 128 * j:128 * (j + 1)] for j in range(3)], 0
-    )
-    main, side = gather((main_part, side_part), (MAIN, SIDE))
-    pos2 = jnp.stack([x_at, y_at, z_at, core]).astype(jnp.int32)
-    own_sums, own_ss, theirs = gate_up(pos2, main, side, weights)
+    chip = jnp.where(core == 0, jnp.concatenate([keep, got], 0), jnp.concatenate([got, keep], 0))
+    main, side = gather((chip[:, :MCOLS], chip[:, MCOLS:]), (MAIN, SIDE))
+    sums = gate_up(pos2, (0,), main, side, weights, None, False)
+    sums = gate_up(pos2, (1, 2), main, side, weights, sums, False)
+    own_sums, own_ss, theirs = gate_up(pos2, (3,), main, side, weights, sums, True)
     out = finish(own_sums, own_ss, swap_core(theirs), norm_gain.shape[0])
     return out.T, hidden
 

time: 215 us -> 204 us (0.949)
  waiting for transfers between devices: 97.2 us -> 67.8 us
  Pallas kernels: 41.6 us -> 63.9 us
  other arithmetic: 7.78 us -> 3.75 us
  local copies, waits for them, and re-layouts: 5.99 us -> 3.55 us
    ppermute x24, waiting for transfers between devices: 64.6 us -> 35.4 us  [shift(): return lax.ppermute(x, MESH, pairs)]
    pallas_call x1 -> x4, Pallas kernels: 27.8 us -> 50.1 us  [the longest x3 44.5 us: gate_up(): pl.pallas_call(functools.partial(gate_kernel, which, first, last), out_sh...]
    convert_element_type x1 -> x0, other arithmetic: 4.67 us -> none  [per_device(): up_t = (up_raw.astype(F32) * gain).astype(BF)]
    ppermute x5, starting transfers between devices: 8.49 us -> 12.1 us  [swap_core(): return lax.ppermute(x, 'c', [(0, 1), (1, 0)])]
    ppermute x24, starting transfers between devices: 29.2 us -> 26 us  [shift(): return lax.ppermute(x, MESH, pairs)]
    unnamed x24 -> x22, local copies, waits for them, and re-layouts: 5.92 us -> 3.48 us
    all_to_all x1, waiting for transfers between devices: 26.4 us -> 24.2 us  [per_device(): terms = lax.all_to_all(partial, HEAD, 0, 0, tiled=True)]
  transfers between devices with their start and end apart: 30 -> 30, of which waited for: 18 -> 14; matrix products, arithmetic and copies ran while one was open for 0% -> 0% of each run, Pallas kernels for 0% -> 15%
where the time goes in v1:
time: 204 us; the launch traced here: 201 us
  waiting for transfers between devices  67.8 us (33%)
  Pallas kernels  63.9 us (31%)
  starting transfers between devices  43.1 us (21%)
  blocking collectives  18 us (9%)
  other arithmetic  3.75 us (2%)
  local copies, waits for them, and re-layouts  3.55 us (2%)
    pallas_call x3, Pallas kernels, gate_up(): pl.pallas_call(functools.partial(gate_kernel, which, first, last), out_sh...  44.5 us
    ppermute x24, waiting for transfers between devices, shift(): return lax.ppermute(x, MESH, pairs)  35.4 us
    ppermute x24, starting transfers between devices, shift(): return lax.ppermute(x, MESH, pairs)  26 us
    all_to_all x1, waiting for transfers between devices, per_device(): terms = lax.all_to_all(partial, HEAD, 0, 0, tiled=True)  24.2 us
    all_to_all x1, blocking collectives, per_device(): own = lax.all_to_all(spread, ('y', 'xh'), 0, 0, tiled=True)  18 us
    ppermute x5, starting transfers between devices, swap_core(): return lax.ppermute(x, 'c', [(0, 1), (1, 0)])  12.1 us
    pallas_call x1, Pallas kernels, attend_project(): pl.pallas_call(attend_kernel, out_shape=jax.ShapeDtypeStruct((blocks, row...  9.26 us
    ppermute x5, waiting for transfers between devices, swap_core(): return lax.ppermute(x, 'c', [(0, 1), (1, 0)])  8.19 us
  transfers between devices with their start and end apart: 30, of which 14 were waited for; matrix products, arithmetic and copies ran while one was open for 0% of the time, Pallas kernels for 15%

profile of v1, /device:TPU:1, one launch (start us, length us, event | category | flops | bytes accessed | tf_op | source)
XLA Modules:
  0.0 201.0 jit_solution(7310874360381622900)
XLA Ops:
  0.6 0.8 pad_maximum_fusion.6
  1.5 18.0 %all_to_all.10.own_ref = bf16[8,128,256]{2,1,0:T(8,128)(2,1)S(1)} all-to-all(bf16[8,128,256]{2,1,0:T(8,128)(2,1)S(1)} %broadcast_in_dim.4), channel_id=1, replica_groups=mesh['y'=4,'xh'=2,'c'=2,'z'=4,'xl'=2] {'y','xh'}, dimensions={0} | all-to-all | bytes 1048576 | tf_op jit(solution)/shard_map/all_to_all | solution.py:378
  19.5 1.8 collective-permute-start
  21.5 1.4 collective-permute-done.oth_ref
  22.9 9.3 %attend_project.1 = bf16[8,128,1024]{2,1,0:T(8,128)(2,1)} custom-call(s32[2]{0:T(128)S(1)} %pad_add_fusion.1.pos_ref, bf16[128,1024]{1,0:T(8,128)(2,1)S(1)} %copy-done.3, bf16[8,128,256]{2,1,0:T(8,128)(2,1)S(1)} %all_to_all.10.own_ref, bf16[8,128,256]{2,1,0:T(8,128)(2,1)S(1)} %collective-permute-done.oth_ref, bf16[1024,8192]{1,0:T(8,128)(2,1)} %w_hbm.1), custom_call_target="tpu_custom_call" | custom-call | flops 4294967296 | bytes 20971520 | tf_op jit(solution)/shard_map/attend_project/pallas_call | solution.py:111
  32.1 5.6 %prepare.1 = (bf16[2,448,1536]{2,1,0:T(8,128)(2,1)S(1)}, bf16[4,448,256]{2,1,0:T(8,128)(2,1)S(1)}, bf16[2,448,1536]{2,1,0:T(8,128)(2,1)}, bf16[4,448,256]{2,1,0:T(8,128)(2,1)S(1)}) custom-call(s32[4]{0:T(128)S(1)} %pad_add_fusion.pos_ref, bf16[224,8192]{1,0:T(8,128)(2,1)S(1)} %bitcast.17, bf16[224,8192]{1,0:T(8,128)(2,1)S(1)} %bitcast.18, f32[1,8192]{1,0:T(1,128)S(1)} %bitcast.19), custom_call_target="tpu_custom_call" | custom-call | flops 8388608 | bytes 15728640 | tf_op jit(solution)/shard_map/prepare/pallas_call | solution.py:152
  37.7 1.5 copy-done
  39.2 0.4 collective-permute-start.1
  39.6 5.1 %all-to-all-start.1 = ((bf16[8,128,1024]{2,1,0:T(8,128)(2,1)}), bf16[8,128,1024]{2,1,0:T(8,128)(2,1)}, u32[]{:S(2)}, u32[]{:S(2)}) async-start(bf16[8,128,1024]{2,1,0:T(8,128)(2,1)} %attend_project.1), calls=%async_computation.1 | async-start | bytes 4194304 | tf_op jit(solution)/shard_map/all_to_all | solution.py:385
  44.7 0.5 collective-permute-start.2
  45.2 2.1 %collective-permute-done.2.refs_7_.refs_11_ = bf16[4,448,256]{2,1,0:T(8,128)(2,1)S(1)} collective-permute-done((bf16[4,448,256]{2,1,0:T(8,128)(2,1)S(1)}, bf16[4,448,256]{2,1,0:T(8,128)(2,1)S(1)}, u32[]{:S(2)}, u32[]{:S(2)}) %collective-permute-start.2) | collective-permute-done | bytes 917536 | tf_op jit(solution)/shard_map/ppermute | solution.py:41
  47.3 24.2 %all-to-all-done.1 = bf16[8,128,1024]{2,1,0:T(8,128)(2,1)} async-done(((bf16[8,128,1024]{2,1,0:T(8,128)(2,1)}), bf16[8,128,1024]{2,1,0:T(8,128)(2,1)}, u32[]{:S(2)}, u32[]{:S(2)}) %all-to-all-start.1) | async-done | bytes 2097184 | tf_op jit(solution)/shard_map/all_to_all | solution.py:385
  71.4 2.0 %convert_reduce_fusion = f32[128,1024]{1,0:T(8,128)S(1)} fusion(bf16[8,128,1024]{2,1,0:T(8,128)(2,1)} %all-to-all-done.1), kind=kLoop, calls=%fused_computation | loop fusion | flops 1966080 | bytes 2621440 | tf_op jit(solution)/shard_map/reduce_sum | solution.py:388
  73.6 1.4 collective-permute-start.3
  74.9 1.0 collective-permute-done.3
  76.1 2.7 %collective-permute-start.5 = (bf16[256,384]{1,0:T(8,128)(2,1)S(1)}, bf16[256,384]{1,0:T(8,128)(2,1)S(1)}, u32[]{:S(2)}, u32[]{:S(2)}) collective-permute-start(bf16[256,384]{1,0:T(8,128)(2,1)S(1)} %slice.20), channel_id=1, source_target_pairs={{0,96},{2,98},{4,100},{6,102},{32,0},{34,2},{36,4},{38,6},{64,32},... | collective-permute-start | bytes 589832 | tf_op jit(solution)/shard_map/ppermute | solution.py:37
  78.8 0.6 collective-permute-start.7
  79.4 2.1 %collective-permute-start.8 = (bf16[256,128]{1,0:T(8,128)(2,1)S(1)}, bf16[256,128]{1,0:T(8,128)(2,1)S(1)}, u32[]{:S(2)}, u32[]{:S(2)}) collective-permute-start(bf16[256,128]{1,0:T(8,128)(2,1)S(1)} %slice.21), channel_id=1, source_target_pairs={{0,17},{2,19},{4,21},{6,23},{32,49},{34,51},{36,53},{38,55},{64,81... | collective-permute-start | bytes 196616 | tf_op jit(solution)/shard_map/ppermute | solution.py:37
  81.5 1.6 collective-permute-done.7
  83.5 4.4 %collective-permute-done.9 = bf16[256,128]{1,0:T(8,128)(2,1)S(1)} collective-permute-done((bf16[256,128]{1,0:T(8,128)(2,1)S(1)}, bf16[256,128]{1,0:T(8,128)(2,1)S(1)}, u32[]{:S(2)}, u32[]{:S(2)}) %collective-permute-start.9) | collective-permute-done | bytes 65568 | tf_op jit(solution)/shard_map/ppermute | solution.py:37
  88.0 2.7 %collective-permute-start.11 = (bf16[4,256,384]{2,1,0:T(8,128)(2,1)S(1)}, bf16[4,256,384]{2,1,0:T(8,128)(2,1)S(1)}, u32[]{:S(2)}, u32[]{:S(2)}) collective-permute-start(bf16[4,256,384]{2,1,0:T(8,128)(2,1)S(1)} %pad_maximum_fusion.2), channel_id=1, source_target_pairs={{0,6},{2,0},{4,2},{6,4},{32,38},{34,32},{36,34},{38,36},{64,70},{6... | collective-permute-start | bytes 2359304 | tf_op jit(solution)/shard_map/ppermute | solution.py:37
  90.8 3.0 %collective-permute-start.14 = (bf16[4,256,128]{2,1,0:T(8,128)(2,1)S(1)}, bf16[4,256,128]{2,1,0:T(8,128)(2,1)S(1)}, u32[]{:S(2)}, u32[]{:S(2)}) collective-permute-start(bf16[4,256,128]{2,1,0:T(8,128)(2,1)S(1)} %pad_maximum_fusion.5), channel_id=1, source_target_pairs={{0,96},{2,98},{4,100},{6,102},{32,0},{34,2},{36,4},{38,6},{64,32},... | collective-permute-start | bytes 786440 | tf_op jit(solution)/shard_map/ppermute | solution.py:37
  93.8 4.0 %collective-permute-done.13 = bf16[4,256,128]{2,1,0:T(8,128)(2,1)S(1)} collective-permute-done((bf16[4,256,128]{2,1,0:T(8,128)(2,1)S(1)}, bf16[4,256,128]{2,1,0:T(8,128)(2,1)S(1)}, u32[]{:S(2)}, u32[]{:S(2)}) %collective-permute-start.13) | collective-permute-done | bytes 262176 | tf_op jit(solution)/shard_map/ppermute | solution.py:37
  97.8 0.4 collective-permute-start.15
  98.3 7.4 %collective-permute-done.15 = bf16[4,256,128]{2,1,0:T(8,128)(2,1)S(1)} collective-permute-done((bf16[4,256,128]{2,1,0:T(8,128)(2,1)S(1)}, bf16[4,256,128]{2,1,0:T(8,128)(2,1)S(1)}, u32[]{:S(2)}, u32[]{:S(2)}) %collective-permute-start.15) | collective-permute-done | bytes 262176 | tf_op jit(solution)/shard_map/ppermute | solution.py:37
  105.6 3.2 %collective-permute-done.10 = bf16[4,256,384]{2,1,0:T(8,128)(2,1)S(1)} collective-permute-done((bf16[4,256,384]{2,1,0:T(8,128)(2,1)S(1)}, bf16[4,256,384]{2,1,0:T(8,128)(2,1)S(1)}, u32[]{:S(2)}, u32[]{:S(2)}) %collective-permute-start.10) | collective-permute-done | bytes 786464 | tf_op jit(solution)/shard_map/ppermute | solution.py:37
  108.9 0.3 pad_maximum_fusion
  109.3 0.7 collective-permute-start.16
  109.9 2.1 %collective-permute-start.18 = (bf16[8,256,384]{2,1,0:T(8,128)(2,1)S(1)}, bf16[8,256,384]{2,1,0:T(8,128)(2,1)S(1)}, u32[]{:S(2)}, u32[]{:S(2)}) collective-permute-start(bf16[8,256,384]{2,1,0:T(8,128)(2,1)S(1)} %get-tuple-element.62.refs_1_), channel_id=1, source_target_pairs={{0,17},{2,19},{4,21},{6,23},{32,49},{34,51},{36,53},{38,55},{64,81... | collective-permute-start | bytes 4718600 | tf_op jit(solution)/shard_map/ppermute | solution.py:37
  112.1 1.1 collective-permute-start.20
  113.2 1.5 collective-permute-start.22
  114.7 6.9 %collective-permute-done.20.refs_4_ = bf16[8,256,128]{2,1,0:T(8,128)(2,1)S(1)} collective-permute-done((bf16[8,256,128]{2,1,0:T(8,128)(2,1)S(1)}, bf16[8,256,128]{2,1,0:T(8,128)(2,1)S(1)}, u32[]{:S(2)}, u32[]{:S(2)}) %collective-permute-start.20) | collective-permute-done | bytes 524320 | tf_op jit(solution)/shard_map/ppermute | solution.py:37
  121.6 1.8 collective-permute-start.25
  123.4 0.6 collective-permute-start.26
  124.0 6.7 %collective-permute-done.16.refs_0_ = bf16[8,256,384]{2,1,0:T(8,128)(2,1)S(1)} collective-permute-done((bf16[8,256,384]{2,1,0:T(8,128)(2,1)S(1)}, bf16[8,256,384]{2,1,0:T(8,128)(2,1)S(1)}, u32[]{:S(2)}, u32[]{:S(2)}) %collective-permute-start.16) | collective-permute-done | bytes 1572896 | tf_op jit(solution)/shard_map/ppermute | solution.py:37
  130.7 2.7 %collective-permute-start.19 = (bf16[8,256,384]{2,1,0:T(8,128)(2,1)S(1)}, bf16[8,256,384]{2,1,0:T(8,128)(2,1)S(1)}, u32[]{:S(2)}, u32[]{:S(2)}) collective-permute-start(bf16[8,256,384]{2,1,0:T(8,128)(2,1)S(1)} %collective-permute-done.18.refs_3_), channel_id=1, source_target_pairs={{0,17},{2,19},{4,21},{6,23},{32,49},{34,51},{36,53},{38,55},{64,81... | collective-permute-start | bytes 4718600 | tf_op jit(solution)/shard_map/ppermute | solution.py:37
  133.4 0.3 collective-permute-done.26.refs_5_
  133.7 1.7 collective-permute-start.27
  135.4 11.1 %gate_up.3.refs_12_ = f32[904,2048]{1,0:T(8,128)} custom-call(s32[4]{0:T(128)S(1)} %pad_add_fusion.pos_ref, bf16[8,256,384]{2,1,0:T(8,128)(2,1)S(1)} %get-tuple-element.61.refs_0_, bf16[8,256,384]{2,1,0:T(8,128)(2,1)S(1)} %get-tuple-element.62.refs_1_, bf16[8,256,128]{2,1,0:T(8,128)(2,1)S(1)} %get-tuple-element.63.refs_2_, ...), custom_call_target="tpu_custom_call" | custom-call | flops 3758096384 | bytes 20971520 | tf_op jit(solution)/shard_map/gate_up/pallas_call | solution.py:296
  146.6 1.0 collective-permute-done.24.refs_1_
  147.5 1.7 collective-permute-start.23
  149.2 19.3 %gate_up.4.refs_8_ = f32[904,2048]{1,0:T(8,128)} custom-call(s32[4]{0:T(128)S(1)} %pad_add_fusion.pos_ref, bf16[8,256,384]{2,1,0:T(8,128)(2,1)S(1)} %collective-permute-done.16.refs_0_, bf16[8,256,384]{2,1,0:T(8,128)(2,1)} %copy-done.8, bf16[8,256,384]{2,1,0:T(8,128)(2,1)} %collective-permute-done.25.refs_2_, bf16[8,256,384]{2,1,0:T(8,128)(2,1)} %copy-done.7, ...), custom_call_target="tpu_custom_call" | custom-call | flops 7516192768 | bytes 20971520 | tf_op jit(solution)/shard_map/gate_up/pallas_call | solution.py:296
  168.6 14.1 %gate_up.5 = (f32[448,2048]{1,0:T(8,128)}, f32[8,2048]{1,0:T(8,128)S(1)}, bf16[464,2048]{1,0:T(8,128)(2,1)}) custom-call(s32[4]{0:T(128)S(1)} %pad_add_fusion.pos_ref, bf16[8,256,384]{2,1,0:T(8,128)(2,1)S(1)} %collective-permute-done.17.refs_0_, bf16[8,256,384]{2,1,0:T(8,128)(2,1)S(1)} %collective-permute-done.19.refs_1_, ...), custom_call_target="tpu_custom_call" | custom-call | flops 3758096384 | bytes 20971520 | tf_op jit(solution)/shard_map/gate_up/pallas_call | solution.py:296
  182.7 0.6 copy-done.4
  183.3 8.1 %collective-permute-start.28 = (bf16[464,2048]{1,0:T(8,128)(2,1)}, bf16[464,2048]{1,0:T(8,128)(2,1)S(1)}, u32[]{:S(2)}, u32[]{:S(2)}) collective-permute-start(bf16[464,2048]{1,0:T(8,128)(2,1)} %get-tuple-element.71), channel_id=1, source_target_pairs={{0,8},{8,0},{1,9},{9,1},{2,10},{10,2},{3,11},{11,3},{4,12},{12,4},... | collective-permute-start | bytes 5701640 | tf_op jit(solution)/shard_map/ppermute | solution.py:41
  191.4 3.7 %collective-permute-done.28.got_ref = bf16[464,2048]{1,0:T(8,128)(2,1)S(1)} collective-permute-done((bf16[464,2048]{1,0:T(8,128)(2,1)}, bf16[464,2048]{1,0:T(8,128)(2,1)S(1)}, u32[]{:S(2)}, u32[]{:S(2)}) %collective-permute-start.28) | collective-permute-done | bytes 1900576 | tf_op jit(solution)/shard_map/ppermute | solution.py:41
  195.1 1.3 copy-done.6
  196.4 4.6 %finish.1 = bf16[224,2048]{1,0:T(8,128)(2,1)} custom-call(f32[448,2048]{1,0:T(8,128)} %get-tuple-element.69.own_ref, f32[8,2048]{1,0:T(8,128)} %copy-done.4, bf16[464,2048]{1,0:T(8,128)(2,1)} %copy-done.6), custom_call_target="tpu_custom_call" | custom-call | flops 8388608 | bytes 7340032 | tf_op jit(solution)/shard_map/finish/pallas_call | solution.py:337
  (55 shorter events, 1.3 us)
Async XLA Ops:
  0.6 22.2 %copy-start.3 = (bf16[128,1024]{1,0:T(8,128)(2,1)S(1)}, bf16[128,1024]{1,0:T(8,128)(2,1)}, u32[]{:S(2)}) copy-start(bf16[128,1024]{1,0:T(8,128)(2,1)} %q_ref.1) | copy-start | bytes 786436
  19.5 3.3 %collective-permute-start = (bf16[8,128,256]{2,1,0:T(8,128)(2,1)S(1)}, bf16[8,128,256]{2,1,0:T(8,128)(2,1)S(1)}, u32[]{:S(2)}, u32[]{:S(2)}) collective-permute-start(bf16[8,128,256]{2,1,0:T(8,128)(2,1)S(1)} %all_to_all.10.own_ref), channel_id=1, source_target_pairs={{0,8},{8,0},{1,9},{9,1},{2,10},{10,2},{3,11},{11,3},{4,12},{12,4},... | collective-permute-start | bytes 1572872 | tf_op jit(solution)/shard_map/ppermute | solution.py:41
  21.5 10.7 %copy-start.5 = (f32[8192]{0:T(1024)S(1)}, f32[8192]{0:T(1024)}, u32[]{:S(2)}) copy-start(f32[8192]{0:T(1024)} %param.13) | copy-start | bytes 98308
  22.9 9.3 %copy-start.1 = (bf16[8192,224]{0,1:T(8,128)(2,1)S(1)}, bf16[8192,224]{0,1:T(8,128)(2,1)}, u32[]{:S(2)}) copy-start(bf16[8192,224]{0,1:T(8,128)(2,1)} %param.14) | copy-start | bytes 11010052
  22.9 9.3 %copy-start.2 = (bf16[8192,224]{0,1:T(8,128)(2,1)S(1)}, bf16[8192,224]{0,1:T(8,128)(2,1)}, u32[]{:S(2)}) copy-start(bf16[8192,224]{0,1:T(8,128)(2,1)} %param.15) | copy-start | bytes 11010052
  37.7 1.5 copy-start
  39.2 32.2 %collective-permute-start.1 = (bf16[2,448,1536]{2,1,0:T(8,128)(2,1)}, bf16[2,448,1536]{2,1,0:T(8,128)(2,1)}, u32[]{:S(2)}, u32[]{:S(2)}) collective-permute-start(bf16[2,448,1536]{2,1,0:T(8,128)(2,1)} %get-tuple-element.42), channel_id=1, source_target_pairs={{0,8},{8,0},{1,9},{9,1},{2,10},{10,2},{3,11},{11,3},{4,12},{12,4},... | collective-permute-start | bytes 8257544 | tf_op jit(solution)/shard_map/ppermute | solution.py:41
  39.6 31.8 %all-to-all-start.1 = ((bf16[8,128,1024]{2,1,0:T(8,128)(2,1)}), bf16[8,128,1024]{2,1,0:T(8,128)(2,1)}, u32[]{:S(2)}, u32[]{:S(2)}) async-start(bf16[8,128,1024]{2,1,0:T(8,128)(2,1)} %attend_project.1), calls=%async_computation.1 | async-start | bytes 4194304 | tf_op jit(solution)/shard_map/all_to_all | solution.py:385
  44.7 28.8 %copy-start.10 = (bf16[128,1024]{1,0:T(8,128)(2,1)S(1)}, bf16[128,1024]{1,0:T(8,128)(2,1)}, u32[]{:S(2)}) copy-start(bf16[128,1024]{1,0:T(8,128)(2,1)} %param.12) | copy-start | bytes 786436
  44.7 2.6 %collective-permute-start.2 = (bf16[4,448,256]{2,1,0:T(8,128)(2,1)S(1)}, bf16[4,448,256]{2,1,0:T(8,128)(2,1)S(1)}, u32[]{:S(2)}, u32[]{:S(2)}) collective-permute-start(bf16[4,448,256]{2,1,0:T(8,128)(2,1)S(1)} %get-tuple-element.43), channel_id=1, source_target_pairs={{0,8},{8,0},{1,9},{9,1},{2,10},{10,2},{3,11},{11,3},{4,12},{12,4},... | collective-permute-start | bytes 2752520 | tf_op jit(solution)/shard_map/ppermute | solution.py:41
  73.5 2.4 %copy-start.9 = (bf16[128,1024]{1,0:T(8,128)(2,1)}, bf16[128,1024]{1,0:T(8,128)(2,1)S(1)}, u32[]{:S(2)}) copy-start(bf16[128,1024]{1,0:T(8,128)(2,1)S(1)} %add_convert_fusion) | copy-start | bytes 786436
  73.6 2.3 %collective-permute-start.3 = (bf16[128,512]{1,0:T(8,128)(2,1)S(1)}, bf16[128,512]{1,0:T(8,128)(2,1)S(1)}, u32[]{:S(2)}, u32[]{:S(2)}) collective-permute-start(bf16[128,512]{1,0:T(8,128)(2,1)S(1)} %get-tuple-element.73), channel_id=1, source_target_pairs={{0,8},{8,0},{1,9},{9,1},{2,10},{10,2},{3,11},{11,3},{4,12},{12,4},... | collective-permute-start | bytes 393224 | tf_op jit(solution)/shard_map/ppermute | solution.py:41
  76.0 11.8 %collective-permute-start.4 = (bf16[256,384]{1,0:T(8,128)(2,1)S(1)}, bf16[256,384]{1,0:T(8,128)(2,1)S(1)}, u32[]{:S(2)}, u32[]{:S(2)}) collective-permute-start(bf16[256,384]{1,0:T(8,128)(2,1)S(1)} %slice.20), channel_id=1, source_target_pairs={{0,32},{2,34},{4,36},{6,38},{32,64},{34,66},{36,68},{38,70},{64,96... | collective-permute-start | bytes 589832 | tf_op jit(solution)/shard_map/ppermute | solution.py:37
  76.1 11.7 %collective-permute-start.5 = (bf16[256,384]{1,0:T(8,128)(2,1)S(1)}, bf16[256,384]{1,0:T(8,128)(2,1)S(1)}, u32[]{:S(2)}, u32[]{:S(2)}) collective-permute-start(bf16[256,384]{1,0:T(8,128)(2,1)S(1)} %slice.20), channel_id=1, source_target_pairs={{0,96},{2,98},{4,100},{6,102},{32,0},{34,2},{36,4},{38,6},{64,32},... | collective-permute-start | bytes 589832 | tf_op jit(solution)/shard_map/ppermute | solution.py:37
  78.8 9.0 %collective-permute-start.6 = (bf16[256,384]{1,0:T(8,128)(2,1)S(1)}, bf16[256,384]{1,0:T(8,128)(2,1)S(1)}, u32[]{:S(2)}, u32[]{:S(2)}) collective-permute-start(bf16[256,384]{1,0:T(8,128)(2,1)S(1)} %slice.20), channel_id=1, source_target_pairs={{0,64},{2,66},{4,68},{6,70},{32,96},{34,98},{36,100},{38,102},{64,... | collective-permute-start | bytes 589832 | tf_op jit(solution)/shard_map/ppermute | solution.py:37
  78.8 4.4 %collective-permute-start.7 = (bf16[256,128]{1,0:T(8,128)(2,1)S(1)}, bf16[256,128]{1,0:T(8,128)(2,1)S(1)}, u32[]{:S(2)}, u32[]{:S(2)}) collective-permute-start(bf16[256,128]{1,0:T(8,128)(2,1)S(1)} %slice.21), channel_id=1, source_target_pairs={{0,1},{2,3},{4,5},{6,7},{32,33},{34,35},{36,37},{38,39},{64,65},{6... | collective-permute-start | bytes 196616 | tf_op jit(solution)/shard_map/ppermute | solution.py:37
  79.4 4.1 %collective-permute-start.8 = (bf16[256,128]{1,0:T(8,128)(2,1)S(1)}, bf16[256,128]{1,0:T(8,128)(2,1)S(1)}, u32[]{:S(2)}, u32[]{:S(2)}) collective-permute-start(bf16[256,128]{1,0:T(8,128)(2,1)S(1)} %slice.21), channel_id=1, source_target_pairs={{0,17},{2,19},{4,21},{6,23},{32,49},{34,51},{36,53},{38,55},{64,81... | collective-permute-start | bytes 196616 | tf_op jit(solution)/shard_map/ppermute | solution.py:37
  83.2 4.6 %collective-permute-start.9 = (bf16[256,128]{1,0:T(8,128)(2,1)S(1)}, bf16[256,128]{1,0:T(8,128)(2,1)S(1)}, u32[]{:S(2)}, u32[]{:S(2)}) collective-permute-start(bf16[256,128]{1,0:T(8,128)(2,1)S(1)} %slice.21), channel_id=1, source_target_pairs={{0,16},{2,18},{4,20},{6,22},{32,48},{34,50},{36,52},{38,54},{64,80... | collective-permute-start | bytes 196616 | tf_op jit(solution)/shard_map/ppermute | solution.py:37
  88.0 20.9 %collective-permute-start.10 = (bf16[4,256,384]{2,1,0:T(8,128)(2,1)S(1)}, bf16[4,256,384]{2,1,0:T(8,128)(2,1)S(1)}, u32[]{:S(2)}, u32[]{:S(2)}) collective-permute-start(bf16[4,256,384]{2,1,0:T(8,128)(2,1)S(1)} %pad_maximum_fusion.2), channel_id=1, source_target_pairs={{0,2},{2,4},{4,6},{6,0},{32,34},{34,36},{36,38},{38,32},{64,66},{6... | collective-permute-start | bytes 2359304 | tf_op jit(solution)/shard_map/ppermute | solution.py:37
  88.0 20.8 %collective-permute-start.11 = (bf16[4,256,384]{2,1,0:T(8,128)(2,1)S(1)}, bf16[4,256,384]{2,1,0:T(8,128)(2,1)S(1)}, u32[]{:S(2)}, u32[]{:S(2)}) collective-permute-start(bf16[4,256,384]{2,1,0:T(8,128)(2,1)S(1)} %pad_maximum_fusion.2), channel_id=1, source_target_pairs={{0,6},{2,0},{4,2},{6,4},{32,38},{34,32},{36,34},{38,36},{64,70},{6... | collective-permute-start | bytes 2359304 | tf_op jit(solution)/shard_map/ppermute | solution.py:37
  90.7 18.1 %collective-permute-start.12 = (bf16[4,256,384]{2,1,0:T(8,128)(2,1)S(1)}, bf16[4,256,384]{2,1,0:T(8,128)(2,1)S(1)}, u32[]{:S(2)}, u32[]{:S(2)}) collective-permute-start(bf16[4,256,384]{2,1,0:T(8,128)(2,1)S(1)} %pad_maximum_fusion.2), channel_id=1, source_target_pairs={{0,4},{2,6},{4,0},{6,2},{32,36},{34,38},{36,32},{38,34},{64,68},{6... | collective-permute-start | bytes 2359304 | tf_op jit(solution)/shard_map/ppermute | solution.py:37
  90.7 7.1 %collective-permute-start.13 = (bf16[4,256,128]{2,1,0:T(8,128)(2,1)S(1)}, bf16[4,256,128]{2,1,0:T(8,128)(2,1)S(1)}, u32[]{:S(2)}, u32[]{:S(2)}) collective-permute-start(bf16[4,256,128]{2,1,0:T(8,128)(2,1)S(1)} %pad_maximum_fusion.5), channel_id=1, source_target_pairs={{0,32},{2,34},{4,36},{6,38},{32,64},{34,66},{36,68},{38,70},{64,96... | collective-permute-start | bytes 786440 | tf_op jit(solution)/shard_map/ppermute | solution.py:37
  90.8 7.4 %collective-permute-start.14 = (bf16[4,256,128]{2,1,0:T(8,128)(2,1)S(1)}, bf16[4,256,128]{2,1,0:T(8,128)(2,1)S(1)}, u32[]{:S(2)}, u32[]{:S(2)}) collective-permute-start(bf16[4,256,128]{2,1,0:T(8,128)(2,1)S(1)} %pad_maximum_fusion.5), channel_id=1, source_target_pairs={{0,96},{2,98},{4,100},{6,102},{32,0},{34,2},{36,4},{38,6},{64,32},... | collective-permute-start | bytes 786440 | tf_op jit(solution)/shard_map/ppermute | solution.py:37
  97.8 7.8 %collective-permute-start.15 = (bf16[4,256,128]{2,1,0:T(8,128)(2,1)S(1)}, bf16[4,256,128]{2,1,0:T(8,128)(2,1)S(1)}, u32[]{:S(2)}, u32[]{:S(2)}) collective-permute-start(bf16[4,256,128]{2,1,0:T(8,128)(2,1)S(1)} %pad_maximum_fusion.5), channel_id=1, source_target_pairs={{0,64},{2,66},{4,68},{6,70},{32,96},{34,98},{36,100},{38,102},{64,... | collective-permute-start | bytes 786440 | tf_op jit(solution)/shard_map/ppermute | solution.py:37
  109.3 21.4 %collective-permute-start.16 = (bf16[8,256,384]{2,1,0:T(8,128)(2,1)S(1)}, bf16[8,256,384]{2,1,0:T(8,128)(2,1)S(1)}, u32[]{:S(2)}, u32[]{:S(2)}) collective-permute-start(bf16[8,256,384]{2,1,0:T(8,128)(2,1)S(1)} %get-tuple-element.61.refs_0_), channel_id=1, source_target_pairs={{0,1},{2,3},{4,5},{6,7},{32,33},{34,35},{36,37},{38,39},{64,65},{6... | collective-permute-start | bytes 4718600 | tf_op jit(solution)/shard_map/ppermute | solution.py:37
  109.9 20.7 %collective-permute-start.18 = (bf16[8,256,384]{2,1,0:T(8,128)(2,1)S(1)}, bf16[8,256,384]{2,1,0:T(8,128)(2,1)S(1)}, u32[]{:S(2)}, u32[]{:S(2)}) collective-permute-start(bf16[8,256,384]{2,1,0:T(8,128)(2,1)S(1)} %get-tuple-element.62.refs_1_), channel_id=1, source_target_pairs={{0,17},{2,19},{4,21},{6,23},{32,49},{34,51},{36,53},{38,55},{64,81... | collective-permute-start | bytes 4718600 | tf_op jit(solution)/shard_map/ppermute | solution.py:37
  112.1 9.5 %collective-permute-start.20 = (bf16[8,256,128]{2,1,0:T(8,128)(2,1)S(1)}, bf16[8,256,128]{2,1,0:T(8,128)(2,1)S(1)}, u32[]{:S(2)}, u32[]{:S(2)}) collective-permute-start(bf16[8,256,128]{2,1,0:T(8,128)(2,1)S(1)} %get-tuple-element.63.refs_2_), channel_id=1, source_target_pairs={{0,2},{2,4},{4,6},{6,0},{32,34},{34,36},{36,38},{38,32},{64,66},{6... | collective-permute-start | bytes 1572872 | tf_op jit(solution)/shard_map/ppermute | solution.py:37
  113.2 10.2 %collective-permute-start.22 = (bf16[8,256,128]{2,1,0:T(8,128)(2,1)S(1)}, bf16[8,256,128]{2,1,0:T(8,128)(2,1)S(1)}, u32[]{:S(2)}, u32[]{:S(2)}) collective-permute-start(bf16[8,256,128]{2,1,0:T(8,128)(2,1)S(1)} %get-tuple-element.64.refs_3_), channel_id=1, source_target_pairs={{0,6},{2,0},{4,2},{6,4},{32,38},{34,32},{36,34},{38,36},{64,70},{6... | collective-permute-start | bytes 1572872 | tf_op jit(solution)/shard_map/ppermute | solution.py:37
  114.7 32.8 %collective-permute-start.24 = (bf16[8,256,384]{2,1,0:T(8,128)(2,1)S(1)}, bf16[8,256,384]{2,1,0:T(8,128)(2,1)S(1)}, u32[]{:S(2)}, u32[]{:S(2)}) collective-permute-start(bf16[8,256,384]{2,1,0:T(8,128)(2,1)S(1)} %get-tuple-element.62.refs_1_), channel_id=1, source_target_pairs={{0,1},{2,3},{4,5},{6,7},{32,33},{34,35},{36,37},{38,39},{64,65},{6... | collective-permute-start | bytes 4718600 | tf_op jit(solution)/shard_map/ppermute | solution.py:37
  121.6 27.6 %collective-permute-start.25 = (bf16[8,256,384]{2,1,0:T(8,128)(2,1)S(1)}, bf16[8,256,384]{2,1,0:T(8,128)(2,1)}, u32[]{:S(2)}, u32[]{:S(2)}) collective-permute-start(bf16[8,256,384]{2,1,0:T(8,128)(2,1)S(1)} %get-tuple-element.61.refs_0_), channel_id=1, source_target_pairs={{0,17},{2,19},{4,21},{6,23},{32,49},{34,51},{36,53},{38,55},{64,81... | collective-permute-start | bytes 4718600 | tf_op jit(solution)/shard_map/ppermute | solution.py:37
  123.4 10.3 %collective-permute-start.26 = (bf16[8,256,128]{2,1,0:T(8,128)(2,1)S(1)}, bf16[8,256,128]{2,1,0:T(8,128)(2,1)S(1)}, u32[]{:S(2)}, u32[]{:S(2)}) collective-permute-start(bf16[8,256,128]{2,1,0:T(8,128)(2,1)S(1)} %get-tuple-element.64.refs_3_), channel_id=1, source_target_pairs={{0,2},{2,4},{4,6},{6,0},{32,34},{34,36},{36,38},{38,32},{64,66},{6... | collective-permute-start | bytes 1572872 | tf_op jit(solution)/shard_map/ppermute | solution.py:37
  130.7 37.9 %collective-permute-start.17 = (bf16[8,256,384]{2,1,0:T(8,128)(2,1)S(1)}, bf16[8,256,384]{2,1,0:T(8,128)(2,1)S(1)}, u32[]{:S(2)}, u32[]{:S(2)}) collective-permute-start(bf16[8,256,384]{2,1,0:T(8,128)(2,1)S(1)} %collective-permute-done.16.refs_0_), channel_id=1, source_target_pairs={{0,1},{2,3},{4,5},{6,7},{32,33},{34,35},{36,37},{38,39},{64,65},{6... | collective-permute-start | bytes 4718600 | tf_op jit(solution)/shard_map/ppermute | solution.py:37
  130.7 15.8 %copy-start.7 = (bf16[8,256,384]{2,1,0:T(8,128)(2,1)}, bf16[8,256,384]{2,1,0:T(8,128)(2,1)S(1)}, u32[]{:S(2)}) copy-start(bf16[8,256,384]{2,1,0:T(8,128)(2,1)S(1)} %collective-permute-done.18.refs_3_) | copy-start | bytes 4718596
  130.7 37.9 %collective-permute-start.19 = (bf16[8,256,384]{2,1,0:T(8,128)(2,1)S(1)}, bf16[8,256,384]{2,1,0:T(8,128)(2,1)S(1)}, u32[]{:S(2)}, u32[]{:S(2)}) collective-permute-start(bf16[8,256,384]{2,1,0:T(8,128)(2,1)S(1)} %collective-permute-done.18.refs_3_), channel_id=1, source_target_pairs={{0,17},{2,19},{4,21},{6,23},{32,49},{34,51},{36,53},{38,55},{64,81... | collective-permute-start | bytes 4718600 | tf_op jit(solution)/shard_map/ppermute | solution.py:37
  133.7 12.8 %collective-permute-start.27 = (bf16[8,256,128]{2,1,0:T(8,128)(2,1)S(1)}, bf16[8,256,128]{2,1,0:T(8,128)(2,1)S(1)}, u32[]{:S(2)}, u32[]{:S(2)}) collective-permute-start(bf16[8,256,128]{2,1,0:T(8,128)(2,1)S(1)} %get-tuple-element.63.refs_2_), channel_id=1, source_target_pairs={{0,6},{2,0},{4,2},{6,4},{32,38},{34,32},{36,34},{38,36},{64,70},{6... | collective-permute-start | bytes 1572872 | tf_op jit(solution)/shard_map/ppermute | solution.py:37
  146.5 22.1 %collective-permute-start.21 = (bf16[8,256,128]{2,1,0:T(8,128)(2,1)S(1)}, bf16[8,256,128]{2,1,0:T(8,128)(2,1)S(1)}, u32[]{:S(2)}, u32[]{:S(2)}) collective-permute-start(bf16[8,256,128]{2,1,0:T(8,128)(2,1)S(1)} %collective-permute-done.20.refs_4_), channel_id=1, source_target_pairs={{0,2},{2,4},{4,6},{6,0},{32,34},{34,36},{36,38},{38,32},{64,66},{6... | collective-permute-start | bytes 1572872 | tf_op jit(solution)/shard_map/ppermute | solution.py:37
  147.5 1.7 copy-start.8
  147.5 21.0 %collective-permute-start.23 = (bf16[8,256,128]{2,1,0:T(8,128)(2,1)S(1)}, bf16[8,256,128]{2,1,0:T(8,128)(2,1)S(1)}, u32[]{:S(2)}, u32[]{:S(2)}) collective-permute-start(bf16[8,256,128]{2,1,0:T(8,128)(2,1)S(1)} %collective-permute-done.22.refs_7_), channel_id=1, source_target_pairs={{0,6},{2,0},{4,2},{6,4},{32,38},{34,32},{36,34},{38,36},{64,70},{6... | collective-permute-start | bytes 1572872 | tf_op jit(solution)/shard_map/ppermute | solution.py:37
  182.7 0.6 copy-start.4
  183.3 11.8 %collective-permute-start.28 = (bf16[464,2048]{1,0:T(8,128)(2,1)}, bf16[464,2048]{1,0:T(8,128)(2,1)S(1)}, u32[]{:S(2)}, u32[]{:S(2)}) collective-permute-start(bf16[464,2048]{1,0:T(8,128)(2,1)} %get-tuple-element.71), channel_id=1, source_target_pairs={{0,8},{8,0},{1,9},{9,1},{2,10},{10,2},{3,11},{11,3},{4,12},{12,4},... | collective-permute-start | bytes 5701640 | tf_op jit(solution)/shard_map/ppermute | solution.py:41
  195.1 1.3 copy-start.6

commit v2 on v1

--- a/solution.py
+++ b/solution.py
@@ -169,24 +169,20 @@
     refs = list(refs)
     main = {c: (refs.pop(0), refs.pop(0)) for c in which}
     side = {c: (refs.pop(0), refs.pop(0)) for c in which}
-    km, ks, gm, gs = (refs.pop(0) for _ in range(4))
+    wm, ws = refs.pop(0), refs.pop(0)
     before = None if first else refs.pop(0)
     if last:
         own_ref, own_ss, par_ref = (refs.pop(0) for _ in range(3))
+        acc = before
     else:
-        after = refs.pop(0)
-    acc, wm, ws, hm, hs, table, wsem, asem, msem, ssem, osem = refs
+        acc = refs.pop(0)
+    hm, hs, ssq, table, msem, ssem = refs
     x_at, y_at, z_at, core = (pos_ref[m] for m in range(4))
-    n2 = km.shape[1]
-    rows = 2 * n2
+    rows = wm.shape[1]
+    n2 = rows // 2
 
     def at(base, slot):
         return (base + OFFSETS[slot] + 4) & 3
-
-    if not first:
-        pltpu.make_async_copy(before, acc, asem).start()
-    for src, dst, half, sem in ((km, wm, 0, 0), (gm, wm, 1, 0), (ks, ws, 0, 1), (gs, ws, 1, 1)):
-        pltpu.make_async_copy(src, dst.at[:, pl.ds(half * n2, n2), :], wsem.at[sem]).start()
 
     def fetch(u, c, j, on):
         for k in range(4):
@@ -218,18 +214,22 @@
                 ).start()
     if first:
         acc[...] = jnp.zeros_like(acc)
-    else:
-        pltpu.make_async_copy(before, acc, asem).wait()
-    ones = jnp.ones((8, 128), F32)
+    ssq[...] = jnp.zeros_like(ssq)
+    ones = jnp.ones((8, 128), BF)
 
     def squares(block):
         part = jnp.zeros((block.shape[0], 128), F32)
         for j in range(block.shape[1] // 128):
             wide = block[:, j * 128:(j + 1) * 128].astype(F32)
             part = part + wide * wide
-        return lax.dot_general(
-            ones, part, (((1,), (1,)), ((), ())),
-            preferred_element_type=F32, precision=lax.Precision.HIGHEST,
+        return part
+
+    def lane_sums(part):
+        big = part.astype(BF)
+        small = (part - big.astype(F32)).astype(BF)
+        return sum(
+            lax.dot_general(ones, t, (((1,), (1,)), ((), ())), preferred_element_type=F32)
+            for t in (big, small)
         )
 
     def unit(u, _):
@@ -239,12 +239,10 @@
         acc[:rows, cols] += lax.dot_general(
             wm[table[2 * u + 1]], block, (((1,), (1,)), ((), ())), preferred_element_type=F32
         )
-        acc[rows:, cols] += squares(block)
+        ssq[cols, :] += squares(block)
         return 0
 
-    pltpu.make_async_copy(wm, wm, wsem.at[0]).wait()
     lax.fori_loop(0, 4 * count, unit, 0)
-    pltpu.make_async_copy(ws, ws, wsem.at[1]).wait()
     for m in range(count):
         pltpu.make_async_copy(hs.at[m], hs.at[m], ssem.at[m]).wait()
     piece = 512
@@ -252,13 +250,14 @@
     def tail(p, _):
         cols = pl.ds(pl.multiple_of(p * piece, piece), piece)
         total = acc[:rows, cols]
-        sq = acc[rows:, cols]
+        part = ssq[cols, :]
         for m, c in enumerate(which):
             block = hs[m, cols, :]
             total = total + lax.dot_general(
                 ws[at(z_at, c)], block, (((1,), (1,)), ((), ())), preferred_element_type=F32
             )
-            sq = sq + squares(block)
+            part = part + squares(block)
+        sq = acc[rows:, cols] + lane_sums(part)
         if last:
             own_ref[:, cols] = total[:n2]
             par_ref[:n2, cols] = total[n2:].astype(BF)
@@ -270,16 +269,13 @@
         else:
             acc[:rows, cols] = total
             acc[rows:, cols] = sq
-            pltpu.make_async_copy(acc.at[:, cols], after.at[:, cols], osem).start()
         return 0
 
     lax.fori_loop(0, acc.shape[1] // piece, tail, 0)
-    if not last:
-        pltpu.make_async_copy(acc, after, osem).wait()
 
 
 def gate_up(pos, which, main, side, weights, before, last):
-    n2 = weights[0].shape[1]
+    n2 = weights[0].shape[1] // 2
     tokens = 2048
     count = len(which)
     first = before is None
@@ -296,22 +292,20 @@
     return pl.pallas_call(
         functools.partial(gate_kernel, which, first, last),
         out_shape=out_shape,
-        in_specs=[pl.BlockSpec(memory_space=pltpu.SMEM)] + [any_spec] * len(operands),
-        out_specs=[vm] * 3 if last else any_spec,
+        in_specs=[pl.BlockSpec(memory_space=pltpu.SMEM)]
+        + [any_spec] * len(pieces)
+        + [vm] * (len(operands) - len(pieces)),
+        out_specs=[vm] * 3 if last else vm,
         scratch_shapes=[
-            pltpu.VMEM(partial.shape, F32),
-            pltpu.VMEM((2, 2 * n2, 4 * MCOLS), BF),
-            pltpu.VMEM((4, 2 * n2, 2 * SCOLS), BF),
             pltpu.VMEM((4 * count, 256, 4 * MCOLS), BF),
             pltpu.VMEM((count, tokens, 2 * SCOLS), BF),
+            pltpu.VMEM((tokens, 128), F32),
             pltpu.SMEM((8 * count,), jnp.int32),
-            pltpu.SemaphoreType.DMA((2,)),
-            pltpu.SemaphoreType.DMA,
             pltpu.SemaphoreType.DMA((4 * count,)),
             pltpu.SemaphoreType.DMA((count,)),
-            pltpu.SemaphoreType.DMA,
         ],
-        compiler_params=pltpu.CompilerParams(vmem_limit_bytes=48 << 20),
+        input_output_aliases={} if first or last else {len(operands): 0},
+        compiler_params=pltpu.CompilerParams(vmem_limit_bytes=(10 + 8 * count) << 20),
         cost_estimate=pl.CostEstimate(
             flops=count * n2 * tokens * 4096, bytes_accessed=20 << 20, transcendentals=0
         ),
@@ -319,27 +313,38 @@
     )(pos, *operands)
 
 
-def finish_kernel(own_ref, ss_ref, got_ref, out_ref, *, depth):
-    n = out_ref.shape[0]
-    got = got_ref[...].astype(F32)
-    total = ss_ref[:1] + got[2 * n:2 * n + 1] + got[2 * n + 8:2 * n + 9]
-    scale = lax.rsqrt(total / depth + EPS)
-    gate = (own_ref[:n] + got[:n]) * scale
-    up = (own_ref[n:] + got[n:2 * n]) * scale
-    out_ref[...] = (gate / (1.0 + jnp.exp(-gate)) * up).astype(BF)
+def finish_kernel(own_ref, ss_ref, got_ref, out_ref, buf, sems, *, depth):
+    n = buf.shape[0]
+    piece = 512
+
+    def put(p):
+        cols = pl.ds(p * piece, piece)
+        return pltpu.make_async_copy(buf.at[:, cols], out_ref.at[:, cols], sems.at[p])
+
+    for p in range(buf.shape[1] // piece):
+        cols = pl.ds(p * piece, piece)
+        got = got_ref[:, cols].astype(F32)
+        total = ss_ref[:1, cols] + got[2 * n:2 * n + 1] + got[2 * n + 8:2 * n + 9]
+        scale = lax.rsqrt(total / depth + EPS)
+        gate = (own_ref[:n, cols] + got[:n]) * scale
+        up = (own_ref[n:, cols] + got[n:2 * n]) * scale
+        buf[:, cols] = (gate / (1.0 + jnp.exp(-gate)) * up).astype(BF)
+        put(p).start()
+    for p in range(buf.shape[1] // piece):
+        put(p).wait()
 
 
 def finish(own, ss, got, depth):
     rows, tokens = own.shape
     n = rows // 2
-    piece = 512
-    spec = lambda r: pl.BlockSpec((r, piece), lambda i: (0, i))
+    vm = pl.BlockSpec(memory_space=pltpu.VMEM)
     return pl.pallas_call(
         functools.partial(finish_kernel, depth=depth),
         out_shape=jax.ShapeDtypeStruct((n, tokens), BF),
-        grid=(tokens // piece,),
-        in_specs=[spec(rows), spec(8), spec(rows + 16)],
-        out_specs=spec(n),
+        in_specs=[vm] * 3,
+        out_specs=pl.BlockSpec(memory_space=pl.ANY),
+        scratch_shapes=[pltpu.VMEM((n, tokens), BF), pltpu.SemaphoreType.DMA((tokens // 512,))],
+        compiler_params=pltpu.CompilerParams(vmem_limit_bytes=16 << 20),
         cost_estimate=pl.CostEstimate(flops=8 << 20, bytes_accessed=7 << 20, transcendentals=1 << 20),
         name="finish",
     )(own, ss, got)
@@ -350,17 +355,16 @@
     near = lax.optimization_barrier(
         [[b] + [shift(b, a[0], by) for by in (1, -1, 2)] for b, a in zip(blocks, axes)]
     )
-    cur = [jnp.stack(p) for p in near]
-    near = lax.optimization_barrier(
-        [[b] + [shift(b, a[1], by) for by in (1, -1, 2)] for b, a in zip(cur, axes)]
-    )
-    lows = [jnp.concatenate(p[:2], 0) for p in near]
-    highs = [jnp.concatenate(p[2:], 0) for p in near]
-    lows, highs = lax.optimization_barrier((lows, highs))
-    near = [
-        (shift(low, a[2], 1), shift(high, a[2], 1), shift(low, a[2], -1), shift(high, a[2], -1))
-        for low, high, a in zip(lows, highs, axes)
-    ]
+    cur = lax.optimization_barrier([jnp.stack(p) for p in near])
+    ahead = [shift(b, a[1], 1) for b, a in zip(cur, axes)]
+    rest = [[shift(b, a[1], by) for by in (-1, 2)] for b, a in zip(cur, axes)]
+    lows = [jnp.concatenate([b, n], 0) for b, n in zip(cur, ahead)]
+    lows = lax.optimization_barrier(lows)
+    low_near = [(shift(b, a[2], 1), shift(b, a[2], -1)) for b, a in zip(lows, axes)]
+    highs = [jnp.concatenate(p, 0) for p in rest]
+    highs = lax.optimization_barrier(highs)
+    high_near = [(shift(b, a[2], 1), shift(b, a[2], -1)) for b, a in zip(highs, axes)]
+    near = [(l[0], h[0], l[1], h[1]) for l, h in zip(low_near, high_near)]
     far = [(shift(t[0], a[2], 1), shift(t[3], a[2], -1)) for t, a in zip(near, axes)]
     return [
         {0: own, 1: t[:2], 2: t[2:], 3: o} for own, t, o in zip(zip(lows, highs), near, far)
@@ -384,7 +388,8 @@
     partial, gate_raw, up_raw = lax.optimization_barrier((partial, gate_weight.T, up_weight.T))
     terms = lax.all_to_all(partial, HEAD, 0, 0, tiled=True)
     km, ks, sm, ss = prepare(pos2, gate_raw, up_raw, norm_gain[None, :])
-    terms, weights = lax.optimization_barrier((terms, (km, ks, swap_core(sm), swap_core(ss))))
+    weights = [jnp.concatenate([k, swap_core(t)], 1) for k, t in ((km, sm), (ks, ss))]
+    terms, weights = lax.optimization_barrier((terms, weights))
     hidden = (residual.astype(F32) + jnp.sum(terms.astype(F32), axis=0)).astype(BF)
 
     keep = jnp.where(core == 0, hidden[:, :512], hidden[:, 512:])

time: 204 us -> 186 us (0.912); the launches traced: 201 us -> 185 us
  Pallas kernels: 63.9 us -> 43.3 us
  other arithmetic: 3.75 us -> 10.5 us
  waiting for transfers between devices: 67.8 us -> 65.7 us
    pallas_call x3, Pallas kernels: 44.5 us -> 26.7 us  [gate_up(): pl.pallas_call(functools.partial(gate_kernel, which, first, last), out_sh...]
    all_to_all x1, waiting for transfers between devices: 24.2 us -> 17.4 us  [per_device(): terms = lax.all_to_all(partial, HEAD, 0, 0, tiled=True)]
    concatenate x2 -> x6, other arithmetic: 0.44 us -> 7.13 us  [the longest x2 6.68 us: per_device(): jnp.concatenate([k, swap_core(t)], 1)]
    ppermute x24, starting transfers between devices: 26 us -> 31.8 us  [shift(): return lax.ppermute(x, MESH, pairs)]
    ppermute x5, starting transfers between devices: 12.1 us -> 7.27 us  [swap_core(): return lax.ppermute(x, 'c', [(0, 1), (1, 0)])]
    ppermute x24, waiting for transfers between devices: 35.4 us -> 40.2 us  [shift(): return lax.ppermute(x, MESH, pairs)]
    pallas_call x1, Pallas kernels: 4.56 us -> 1.58 us  [finish(): pl.pallas_call(functools.partial(finish_kernel, depth=depth), out_shape=j...]
  transfers between devices with their start and end apart: 30 -> 30, of which waited for: 14 -> 14; matrix products, arithmetic and copies ran while one was open for 0% -> 4% of each run, Pallas kernels for 15% -> 11%
where the time goes in v2:
time: 186 us; the launch traced here: 185 us
  waiting for transfers between devices  65.7 us (35%)
  starting transfers between devices  44.1 us (24%)
  Pallas kernels  43.3 us (23%)
  blocking collectives  18 us (10%)
  other arithmetic  10.5 us (6%)
  local copies, waits for them, and re-layouts  2.62 us (1%)
    ppermute x24, waiting for transfers between devices, shift(): return lax.ppermute(x, MESH, pairs)  40.2 us
    ppermute x24, starting transfers between devices, shift(): return lax.ppermute(x, MESH, pairs)  31.8 us
    pallas_call x3, Pallas kernels, gate_up(): pl.pallas_call(functools.partial(gate_kernel, which, first, last), out_sh...  26.7 us
    all_to_all x1, blocking collectives, per_device(): own = lax.all_to_all(spread, ('y', 'xh'), 0, 0, tiled=True)  18 us
    all_to_all x1, waiting for transfers between devices, per_device(): terms = lax.all_to_all(partial, HEAD, 0, 0, tiled=True)  17.4 us
    pallas_call x1, Pallas kernels, attend_project(): pl.pallas_call(attend_kernel, out_shape=jax.ShapeDtypeStruct((blocks, row...  9.34 us
    ppermute x5, waiting for transfers between devices, swap_core(): return lax.ppermute(x, 'c', [(0, 1), (1, 0)])  8.11 us
    ppermute x5, starting transfers between devices, swap_core(): return lax.ppermute(x, 'c', [(0, 1), (1, 0)])  7.27 us
  transfers between devices with their start and end apart: 30, of which 14 were waited for; matrix products, arithmetic and copies ran while one was open for 4% of the time, Pallas kernels for 11%

profile of v2, /device:TPU:1, one launch (start us, length us, event | category | flops | bytes accessed | tf_op | source)
XLA Modules:
  0.0 185.3 jit_solution(7190508513163449099)
XLA Ops:
  0.6 0.8 pad_maximum_fusion.8
  1.5 18.0 %all_to_all.10.own_ref = bf16[8,128,256]{2,1,0:T(8,128)(2,1)S(1)} all-to-all(bf16[8,128,256]{2,1,0:T(8,128)(2,1)S(1)} %broadcast_in_dim.4), channel_id=1, replica_groups=mesh['y'=4,'xh'=2,'c'=2,'z'=4,'xl'=2] {'y','xh'}, dimensions={0} | all-to-all | bytes 1048576 | tf_op jit(solution)/shard_map/all_to_all | solution.py:382
  19.4 1.8 collective-permute-start
  21.4 1.4 collective-permute-done.oth_ref
  22.8 0.9 copy-done.3
  23.8 9.3 %attend_project.1 = bf16[8,128,1024]{2,1,0:T(8,128)(2,1)} custom-call(s32[2]{0:T(128)S(1)} %pad_add_fusion.1.pos_ref, bf16[128,1024]{1,0:T(8,128)(2,1)S(1)} %copy-done.3, bf16[8,128,256]{2,1,0:T(8,128)(2,1)S(1)} %all_to_all.10.own_ref, bf16[8,128,256]{2,1,0:T(8,128)(2,1)S(1)} %collective-permute-done.oth_ref, bf16[1024,8192]{1,0:T(8,128)(2,1)} %w_hbm.1), custom_call_target="tpu_custom_call" | custom-call | flops 4294967296 | bytes 20971520 | tf_op jit(solution)/shard_map/attend_project/pallas_call | solution.py:111
  33.1 5.7 %prepare.1 = (bf16[2,448,1536]{2,1,0:T(8,128)(2,1)S(1)}, bf16[4,448,256]{2,1,0:T(8,128)(2,1)S(1)}, bf16[2,448,1536]{2,1,0:T(8,128)(2,1)}, bf16[4,448,256]{2,1,0:T(8,128)(2,1)S(1)}) custom-call(s32[4]{0:T(128)S(1)} %pad_add_fusion.pos_ref, bf16[224,8192]{1,0:T(8,128)(2,1)S(1)} %bitcast.19, bf16[224,8192]{1,0:T(8,128)(2,1)S(1)} %bitcast.20, f32[1,8192]{1,0:T(1,128)S(1)} %bitcast.21), custom_call_target="tpu_custom_call" | custom-call | flops 8388608 | bytes 15728640 | tf_op jit(solution)/shard_map/prepare/pallas_call | solution.py:152
  38.8 1.6 copy-done.2
  40.4 0.4 collective-permute-start.1
  40.7 5.1 %all-to-all-start.1 = ((bf16[8,128,1024]{2,1,0:T(8,128)(2,1)}), bf16[8,128,1024]{2,1,0:T(8,128)(2,1)}, u32[]{:S(2)}, u32[]{:S(2)}) async-start(bf16[8,128,1024]{2,1,0:T(8,128)(2,1)} %attend_project.1), calls=%async_computation.1 | async-start | bytes 4194304 | tf_op jit(solution)/shard_map/all_to_all | solution.py:389
  45.8 0.4 collective-permute-start.2
  46.2 2.2 %collective-permute-done.2 = bf16[4,448,256]{2,1,0:T(8,128)(2,1)} collective-permute-done((bf16[4,448,256]{2,1,0:T(8,128)(2,1)S(1)}, bf16[4,448,256]{2,1,0:T(8,128)(2,1)}, u32[]{:S(2)}, u32[]{:S(2)}) %collective-permute-start.2) | collective-permute-done | bytes 917536 | tf_op jit(solution)/shard_map/ppermute | solution.py:41
  48.5 1.3 pad_maximum_fusion.1.refs_5_.refs_9_
  49.8 5.4 %pad_maximum_fusion.refs_4_.refs_8_ = bf16[2,896,1536]{2,1,0:T(8,128)(2,1)} fusion(bf16[2,448,1536]{2,1,0:T(8,128)(2,1)} %collective-permute-done.1, bf16[2,448,1536]{2,1,0:T(8,128)(2,1)} %copy-done.2), kind=kLoop, calls=%fused_computation | loop fusion | flops 11010048 | bytes 11010048 | tf_op jit(solution)/shard_map/concatenate | solution.py:391
  55.2 17.4 %all-to-all-done.1 = bf16[8,128,1024]{2,1,0:T(8,128)(2,1)} async-done(((bf16[8,128,1024]{2,1,0:T(8,128)(2,1)}), bf16[8,128,1024]{2,1,0:T(8,128)(2,1)}, u32[]{:S(2)}, u32[]{:S(2)}) %all-to-all-start.1) | async-done | bytes 2097184 | tf_op jit(solution)/shard_map/all_to_all | solution.py:389
  72.6 2.2 %convert_reduce_fusion = f32[128,1024]{1,0:T(8,128)S(1)} fusion(bf16[8,128,1024]{2,1,0:T(8,128)(2,1)} %all-to-all-done.1), kind=kLoop, calls=%fused_computation.1 | loop fusion | flops 1966080 | bytes 2621440 | tf_op jit(solution)/shard_map/reduce_sum | solution.py:393
  74.8 1.4 collective-permute-start.3
  76.2 1.0 collective-permute-done.3
  77.4 2.7 %collective-permute-start.5 = (bf16[256,384]{1,0:T(8,128)(2,1)S(1)}, bf16[256,384]{1,0:T(8,128)(2,1)S(1)}, u32[]{:S(2)}, u32[]{:S(2)}) collective-permute-start(bf16[256,384]{1,0:T(8,128)(2,1)S(1)} %slice.20), channel_id=1, source_target_pairs={{0,96},{2,98},{4,100},{6,102},{32,0},{34,2},{36,4},{38,6},{64,32},... | collective-permute-start | bytes 589832 | tf_op jit(solution)/shard_map/ppermute | solution.py:37
  80.0 0.6 collective-permute-start.7
  80.6 2.1 %collective-permute-start.8 = (bf16[256,128]{1,0:T(8,128)(2,1)S(1)}, bf16[256,128]{1,0:T(8,128)(2,1)S(1)}, u32[]{:S(2)}, u32[]{:S(2)}) collective-permute-start(bf16[256,128]{1,0:T(8,128)(2,1)S(1)} %slice.21), channel_id=1, source_target_pairs={{0,17},{2,19},{4,21},{6,23},{32,49},{34,51},{36,53},{38,55},{64,81... | collective-permute-start | bytes 196616 | tf_op jit(solution)/shard_map/ppermute | solution.py:37
  82.8 1.6 collective-permute-done.7
  84.7 4.3 %collective-permute-done.9 = bf16[256,128]{1,0:T(8,128)(2,1)S(1)} collective-permute-done((bf16[256,128]{1,0:T(8,128)(2,1)S(1)}, bf16[256,128]{1,0:T(8,128)(2,1)S(1)}, u32[]{:S(2)}, u32[]{:S(2)}) %collective-permute-start.9) | collective-permute-done | bytes 65568 | tf_op jit(solution)/shard_map/ppermute | solution.py:37
  89.3 0.4 collective-permute-start.14
  89.6 1.1 collective-permute-start.15
  90.7 0.3 collective-permute-start.11
  91.0 3.3 %collective-permute-start.16 = (bf16[4,256,128]{2,1,0:T(8,128)(2,1)S(1)}, bf16[4,256,128]{2,1,0:T(8,128)(2,1)S(1)}, u32[]{:S(2)}, u32[]{:S(2)}) collective-permute-start(bf16[4,256,128]{2,1,0:T(8,128)(2,1)S(1)} %pad_maximum_fusion.7), channel_id=1, source_target_pairs={{0,96},{2,98},{4,100},{6,102},{32,0},{34,2},{36,4},{38,6},{64,32},... | collective-permute-start | bytes 786440 | tf_op jit(solution)/shard_map/ppermute | solution.py:37
  94.4 3.0 %collective-permute-done.11 = bf16[4,256,128]{2,1,0:T(8,128)(2,1)S(1)} collective-permute-done((bf16[4,256,128]{2,1,0:T(8,128)(2,1)S(1)}, bf16[4,256,128]{2,1,0:T(8,128)(2,1)S(1)}, u32[]{:S(2)}, u32[]{:S(2)}) %collective-permute-start.11) | collective-permute-done | bytes 262176 | tf_op jit(solution)/shard_map/ppermute | solution.py:37
  97.3 0.7 collective-permute-start.17
  98.2 7.4 %collective-permute-done.17 = bf16[4,256,128]{2,1,0:T(8,128)(2,1)S(1)} collective-permute-done((bf16[4,256,128]{2,1,0:T(8,128)(2,1)S(1)}, bf16[4,256,128]{2,1,0:T(8,128)(2,1)S(1)}, u32[]{:S(2)}, u32[]{:S(2)}) %collective-permute-start.17) | collective-permute-done | bytes 262176 | tf_op jit(solution)/shard_map/ppermute | solution.py:37
  105.8 4.9 %collective-permute-done.10 = bf16[4,256,384]{2,1,0:T(8,128)(2,1)S(1)} collective-permute-done((bf16[4,256,384]{2,1,0:T(8,128)(2,1)S(1)}, bf16[4,256,384]{2,1,0:T(8,128)(2,1)S(1)}, u32[]{:S(2)}, u32[]{:S(2)}) %collective-permute-start.10) | collective-permute-done | bytes 786464 | tf_op jit(solution)/shard_map/ppermute | solution.py:37
  110.9 3.3 %collective-permute-start.18 = (bf16[8,256,384]{2,1,0:T(8,128)(2,1)S(1)}, bf16[8,256,384]{2,1,0:T(8,128)(2,1)S(1)}, u32[]{:S(2)}, u32[]{:S(2)}) collective-permute-start(bf16[8,256,384]{2,1,0:T(8,128)(2,1)S(1)} %pad_maximum_fusion.3.refs_1_), channel_id=1, source_target_pairs={{0,17},{2,19},{4,21},{6,23},{32,49},{34,51},{36,53},{38,55},{64,81... | collective-permute-start | bytes 4718600 | tf_op jit(solution)/shard_map/ppermute | solution.py:37
  114.2 1.5 collective-permute-start.22
  115.7 7.7 %collective-permute-done.22.refs_7_ = bf16[8,256,128]{2,1,0:T(8,128)(2,1)S(1)} collective-permute-done((bf16[8,256,128]{2,1,0:T(8,128)(2,1)S(1)}, bf16[8,256,128]{2,1,0:T(8,128)(2,1)S(1)}, u32[]{:S(2)}, u32[]{:S(2)}) %collective-permute-start.22) | collective-permute-done | bytes 524320 | tf_op jit(solution)/shard_map/ppermute | solution.py:37
  123.4 4.5 %collective-permute-start.25 = (bf16[8,256,384]{2,1,0:T(8,128)(2,1)S(1)}, bf16[8,256,384]{2,1,0:T(8,128)(2,1)S(1)}, u32[]{:S(2)}, u32[]{:S(2)}) collective-permute-start(bf16[8,256,384]{2,1,0:T(8,128)(2,1)S(1)} %pad_maximum_fusion.2.refs_0_), channel_id=1, source_target_pairs={{0,17},{2,19},{4,21},{6,23},{32,49},{34,51},{36,53},{38,55},{64,81... | collective-permute-start | bytes 4718600 | tf_op jit(solution)/shard_map/ppermute | solution.py:37
  127.9 0.6 collective-permute-start.20
  128.5 3.1 %collective-permute-done.18.refs_3_ = bf16[8,256,384]{2,1,0:T(8,128)(2,1)S(1)} collective-permute-done((bf16[8,256,384]{2,1,0:T(8,128)(2,1)S(1)}, bf16[8,256,384]{2,1,0:T(8,128)(2,1)S(1)}, u32[]{:S(2)}, u32[]{:S(2)}) %collective-permute-start.18) | collective-permute-done | bytes 1572896 | tf_op jit(solution)/shard_map/ppermute | solution.py:37
  131.5 3.4 %collective-permute-start.19 = (bf16[8,256,384]{2,1,0:T(8,128)(2,1)S(1)}, bf16[8,256,384]{2,1,0:T(8,128)(2,1)S(1)}, u32[]{:S(2)}, u32[]{:S(2)}) collective-permute-start(bf16[8,256,384]{2,1,0:T(8,128)(2,1)S(1)} %collective-permute-done.18.refs_3_), channel_id=1, source_target_pairs={{0,17},{2,19},{4,21},{6,23},{32,49},{34,51},{36,53},{38,55},{64,81... | collective-permute-start | bytes 4718600 | tf_op jit(solution)/shard_map/ppermute | solution.py:37
  134.9 5.7 %collective-permute-done.20.refs_4_ = bf16[8,256,128]{2,1,0:T(8,128)(2,1)S(1)} collective-permute-done((bf16[8,256,128]{2,1,0:T(8,128)(2,1)S(1)}, bf16[8,256,128]{2,1,0:T(8,128)(2,1)S(1)}, u32[]{:S(2)}, u32[]{:S(2)}) %collective-permute-start.20) | collective-permute-done | bytes 524320 | tf_op jit(solution)/shard_map/ppermute | solution.py:37
  140.7 3.5 %collective-permute-start.27 = (bf16[8,256,128]{2,1,0:T(8,128)(2,1)S(1)}, bf16[8,256,128]{2,1,0:T(8,128)(2,1)S(1)}, u32[]{:S(2)}, u32[]{:S(2)}) collective-permute-start(bf16[8,256,128]{2,1,0:T(8,128)(2,1)S(1)} %pad_maximum_fusion.5.refs_2_), channel_id=1, source_target_pairs={{0,6},{2,0},{4,2},{6,4},{32,38},{34,32},{36,34},{38,36},{64,70},{6... | collective-permute-start | bytes 1572872 | tf_op jit(solution)/shard_map/ppermute | solution.py:37
  144.2 7.4 %gate_up.3.refs_10_ = f32[904,2048]{1,0:T(8,128)S(1)} custom-call(s32[4]{0:T(128)S(1)} %pad_add_fusion.pos_ref, bf16[8,256,384]{2,1,0:T(8,128)(2,1)S(1)} %pad_maximum_fusion.2.refs_0_, bf16[8,256,384]{2,1,0:T(8,128)(2,1)S(1)} %pad_maximum_fusion.3.refs_1_, bf16[8,256,128]{2,1,0:T(8,128)(2,1)S(1)} %pad_maximum_fusion.5.refs_2_, ...), custom_call_target="tpu_custom_call" | custom-call | flops 3758096384 | bytes 20971520 | tf_op jit(solution)/shard_map/gate_up/pallas_call | solution.py:292
  151.6 2.4 %collective-permute-done.27.refs_6_ = bf16[8,256,128]{2,1,0:T(8,128)(2,1)S(1)} collective-permute-done((bf16[8,256,128]{2,1,0:T(8,128)(2,1)S(1)}, bf16[8,256,128]{2,1,0:T(8,128)(2,1)S(1)}, u32[]{:S(2)}, u32[]{:S(2)}) %collective-permute-start.27) | collective-permute-done | bytes 524320 | tf_op jit(solution)/shard_map/ppermute | solution.py:37
  154.0 3.4 %collective-permute-start.23 = (bf16[8,256,128]{2,1,0:T(8,128)(2,1)S(1)}, bf16[8,256,128]{2,1,0:T(8,128)(2,1)S(1)}, u32[]{:S(2)}, u32[]{:S(2)}) collective-permute-start(bf16[8,256,128]{2,1,0:T(8,128)(2,1)S(1)} %collective-permute-done.22.refs_7_), channel_id=1, source_target_pairs={{0,6},{2,0},{4,2},{6,4},{32,38},{34,32},{36,34},{38,36},{64,70},{6... | collective-permute-start | bytes 1572872 | tf_op jit(solution)/shard_map/ppermute | solution.py:37
  157.5 12.3 %gate_up.4.refs_6_ = f32[904,2048]{1,0:T(8,128)S(1)} custom-call(s32[4]{0:T(128)S(1)} %pad_add_fusion.pos_ref, bf16[8,256,384]{2,1,0:T(8,128)(2,1)S(1)} %collective-permute-done.12.refs_0_, bf16[8,256,384]{2,1,0:T(8,128)(2,1)S(1)} %collective-permute-done.24.refs_1_, ...), custom_call_target="tpu_custom_call", output_to_operand_aliasing={{}: (11, {})} | custom-call | flops 7516192768 | bytes 20971520 | tf_op jit(solution)/shard_map/gate_up/pallas_call | solution.py:292
  169.8 7.0 %gate_up.5 = (f32[448,2048]{1,0:T(8,128)S(1)}, f32[8,2048]{1,0:T(8,128)S(1)}, bf16[464,2048]{1,0:T(8,128)(2,1)S(1)}) custom-call(s32[4]{0:T(128)S(1)} %pad_add_fusion.pos_ref, bf16[8,256,384]{2,1,0:T(8,128)(2,1)S(1)} %collective-permute-done.13.refs_0_, bf16[8,256,384]{2,1,0:T(8,128)(2,1)S(1)} %collective-permute-done.19.refs_1_, ...), custom_call_target="tpu_custom_call" | custom-call | flops 3758096384 | bytes 20971520 | tf_op jit(solution)/shard_map/gate_up/pallas_call | solution.py:292
  176.8 3.3 %collective-permute-start.28 = (bf16[464,2048]{1,0:T(8,128)(2,1)S(1)}, bf16[464,2048]{1,0:T(8,128)(2,1)S(1)}, u32[]{:S(2)}, u32[]{:S(2)}) collective-permute-start(bf16[464,2048]{1,0:T(8,128)(2,1)S(1)} %get-tuple-element.55), channel_id=1, source_target_pairs={{0,8},{8,0},{1,9},{9,1},{2,10},{10,2},{3,11},{11,3},{4,12},{12,4},... | collective-permute-start | bytes 5701640 | tf_op jit(solution)/shard_map/ppermute | solution.py:41
  180.1 3.5 %collective-permute-done.28.got_ref = bf16[464,2048]{1,0:T(8,128)(2,1)S(1)} collective-permute-done((bf16[464,2048]{1,0:T(8,128)(2,1)S(1)}, bf16[464,2048]{1,0:T(8,128)(2,1)S(1)}, u32[]{:S(2)}, u32[]{:S(2)}) %collective-permute-start.28) | collective-permute-done | bytes 1900576 | tf_op jit(solution)/shard_map/ppermute | solution.py:41
  183.6 1.6 finish.1
  (56 shorter events, 1.4 us)
Async XLA Ops:
  19.4 3.3 %collective-permute-start = (bf16[8,128,256]{2,1,0:T(8,128)(2,1)S(1)}, bf16[8,128,256]{2,1,0:T(8,128)(2,1)S(1)}, u32[]{:S(2)}, u32[]{:S(2)}) collective-permute-start(bf16[8,128,256]{2,1,0:T(8,128)(2,1)S(1)} %all_to_all.10.own_ref), channel_id=1, source_target_pairs={{0,8},{8,0},{1,9},{9,1},{2,10},{10,2},{3,11},{11,3},{4,12},{12,4},... | collective-permute-start | bytes 1572872 | tf_op jit(solution)/shard_map/ppermute | solution.py:41
  22.8 0.9 copy-start.3
  23.7 9.4 %copy-start = (bf16[8192,224]{0,1:T(8,128)(2,1)S(1)}, bf16[8192,224]{0,1:T(8,128)(2,1)}, u32[]{:S(2)}) copy-start(bf16[8192,224]{0,1:T(8,128)(2,1)} %param.14) | copy-start | bytes 11010052
  23.7 9.4 %copy-start.1 = (bf16[8192,224]{0,1:T(8,128)(2,1)S(1)}, bf16[8192,224]{0,1:T(8,128)(2,1)}, u32[]{:S(2)}) copy-start(bf16[8192,224]{0,1:T(8,128)(2,1)} %param.15) | copy-start | bytes 11010052
  23.8 9.4 %copy-start.4 = (f32[8192]{0:T(1024)S(1)}, f32[8192]{0:T(1024)}, u32[]{:S(2)}) copy-start(f32[8192]{0:T(1024)} %param.13) | copy-start | bytes 98308
  38.8 1.6 copy-start.2
  40.4 9.4 %collective-permute-start.1 = (bf16[2,448,1536]{2,1,0:T(8,128)(2,1)}, bf16[2,448,1536]{2,1,0:T(8,128)(2,1)}, u32[]{:S(2)}, u32[]{:S(2)}) collective-permute-start(bf16[2,448,1536]{2,1,0:T(8,128)(2,1)} %get-tuple-element.33), channel_id=1, source_target_pairs={{0,8},{8,0},{1,9},{9,1},{2,10},{10,2},{3,11},{11,3},{4,12},{12,4},... | collective-permute-start | bytes 8257544 | tf_op jit(solution)/shard_map/ppermute | solution.py:41
  40.7 31.8 %all-to-all-start.1 = ((bf16[8,128,1024]{2,1,0:T(8,128)(2,1)}), bf16[8,128,1024]{2,1,0:T(8,128)(2,1)}, u32[]{:S(2)}, u32[]{:S(2)}) async-start(bf16[8,128,1024]{2,1,0:T(8,128)(2,1)} %attend_project.1), calls=%async_computation.1 | async-start | bytes 4194304 | tf_op jit(solution)/shard_map/all_to_all | solution.py:389
  45.8 2.6 %collective-permute-start.2 = (bf16[4,448,256]{2,1,0:T(8,128)(2,1)S(1)}, bf16[4,448,256]{2,1,0:T(8,128)(2,1)}, u32[]{:S(2)}, u32[]{:S(2)}) collective-permute-start(bf16[4,448,256]{2,1,0:T(8,128)(2,1)S(1)} %get-tuple-element.35), channel_id=1, source_target_pairs={{0,8},{8,0},{1,9},{9,1},{2,10},{10,2},{3,11},{11,3},{4,12},{12,4},... | collective-permute-start | bytes 2752520 | tf_op jit(solution)/shard_map/ppermute | solution.py:41
  55.1 19.6 %copy-start.6 = (bf16[128,1024]{1,0:T(8,128)(2,1)S(1)}, bf16[128,1024]{1,0:T(8,128)(2,1)}, u32[]{:S(2)}) copy-start(bf16[128,1024]{1,0:T(8,128)(2,1)} %param.12) | copy-start | bytes 786436
  72.6 71.6 %slice-start = ((s8[5505024]{0:T(1024)(128)(4,1)}), s8[4194304]{0:T(1024)(128)(4,1)S(1)}, s32[]{:S(2)}) async-start(s8[5505024]{0:T(1024)(128)(4,1)} %bitcast.17), calls=%async_computation.2 | async-start | bytes 8388608
  74.8 23.3 %copy-start.5 = (bf16[128,1024]{1,0:T(8,128)(2,1)}, bf16[128,1024]{1,0:T(8,128)(2,1)S(1)}, u32[]{:S(2)}) copy-start(bf16[128,1024]{1,0:T(8,128)(2,1)S(1)} %add_convert_fusion) | copy-start | bytes 786436
  74.8 2.3 %collective-permute-start.3 = (bf16[128,512]{1,0:T(8,128)(2,1)S(1)}, bf16[128,512]{1,0:T(8,128)(2,1)S(1)}, u32[]{:S(2)}, u32[]{:S(2)}) collective-permute-start(bf16[128,512]{1,0:T(8,128)(2,1)S(1)} %get-tuple-element.57), channel_id=1, source_target_pairs={{0,8},{8,0},{1,9},{9,1},{2,10},{10,2},{3,11},{11,3},{4,12},{12,4},... | collective-permute-start | bytes 393224 | tf_op jit(solution)/shard_map/ppermute | solution.py:41
  77.3 11.8 %collective-permute-start.4 = (bf16[256,384]{1,0:T(8,128)(2,1)S(1)}, bf16[256,384]{1,0:T(8,128)(2,1)S(1)}, u32[]{:S(2)}, u32[]{:S(2)}) collective-permute-start(bf16[256,384]{1,0:T(8,128)(2,1)S(1)} %slice.20), channel_id=1, source_target_pairs={{0,32},{2,34},{4,36},{6,38},{32,64},{34,66},{36,68},{38,70},{64,96... | collective-permute-start | bytes 589832 | tf_op jit(solution)/shard_map/ppermute | solution.py:37
  77.4 11.7 %collective-permute-start.5 = (bf16[256,384]{1,0:T(8,128)(2,1)S(1)}, bf16[256,384]{1,0:T(8,128)(2,1)S(1)}, u32[]{:S(2)}, u32[]{:S(2)}) collective-permute-start(bf16[256,384]{1,0:T(8,128)(2,1)S(1)} %slice.20), channel_id=1, source_target_pairs={{0,96},{2,98},{4,100},{6,102},{32,0},{34,2},{36,4},{38,6},{64,32},... | collective-permute-start | bytes 589832 | tf_op jit(solution)/shard_map/ppermute | solution.py:37
  80.0 9.0 %collective-permute-start.6 = (bf16[256,384]{1,0:T(8,128)(2,1)S(1)}, bf16[256,384]{1,0:T(8,128)(2,1)S(1)}, u32[]{:S(2)}, u32[]{:S(2)}) collective-permute-start(bf16[256,384]{1,0:T(8,128)(2,1)S(1)} %slice.20), channel_id=1, source_target_pairs={{0,64},{2,66},{4,68},{6,70},{32,96},{34,98},{36,100},{38,102},{64,... | collective-permute-start | bytes 589832 | tf_op jit(solution)/shard_map/ppermute | solution.py:37
  80.0 4.4 %collective-permute-start.7 = (bf16[256,128]{1,0:T(8,128)(2,1)S(1)}, bf16[256,128]{1,0:T(8,128)(2,1)S(1)}, u32[]{:S(2)}, u32[]{:S(2)}) collective-permute-start(bf16[256,128]{1,0:T(8,128)(2,1)S(1)} %slice.21), channel_id=1, source_target_pairs={{0,1},{2,3},{4,5},{6,7},{32,33},{34,35},{36,37},{38,39},{64,65},{6... | collective-permute-start | bytes 196616 | tf_op jit(solution)/shard_map/ppermute | solution.py:37
  80.6 4.1 %collective-permute-start.8 = (bf16[256,128]{1,0:T(8,128)(2,1)S(1)}, bf16[256,128]{1,0:T(8,128)(2,1)S(1)}, u32[]{:S(2)}, u32[]{:S(2)}) collective-permute-start(bf16[256,128]{1,0:T(8,128)(2,1)S(1)} %slice.21), channel_id=1, source_target_pairs={{0,17},{2,19},{4,21},{6,23},{32,49},{34,51},{36,53},{38,55},{64,81... | collective-permute-start | bytes 196616 | tf_op jit(solution)/shard_map/ppermute | solution.py:37
  84.4 4.6 %collective-permute-start.9 = (bf16[256,128]{1,0:T(8,128)(2,1)S(1)}, bf16[256,128]{1,0:T(8,128)(2,1)S(1)}, u32[]{:S(2)}, u32[]{:S(2)}) collective-permute-start(bf16[256,128]{1,0:T(8,128)(2,1)S(1)} %slice.21), channel_id=1, source_target_pairs={{0,16},{2,18},{4,20},{6,22},{32,48},{34,50},{36,52},{38,54},{64,80... | collective-permute-start | bytes 196616 | tf_op jit(solution)/shard_map/ppermute | solution.py:37
  89.2 54.9 %slice-start.1 = ((s8[5505024]{0:T(1024)(128)(4,1)}), s8[1310720]{0:T(1024)(128)(4,1)S(1)}, s32[]{:S(2)}) async-start(s8[5505024]{0:T(1024)(128)(4,1)} %bitcast.17), calls=%async_computation.3 | async-start | bytes 2621440
  89.3 16.3 %collective-permute-start.14 = (bf16[4,256,384]{2,1,0:T(8,128)(2,1)S(1)}, bf16[4,256,384]{2,1,0:T(8,128)(2,1)S(1)}, u32[]{:S(2)}, u32[]{:S(2)}) collective-permute-start(bf16[4,256,384]{2,1,0:T(8,128)(2,1)S(1)} %pad_maximum_fusion.4), channel_id=1, source_target_pairs={{0,6},{2,0},{4,2},{6,4},{32,38},{34,32},{36,34},{38,36},{64,70},{6... | collective-permute-start | bytes 2359304 | tf_op jit(solution)/shard_map/ppermute | solution.py:37
  89.6 16.0 %collective-permute-start.15 = (bf16[4,256,384]{2,1,0:T(8,128)(2,1)S(1)}, bf16[4,256,384]{2,1,0:T(8,128)(2,1)S(1)}, u32[]{:S(2)}, u32[]{:S(2)}) collective-permute-start(bf16[4,256,384]{2,1,0:T(8,128)(2,1)S(1)} %pad_maximum_fusion.4), channel_id=1, source_target_pairs={{0,4},{2,6},{4,0},{6,2},{32,36},{34,38},{36,32},{38,34},{64,68},{6... | collective-permute-start | bytes 2359304 | tf_op jit(solution)/shard_map/ppermute | solution.py:37
  90.7 6.6 %collective-permute-start.11 = (bf16[4,256,128]{2,1,0:T(8,128)(2,1)S(1)}, bf16[4,256,128]{2,1,0:T(8,128)(2,1)S(1)}, u32[]{:S(2)}, u32[]{:S(2)}) collective-permute-start(bf16[4,256,128]{2,1,0:T(8,128)(2,1)S(1)} %pad_maximum_fusion.7), channel_id=1, source_target_pairs={{0,32},{2,34},{4,36},{6,38},{32,64},{34,66},{36,68},{38,70},{64,96... | collective-permute-start | bytes 786440 | tf_op jit(solution)/shard_map/ppermute | solution.py:37
  91.0 19.6 %collective-permute-start.10 = (bf16[4,256,384]{2,1,0:T(8,128)(2,1)S(1)}, bf16[4,256,384]{2,1,0:T(8,128)(2,1)S(1)}, u32[]{:S(2)}, u32[]{:S(2)}) collective-permute-start(bf16[4,256,384]{2,1,0:T(8,128)(2,1)S(1)} %pad_maximum_fusion.4), channel_id=1, source_target_pairs={{0,2},{2,4},{4,6},{6,0},{32,34},{34,36},{36,38},{38,32},{64,66},{6... | collective-permute-start | bytes 2359304 | tf_op jit(solution)/shard_map/ppermute | solution.py:37
  91.0 7.1 %collective-permute-start.16 = (bf16[4,256,128]{2,1,0:T(8,128)(2,1)S(1)}, bf16[4,256,128]{2,1,0:T(8,128)(2,1)S(1)}, u32[]{:S(2)}, u32[]{:S(2)}) collective-permute-start(bf16[4,256,128]{2,1,0:T(8,128)(2,1)S(1)} %pad_maximum_fusion.7), channel_id=1, source_target_pairs={{0,96},{2,98},{4,100},{6,102},{32,0},{34,2},{36,4},{38,6},{64,32},... | collective-permute-start | bytes 786440 | tf_op jit(solution)/shard_map/ppermute | solution.py:37
  97.3 8.2 %collective-permute-start.17 = (bf16[4,256,128]{2,1,0:T(8,128)(2,1)S(1)}, bf16[4,256,128]{2,1,0:T(8,128)(2,1)S(1)}, u32[]{:S(2)}, u32[]{:S(2)}) collective-permute-start(bf16[4,256,128]{2,1,0:T(8,128)(2,1)S(1)} %pad_maximum_fusion.7), channel_id=1, source_target_pairs={{0,64},{2,66},{4,68},{6,70},{32,96},{34,98},{36,100},{38,102},{64,... | collective-permute-start | bytes 786440 | tf_op jit(solution)/shard_map/ppermute | solution.py:37
  110.9 20.6 %collective-permute-start.18 = (bf16[8,256,384]{2,1,0:T(8,128)(2,1)S(1)}, bf16[8,256,384]{2,1,0:T(8,128)(2,1)S(1)}, u32[]{:S(2)}, u32[]{:S(2)}) collective-permute-start(bf16[8,256,384]{2,1,0:T(8,128)(2,1)S(1)} %pad_maximum_fusion.3.refs_1_), channel_id=1, source_target_pairs={{0,17},{2,19},{4,21},{6,23},{32,49},{34,51},{36,53},{38,55},{64,81... | collective-permute-start | bytes 4718600 | tf_op jit(solution)/shard_map/ppermute | solution.py:37
  114.2 20.8 %collective-permute-start.12 = (bf16[8,256,384]{2,1,0:T(8,128)(2,1)S(1)}, bf16[8,256,384]{2,1,0:T(8,128)(2,1)S(1)}, u32[]{:S(2)}, u32[]{:S(2)}) collective-permute-start(bf16[8,256,384]{2,1,0:T(8,128)(2,1)S(1)} %pad_maximum_fusion.2.refs_0_), channel_id=1, source_target_pairs={{0,1},{2,3},{4,5},{6,7},{32,33},{34,35},{36,37},{38,39},{64,65},{6... | collective-permute-start | bytes 4718600 | tf_op jit(solution)/shard_map/ppermute | solution.py:37
  114.2 9.2 %collective-permute-start.22 = (bf16[8,256,128]{2,1,0:T(8,128)(2,1)S(1)}, bf16[8,256,128]{2,1,0:T(8,128)(2,1)S(1)}, u32[]{:S(2)}, u32[]{:S(2)}) collective-permute-start(bf16[8,256,128]{2,1,0:T(8,128)(2,1)S(1)} %pad_maximum_fusion.6.refs_3_), channel_id=1, source_target_pairs={{0,6},{2,0},{4,2},{6,4},{32,38},{34,32},{36,34},{38,36},{64,70},{6... | collective-permute-start | bytes 1572872 | tf_op jit(solution)/shard_map/ppermute | solution.py:37
  115.7 12.2 %collective-permute-start.26 = (bf16[8,256,128]{2,1,0:T(8,128)(2,1)S(1)}, bf16[8,256,128]{2,1,0:T(8,128)(2,1)S(1)}, u32[]{:S(2)}, u32[]{:S(2)}) collective-permute-start(bf16[8,256,128]{2,1,0:T(8,128)(2,1)S(1)} %pad_maximum_fusion.6.refs_3_), channel_id=1, source_target_pairs={{0,2},{2,4},{4,6},{6,0},{32,34},{34,36},{36,38},{38,32},{64,66},{6... | collective-permute-start | bytes 1572872 | tf_op jit(solution)/shard_map/ppermute | solution.py:37
  115.7 41.7 %collective-permute-start.24 = (bf16[8,256,384]{2,1,0:T(8,128)(2,1)S(1)}, bf16[8,256,384]{2,1,0:T(8,128)(2,1)S(1)}, u32[]{:S(2)}, u32[]{:S(2)}) collective-permute-start(bf16[8,256,384]{2,1,0:T(8,128)(2,1)S(1)} %pad_maximum_fusion.3.refs_1_), channel_id=1, source_target_pairs={{0,1},{2,3},{4,5},{6,7},{32,33},{34,35},{36,37},{38,39},{64,65},{6... | collective-permute-start | bytes 4718600 | tf_op jit(solution)/shard_map/ppermute | solution.py:37
  123.4 34.0 %collective-permute-start.25 = (bf16[8,256,384]{2,1,0:T(8,128)(2,1)S(1)}, bf16[8,256,384]{2,1,0:T(8,128)(2,1)S(1)}, u32[]{:S(2)}, u32[]{:S(2)}) collective-permute-start(bf16[8,256,384]{2,1,0:T(8,128)(2,1)S(1)} %pad_maximum_fusion.2.refs_0_), channel_id=1, source_target_pairs={{0,17},{2,19},{4,21},{6,23},{32,49},{34,51},{36,53},{38,55},{64,81... | collective-permute-start | bytes 4718600 | tf_op jit(solution)/shard_map/ppermute | solution.py:37
  127.9 12.8 %collective-permute-start.20 = (bf16[8,256,128]{2,1,0:T(8,128)(2,1)S(1)}, bf16[8,256,128]{2,1,0:T(8,128)(2,1)S(1)}, u32[]{:S(2)}, u32[]{:S(2)}) collective-permute-start(bf16[8,256,128]{2,1,0:T(8,128)(2,1)S(1)} %pad_maximum_fusion.5.refs_2_), channel_id=1, source_target_pairs={{0,2},{2,4},{4,6},{6,0},{32,34},{34,36},{36,38},{38,32},{64,66},{6... | collective-permute-start | bytes 1572872 | tf_op jit(solution)/shard_map/ppermute | solution.py:37
  131.5 38.2 %collective-permute-start.19 = (bf16[8,256,384]{2,1,0:T(8,128)(2,1)S(1)}, bf16[8,256,384]{2,1,0:T(8,128)(2,1)S(1)}, u32[]{:S(2)}, u32[]{:S(2)}) collective-permute-start(bf16[8,256,384]{2,1,0:T(8,128)(2,1)S(1)} %collective-permute-done.18.refs_3_), channel_id=1, source_target_pairs={{0,17},{2,19},{4,21},{6,23},{32,49},{34,51},{36,53},{38,55},{64,81... | collective-permute-start | bytes 4718600 | tf_op jit(solution)/shard_map/ppermute | solution.py:37
  134.9 34.8 %collective-permute-start.13 = (bf16[8,256,384]{2,1,0:T(8,128)(2,1)S(1)}, bf16[8,256,384]{2,1,0:T(8,128)(2,1)S(1)}, u32[]{:S(2)}, u32[]{:S(2)}) collective-permute-start(bf16[8,256,384]{2,1,0:T(8,128)(2,1)S(1)} %collective-permute-done.12.refs_0_), channel_id=1, source_target_pairs={{0,1},{2,3},{4,5},{6,7},{32,33},{34,35},{36,37},{38,39},{64,65},{6... | collective-permute-start | bytes 4718600 | tf_op jit(solution)/shard_map/ppermute | solution.py:37
  140.7 13.4 %collective-permute-start.27 = (bf16[8,256,128]{2,1,0:T(8,128)(2,1)S(1)}, bf16[8,256,128]{2,1,0:T(8,128)(2,1)S(1)}, u32[]{:S(2)}, u32[]{:S(2)}) collective-permute-start(bf16[8,256,128]{2,1,0:T(8,128)(2,1)S(1)} %pad_maximum_fusion.5.refs_2_), channel_id=1, source_target_pairs={{0,6},{2,0},{4,2},{6,4},{32,38},{34,32},{36,34},{38,36},{64,70},{6... | collective-permute-start | bytes 1572872 | tf_op jit(solution)/shard_map/ppermute | solution.py:37
  154.0 15.7 %collective-permute-start.23 = (bf16[8,256,128]{2,1,0:T(8,128)(2,1)S(1)}, bf16[8,256,128]{2,1,0:T(8,128)(2,1)S(1)}, u32[]{:S(2)}, u32[]{:S(2)}) collective-permute-start(bf16[8,256,128]{2,1,0:T(8,128)(2,1)S(1)} %collective-permute-done.22.refs_7_), channel_id=1, source_target_pairs={{0,6},{2,0},{4,2},{6,4},{32,38},{34,32},{36,34},{38,36},{64,70},{6... | collective-permute-start | bytes 1572872 | tf_op jit(solution)/shard_map/ppermute | solution.py:37
  157.4 12.3 %collective-permute-start.21 = (bf16[8,256,128]{2,1,0:T(8,128)(2,1)S(1)}, bf16[8,256,128]{2,1,0:T(8,128)(2,1)S(1)}, u32[]{:S(2)}, u32[]{:S(2)}) collective-permute-start(bf16[8,256,128]{2,1,0:T(8,128)(2,1)S(1)} %collective-permute-done.20.refs_4_), channel_id=1, source_target_pairs={{0,2},{2,4},{4,6},{6,0},{32,34},{34,36},{36,38},{38,32},{64,66},{6... | collective-permute-start | bytes 1572872 | tf_op jit(solution)/shard_map/ppermute | solution.py:37
  176.8 6.8 %collective-permute-start.28 = (bf16[464,2048]{1,0:T(8,128)(2,1)S(1)}, bf16[464,2048]{1,0:T(8,128)(2,1)S(1)}, u32[]{:S(2)}, u32[]{:S(2)}) collective-permute-start(bf16[464,2048]{1,0:T(8,128)(2,1)S(1)} %get-tuple-element.55), channel_id=1, source_target_pairs={{0,8},{8,0},{1,9},{9,1},{2,10},{10,2},{3,11},{11,3},{4,12},{12,4},... | collective-permute-start | bytes 5701640 | tf_op jit(solution)/shard_map/ppermute | solution.py:41

commit v3 on v2

--- a/solution.py
+++ b/solution.py
@@ -158,7 +158,7 @@
             in_specs=[wspec, wspec, pl.BlockSpec((1, 1024), lambda i, pos: (0, i))],
             out_specs=[mspec, sspec, mspec, sspec],
         ),
-        compiler_params=pltpu.CompilerParams(vmem_limit_bytes=16 << 20),
+        compiler_params=pltpu.CompilerParams(vmem_limit_bytes=58 << 20),
         cost_estimate=pl.CostEstimate(flops=8 << 20, bytes_accessed=15 << 20, transcendentals=0),
         name="prepare",
     )(pos, gate_t, up_t, gain)
@@ -358,12 +358,18 @@
     cur = lax.optimization_barrier([jnp.stack(p) for p in near])
     ahead = [shift(b, a[1], 1) for b, a in zip(cur, axes)]
     rest = [[shift(b, a[1], by) for by in (-1, 2)] for b, a in zip(cur, axes)]
-    lows = [jnp.concatenate([b, n], 0) for b, n in zip(cur, ahead)]
-    lows = lax.optimization_barrier(lows)
-    low_near = [(shift(b, a[2], 1), shift(b, a[2], -1)) for b, a in zip(lows, axes)]
+
+    def both_ways(block, a):
+        return shift(block, a[2], 1), shift(block, a[2], -1)
+
+    low = jnp.concatenate([cur[0], ahead[0]], 0)
+    low = lax.optimization_barrier(low)
+    first_near = both_ways(low, axes[0])
     highs = [jnp.concatenate(p, 0) for p in rest]
-    highs = lax.optimization_barrier(highs)
-    high_near = [(shift(b, a[2], 1), shift(b, a[2], -1)) for b, a in zip(highs, axes)]
+    highs, side_low = lax.optimization_barrier((highs, jnp.concatenate([cur[1], ahead[1]], 0)))
+    lows = [low, side_low]
+    low_near = [first_near, both_ways(side_low, axes[1])]
+    high_near = [both_ways(b, a) for b, a in zip(highs, axes)]
     near = [(l[0], h[0], l[1], h[1]) for l, h in zip(low_near, high_near)]
     far = [(shift(t[0], a[2], 1), shift(t[3], a[2], -1)) for t, a in zip(near, axes)]
     return [
@@ -379,15 +385,13 @@
 
     pair = jnp.concatenate([key_rows, value_rows], axis=1)
     spread = jnp.broadcast_to(pair[None], (8,) + pair.shape)
+    pos2 = jnp.stack([x_at, y_at, z_at, core]).astype(jnp.int32)
+    pos = jnp.stack([group, core]).astype(jnp.int32)
     own = lax.all_to_all(spread, ("y", "xh"), 0, 0, tiled=True)
+    km, ks, sm, ss = prepare(pos2, gate_weight.T, up_weight.T, norm_gain[None, :])
     oth = swap_core(own)
-
-    pos = jnp.stack([group, core]).astype(jnp.int32)
     partial = attend_project(pos, queries, own, oth, out_weight, 8)
-    pos2 = jnp.stack([x_at, y_at, z_at, core]).astype(jnp.int32)
-    partial, gate_raw, up_raw = lax.optimization_barrier((partial, gate_weight.T, up_weight.T))
     terms = lax.all_to_all(partial, HEAD, 0, 0, tiled=True)
-    km, ks, sm, ss = prepare(pos2, gate_raw, up_raw, norm_gain[None, :])
     weights = [jnp.concatenate([k, swap_core(t)], 1) for k, t in ((km, sm), (ks, ss))]
     terms, weights = lax.optimization_barrier((terms, weights))
     hidden = (residual.astype(F32) + jnp.sum(terms.astype(F32), axis=0)).astype(BF)

time: 186 us -> 188 us (1.011)
  the two profiles are of different devices: /device:TPU:1 before, /device:TPU:11 now
where the time goes in v3:
time: 188 us; the launch traced here: 187 us
  starting transfers between devices  64.6 us (34%)
  waiting for transfers between devices  63.4 us (34%)
  Pallas kernels  46.5 us (25%)
  other arithmetic  11.1 us (6%)
    ppermute x24, waiting for transfers between devices, shift(): return lax.ppermute(x, MESH, pairs)  35.4 us
    ppermute x24, starting transfers between devices, shift(): return lax.ppermute(x, MESH, pairs)  35.3 us
    pallas_call x3, Pallas kernels, gate_up(): pl.pallas_call(functools.partial(gate_kernel, which, first, last), out_sh...  26.7 us
    ppermute x5, starting transfers between devices, swap_core(): return lax.ppermute(x, 'c', [(0, 1), (1, 0)])  17 us
    all_to_all x1, waiting for transfers between devices, per_device(): terms = lax.all_to_all(partial, HEAD, 0, 0, tiled=True)  15.7 us
    ppermute x5, waiting for transfers between devices, swap_core(): return lax.ppermute(x, 'c', [(0, 1), (1, 0)])  12.2 us
    pallas_call x1, Pallas kernels, prepare(): pl.pallas_call(prep_kernel, out_shape=[mshape, sshape, mshape, sshape], g...  9.52 us
    pallas_call x1, Pallas kernels, attend_project(): pl.pallas_call(attend_kernel, out_shape=jax.ShapeDtypeStruct((blocks, row...  8.73 us
  transfers between devices with their start and end apart: 31, of which 17 were waited for; matrix products, arithmetic and copies ran while one was open for 4% of the time, Pallas kernels for 20%

profile of v3, /device:TPU:11, one launch (start us, length us, event | category | flops | bytes accessed | tf_op | source)
XLA Modules:
  0.0 187.5 jit_solution(10119666649368687088)
XLA Ops:
  1.4 0.8 broadcast_in_dim.4
  2.2 5.9 %all-to-all-start = ((bf16[8,128,256]{2,1,0:T(8,128)(2,1)}), bf16[8,128,256]{2,1,0:T(8,128)(2,1)S(1)}, u32[]{:S(2)}, u32[]{:S(2)}) async-start(bf16[8,128,256]{2,1,0:T(8,128)(2,1)} %broadcast_in_dim.4), calls=%async_computation | async-start | bytes 1048576 | tf_op jit(solution)/shard_map/all_to_all | solution.py:390
  8.8 9.5 %prepare.1 = (bf16[2,448,1536]{2,1,0:T(8,128)(2,1)}, bf16[4,448,256]{2,1,0:T(8,128)(2,1)}, bf16[2,448,1536]{2,1,0:T(8,128)(2,1)}, bf16[4,448,256]{2,1,0:T(8,128)(2,1)}) custom-call(s32[4]{0:T(128)} %pad_add_fusion.pos_ref, bf16[224,8192]{1,0:T(8,128)(2,1)} %bitcast.19, bf16[224,8192]{1,0:T(8,128)(2,1)} %bitcast.20, f32[1,8192]{1,0:T(1,128)} %bitcast.30), custom_call_target="tpu_custom_call" | custom-call | flops 8388608 | bytes 15728640 | tf_op jit(solution)/shard_map/prepare/pallas_call | solution.py:152
  18.3 1.2 collective-permute-start.1
  19.7 5.5 %collective-permute-done.oth_ref = bf16[8,128,256]{2,1,0:T(8,128)(2,1)S(1)} collective-permute-done((bf16[8,128,256]{2,1,0:T(8,128)(2,1)S(1)}, bf16[8,128,256]{2,1,0:T(8,128)(2,1)S(1)}, u32[]{:S(2)}, u32[]{:S(2)}) %collective-permute-start) | collective-permute-done | bytes 524320 | tf_op jit(solution)/shard_map/ppermute | solution.py:41
  25.2 8.7 %attend_project.1 = bf16[8,128,1024]{2,1,0:T(8,128)(2,1)} custom-call(s32[2]{0:T(128)S(1)} %pad_add_fusion.1.pos_ref, bf16[128,1024]{1,0:T(8,128)(2,1)S(1)} %copy-done, bf16[8,128,256]{2,1,0:T(8,128)(2,1)S(1)} %all-to-all-done.own_ref, bf16[8,128,256]{2,1,0:T(8,128)(2,1)S(1)} %collective-permute-done.oth_ref, bf16[1024,8192]{1,0:T(8,128)(2,1)} %w_hbm.1), custom_call_target="tpu_custom_call" | custom-call | flops 4294967296 | bytes 20971520 | tf_op jit(solution)/shard_map/attend_project/pallas_call | solution.py:111
  34.0 6.4 %all-to-all-start.1 = ((bf16[8,128,1024]{2,1,0:T(8,128)(2,1)}), bf16[8,128,1024]{2,1,0:T(8,128)(2,1)}, u32[]{:S(2)}, u32[]{:S(2)}) async-start(bf16[8,128,1024]{2,1,0:T(8,128)(2,1)} %attend_project.1), calls=%async_computation.1 | async-start | bytes 4194304 | tf_op jit(solution)/shard_map/all_to_all | solution.py:394
  40.3 0.9 collective-permute-start.2
  41.3 2.2 %collective-permute-done.2 = bf16[4,448,256]{2,1,0:T(8,128)(2,1)} collective-permute-done((bf16[4,448,256]{2,1,0:T(8,128)(2,1)S(1)}, bf16[4,448,256]{2,1,0:T(8,128)(2,1)}, u32[]{:S(2)}, u32[]{:S(2)}) %collective-permute-start.2) | collective-permute-done | bytes 917536 | tf_op jit(solution)/shard_map/ppermute | solution.py:41
  43.5 1.3 pad_maximum_fusion.1.refs_5_.refs_9_
  44.8 5.4 %pad_maximum_fusion.refs_4_.refs_8_ = bf16[2,896,1536]{2,1,0:T(8,128)(2,1)} fusion(bf16[2,448,1536]{2,1,0:T(8,128)(2,1)} %collective-permute-done.1, bf16[2,448,1536]{2,1,0:T(8,128)(2,1)} %get-tuple-element.25), kind=kLoop, calls=%fused_computation | loop fusion | flops 11010048 | bytes 11010048 | tf_op jit(solution)/shard_map/concatenate | solution.py:395
  50.2 15.7 %all-to-all-done.1 = bf16[8,128,1024]{2,1,0:T(8,128)(2,1)} async-done(((bf16[8,128,1024]{2,1,0:T(8,128)(2,1)}), bf16[8,128,1024]{2,1,0:T(8,128)(2,1)}, u32[]{:S(2)}, u32[]{:S(2)}) %all-to-all-start.1) | async-done | bytes 2097184 | tf_op jit(solution)/shard_map/all_to_all | solution.py:394
  65.9 2.2 %convert_reduce_fusion = f32[128,1024]{1,0:T(8,128)S(1)} fusion(bf16[8,128,1024]{2,1,0:T(8,128)(2,1)} %all-to-all-done.1), kind=kLoop, calls=%fused_computation.1 | loop fusion | flops 1966080 | bytes 2621440 | tf_op jit(solution)/shard_map/reduce_sum | solution.py:397
  68.2 1.6 collective-permute-start.3
  69.8 1.0 collective-permute-done.3
  71.2 2.4 %collective-permute-start.5 = (bf16[256,384]{1,0:T(8,128)(2,1)S(1)}, bf16[256,384]{1,0:T(8,128)(2,1)S(1)}, u32[]{:S(2)}, u32[]{:S(2)}) collective-permute-start(bf16[256,384]{1,0:T(8,128)(2,1)S(1)} %slice.20), channel_id=1, source_target_pairs={{0,96},{2,98},{4,100},{6,102},{32,0},{34,2},{36,4},{38,6},{64,32},... | collective-permute-start | bytes 589832 | tf_op jit(solution)/shard_map/ppermute | solution.py:37
  73.7 2.5 %collective-permute-start.7 = (bf16[256,128]{1,0:T(8,128)(2,1)S(1)}, bf16[256,128]{1,0:T(8,128)(2,1)S(1)}, u32[]{:S(2)}, u32[]{:S(2)}) collective-permute-start(bf16[256,128]{1,0:T(8,128)(2,1)S(1)} %slice.21), channel_id=1, source_target_pairs={{0,1},{2,3},{4,5},{6,7},{32,33},{34,35},{36,37},{38,39},{64,65},{6... | collective-permute-start | bytes 196616 | tf_op jit(solution)/shard_map/ppermute | solution.py:37
  76.2 1.3 collective-permute-done.7
  77.5 2.0 %collective-permute-start.9 = (bf16[256,128]{1,0:T(8,128)(2,1)S(1)}, bf16[256,128]{1,0:T(8,128)(2,1)S(1)}, u32[]{:S(2)}, u32[]{:S(2)}) collective-permute-start(bf16[256,128]{1,0:T(8,128)(2,1)S(1)} %slice.21), channel_id=1, source_target_pairs={{0,16},{2,18},{4,20},{6,22},{32,48},{34,50},{36,52},{38,54},{64,80... | collective-permute-start | bytes 196616 | tf_op jit(solution)/shard_map/ppermute | solution.py:37
  79.5 2.9 %collective-permute-done.9 = bf16[256,128]{1,0:T(8,128)(2,1)S(1)} collective-permute-done((bf16[256,128]{1,0:T(8,128)(2,1)S(1)}, bf16[256,128]{1,0:T(8,128)(2,1)S(1)}, u32[]{:S(2)}, u32[]{:S(2)}) %collective-permute-start.9) | collective-permute-done | bytes 65568 | tf_op jit(solution)/shard_map/ppermute | solution.py:37
  82.6 1.3 collective-permute-start.13
  83.9 1.7 collective-permute-start.14
  85.6 2.3 %collective-permute-start.17 = (bf16[4,256,128]{2,1,0:T(8,128)(2,1)S(1)}, bf16[4,256,128]{2,1,0:T(8,128)(2,1)S(1)}, u32[]{:S(2)}, u32[]{:S(2)}) collective-permute-start(bf16[4,256,128]{2,1,0:T(8,128)(2,1)S(1)} %pad_maximum_fusion.7), channel_id=1, source_target_pairs={{0,32},{2,34},{4,36},{6,38},{32,64},{34,66},{36,68},{38,70},{64,96... | collective-permute-start | bytes 786440 | tf_op jit(solution)/shard_map/ppermute | solution.py:37
  87.9 1.5 collective-permute-start.10
  89.4 1.9 collective-permute-done.17
  91.2 6.8 %collective-permute-start.16 = (bf16[4,256,128]{2,1,0:T(8,128)(2,1)S(1)}, bf16[4,256,128]{2,1,0:T(8,128)(2,1)S(1)}, u32[]{:S(2)}, u32[]{:S(2)}) collective-permute-start(bf16[4,256,128]{2,1,0:T(8,128)(2,1)S(1)} %pad_maximum_fusion.7), channel_id=1, source_target_pairs={{0,64},{2,66},{4,68},{6,70},{32,96},{34,98},{36,100},{38,102},{64,... | collective-permute-start | bytes 786440 | tf_op jit(solution)/shard_map/ppermute | solution.py:37
  98.1 5.0 %collective-permute-done.16 = bf16[4,256,128]{2,1,0:T(8,128)(2,1)S(1)} collective-permute-done((bf16[4,256,128]{2,1,0:T(8,128)(2,1)S(1)}, bf16[4,256,128]{2,1,0:T(8,128)(2,1)S(1)}, u32[]{:S(2)}, u32[]{:S(2)}) %collective-permute-start.16) | collective-permute-done | bytes 262176 | tf_op jit(solution)/shard_map/ppermute | solution.py:37
  103.1 1.3 collective-permute-done.14
  105.5 1.5 collective-permute-start.11
  107.0 0.9 collective-permute-start.20
  107.9 1.8 collective-permute-start.22
  109.7 3.2 %collective-permute-start.24 = (bf16[8,256,384]{2,1,0:T(8,128)(2,1)S(1)}, bf16[8,256,384]{2,1,0:T(8,128)(2,1)S(1)}, u32[]{:S(2)}, u32[]{:S(2)}) collective-permute-start(bf16[8,256,384]{2,1,0:T(8,128)(2,1)S(1)} %pad_maximum_fusion.3.refs_1_), channel_id=1, source_target_pairs={{0,1},{2,3},{4,5},{6,7},{32,33},{34,35},{36,37},{38,39},{64,65},{6... | collective-permute-start | bytes 4718600 | tf_op jit(solution)/shard_map/ppermute | solution.py:37
  112.9 5.4 %collective-permute-done.20.refs_4_ = bf16[8,256,128]{2,1,0:T(8,128)(2,1)S(1)} collective-permute-done((bf16[8,256,128]{2,1,0:T(8,128)(2,1)S(1)}, bf16[8,256,128]{2,1,0:T(8,128)(2,1)S(1)}, u32[]{:S(2)}, u32[]{:S(2)}) %collective-permute-start.20) | collective-permute-done | bytes 524320 | tf_op jit(solution)/shard_map/ppermute | solution.py:37
  118.2 1.4 collective-permute-start.25
  119.6 4.7 %collective-permute-done.18.refs_3_ = bf16[8,256,384]{2,1,0:T(8,128)(2,1)S(1)} collective-permute-done((bf16[8,256,384]{2,1,0:T(8,128)(2,1)S(1)}, bf16[8,256,384]{2,1,0:T(8,128)(2,1)S(1)}, u32[]{:S(2)}, u32[]{:S(2)}) %collective-permute-start.18) | collective-permute-done | bytes 1572896 | tf_op jit(solution)/shard_map/ppermute | solution.py:37
  124.4 3.1 %collective-permute-start.19 = (bf16[8,256,384]{2,1,0:T(8,128)(2,1)S(1)}, bf16[8,256,384]{2,1,0:T(8,128)(2,1)S(1)}, u32[]{:S(2)}, u32[]{:S(2)}) collective-permute-start(bf16[8,256,384]{2,1,0:T(8,128)(2,1)S(1)} %collective-permute-done.18.refs_3_), channel_id=1, source_target_pairs={{0,17},{2,19},{4,21},{6,23},{32,49},{34,51},{36,53},{38,55},{64,81... | collective-permute-start | bytes 4718600 | tf_op jit(solution)/shard_map/ppermute | solution.py:37
  127.4 1.0 collective-permute-done.11.refs_0_
  128.4 6.2 %collective-permute-done.26.refs_5_ = bf16[8,256,128]{2,1,0:T(8,128)(2,1)S(1)} collective-permute-done((bf16[8,256,128]{2,1,0:T(8,128)(2,1)S(1)}, bf16[8,256,128]{2,1,0:T(8,128)(2,1)S(1)}, u32[]{:S(2)}, u32[]{:S(2)}) %collective-permute-start.26) | collective-permute-done | bytes 524320 | tf_op jit(solution)/shard_map/ppermute | solution.py:37
  134.6 7.4 %gate_up.3.refs_10_ = f32[904,2048]{1,0:T(8,128)S(1)} custom-call(s32[4]{0:T(128)S(1)} %copy-done.1, bf16[8,256,384]{2,1,0:T(8,128)(2,1)S(1)} %pad_maximum_fusion.2.refs_0_, bf16[8,256,384]{2,1,0:T(8,128)(2,1)S(1)} %pad_maximum_fusion.3.refs_1_, bf16[8,256,128]{2,1,0:T(8,128)(2,1)S(1)} %pad_maximum_fusion.6.refs_2_, ...), custom_call_target="tpu_custom_call" | custom-call | flops 3758096384 | bytes 20971520 | tf_op jit(solution)/shard_map/gate_up/pallas_call | solution.py:292
  142.0 0.8 collective-permute-done.27.refs_6_
  143.6 1.7 collective-permute-done.24.refs_1_
  145.3 1.3 collective-permute-start.23
  146.6 12.3 %gate_up.4.refs_6_ = f32[904,2048]{1,0:T(8,128)S(1)} custom-call(s32[4]{0:T(128)S(1)} %copy-done.1, bf16[8,256,384]{2,1,0:T(8,128)(2,1)S(1)} %collective-permute-done.11.refs_0_, bf16[8,256,384]{2,1,0:T(8,128)(2,1)S(1)} %collective-permute-done.24.refs_1_, bf16[8,256,384]{2,1,0:T(8,128)(2,1)S(1)} %collective-permute-done.25.refs_2_, ...), custom_call_target="tpu_custom_call", output_to_operand_aliasing={{}: (11, {})} | custom-call | flops 7516192768 | bytes 20971520 | tf_op jit(solution)/shard_map/gate_up/pallas_call | solution.py:292
  158.9 3.2 %collective-permute-done.12.refs_0_ = bf16[8,256,384]{2,1,0:T(8,128)(2,1)S(1)} collective-permute-done((bf16[8,256,384]{2,1,0:T(8,128)(2,1)S(1)}, bf16[8,256,384]{2,1,0:T(8,128)(2,1)S(1)}, u32[]{:S(2)}, u32[]{:S(2)}) %collective-permute-start.12) | collective-permute-done | bytes 1572896 | tf_op jit(solution)/shard_map/ppermute | solution.py:37
  162.1 7.0 %gate_up.5 = (f32[448,2048]{1,0:T(8,128)S(1)}, f32[8,2048]{1,0:T(8,128)S(1)}, bf16[464,2048]{1,0:T(8,128)(2,1)S(1)}) custom-call(s32[4]{0:T(128)S(1)} %copy-done.1, bf16[8,256,384]{2,1,0:T(8,128)(2,1)S(1)} %collective-permute-done.12.refs_0_, bf16[8,256,384]{2,1,0:T(8,128)(2,1)S(1)} %collective-permute-done.19.refs_1_, ...), custom_call_target="tpu_custom_call" | custom-call | flops 3758096384 | bytes 20971520 | tf_op jit(solution)/shard_map/gate_up/pallas_call | solution.py:292
  169.1 13.1 %collective-permute-start.28 = (bf16[464,2048]{1,0:T(8,128)(2,1)S(1)}, bf16[464,2048]{1,0:T(8,128)(2,1)S(1)}, u32[]{:S(2)}, u32[]{:S(2)}) collective-permute-start(bf16[464,2048]{1,0:T(8,128)(2,1)S(1)} %get-tuple-element.47), channel_id=1, source_target_pairs={{0,8},{8,0},{1,9},{9,1},{2,10},{10,2},{3,11},{11,3},{4,12},{12,4},... | collective-permute-start | bytes 5701640 | tf_op jit(solution)/shard_map/ppermute | solution.py:41
  182.2 3.5 %collective-permute-done.28.got_ref = bf16[464,2048]{1,0:T(8,128)(2,1)S(1)} collective-permute-done((bf16[464,2048]{1,0:T(8,128)(2,1)S(1)}, bf16[464,2048]{1,0:T(8,128)(2,1)S(1)}, u32[]{:S(2)}, u32[]{:S(2)}) %collective-permute-start.28) | collective-permute-done | bytes 1900576 | tf_op jit(solution)/shard_map/ppermute | solution.py:41
  185.7 1.6 finish.1
  (55 shorter events, 4.1 us)
Async XLA Ops:
  2.2 17.3 %all-to-all-start = ((bf16[8,128,256]{2,1,0:T(8,128)(2,1)}), bf16[8,128,256]{2,1,0:T(8,128)(2,1)S(1)}, u32[]{:S(2)}, u32[]{:S(2)}) async-start(bf16[8,128,256]{2,1,0:T(8,128)(2,1)} %broadcast_in_dim.4), calls=%async_computation | async-start | bytes 1048576 | tf_op jit(solution)/shard_map/all_to_all | solution.py:390
  8.8 16.4 %copy-start = (bf16[128,1024]{1,0:T(8,128)(2,1)S(1)}, bf16[128,1024]{1,0:T(8,128)(2,1)}, u32[]{:S(2)}) copy-start(bf16[128,1024]{1,0:T(8,128)(2,1)} %q_ref.1) | copy-start | bytes 786436
  18.3 26.5 %collective-permute-start.1 = (bf16[2,448,1536]{2,1,0:T(8,128)(2,1)}, bf16[2,448,1536]{2,1,0:T(8,128)(2,1)}, u32[]{:S(2)}, u32[]{:S(2)}) collective-permute-start(bf16[2,448,1536]{2,1,0:T(8,128)(2,1)} %get-tuple-element.26), channel_id=1, source_target_pairs={{0,8},{8,0},{1,9},{9,1},{2,10},{10,2},{3,11},{11,3},{4,12},{12,4},... | collective-permute-start | bytes 8257544 | tf_op jit(solution)/shard_map/ppermute | solution.py:41
  19.5 5.7 %collective-permute-start = (bf16[8,128,256]{2,1,0:T(8,128)(2,1)S(1)}, bf16[8,128,256]{2,1,0:T(8,128)(2,1)S(1)}, u32[]{:S(2)}, u32[]{:S(2)}) collective-permute-start(bf16[8,128,256]{2,1,0:T(8,128)(2,1)S(1)} %all-to-all-done.own_ref), channel_id=1, source_target_pairs={{0,8},{8,0},{1,9},{9,1},{2,10},{10,2},{3,11},{11,3},{4,12},{12,4},... | collective-permute-start | bytes 1572872 | tf_op jit(solution)/shard_map/ppermute | solution.py:41
  33.9 6.4 %copy-start.5 = (bf16[4,448,256]{2,1,0:T(8,128)(2,1)S(1)}, bf16[4,448,256]{2,1,0:T(8,128)(2,1)}, u32[]{:S(2)}) copy-start(bf16[4,448,256]{2,1,0:T(8,128)(2,1)} %get-tuple-element.28) | copy-start | bytes 2752516
  34.0 9.5 %copy-start.3 = (bf16[4,448,256]{2,1,0:T(8,128)(2,1)S(1)}, bf16[4,448,256]{2,1,0:T(8,128)(2,1)}, u32[]{:S(2)}) copy-start(bf16[4,448,256]{2,1,0:T(8,128)(2,1)} %get-tuple-element.27) | copy-start | bytes 2752516
  34.0 32.0 %all-to-all-start.1 = ((bf16[8,128,1024]{2,1,0:T(8,128)(2,1)}), bf16[8,128,1024]{2,1,0:T(8,128)(2,1)}, u32[]{:S(2)}, u32[]{:S(2)}) async-start(bf16[8,128,1024]{2,1,0:T(8,128)(2,1)} %attend_project.1), calls=%async_computation.1 | async-start | bytes 4194304 | tf_op jit(solution)/shard_map/all_to_all | solution.py:394
  40.3 3.2 %collective-permute-start.2 = (bf16[4,448,256]{2,1,0:T(8,128)(2,1)S(1)}, bf16[4,448,256]{2,1,0:T(8,128)(2,1)}, u32[]{:S(2)}, u32[]{:S(2)}) collective-permute-start(bf16[4,448,256]{2,1,0:T(8,128)(2,1)S(1)} %copy-done.5), channel_id=1, source_target_pairs={{0,8},{8,0},{1,9},{9,1},{2,10},{10,2},{3,11},{11,3},{4,12},{12,4},... | collective-permute-start | bytes 2752520 | tf_op jit(solution)/shard_map/ppermute | solution.py:41
  50.2 17.9 %copy-start.4 = (bf16[128,1024]{1,0:T(8,128)(2,1)S(1)}, bf16[128,1024]{1,0:T(8,128)(2,1)}, u32[]{:S(2)}) copy-start(bf16[128,1024]{1,0:T(8,128)(2,1)} %param.12) | copy-start | bytes 786436
  65.9 68.7 %slice-start = ((s8[5505024]{0:T(1024)(128)(4,1)}), s8[4194304]{0:T(1024)(128)(4,1)S(1)}, s32[]{:S(2)}) async-start(s8[5505024]{0:T(1024)(128)(4,1)} %bitcast.17), calls=%async_computation.2 | async-start | bytes 8388608
  68.2 29.9 %copy-start.2 = (bf16[128,1024]{1,0:T(8,128)(2,1)}, bf16[128,1024]{1,0:T(8,128)(2,1)S(1)}, u32[]{:S(2)}) copy-start(bf16[128,1024]{1,0:T(8,128)(2,1)S(1)} %add_convert_fusion) | copy-start | bytes 786436
  68.2 2.6 %collective-permute-start.3 = (bf16[128,512]{1,0:T(8,128)(2,1)S(1)}, bf16[128,512]{1,0:T(8,128)(2,1)S(1)}, u32[]{:S(2)}, u32[]{:S(2)}) collective-permute-start(bf16[128,512]{1,0:T(8,128)(2,1)S(1)} %get-tuple-element.49), channel_id=1, source_target_pairs={{0,8},{8,0},{1,9},{9,1},{2,10},{10,2},{3,11},{11,3},{4,12},{12,4},... | collective-permute-start | bytes 393224 | tf_op jit(solution)/shard_map/ppermute | solution.py:41
  70.9 11.5 %collective-permute-start.4 = (bf16[256,384]{1,0:T(8,128)(2,1)S(1)}, bf16[256,384]{1,0:T(8,128)(2,1)S(1)}, u32[]{:S(2)}, u32[]{:S(2)}) collective-permute-start(bf16[256,384]{1,0:T(8,128)(2,1)S(1)} %slice.20), channel_id=1, source_target_pairs={{0,32},{2,34},{4,36},{6,38},{32,64},{34,66},{36,68},{38,70},{64,96... | collective-permute-start | bytes 589832 | tf_op jit(solution)/shard_map/ppermute | solution.py:37
  71.2 11.2 %collective-permute-start.5 = (bf16[256,384]{1,0:T(8,128)(2,1)S(1)}, bf16[256,384]{1,0:T(8,128)(2,1)S(1)}, u32[]{:S(2)}, u32[]{:S(2)}) collective-permute-start(bf16[256,384]{1,0:T(8,128)(2,1)S(1)} %slice.20), channel_id=1, source_target_pairs={{0,96},{2,98},{4,100},{6,102},{32,0},{34,2},{36,4},{38,6},{64,32},... | collective-permute-start | bytes 589832 | tf_op jit(solution)/shard_map/ppermute | solution.py:37
  73.6 8.8 %collective-permute-start.6 = (bf16[256,384]{1,0:T(8,128)(2,1)S(1)}, bf16[256,384]{1,0:T(8,128)(2,1)S(1)}, u32[]{:S(2)}, u32[]{:S(2)}) collective-permute-start(bf16[256,384]{1,0:T(8,128)(2,1)S(1)} %slice.20), channel_id=1, source_target_pairs={{0,64},{2,66},{4,68},{6,70},{32,96},{34,98},{36,100},{38,102},{64,... | collective-permute-start | bytes 589832 | tf_op jit(solution)/shard_map/ppermute | solution.py:37
  73.7 3.8 %collective-permute-start.7 = (bf16[256,128]{1,0:T(8,128)(2,1)S(1)}, bf16[256,128]{1,0:T(8,128)(2,1)S(1)}, u32[]{:S(2)}, u32[]{:S(2)}) collective-permute-start(bf16[256,128]{1,0:T(8,128)(2,1)S(1)} %slice.21), channel_id=1, source_target_pairs={{0,1},{2,3},{4,5},{6,7},{32,33},{34,35},{36,37},{38,39},{64,65},{6... | collective-permute-start | bytes 196616 | tf_op jit(solution)/shard_map/ppermute | solution.py:37
  76.2 3.4 %collective-permute-start.8 = (bf16[256,128]{1,0:T(8,128)(2,1)S(1)}, bf16[256,128]{1,0:T(8,128)(2,1)S(1)}, u32[]{:S(2)}, u32[]{:S(2)}) collective-permute-start(bf16[256,128]{1,0:T(8,128)(2,1)S(1)} %slice.21), channel_id=1, source_target_pairs={{0,17},{2,19},{4,21},{6,23},{32,49},{34,51},{36,53},{38,55},{64,81... | collective-permute-start | bytes 196616 | tf_op jit(solution)/shard_map/ppermute | solution.py:37
  77.5 4.9 %collective-permute-start.9 = (bf16[256,128]{1,0:T(8,128)(2,1)S(1)}, bf16[256,128]{1,0:T(8,128)(2,1)S(1)}, u32[]{:S(2)}, u32[]{:S(2)}) collective-permute-start(bf16[256,128]{1,0:T(8,128)(2,1)S(1)} %slice.21), channel_id=1, source_target_pairs={{0,16},{2,18},{4,20},{6,22},{32,48},{34,50},{36,52},{38,54},{64,80... | collective-permute-start | bytes 196616 | tf_op jit(solution)/shard_map/ppermute | solution.py:37
  82.6 52.0 %slice-start.1 = ((s8[5505024]{0:T(1024)(128)(4,1)}), s8[1310720]{0:T(1024)(128)(4,1)S(1)}, s32[]{:S(2)}) async-start(s8[5505024]{0:T(1024)(128)(4,1)} %bitcast.17), calls=%async_computation.3 | async-start | bytes 2621440
  82.6 20.5 %collective-permute-start.13 = (bf16[4,256,384]{2,1,0:T(8,128)(2,1)S(1)}, bf16[4,256,384]{2,1,0:T(8,128)(2,1)S(1)}, u32[]{:S(2)}, u32[]{:S(2)}) collective-permute-start(bf16[4,256,384]{2,1,0:T(8,128)(2,1)S(1)} %pad_maximum_fusion.4), channel_id=1, source_target_pairs={{0,6},{2,0},{4,2},{6,4},{32,38},{34,32},{36,34},{38,36},{64,70},{6... | collective-permute-start | bytes 2359304 | tf_op jit(solution)/shard_map/ppermute | solution.py:37
  83.9 20.5 %collective-permute-start.14 = (bf16[4,256,384]{2,1,0:T(8,128)(2,1)S(1)}, bf16[4,256,384]{2,1,0:T(8,128)(2,1)S(1)}, u32[]{:S(2)}, u32[]{:S(2)}) collective-permute-start(bf16[4,256,384]{2,1,0:T(8,128)(2,1)S(1)} %pad_maximum_fusion.4), channel_id=1, source_target_pairs={{0,4},{2,6},{4,0},{6,2},{32,36},{34,38},{36,32},{38,34},{64,68},{6... | collective-permute-start | bytes 2359304 | tf_op jit(solution)/shard_map/ppermute | solution.py:37
  85.6 5.6 %collective-permute-start.17 = (bf16[4,256,128]{2,1,0:T(8,128)(2,1)S(1)}, bf16[4,256,128]{2,1,0:T(8,128)(2,1)S(1)}, u32[]{:S(2)}, u32[]{:S(2)}) collective-permute-start(bf16[4,256,128]{2,1,0:T(8,128)(2,1)S(1)} %pad_maximum_fusion.7), channel_id=1, source_target_pairs={{0,32},{2,34},{4,36},{6,38},{32,64},{34,66},{36,68},{38,70},{64,96... | collective-permute-start | bytes 786440 | tf_op jit(solution)/shard_map/ppermute | solution.py:37
  87.9 17.4 %collective-permute-start.10 = (bf16[4,256,384]{2,1,0:T(8,128)(2,1)S(1)}, bf16[4,256,384]{2,1,0:T(8,128)(2,1)S(1)}, u32[]{:S(2)}, u32[]{:S(2)}) collective-permute-start(bf16[4,256,384]{2,1,0:T(8,128)(2,1)S(1)} %pad_maximum_fusion.4), channel_id=1, source_target_pairs={{0,2},{2,4},{4,6},{6,0},{32,34},{34,36},{36,38},{38,32},{64,66},{6... | collective-permute-start | bytes 2359304 | tf_op jit(solution)/shard_map/ppermute | solution.py:37
  89.4 8.7 %collective-permute-start.15 = (bf16[4,256,128]{2,1,0:T(8,128)(2,1)S(1)}, bf16[4,256,128]{2,1,0:T(8,128)(2,1)S(1)}, u32[]{:S(2)}, u32[]{:S(2)}) collective-permute-start(bf16[4,256,128]{2,1,0:T(8,128)(2,1)S(1)} %pad_maximum_fusion.7), channel_id=1, source_target_pairs={{0,96},{2,98},{4,100},{6,102},{32,0},{34,2},{36,4},{38,6},{64,32},... | collective-permute-start | bytes 786440 | tf_op jit(solution)/shard_map/ppermute | solution.py:37
  91.2 11.9 %collective-permute-start.16 = (bf16[4,256,128]{2,1,0:T(8,128)(2,1)S(1)}, bf16[4,256,128]{2,1,0:T(8,128)(2,1)S(1)}, u32[]{:S(2)}, u32[]{:S(2)}) collective-permute-start(bf16[4,256,128]{2,1,0:T(8,128)(2,1)S(1)} %pad_maximum_fusion.7), channel_id=1, source_target_pairs={{0,64},{2,66},{4,68},{6,70},{32,96},{34,98},{36,100},{38,102},{64,... | collective-permute-start | bytes 786440 | tf_op jit(solution)/shard_map/ppermute | solution.py:37
  104.6 30.0 %copy-start.1 = (s32[4]{0:T(128)S(1)}, s32[4]{0:T(128)}, u32[]{:S(2)}) copy-start(s32[4]{0:T(128)} %pad_add_fusion.pos_ref) | copy-start | bytes 52
  104.6 19.7 %collective-permute-start.18 = (bf16[8,256,384]{2,1,0:T(8,128)(2,1)S(1)}, bf16[8,256,384]{2,1,0:T(8,128)(2,1)S(1)}, u32[]{:S(2)}, u32[]{:S(2)}) collective-permute-start(bf16[8,256,384]{2,1,0:T(8,128)(2,1)S(1)} %pad_maximum_fusion.3.refs_1_), channel_id=1, source_target_pairs={{0,17},{2,19},{4,21},{6,23},{32,49},{34,51},{36,53},{38,55},{64,81... | collective-permute-start | bytes 4718600 | tf_op jit(solution)/shard_map/ppermute | solution.py:37
  105.5 22.9 %collective-permute-start.11 = (bf16[8,256,384]{2,1,0:T(8,128)(2,1)S(1)}, bf16[8,256,384]{2,1,0:T(8,128)(2,1)S(1)}, u32[]{:S(2)}, u32[]{:S(2)}) collective-permute-start(bf16[8,256,384]{2,1,0:T(8,128)(2,1)S(1)} %pad_maximum_fusion.2.refs_0_), channel_id=1, source_target_pairs={{0,1},{2,3},{4,5},{6,7},{32,33},{34,35},{36,37},{38,39},{64,65},{6... | collective-permute-start | bytes 4718600 | tf_op jit(solution)/shard_map/ppermute | solution.py:37
  107.0 11.2 %collective-permute-start.20 = (bf16[8,256,128]{2,1,0:T(8,128)(2,1)S(1)}, bf16[8,256,128]{2,1,0:T(8,128)(2,1)S(1)}, u32[]{:S(2)}, u32[]{:S(2)}) collective-permute-start(bf16[8,256,128]{2,1,0:T(8,128)(2,1)S(1)} %pad_maximum_fusion.6.refs_2_), channel_id=1, source_target_pairs={{0,2},{2,4},{4,6},{6,0},{32,34},{34,36},{36,38},{38,32},{64,66},{6... | collective-permute-start | bytes 1572872 | tf_op jit(solution)/shard_map/ppermute | solution.py:37
  107.9 11.8 %collective-permute-start.22 = (bf16[8,256,128]{2,1,0:T(8,128)(2,1)S(1)}, bf16[8,256,128]{2,1,0:T(8,128)(2,1)S(1)}, u32[]{:S(2)}, u32[]{:S(2)}) collective-permute-start(bf16[8,256,128]{2,1,0:T(8,128)(2,1)S(1)} %pad_maximum_fusion.5.refs_3_), channel_id=1, source_target_pairs={{0,6},{2,0},{4,2},{6,4},{32,38},{34,32},{36,34},{38,36},{64,70},{6... | collective-permute-start | bytes 1572872 | tf_op jit(solution)/shard_map/ppermute | solution.py:37
  109.7 35.6 %collective-permute-start.24 = (bf16[8,256,384]{2,1,0:T(8,128)(2,1)S(1)}, bf16[8,256,384]{2,1,0:T(8,128)(2,1)S(1)}, u32[]{:S(2)}, u32[]{:S(2)}) collective-permute-start(bf16[8,256,384]{2,1,0:T(8,128)(2,1)S(1)} %pad_maximum_fusion.3.refs_1_), channel_id=1, source_target_pairs={{0,1},{2,3},{4,5},{6,7},{32,33},{34,35},{36,37},{38,39},{64,65},{6... | collective-permute-start | bytes 4718600 | tf_op jit(solution)/shard_map/ppermute | solution.py:37
  118.2 28.4 %collective-permute-start.25 = (bf16[8,256,384]{2,1,0:T(8,128)(2,1)S(1)}, bf16[8,256,384]{2,1,0:T(8,128)(2,1)S(1)}, u32[]{:S(2)}, u32[]{:S(2)}) collective-permute-start(bf16[8,256,384]{2,1,0:T(8,128)(2,1)S(1)} %pad_maximum_fusion.2.refs_0_), channel_id=1, source_target_pairs={{0,17},{2,19},{4,21},{6,23},{32,49},{34,51},{36,53},{38,55},{64,81... | collective-permute-start | bytes 4718600 | tf_op jit(solution)/shard_map/ppermute | solution.py:37
  119.6 14.9 %collective-permute-start.26 = (bf16[8,256,128]{2,1,0:T(8,128)(2,1)S(1)}, bf16[8,256,128]{2,1,0:T(8,128)(2,1)S(1)}, u32[]{:S(2)}, u32[]{:S(2)}) collective-permute-start(bf16[8,256,128]{2,1,0:T(8,128)(2,1)S(1)} %pad_maximum_fusion.5.refs_3_), channel_id=1, source_target_pairs={{0,2},{2,4},{4,6},{6,0},{32,34},{34,36},{36,38},{38,32},{64,66},{6... | collective-permute-start | bytes 1572872 | tf_op jit(solution)/shard_map/ppermute | solution.py:37
  124.4 34.5 %collective-permute-start.19 = (bf16[8,256,384]{2,1,0:T(8,128)(2,1)S(1)}, bf16[8,256,384]{2,1,0:T(8,128)(2,1)S(1)}, u32[]{:S(2)}, u32[]{:S(2)}) collective-permute-start(bf16[8,256,384]{2,1,0:T(8,128)(2,1)S(1)} %collective-permute-done.18.refs_3_), channel_id=1, source_target_pairs={{0,17},{2,19},{4,21},{6,23},{32,49},{34,51},{36,53},{38,55},{64,81... | collective-permute-start | bytes 4718600 | tf_op jit(solution)/shard_map/ppermute | solution.py:37
  128.4 33.7 %collective-permute-start.12 = (bf16[8,256,384]{2,1,0:T(8,128)(2,1)S(1)}, bf16[8,256,384]{2,1,0:T(8,128)(2,1)S(1)}, u32[]{:S(2)}, u32[]{:S(2)}) collective-permute-start(bf16[8,256,384]{2,1,0:T(8,128)(2,1)S(1)} %collective-permute-done.11.refs_0_), channel_id=1, source_target_pairs={{0,1},{2,3},{4,5},{6,7},{32,33},{34,35},{36,37},{38,39},{64,65},{6... | collective-permute-start | bytes 4718600 | tf_op jit(solution)/shard_map/ppermute | solution.py:37
  134.6 8.3 %collective-permute-start.27 = (bf16[8,256,128]{2,1,0:T(8,128)(2,1)S(1)}, bf16[8,256,128]{2,1,0:T(8,128)(2,1)S(1)}, u32[]{:S(2)}, u32[]{:S(2)}) collective-permute-start(bf16[8,256,128]{2,1,0:T(8,128)(2,1)S(1)} %pad_maximum_fusion.6.refs_2_), channel_id=1, source_target_pairs={{0,6},{2,0},{4,2},{6,4},{32,38},{34,32},{36,34},{38,36},{64,70},{6... | collective-permute-start | bytes 1572872 | tf_op jit(solution)/shard_map/ppermute | solution.py:37
  142.9 16.0 %collective-permute-start.21 = (bf16[8,256,128]{2,1,0:T(8,128)(2,1)S(1)}, bf16[8,256,128]{2,1,0:T(8,128)(2,1)S(1)}, u32[]{:S(2)}, u32[]{:S(2)}) collective-permute-start(bf16[8,256,128]{2,1,0:T(8,128)(2,1)S(1)} %collective-permute-done.20.refs_4_), channel_id=1, source_target_pairs={{0,2},{2,4},{4,6},{6,0},{32,34},{34,36},{36,38},{38,32},{64,66},{6... | collective-permute-start | bytes 1572872 | tf_op jit(solution)/shard_map/ppermute | solution.py:37
  145.3 13.6 %collective-permute-start.23 = (bf16[8,256,128]{2,1,0:T(8,128)(2,1)S(1)}, bf16[8,256,128]{2,1,0:T(8,128)(2,1)S(1)}, u32[]{:S(2)}, u32[]{:S(2)}) collective-permute-start(bf16[8,256,128]{2,1,0:T(8,128)(2,1)S(1)} %collective-permute-done.22.refs_7_), channel_id=1, source_target_pairs={{0,6},{2,0},{4,2},{6,4},{32,38},{34,32},{36,34},{38,36},{64,70},{6... | collective-permute-start | bytes 1572872 | tf_op jit(solution)/shard_map/ppermute | solution.py:37
  169.1 16.6 %collective-permute-start.28 = (bf16[464,2048]{1,0:T(8,128)(2,1)S(1)}, bf16[464,2048]{1,0:T(8,128)(2,1)S(1)}, u32[]{:S(2)}, u32[]{:S(2)}) collective-permute-start(bf16[464,2048]{1,0:T(8,128)(2,1)S(1)} %get-tuple-element.47), channel_id=1, source_target_pairs={{0,8},{8,0},{1,9},{9,1},{2,10},{10,2},{3,11},{11,3},{4,12},{12,4},... | collective-permute-start | bytes 5701640 | tf_op jit(solution)/shard_map/ppermute | solution.py:41

commit v4 on v2

--- a/solution.py
+++ b/solution.py
@@ -167,7 +167,7 @@
 def gate_kernel(which, first, last, pos_ref, *refs):
     count = len(which)
     refs = list(refs)
-    main = {c: (refs.pop(0), refs.pop(0)) for c in which}
+    main = {c: tuple(refs.pop(0) for _ in range(3)) for c in which}
     side = {c: (refs.pop(0), refs.pop(0)) for c in which}
     wm, ws = refs.pop(0), refs.pop(0)
     before = None if first else refs.pop(0)
@@ -188,9 +188,8 @@
         for k in range(4):
             a, b = (j, k) if on == 0 else (k, j)
             col = pl.multiple_of(at(z_at, k) * MCOLS, MCOLS)
-            pltpu.make_async_copy(
-                main[c][b // 2].at[(b % 2) * 4 + a], hm.at[u, :, pl.ds(col, MCOLS)], msem.at[u]
-            ).start()
+            src = main[c][max(b - 1, 0)].at[(b % 2) * 4 + a if b < 2 else a]
+            pltpu.make_async_copy(src, hm.at[u, :, pl.ds(col, MCOLS)], msem.at[u]).start()
 
     for m, c in enumerate(which):
         for j in range(4):
@@ -358,17 +357,38 @@
     cur = lax.optimization_barrier([jnp.stack(p) for p in near])
     ahead = [shift(b, a[1], 1) for b, a in zip(cur, axes)]
     rest = [[shift(b, a[1], by) for by in (-1, 2)] for b, a in zip(cur, axes)]
-    lows = [jnp.concatenate([b, n], 0) for b, n in zip(cur, ahead)]
-    lows = lax.optimization_barrier(lows)
-    low_near = [(shift(b, a[2], 1), shift(b, a[2], -1)) for b, a in zip(lows, axes)]
-    highs = [jnp.concatenate(p, 0) for p in rest]
-    highs = lax.optimization_barrier(highs)
-    high_near = [(shift(b, a[2], 1), shift(b, a[2], -1)) for b, a in zip(highs, axes)]
-    near = [(l[0], h[0], l[1], h[1]) for l, h in zip(low_near, high_near)]
-    far = [(shift(t[0], a[2], 1), shift(t[3], a[2], -1)) for t, a in zip(near, axes)]
-    return [
-        {0: own, 1: t[:2], 2: t[2:], 3: o} for own, t, o in zip(zip(lows, highs), near, far)
-    ]
+
+    def both_ways(block, a):
+        return shift(block, a[2], 1), shift(block, a[2], -1)
+
+    low = jnp.concatenate([cur[0], ahead[0]], 0)
+    low = lax.optimization_barrier(low)
+    third, fourth = rest[0]
+    lows = both_ways(low, axes[0])
+    thirds = both_ways(third, axes[0])
+    fourths = both_ways(fourth, axes[0])
+    side_low = jnp.concatenate([cur[1], ahead[1]], 0)
+    side_high = jnp.concatenate(rest[1], 0)
+    side_low, side_high = lax.optimization_barrier((side_low, side_high))
+    side_lows = both_ways(side_low, axes[1])
+    side_highs = both_ways(side_high, axes[1])
+    far_low = shift(lows[0], axes[0][2], 1)
+    far_side = (shift(side_lows[0], axes[1][2], 1), shift(side_highs[1], axes[1][2], -1))
+    far_third = shift(thirds[1], axes[0][2], -1)
+    far_fourth = shift(fourths[1], axes[0][2], -1)
+    main = {
+        0: (low, third, fourth),
+        1: (lows[0], thirds[0], fourths[0]),
+        2: (lows[1], thirds[1], fourths[1]),
+        3: (far_low, far_third, far_fourth),
+    }
+    side = {
+        0: (side_low, side_high),
+        1: (side_lows[0], side_highs[0]),
+        2: (side_lows[1], side_highs[1]),
+        3: far_side,
+    }
+    return main, side
 
 
 def per_device(queries, key_rows, value_rows, out_weight, residual, norm_gain, gate_weight, up_weight):

time: 186 us -> 210 us (1.13)
  waiting for transfers between devices: 65.7 us -> 78.3 us
  starting transfers between devices: 44.1 us -> 56.2 us
    ppermute x24 -> x27, waiting for transfers between devices: 40.2 us -> 53.3 us  [shift(): return lax.ppermute(x, MESH, pairs)]
    ppermute x24 -> x27, starting transfers between devices: 31.8 us -> 40.3 us  [shift(): return lax.ppermute(x, MESH, pairs)]
    ppermute x5, starting transfers between devices: 7.27 us -> 10.9 us  [swap_core(): return lax.ppermute(x, 'c', [(0, 1), (1, 0)])]
  transfers between devices with their start and end apart: 30 -> 33, of which waited for: 14 -> 17; matrix products, arithmetic and copies ran while one was open for 4% -> 3% of each run, Pallas kernels for 11% -> 9%
where the time goes in v4:
time: 210 us
  waiting for transfers between devices  78.3 us (37%)
  starting transfers between devices  56.2 us (27%)
  Pallas kernels  42.4 us (20%)
  blocking collectives  18 us (9%)
  other arithmetic  10.2 us (5%)
  local copies, waits for them, and re-layouts  3.24 us (2%)
    ppermute x27, waiting for transfers between devices, shift(): return lax.ppermute(x, MESH, pairs)  53.3 us
    ppermute x27, starting transfers between devices, shift(): return lax.ppermute(x, MESH, pairs)  40.3 us
    pallas_call x3, Pallas kernels, gate_up(): pl.pallas_call(functools.partial(gate_kernel, which, first, last), out_sh...  26.3 us
    all_to_all x1, blocking collectives, per_device(): own = lax.all_to_all(spread, ('y', 'xh'), 0, 0, tiled=True)  18 us
    all_to_all x1, waiting for transfers between devices, per_device(): terms = lax.all_to_all(partial, HEAD, 0, 0, tiled=True)  17 us
    ppermute x5, starting transfers between devices, swap_core(): return lax.ppermute(x, 'c', [(0, 1), (1, 0)])  10.9 us
    pallas_call x1, Pallas kernels, attend_project(): pl.pallas_call(attend_kernel, out_shape=jax.ShapeDtypeStruct((blocks, row...  8.88 us
    ppermute x5, waiting for transfers between devices, swap_core(): return lax.ppermute(x, 'c', [(0, 1), (1, 0)])  8.11 us
  transfers between devices with their start and end apart: 33, of which 17 were waited for; matrix products, arithmetic and copies ran while one was open for 3% of the time, Pallas kernels for 9%

profile of v4, /device:TPU:1, one launch (start us, length us, event | category | flops | bytes accessed | tf_op | source)
XLA Modules:
  0.0 209.5 jit_solution(9440318343046336895)
XLA Ops:
  0.6 0.8 pad_maximum_fusion.7
  1.5 18.0 %all_to_all.10.own_ref = bf16[8,128,256]{2,1,0:T(8,128)(2,1)S(1)} all-to-all(bf16[8,128,256]{2,1,0:T(8,128)(2,1)S(1)} %broadcast_in_dim.4), channel_id=1, replica_groups=mesh['y'=4,'xh'=2,'c'=2,'z'=4,'xl'=2] {'y','xh'}, dimensions={0} | all-to-all | bytes 1048576 | tf_op jit(solution)/shard_map/all_to_all | solution.py:402
  19.4 1.8 collective-permute-start
  21.4 1.4 collective-permute-done.oth_ref
  22.8 1.6 copy-done.4
  24.4 8.9 %attend_project.1 = bf16[8,128,1024]{2,1,0:T(8,128)(2,1)} custom-call(s32[2]{0:T(128)S(1)} %pad_add_fusion.1.pos_ref, bf16[128,1024]{1,0:T(8,128)(2,1)S(1)} %copy-done.4, bf16[8,128,256]{2,1,0:T(8,128)(2,1)S(1)} %all_to_all.10.own_ref, bf16[8,128,256]{2,1,0:T(8,128)(2,1)S(1)} %collective-permute-done.oth_ref, bf16[1024,8192]{1,0:T(8,128)(2,1)} %w_hbm.1), custom_call_target="tpu_custom_call" | custom-call | flops 4294967296 | bytes 20971520 | tf_op jit(solution)/shard_map/attend_project/pallas_call | solution.py:111
  33.3 5.7 %prepare.1 = (bf16[2,448,1536]{2,1,0:T(8,128)(2,1)S(1)}, bf16[4,448,256]{2,1,0:T(8,128)(2,1)S(1)}, bf16[2,448,1536]{2,1,0:T(8,128)(2,1)}, bf16[4,448,256]{2,1,0:T(8,128)(2,1)S(1)}) custom-call(s32[4]{0:T(128)S(1)} %pad_add_fusion.pos_ref, bf16[224,8192]{1,0:T(8,128)(2,1)S(1)} %bitcast.17, bf16[224,8192]{1,0:T(8,128)(2,1)S(1)} %bitcast.18, f32[1,8192]{1,0:T(1,128)S(1)} %bitcast.19), custom_call_target="tpu_custom_call" | custom-call | flops 8388608 | bytes 15728640 | tf_op jit(solution)/shard_map/prepare/pallas_call | solution.py:152
  39.0 1.6 copy-done.3
  40.7 5.1 %all-to-all-start.1 = ((bf16[8,128,1024]{2,1,0:T(8,128)(2,1)}), bf16[8,128,1024]{2,1,0:T(8,128)(2,1)}, u32[]{:S(2)}, u32[]{:S(2)}) async-start(bf16[8,128,1024]{2,1,0:T(8,128)(2,1)} %attend_project.1), calls=%async_computation.1 | async-start | bytes 4194304 | tf_op jit(solution)/shard_map/all_to_all | solution.py:409
  45.7 0.6 collective-permute-start.2
  46.4 2.2 %collective-permute-done.2 = bf16[4,448,256]{2,1,0:T(8,128)(2,1)} collective-permute-done((bf16[4,448,256]{2,1,0:T(8,128)(2,1)S(1)}, bf16[4,448,256]{2,1,0:T(8,128)(2,1)}, u32[]{:S(2)}, u32[]{:S(2)}) %collective-permute-start.2) | collective-permute-done | bytes 917536 | tf_op jit(solution)/shard_map/ppermute | solution.py:41
  48.6 1.3 pad_maximum_fusion.1.refs_6_.refs_11_
  49.9 5.4 %pad_maximum_fusion.refs_5_.refs_10_ = bf16[2,896,1536]{2,1,0:T(8,128)(2,1)} fusion(bf16[2,448,1536]{2,1,0:T(8,128)(2,1)} %collective-permute-done.1, bf16[2,448,1536]{2,1,0:T(8,128)(2,1)} %copy-done.3), kind=kLoop, calls=%fused_computation | loop fusion | flops 11010048 | bytes 11010048 | tf_op jit(solution)/shard_map/concatenate | solution.py:411
  55.3 17.0 %all-to-all-done.1 = bf16[8,128,1024]{2,1,0:T(8,128)(2,1)} async-done(((bf16[8,128,1024]{2,1,0:T(8,128)(2,1)}), bf16[8,128,1024]{2,1,0:T(8,128)(2,1)}, u32[]{:S(2)}, u32[]{:S(2)}) %all-to-all-start.1) | async-done | bytes 2097184 | tf_op jit(solution)/shard_map/all_to_all | solution.py:409
  72.3 2.0 convert_reduce_fusion
  74.4 1.6 collective-permute-start.3
  76.0 1.0 collective-permute-done.3
  77.2 2.7 %collective-permute-start.5 = (bf16[256,384]{1,0:T(8,128)(2,1)S(1)}, bf16[256,384]{1,0:T(8,128)(2,1)S(1)}, u32[]{:S(2)}, u32[]{:S(2)}) collective-permute-start(bf16[256,384]{1,0:T(8,128)(2,1)S(1)} %slice.20), channel_id=1, source_target_pairs={{0,96},{2,98},{4,100},{6,102},{32,0},{34,2},{36,4},{38,6},{64,32},... | collective-permute-start | bytes 589832 | tf_op jit(solution)/shard_map/ppermute | solution.py:37
  80.4 2.1 %collective-permute-start.8 = (bf16[256,128]{1,0:T(8,128)(2,1)S(1)}, bf16[256,128]{1,0:T(8,128)(2,1)S(1)}, u32[]{:S(2)}, u32[]{:S(2)}) collective-permute-start(bf16[256,128]{1,0:T(8,128)(2,1)S(1)} %slice.21), channel_id=1, source_target_pairs={{0,17},{2,19},{4,21},{6,23},{32,49},{34,51},{36,53},{38,55},{64,81... | collective-permute-start | bytes 196616 | tf_op jit(solution)/shard_map/ppermute | solution.py:37
  82.6 1.6 collective-permute-done.7
  84.5 4.4 %collective-permute-done.9 = bf16[256,128]{1,0:T(8,128)(2,1)S(1)} collective-permute-done((bf16[256,128]{1,0:T(8,128)(2,1)S(1)}, bf16[256,128]{1,0:T(8,128)(2,1)S(1)}, u32[]{:S(2)}, u32[]{:S(2)}) %collective-permute-start.9) | collective-permute-done | bytes 65568 | tf_op jit(solution)/shard_map/ppermute | solution.py:37
  89.2 3.6 %collective-permute-start.20 = (bf16[4,256,128]{2,1,0:T(8,128)(2,1)S(1)}, bf16[4,256,128]{2,1,0:T(8,128)(2,1)S(1)}, u32[]{:S(2)}, u32[]{:S(2)}) collective-permute-start(bf16[4,256,128]{2,1,0:T(8,128)(2,1)S(1)} %pad_maximum_fusion.6), channel_id=1, source_target_pairs={{0,96},{2,98},{4,100},{6,102},{32,0},{34,2},{36,4},{38,6},{64,32},... | collective-permute-start | bytes 786440 | tf_op jit(solution)/shard_map/ppermute | solution.py:37
  92.8 1.1 collective-permute-start.21
  93.9 2.6 %collective-permute-start.13 = (bf16[4,256,384]{2,1,0:T(8,128)(2,1)S(1)}, bf16[4,256,384]{2,1,0:T(8,128)(2,1)S(1)}, u32[]{:S(2)}, u32[]{:S(2)}) collective-permute-start(bf16[4,256,384]{2,1,0:T(8,128)(2,1)S(1)} %pad_maximum_fusion.3), channel_id=1, source_target_pairs={{0,6},{2,0},{4,2},{6,4},{32,38},{34,32},{36,34},{38,36},{64,70},{6... | collective-permute-start | bytes 2359304 | tf_op jit(solution)/shard_map/ppermute | solution.py:37
  96.5 5.2 %collective-permute-done.10 = bf16[4,256,384]{2,1,0:T(8,128)(2,1)S(1)} collective-permute-done((bf16[4,256,384]{2,1,0:T(8,128)(2,1)S(1)}, bf16[4,256,384]{2,1,0:T(8,128)(2,1)S(1)}, u32[]{:S(2)}, u32[]{:S(2)}) %collective-permute-start.10) | collective-permute-done | bytes 786464 | tf_op jit(solution)/shard_map/ppermute | solution.py:37
  102.5 0.8 collective-permute-done.21
  103.3 2.4 %collective-permute-start.22 = (bf16[8,256,128]{2,1,0:T(8,128)(2,1)S(1)}, bf16[8,256,128]{2,1,0:T(8,128)(2,1)S(1)}, u32[]{:S(2)}, u32[]{:S(2)}) collective-permute-start(bf16[8,256,128]{2,1,0:T(8,128)(2,1)S(1)} %pad_maximum_fusion.4.refs_3_), channel_id=1, source_target_pairs={{0,2},{2,4},{4,6},{6,0},{32,34},{34,36},{36,38},{38,32},{64,66},{6... | collective-permute-start | bytes 1572872 | tf_op jit(solution)/shard_map/ppermute | solution.py:37
  106.1 7.8 %collective-permute-done.13.refs_1_ = bf16[4,256,384]{2,1,0:T(8,128)(2,1)S(1)} collective-permute-done((bf16[4,256,384]{2,1,0:T(8,128)(2,1)S(1)}, bf16[4,256,384]{2,1,0:T(8,128)(2,1)S(1)}, u32[]{:S(2)}, u32[]{:S(2)}) %collective-permute-start.13) | collective-permute-done | bytes 786464 | tf_op jit(solution)/shard_map/ppermute | solution.py:37
  113.9 0.9 collective-permute-start.29
  114.8 3.6 %collective-permute-done.16.refs_2_ = bf16[4,256,384]{2,1,0:T(8,128)(2,1)S(1)} collective-permute-done((bf16[4,256,384]{2,1,0:T(8,128)(2,1)S(1)}, bf16[4,256,384]{2,1,0:T(8,128)(2,1)S(1)}, u32[]{:S(2)}, u32[]{:S(2)}) %collective-permute-start.16) | collective-permute-done | bytes 786464 | tf_op jit(solution)/shard_map/ppermute | solution.py:37
  118.4 0.7 collective-permute-start.30
  119.7 5.3 %collective-permute-start.14 = (bf16[4,256,384]{2,1,0:T(8,128)(2,1)S(1)}, bf16[4,256,384]{2,1,0:T(8,128)(2,1)S(1)}, u32[]{:S(2)}, u32[]{:S(2)}) collective-permute-start(bf16[4,256,384]{2,1,0:T(8,128)(2,1)S(1)} %collective-permute-done.13.refs_1_), channel_id=1, source_target_pairs={{0,17},{2,19},{4,21},{6,23},{32,49},{34,51},{36,53},{38,55},{64,81... | collective-permute-start | bytes 2359304 | tf_op jit(solution)/shard_map/ppermute | solution.py:37
  125.1 3.3 %collective-permute-start.28 = (bf16[8,256,384]{2,1,0:T(8,128)(2,1)S(1)}, bf16[8,256,384]{2,1,0:T(8,128)(2,1)S(1)}, u32[]{:S(2)}, u32[]{:S(2)}) collective-permute-start(bf16[8,256,384]{2,1,0:T(8,128)(2,1)S(1)} %pad_maximum_fusion.2.refs_0_), channel_id=1, source_target_pairs={{0,17},{2,19},{4,21},{6,23},{32,49},{34,51},{36,53},{38,55},{64,81... | collective-permute-start | bytes 4718600 | tf_op jit(solution)/shard_map/ppermute | solution.py:37
  128.3 5.0 %collective-permute-done.29.refs_7_ = bf16[8,256,128]{2,1,0:T(8,128)(2,1)S(1)} collective-permute-done((bf16[8,256,128]{2,1,0:T(8,128)(2,1)S(1)}, bf16[8,256,128]{2,1,0:T(8,128)(2,1)S(1)}, u32[]{:S(2)}, u32[]{:S(2)}) %collective-permute-start.29) | collective-permute-done | bytes 524320 | tf_op jit(solution)/shard_map/ppermute | solution.py:37
  133.3 3.8 %collective-permute-start.17 = (bf16[4,256,384]{2,1,0:T(8,128)(2,1)S(1)}, bf16[4,256,384]{2,1,0:T(8,128)(2,1)S(1)}, u32[]{:S(2)}, u32[]{:S(2)}) collective-permute-start(bf16[4,256,384]{2,1,0:T(8,128)(2,1)S(1)} %collective-permute-done.16.refs_2_), channel_id=1, source_target_pairs={{0,17},{2,19},{4,21},{6,23},{32,49},{34,51},{36,53},{38,55},{64,81... | collective-permute-start | bytes 2359304 | tf_op jit(solution)/shard_map/ppermute | solution.py:37
  137.5 0.7 collective-permute-start.26
  138.2 2.2 %collective-permute-start.12 = (bf16[8,256,384]{2,1,0:T(8,128)(2,1)S(1)}, bf16[8,256,384]{2,1,0:T(8,128)(2,1)S(1)}, u32[]{:S(2)}, u32[]{:S(2)}) collective-permute-start(bf16[8,256,384]{2,1,0:T(8,128)(2,1)S(1)} %collective-permute-done.11.refs_0_), channel_id=1, source_target_pairs={{0,1},{2,3},{4,5},{6,7},{32,33},{34,35},{36,37},{38,39},{64,65},{6... | collective-permute-start | bytes 4718600 | tf_op jit(solution)/shard_map/ppermute | solution.py:37
  140.5 18.7 %collective-permute-done.17.refs_5_ = bf16[4,256,384]{2,1,0:T(8,128)(2,1)S(1)} collective-permute-done((bf16[4,256,384]{2,1,0:T(8,128)(2,1)S(1)}, bf16[4,256,384]{2,1,0:T(8,128)(2,1)S(1)}, u32[]{:S(2)}, u32[]{:S(2)}) %collective-permute-start.17) | collective-permute-done | bytes 786464 | tf_op jit(solution)/shard_map/ppermute | solution.py:37
  159.2 3.4 %collective-permute-start.15 = (bf16[4,256,384]{2,1,0:T(8,128)(2,1)S(1)}, bf16[4,256,384]{2,1,0:T(8,128)(2,1)S(1)}, u32[]{:S(2)}, u32[]{:S(2)}) collective-permute-start(bf16[4,256,384]{2,1,0:T(8,128)(2,1)S(1)} %collective-permute-done.14.refs_4_), channel_id=1, source_target_pairs={{0,17},{2,19},{4,21},{6,23},{32,49},{34,51},{36,53},{38,55},{64,81... | collective-permute-start | bytes 2359304 | tf_op jit(solution)/shard_map/ppermute | solution.py:37
  162.7 7.3 %gate_up.3.refs_12_ = f32[904,2048]{1,0:T(8,128)S(1)} custom-call(s32[4]{0:T(128)S(1)} %pad_add_fusion.pos_ref, bf16[8,256,384]{2,1,0:T(8,128)(2,1)S(1)} %pad_maximum_fusion.2.refs_0_, bf16[4,256,384]{2,1,0:T(8,128)(2,1)S(1)} %collective-permute-done.13.refs_1_, bf16[4,256,384]{2,1,0:T(8,128)(2,1)S(1)} %collective-permute-done.16.refs_2_, ...), custom_call_target="tpu_custom_call" | custom-call | flops 3758096384 | bytes 20971520 | tf_op jit(solution)/shard_map/gate_up/pallas_call | solution.py:291
  170.0 5.1 %collective-permute-done.27.refs_2_ = bf16[4,256,384]{2,1,0:T(8,128)(2,1)S(1)} collective-permute-done((bf16[4,256,384]{2,1,0:T(8,128)(2,1)S(1)}, bf16[4,256,384]{2,1,0:T(8,128)(2,1)S(1)}, u32[]{:S(2)}, u32[]{:S(2)}) %collective-permute-start.27) | collective-permute-done | bytes 786464 | tf_op jit(solution)/shard_map/ppermute | solution.py:37
  175.1 0.8 collective-permute-start.23
  175.9 2.6 %collective-permute-start.25 = (bf16[8,256,128]{2,1,0:T(8,128)(2,1)S(1)}, bf16[8,256,128]{2,1,0:T(8,128)(2,1)S(1)}, u32[]{:S(2)}, u32[]{:S(2)}) collective-permute-start(bf16[8,256,128]{2,1,0:T(8,128)(2,1)S(1)} %collective-permute-done.24.refs_9_), channel_id=1, source_target_pairs={{0,6},{2,0},{4,2},{6,4},{32,38},{34,32},{36,34},{38,36},{64,70},{6... | collective-permute-start | bytes 1572872 | tf_op jit(solution)/shard_map/ppermute | solution.py:37
  178.5 12.1 %gate_up.4.refs_7_ = f32[904,2048]{1,0:T(8,128)S(1)} custom-call(s32[4]{0:T(128)S(1)} %pad_add_fusion.pos_ref, bf16[8,256,384]{2,1,0:T(8,128)(2,1)S(1)} %collective-permute-done.11.refs_0_, bf16[4,256,384]{2,1,0:T(8,128)(2,1)S(1)} %collective-permute-done.26.refs_1_, ...), custom_call_target="tpu_custom_call", output_to_operand_aliasing={{}: (13, {})} | custom-call | flops 7516192768 | bytes 20971520 | tf_op jit(solution)/shard_map/gate_up/pallas_call | solution.py:291
  190.7 6.9 %gate_up.5 = (f32[448,2048]{1,0:T(8,128)S(1)}, f32[8,2048]{1,0:T(8,128)S(1)}, bf16[464,2048]{1,0:T(8,128)(2,1)S(1)}) custom-call(s32[4]{0:T(128)S(1)} %pad_add_fusion.pos_ref, bf16[8,256,384]{2,1,0:T(8,128)(2,1)S(1)} %collective-permute-done.12.refs_0_, bf16[4,256,384]{2,1,0:T(8,128)(2,1)S(1)} %collective-permute-done.15.refs_1_, ...), custom_call_target="tpu_custom_call" | custom-call | flops 3758096384 | bytes 20971520 | tf_op jit(solution)/shard_map/gate_up/pallas_call | solution.py:291
  197.6 6.7 %collective-permute-start.31 = (bf16[464,2048]{1,0:T(8,128)(2,1)S(1)}, bf16[464,2048]{1,0:T(8,128)(2,1)S(1)}, u32[]{:S(2)}, u32[]{:S(2)}) collective-permute-start(bf16[464,2048]{1,0:T(8,128)(2,1)S(1)} %get-tuple-element.51), channel_id=1, source_target_pairs={{0,8},{8,0},{1,9},{9,1},{2,10},{10,2},{3,11},{11,3},{4,12},{12,4},... | collective-permute-start | bytes 5701640 | tf_op jit(solution)/shard_map/ppermute | solution.py:41
  204.3 3.5 %collective-permute-done.31.got_ref = bf16[464,2048]{1,0:T(8,128)(2,1)S(1)} collective-permute-done((bf16[464,2048]{1,0:T(8,128)(2,1)S(1)}, bf16[464,2048]{1,0:T(8,128)(2,1)S(1)}, u32[]{:S(2)}, u32[]{:S(2)}) %collective-permute-start.31) | collective-permute-done | bytes 1900576 | tf_op jit(solution)/shard_map/ppermute | solution.py:41
  207.8 1.5 finish.1
  (58 shorter events, 4.0 us)
Async XLA Ops:
  19.4 3.3 %collective-permute-start = (bf16[8,128,256]{2,1,0:T(8,128)(2,1)S(1)}, bf16[8,128,256]{2,1,0:T(8,128)(2,1)S(1)}, u32[]{:S(2)}, u32[]{:S(2)}) collective-permute-start(bf16[8,128,256]{2,1,0:T(8,128)(2,1)S(1)} %all_to_all.10.own_ref), channel_id=1, source_target_pairs={{0,8},{8,0},{1,9},{9,1},{2,10},{10,2},{3,11},{11,3},{4,12},{12,4},... | collective-permute-start | bytes 1572872 | tf_op jit(solution)/shard_map/ppermute | solution.py:41
  21.4 11.9 %copy-start.1 = (bf16[8192,224]{0,1:T(8,128)(2,1)S(1)}, bf16[8192,224]{0,1:T(8,128)(2,1)}, u32[]{:S(2)}) copy-start(bf16[8192,224]{0,1:T(8,128)(2,1)} %param.14) | copy-start | bytes 11010052
  21.4 11.9 %copy-start.2 = (bf16[8192,224]{0,1:T(8,128)(2,1)S(1)}, bf16[8192,224]{0,1:T(8,128)(2,1)}, u32[]{:S(2)}) copy-start(bf16[8192,224]{0,1:T(8,128)(2,1)} %param.15) | copy-start | bytes 11010052
  22.8 1.6 copy-start.4
  24.4 8.9 %copy-start.5 = (f32[8192]{0:T(1024)S(1)}, f32[8192]{0:T(1024)}, u32[]{:S(2)}) copy-start(f32[8192]{0:T(1024)} %param.13) | copy-start | bytes 98308
  39.0 1.6 copy-start.3
  40.5 9.4 %collective-permute-start.1 = (bf16[2,448,1536]{2,1,0:T(8,128)(2,1)}, bf16[2,448,1536]{2,1,0:T(8,128)(2,1)}, u32[]{:S(2)}, u32[]{:S(2)}) collective-permute-start(bf16[2,448,1536]{2,1,0:T(8,128)(2,1)} %get-tuple-element.31), channel_id=1, source_target_pairs={{0,8},{8,0},{1,9},{9,1},{2,10},{10,2},{3,11},{11,3},{4,12},{12,4},... | collective-permute-start | bytes 8257544 | tf_op jit(solution)/shard_map/ppermute | solution.py:41
  40.7 31.6 %all-to-all-start.1 = ((bf16[8,128,1024]{2,1,0:T(8,128)(2,1)}), bf16[8,128,1024]{2,1,0:T(8,128)(2,1)}, u32[]{:S(2)}, u32[]{:S(2)}) async-start(bf16[8,128,1024]{2,1,0:T(8,128)(2,1)} %attend_project.1), calls=%async_computation.1 | async-start | bytes 4194304 | tf_op jit(solution)/shard_map/all_to_all | solution.py:409
  45.7 2.9 %collective-permute-start.2 = (bf16[4,448,256]{2,1,0:T(8,128)(2,1)S(1)}, bf16[4,448,256]{2,1,0:T(8,128)(2,1)}, u32[]{:S(2)}, u32[]{:S(2)}) collective-permute-start(bf16[4,448,256]{2,1,0:T(8,128)(2,1)S(1)} %get-tuple-element.33), channel_id=1, source_target_pairs={{0,8},{8,0},{1,9},{9,1},{2,10},{10,2},{3,11},{11,3},{4,12},{12,4},... | collective-permute-start | bytes 2752520 | tf_op jit(solution)/shard_map/ppermute | solution.py:41
  55.3 19.0 %copy-start.7 = (bf16[128,1024]{1,0:T(8,128)(2,1)S(1)}, bf16[128,1024]{1,0:T(8,128)(2,1)}, u32[]{:S(2)}) copy-start(bf16[128,1024]{1,0:T(8,128)(2,1)} %param.12) | copy-start | bytes 786436
  74.4 27.6 %copy-start.6 = (bf16[128,1024]{1,0:T(8,128)(2,1)}, bf16[128,1024]{1,0:T(8,128)(2,1)S(1)}, u32[]{:S(2)}) copy-start(bf16[128,1024]{1,0:T(8,128)(2,1)S(1)} %add_convert_fusion) | copy-start | bytes 786436
  74.4 2.6 %collective-permute-start.3 = (bf16[128,512]{1,0:T(8,128)(2,1)S(1)}, bf16[128,512]{1,0:T(8,128)(2,1)S(1)}, u32[]{:S(2)}, u32[]{:S(2)}) collective-permute-start(bf16[128,512]{1,0:T(8,128)(2,1)S(1)} %get-tuple-element.53), channel_id=1, source_target_pairs={{0,8},{8,0},{1,9},{9,1},{2,10},{10,2},{3,11},{11,3},{4,12},{12,4},... | collective-permute-start | bytes 393224 | tf_op jit(solution)/shard_map/ppermute | solution.py:41
  77.1 11.8 %collective-permute-start.4 = (bf16[256,384]{1,0:T(8,128)(2,1)S(1)}, bf16[256,384]{1,0:T(8,128)(2,1)S(1)}, u32[]{:S(2)}, u32[]{:S(2)}) collective-permute-start(bf16[256,384]{1,0:T(8,128)(2,1)S(1)} %slice.20), channel_id=1, source_target_pairs={{0,32},{2,34},{4,36},{6,38},{32,64},{34,66},{36,68},{38,70},{64,96... | collective-permute-start | bytes 589832 | tf_op jit(solution)/shard_map/ppermute | solution.py:37
  77.2 11.7 %collective-permute-start.5 = (bf16[256,384]{1,0:T(8,128)(2,1)S(1)}, bf16[256,384]{1,0:T(8,128)(2,1)S(1)}, u32[]{:S(2)}, u32[]{:S(2)}) collective-permute-start(bf16[256,384]{1,0:T(8,128)(2,1)S(1)} %slice.20), channel_id=1, source_target_pairs={{0,96},{2,98},{4,100},{6,102},{32,0},{34,2},{36,4},{38,6},{64,32},... | collective-permute-start | bytes 589832 | tf_op jit(solution)/shard_map/ppermute | solution.py:37
  79.8 9.0 %collective-permute-start.6 = (bf16[256,384]{1,0:T(8,128)(2,1)S(1)}, bf16[256,384]{1,0:T(8,128)(2,1)S(1)}, u32[]{:S(2)}, u32[]{:S(2)}) collective-permute-start(bf16[256,384]{1,0:T(8,128)(2,1)S(1)} %slice.20), channel_id=1, source_target_pairs={{0,64},{2,66},{4,68},{6,70},{32,96},{34,98},{36,100},{38,102},{64,... | collective-permute-start | bytes 589832 | tf_op jit(solution)/shard_map/ppermute | solution.py:37
  79.8 4.4 %collective-permute-start.7 = (bf16[256,128]{1,0:T(8,128)(2,1)S(1)}, bf16[256,128]{1,0:T(8,128)(2,1)S(1)}, u32[]{:S(2)}, u32[]{:S(2)}) collective-permute-start(bf16[256,128]{1,0:T(8,128)(2,1)S(1)} %slice.21), channel_id=1, source_target_pairs={{0,1},{2,3},{4,5},{6,7},{32,33},{34,35},{36,37},{38,39},{64,65},{6... | collective-permute-start | bytes 196616 | tf_op jit(solution)/shard_map/ppermute | solution.py:37
  80.4 4.1 %collective-permute-start.8 = (bf16[256,128]{1,0:T(8,128)(2,1)S(1)}, bf16[256,128]{1,0:T(8,128)(2,1)S(1)}, u32[]{:S(2)}, u32[]{:S(2)}) collective-permute-start(bf16[256,128]{1,0:T(8,128)(2,1)S(1)} %slice.21), channel_id=1, source_target_pairs={{0,17},{2,19},{4,21},{6,23},{32,49},{34,51},{36,53},{38,55},{64,81... | collective-permute-start | bytes 196616 | tf_op jit(solution)/shard_map/ppermute | solution.py:37
  84.2 4.6 %collective-permute-start.9 = (bf16[256,128]{1,0:T(8,128)(2,1)S(1)}, bf16[256,128]{1,0:T(8,128)(2,1)S(1)}, u32[]{:S(2)}, u32[]{:S(2)}) collective-permute-start(bf16[256,128]{1,0:T(8,128)(2,1)S(1)} %slice.21), channel_id=1, source_target_pairs={{0,16},{2,18},{4,20},{6,22},{32,48},{34,50},{36,52},{38,54},{64,80... | collective-permute-start | bytes 196616 | tf_op jit(solution)/shard_map/ppermute | solution.py:37
  88.9 73.7 %copy-start = (bf16[2,896,1536]{2,1,0:T(8,128)(2,1)S(1)}, bf16[2,896,1536]{2,1,0:T(8,128)(2,1)}, u32[]{:S(2)}) copy-start(bf16[2,896,1536]{2,1,0:T(8,128)(2,1)} %pad_maximum_fusion.refs_5_.refs_10_) | copy-start | bytes 16515076
  89.1 12.7 %collective-permute-start.10 = (bf16[4,256,384]{2,1,0:T(8,128)(2,1)S(1)}, bf16[4,256,384]{2,1,0:T(8,128)(2,1)S(1)}, u32[]{:S(2)}, u32[]{:S(2)}) collective-permute-start(bf16[4,256,384]{2,1,0:T(8,128)(2,1)S(1)} %pad_maximum_fusion.3), channel_id=1, source_target_pairs={{0,2},{2,4},{4,6},{6,0},{32,34},{34,36},{36,38},{38,32},{64,66},{6... | collective-permute-start | bytes 2359304 | tf_op jit(solution)/shard_map/ppermute | solution.py:37
  89.1 12.8 %collective-permute-start.19 = (bf16[4,256,128]{2,1,0:T(8,128)(2,1)S(1)}, bf16[4,256,128]{2,1,0:T(8,128)(2,1)S(1)}, u32[]{:S(2)}, u32[]{:S(2)}) collective-permute-start(bf16[4,256,128]{2,1,0:T(8,128)(2,1)S(1)} %pad_maximum_fusion.6), channel_id=1, source_target_pairs={{0,32},{2,34},{4,36},{6,38},{32,64},{34,66},{36,68},{38,70},{64,96... | collective-permute-start | bytes 786440 | tf_op jit(solution)/shard_map/ppermute | solution.py:37
  89.2 13.2 %collective-permute-start.20 = (bf16[4,256,128]{2,1,0:T(8,128)(2,1)S(1)}, bf16[4,256,128]{2,1,0:T(8,128)(2,1)S(1)}, u32[]{:S(2)}, u32[]{:S(2)}) collective-permute-start(bf16[4,256,128]{2,1,0:T(8,128)(2,1)S(1)} %pad_maximum_fusion.6), channel_id=1, source_target_pairs={{0,96},{2,98},{4,100},{6,102},{32,0},{34,2},{36,4},{38,6},{64,32},... | collective-permute-start | bytes 786440 | tf_op jit(solution)/shard_map/ppermute | solution.py:37
  92.8 10.5 %collective-permute-start.21 = (bf16[4,256,128]{2,1,0:T(8,128)(2,1)S(1)}, bf16[4,256,128]{2,1,0:T(8,128)(2,1)S(1)}, u32[]{:S(2)}, u32[]{:S(2)}) collective-permute-start(bf16[4,256,128]{2,1,0:T(8,128)(2,1)S(1)} %pad_maximum_fusion.6), channel_id=1, source_target_pairs={{0,64},{2,66},{4,68},{6,70},{32,96},{34,98},{36,100},{38,102},{64,... | collective-permute-start | bytes 786440 | tf_op jit(solution)/shard_map/ppermute | solution.py:37
  93.9 20.0 %collective-permute-start.13 = (bf16[4,256,384]{2,1,0:T(8,128)(2,1)S(1)}, bf16[4,256,384]{2,1,0:T(8,128)(2,1)S(1)}, u32[]{:S(2)}, u32[]{:S(2)}) collective-permute-start(bf16[4,256,384]{2,1,0:T(8,128)(2,1)S(1)} %pad_maximum_fusion.3), channel_id=1, source_target_pairs={{0,6},{2,0},{4,2},{6,4},{32,38},{34,32},{36,34},{38,36},{64,70},{6... | collective-permute-start | bytes 2359304 | tf_op jit(solution)/shard_map/ppermute | solution.py:37
  101.7 16.7 %collective-permute-start.16 = (bf16[4,256,384]{2,1,0:T(8,128)(2,1)S(1)}, bf16[4,256,384]{2,1,0:T(8,128)(2,1)S(1)}, u32[]{:S(2)}, u32[]{:S(2)}) collective-permute-start(bf16[4,256,384]{2,1,0:T(8,128)(2,1)S(1)} %pad_maximum_fusion.3), channel_id=1, source_target_pairs={{0,4},{2,6},{4,0},{6,2},{32,36},{34,38},{36,32},{38,34},{64,68},{6... | collective-permute-start | bytes 2359304 | tf_op jit(solution)/shard_map/ppermute | solution.py:37
  102.0 36.2 %collective-permute-start.11 = (bf16[8,256,384]{2,1,0:T(8,128)(2,1)S(1)}, bf16[8,256,384]{2,1,0:T(8,128)(2,1)S(1)}, u32[]{:S(2)}, u32[]{:S(2)}) collective-permute-start(bf16[8,256,384]{2,1,0:T(8,128)(2,1)S(1)} %pad_maximum_fusion.2.refs_0_), channel_id=1, source_target_pairs={{0,1},{2,3},{4,5},{6,7},{32,33},{34,35},{36,37},{38,39},{64,65},{6... | collective-permute-start | bytes 4718600 | tf_op jit(solution)/shard_map/ppermute | solution.py:37
  103.3 16.3 %collective-permute-start.22 = (bf16[8,256,128]{2,1,0:T(8,128)(2,1)S(1)}, bf16[8,256,128]{2,1,0:T(8,128)(2,1)S(1)}, u32[]{:S(2)}, u32[]{:S(2)}) collective-permute-start(bf16[8,256,128]{2,1,0:T(8,128)(2,1)S(1)} %pad_maximum_fusion.4.refs_3_), channel_id=1, source_target_pairs={{0,2},{2,4},{4,6},{6,0},{32,34},{34,36},{36,38},{38,32},{64,66},{6... | collective-permute-start | bytes 1572872 | tf_op jit(solution)/shard_map/ppermute | solution.py:37
  105.7 19.3 %collective-permute-start.24 = (bf16[8,256,128]{2,1,0:T(8,128)(2,1)S(1)}, bf16[8,256,128]{2,1,0:T(8,128)(2,1)S(1)}, u32[]{:S(2)}, u32[]{:S(2)}) collective-permute-start(bf16[8,256,128]{2,1,0:T(8,128)(2,1)S(1)} %pad_maximum_fusion.5.refs_4_), channel_id=1, source_target_pairs={{0,6},{2,0},{4,2},{6,4},{32,38},{34,32},{36,34},{38,36},{64,70},{6... | collective-permute-start | bytes 1572872 | tf_op jit(solution)/shard_map/ppermute | solution.py:37
  113.9 19.4 %collective-permute-start.29 = (bf16[8,256,128]{2,1,0:T(8,128)(2,1)S(1)}, bf16[8,256,128]{2,1,0:T(8,128)(2,1)S(1)}, u32[]{:S(2)}, u32[]{:S(2)}) collective-permute-start(bf16[8,256,128]{2,1,0:T(8,128)(2,1)S(1)} %pad_maximum_fusion.5.refs_4_), channel_id=1, source_target_pairs={{0,2},{2,4},{4,6},{6,0},{32,34},{34,36},{36,38},{38,32},{64,66},{6... | collective-permute-start | bytes 1572872 | tf_op jit(solution)/shard_map/ppermute | solution.py:37
  118.4 19.1 %collective-permute-start.30 = (bf16[8,256,128]{2,1,0:T(8,128)(2,1)S(1)}, bf16[8,256,128]{2,1,0:T(8,128)(2,1)S(1)}, u32[]{:S(2)}, u32[]{:S(2)}) collective-permute-start(bf16[8,256,128]{2,1,0:T(8,128)(2,1)S(1)} %pad_maximum_fusion.4.refs_3_), channel_id=1, source_target_pairs={{0,6},{2,0},{4,2},{6,4},{32,38},{34,32},{36,34},{38,36},{64,70},{6... | collective-permute-start | bytes 1572872 | tf_op jit(solution)/shard_map/ppermute | solution.py:37
  119.7 20.7 %collective-permute-start.14 = (bf16[4,256,384]{2,1,0:T(8,128)(2,1)S(1)}, bf16[4,256,384]{2,1,0:T(8,128)(2,1)S(1)}, u32[]{:S(2)}, u32[]{:S(2)}) collective-permute-start(bf16[4,256,384]{2,1,0:T(8,128)(2,1)S(1)} %collective-permute-done.13.refs_1_), channel_id=1, source_target_pairs={{0,17},{2,19},{4,21},{6,23},{32,49},{34,51},{36,53},{38,55},{64,81... | collective-permute-start | bytes 2359304 | tf_op jit(solution)/shard_map/ppermute | solution.py:37
  125.1 50.9 %collective-permute-start.28 = (bf16[8,256,384]{2,1,0:T(8,128)(2,1)S(1)}, bf16[8,256,384]{2,1,0:T(8,128)(2,1)S(1)}, u32[]{:S(2)}, u32[]{:S(2)}) collective-permute-start(bf16[8,256,384]{2,1,0:T(8,128)(2,1)S(1)} %pad_maximum_fusion.2.refs_0_), channel_id=1, source_target_pairs={{0,17},{2,19},{4,21},{6,23},{32,49},{34,51},{36,53},{38,55},{64,81... | collective-permute-start | bytes 4718600 | tf_op jit(solution)/shard_map/ppermute | solution.py:37
  133.3 25.9 %collective-permute-start.17 = (bf16[4,256,384]{2,1,0:T(8,128)(2,1)S(1)}, bf16[4,256,384]{2,1,0:T(8,128)(2,1)S(1)}, u32[]{:S(2)}, u32[]{:S(2)}) collective-permute-start(bf16[4,256,384]{2,1,0:T(8,128)(2,1)S(1)} %collective-permute-done.16.refs_2_), channel_id=1, source_target_pairs={{0,17},{2,19},{4,21},{6,23},{32,49},{34,51},{36,53},{38,55},{64,81... | collective-permute-start | bytes 2359304 | tf_op jit(solution)/shard_map/ppermute | solution.py:37
  137.5 25.1 %collective-permute-start.26 = (bf16[4,256,384]{2,1,0:T(8,128)(2,1)S(1)}, bf16[4,256,384]{2,1,0:T(8,128)(2,1)S(1)}, u32[]{:S(2)}, u32[]{:S(2)}) collective-permute-start(bf16[4,256,384]{2,1,0:T(8,128)(2,1)S(1)} %collective-permute-done.13.refs_1_), channel_id=1, source_target_pairs={{0,1},{2,3},{4,5},{6,7},{32,33},{34,35},{36,37},{38,39},{64,65},{6... | collective-permute-start | bytes 2359304 | tf_op jit(solution)/shard_map/ppermute | solution.py:37
  138.2 52.5 %collective-permute-start.12 = (bf16[8,256,384]{2,1,0:T(8,128)(2,1)S(1)}, bf16[8,256,384]{2,1,0:T(8,128)(2,1)S(1)}, u32[]{:S(2)}, u32[]{:S(2)}) collective-permute-start(bf16[8,256,384]{2,1,0:T(8,128)(2,1)S(1)} %collective-permute-done.11.refs_0_), channel_id=1, source_target_pairs={{0,1},{2,3},{4,5},{6,7},{32,33},{34,35},{36,37},{38,39},{64,65},{6... | collective-permute-start | bytes 4718600 | tf_op jit(solution)/shard_map/ppermute | solution.py:37
  140.4 34.7 %collective-permute-start.27 = (bf16[4,256,384]{2,1,0:T(8,128)(2,1)S(1)}, bf16[4,256,384]{2,1,0:T(8,128)(2,1)S(1)}, u32[]{:S(2)}, u32[]{:S(2)}) collective-permute-start(bf16[4,256,384]{2,1,0:T(8,128)(2,1)S(1)} %collective-permute-done.16.refs_2_), channel_id=1, source_target_pairs={{0,1},{2,3},{4,5},{6,7},{32,33},{34,35},{36,37},{38,39},{64,65},{6... | collective-permute-start | bytes 2359304 | tf_op jit(solution)/shard_map/ppermute | solution.py:37
  159.2 31.5 %collective-permute-start.15 = (bf16[4,256,384]{2,1,0:T(8,128)(2,1)S(1)}, bf16[4,256,384]{2,1,0:T(8,128)(2,1)S(1)}, u32[]{:S(2)}, u32[]{:S(2)}) collective-permute-start(bf16[4,256,384]{2,1,0:T(8,128)(2,1)S(1)} %collective-permute-done.14.refs_4_), channel_id=1, source_target_pairs={{0,17},{2,19},{4,21},{6,23},{32,49},{34,51},{36,53},{38,55},{64,81... | collective-permute-start | bytes 2359304 | tf_op jit(solution)/shard_map/ppermute | solution.py:37
  162.6 28.1 %collective-permute-start.18 = (bf16[4,256,384]{2,1,0:T(8,128)(2,1)S(1)}, bf16[4,256,384]{2,1,0:T(8,128)(2,1)S(1)}, u32[]{:S(2)}, u32[]{:S(2)}) collective-permute-start(bf16[4,256,384]{2,1,0:T(8,128)(2,1)S(1)} %collective-permute-done.17.refs_5_), channel_id=1, source_target_pairs={{0,17},{2,19},{4,21},{6,23},{32,49},{34,51},{36,53},{38,55},{64,81... | collective-permute-start | bytes 2359304 | tf_op jit(solution)/shard_map/ppermute | solution.py:37
  175.1 15.5 %collective-permute-start.23 = (bf16[8,256,128]{2,1,0:T(8,128)(2,1)S(1)}, bf16[8,256,128]{2,1,0:T(8,128)(2,1)S(1)}, u32[]{:S(2)}, u32[]{:S(2)}) collective-permute-start(bf16[8,256,128]{2,1,0:T(8,128)(2,1)S(1)} %collective-permute-done.22.refs_6_), channel_id=1, source_target_pairs={{0,2},{2,4},{4,6},{6,0},{32,34},{34,36},{36,38},{38,32},{64,66},{6... | collective-permute-start | bytes 1572872 | tf_op jit(solution)/shard_map/ppermute | solution.py:37
  175.9 14.7 %collective-permute-start.25 = (bf16[8,256,128]{2,1,0:T(8,128)(2,1)S(1)}, bf16[8,256,128]{2,1,0:T(8,128)(2,1)S(1)}, u32[]{:S(2)}, u32[]{:S(2)}) collective-permute-start(bf16[8,256,128]{2,1,0:T(8,128)(2,1)S(1)} %collective-permute-done.24.refs_9_), channel_id=1, source_target_pairs={{0,6},{2,0},{4,2},{6,4},{32,38},{34,32},{36,34},{38,36},{64,70},{6... | collective-permute-start | bytes 1572872 | tf_op jit(solution)/shard_map/ppermute | solution.py:37
  197.6 10.2 %collective-permute-start.31 = (bf16[464,2048]{1,0:T(8,128)(2,1)S(1)}, bf16[464,2048]{1,0:T(8,128)(2,1)S(1)}, u32[]{:S(2)}, u32[]{:S(2)}) collective-permute-start(bf16[464,2048]{1,0:T(8,128)(2,1)S(1)} %get-tuple-element.51), channel_id=1, source_target_pairs={{0,8},{8,0},{1,9},{9,1},{2,10},{10,2},{3,11},{11,3},{4,12},{12,4},... | collective-permute-start | bytes 5701640 | tf_op jit(solution)/shard_map/ppermute | solution.py:41

commit v5 on v4

--- a/solution.py
+++ b/solution.py
@@ -164,22 +164,30 @@
     )(pos, gate_t, up_t, gain)
 
 
-def gate_kernel(which, first, last, pos_ref, *refs):
+def gate_kernel(which, stage, pos_ref, *refs):
     count = len(which)
     refs = list(refs)
     main = {c: tuple(refs.pop(0) for _ in range(3)) for c in which}
     side = {c: (refs.pop(0), refs.pop(0)) for c in which}
     wm, ws = refs.pop(0), refs.pop(0)
+    first = stage == "first"
+    last = stage in ("theirs", "mine")
     before = None if first else refs.pop(0)
-    if last:
-        own_ref, own_ss, par_ref = (refs.pop(0) for _ in range(3))
-        acc = before
+    if stage == "theirs":
+        own_ss, par_ref = refs.pop(0), refs.pop(0)
+    elif stage == "mine":
+        own_ref = refs.pop(0)
     else:
         acc = refs.pop(0)
+    if last:
+        acc = refs.pop()
     hm, hs, ssq, table, msem, ssem = refs
     x_at, y_at, z_at, core = (pos_ref[m] for m in range(4))
-    rows = wm.shape[1]
-    n2 = rows // 2
+    both = wm.shape[1]
+    n2 = both // 2
+    lead = n2 if stage == "theirs" else 0
+    rows = n2 if last else both
+    squared = stage != "mine"
 
     def at(base, slot):
         return (base + OFFSETS[slot] + 4) & 3
@@ -211,9 +219,10 @@
                     hs.at[m, pl.ds(row, 256), pl.ds(col, SCOLS)],
                     ssem.at[m],
                 ).start()
-    if first:
+    if first or last:
         acc[...] = jnp.zeros_like(acc)
-    ssq[...] = jnp.zeros_like(ssq)
+    if squared:
+        ssq[...] = jnp.zeros_like(ssq)
     ones = jnp.ones((8, 128), BF)
 
     def squares(block):
@@ -236,9 +245,11 @@
         cols = pl.ds(pl.multiple_of(table[2 * u] * 256, 256), 256)
         block = hm[u]
         acc[:rows, cols] += lax.dot_general(
-            wm[table[2 * u + 1]], block, (((1,), (1,)), ((), ())), preferred_element_type=F32
+            wm[table[2 * u + 1], pl.ds(lead, rows), :], block, (((1,), (1,)), ((), ())),
+            preferred_element_type=F32,
         )
-        ssq[cols, :] += squares(block)
+        if squared:
+            ssq[cols, :] += squares(block)
         return 0
 
     lax.fori_loop(0, 4 * count, unit, 0)
@@ -249,52 +260,61 @@
     def tail(p, _):
         cols = pl.ds(pl.multiple_of(p * piece, piece), piece)
         total = acc[:rows, cols]
-        part = ssq[cols, :]
+        if last:
+            total = total + before[pl.ds(lead, rows), cols]
+        part = ssq[cols, :] if squared else None
         for m, c in enumerate(which):
             block = hs[m, cols, :]
             total = total + lax.dot_general(
-                ws[at(z_at, c)], block, (((1,), (1,)), ((), ())), preferred_element_type=F32
+                ws[at(z_at, c), pl.ds(lead, rows), :], block, (((1,), (1,)), ((), ())),
+                preferred_element_type=F32,
             )
-            part = part + squares(block)
-        sq = acc[rows:, cols] + lane_sums(part)
-        if last:
-            own_ref[:, cols] = total[:n2]
-            par_ref[:n2, cols] = total[n2:].astype(BF)
+            if squared:
+                part = part + squares(block)
+        if squared:
+            sq = (before if last else acc)[both:, cols] + lane_sums(part)
+        if stage == "theirs":
+            par_ref[:n2, cols] = total.astype(BF)
             own_ss[:, cols] = sq
             big = sq.astype(BF)
             par_ref[n2:, cols] = jnp.concatenate(
                 [big.astype(F32), sq - big.astype(F32)], axis=0
             ).astype(BF)
+        elif stage == "mine":
+            own_ref[:, cols] = total
         else:
             acc[:rows, cols] = total
             acc[rows:, cols] = sq
         return 0
 
-    lax.fori_loop(0, acc.shape[1] // piece, tail, 0)
-
-
-def gate_up(pos, which, main, side, weights, before, last):
+    lax.fori_loop(0, hs.shape[1] // piece, tail, 0)
+
+
+def gate_up(pos, which, main, side, weights, before, stage):
     n2 = weights[0].shape[1] // 2
     tokens = 2048
     count = len(which)
     first = before is None
+    last = stage in ("theirs", "mine")
     any_spec = pl.BlockSpec(memory_space=pl.ANY)
     vm = pl.BlockSpec(memory_space=pltpu.VMEM)
     pieces = [p for part in (main, side) for c in which for p in part[c]]
     operands = pieces + list(weights) + ([] if first else [before])
     partial = jax.ShapeDtypeStruct((2 * n2 + 8, tokens), F32)
-    out_shape = [
-        jax.ShapeDtypeStruct((n2, tokens), F32),
-        jax.ShapeDtypeStruct((8, tokens), F32),
-        jax.ShapeDtypeStruct((n2 + 16, tokens), BF),
-    ] if last else partial
+    out_shape = {
+        "theirs": [
+            jax.ShapeDtypeStruct((8, tokens), F32),
+            jax.ShapeDtypeStruct((n2 + 16, tokens), BF),
+        ],
+        "mine": jax.ShapeDtypeStruct((n2, tokens), F32),
+    }.get(stage, partial)
     return pl.pallas_call(
-        functools.partial(gate_kernel, which, first, last),
+        functools.partial(gate_kernel, which, stage),
         out_shape=out_shape,
         in_specs=[pl.BlockSpec(memory_space=pltpu.SMEM)]
         + [any_spec] * len(pieces)
         + [vm] * (len(operands) - len(pieces)),
-        out_specs=[vm] * 3 if last else vm,
+        out_specs=[vm] * 2 if stage == "theirs" else vm,
         scratch_shapes=[
             pltpu.VMEM((4 * count, 256, 4 * MCOLS), BF),
             pltpu.VMEM((count, tokens, 2 * SCOLS), BF),
@@ -302,7 +322,8 @@
             pltpu.SMEM((8 * count,), jnp.int32),
             pltpu.SemaphoreType.DMA((4 * count,)),
             pltpu.SemaphoreType.DMA((count,)),
-        ],
+        ]
+        + ([pltpu.VMEM((n2, tokens), F32)] if last else []),
         input_output_aliases={} if first or last else {len(operands): 0},
         compiler_params=pltpu.CompilerParams(vmem_limit_bytes=(10 + 8 * count) << 20),
         cost_estimate=pl.CostEstimate(
@@ -351,24 +372,30 @@
 
 def gather(blocks, orders):
     axes = [[(o[0][p], o[1][p]) for p in range(3)] for o in orders]
-    near = lax.optimization_barrier(
-        [[b] + [shift(b, a[0], by) for by in (1, -1, 2)] for b, a in zip(blocks, axes)]
-    )
-    cur = lax.optimization_barrier([jnp.stack(p) for p in near])
-    ahead = [shift(b, a[1], 1) for b, a in zip(cur, axes)]
-    rest = [[shift(b, a[1], by) for by in (-1, 2)] for b, a in zip(cur, axes)]
+
+    def around(block, a):
+        return [shift(block, a, by) for by in (1, -1, 2)]
+
+    main_near = around(blocks[0], axes[0][0])
+    side_near = around(blocks[1], axes[1][0])
+    main_near = lax.optimization_barrier([blocks[0]] + main_near)
+    cur_main = lax.optimization_barrier(jnp.stack(main_near))
+    ahead = shift(cur_main, axes[0][1], 1)
+    third, fourth = (shift(cur_main, axes[0][1], by) for by in (-1, 2))
+    side_near = lax.optimization_barrier([blocks[1]] + side_near)
+    cur_side = lax.optimization_barrier(jnp.stack(side_near))
+    side_next = around(cur_side, axes[1][1])
 
     def both_ways(block, a):
         return shift(block, a[2], 1), shift(block, a[2], -1)
 
-    low = jnp.concatenate([cur[0], ahead[0]], 0)
+    low = jnp.concatenate([cur_main, ahead], 0)
     low = lax.optimization_barrier(low)
-    third, fourth = rest[0]
     lows = both_ways(low, axes[0])
     thirds = both_ways(third, axes[0])
     fourths = both_ways(fourth, axes[0])
-    side_low = jnp.concatenate([cur[1], ahead[1]], 0)
-    side_high = jnp.concatenate(rest[1], 0)
+    side_low = jnp.concatenate([cur_side, side_next[0]], 0)
+    side_high = jnp.concatenate(side_next[1:], 0)
     side_low, side_high = lax.optimization_barrier((side_low, side_high))
     side_lows = both_ways(side_low, axes[1])
     side_highs = both_ways(side_high, axes[1])
@@ -416,10 +443,12 @@
     got = swap_core(jnp.where(core == 0, hidden[:, 512:], hidden[:, :512]))
     chip = jnp.where(core == 0, jnp.concatenate([keep, got], 0), jnp.concatenate([got, keep], 0))
     main, side = gather((chip[:, :MCOLS], chip[:, MCOLS:]), (MAIN, SIDE))
-    sums = gate_up(pos2, (0,), main, side, weights, None, False)
-    sums = gate_up(pos2, (1, 2), main, side, weights, sums, False)
-    own_sums, own_ss, theirs = gate_up(pos2, (3,), main, side, weights, sums, True)
-    out = finish(own_sums, own_ss, swap_core(theirs), norm_gain.shape[0])
+    sums = gate_up(pos2, (0,), main, side, weights, None, "first")
+    sums = gate_up(pos2, (1, 2), main, side, weights, sums, "middle")
+    own_ss, theirs = gate_up(pos2, (3,), main, side, weights, sums, "theirs")
+    got = swap_core(theirs)
+    own_sums = gate_up(pos2, (3,), main, side, weights, sums, "mine")
+    out = finish(own_sums, own_ss, got, norm_gain.shape[0])
     return out.T, hidden
 
 

time: 210 us -> 231 us (1.10); the launches traced: 210 us -> 228 us
  waiting for transfers between devices: 78.3 us -> 86.5 us
  starting transfers between devices: 56.2 us -> 62.5 us
  Pallas kernels: 42.4 us -> 46 us
    ppermute x27, waiting for transfers between devices: 53.3 us -> 64.9 us  [shift(): return lax.ppermute(x, MESH, pairs)]
    pallas_call x3 -> x4, Pallas kernels: 26.3 us -> 29.9 us  [gate_up(): pl.pallas_call(functools.partial(gate_kernel, which, stage), out_shape=ou...]
    ppermute x5, waiting for transfers between devices: 8.11 us -> 4.6 us  [swap_core(): return lax.ppermute(x, 'c', [(0, 1), (1, 0)])]
    ppermute x5, starting transfers between devices: 10.9 us -> 14.4 us  [swap_core(): return lax.ppermute(x, 'c', [(0, 1), (1, 0)])]
    ppermute x27, starting transfers between devices: 40.3 us -> 43.1 us  [shift(): return lax.ppermute(x, MESH, pairs)]
  transfers between devices with their start and end apart: 33 -> 33, of which waited for: 17 -> 15; matrix products, arithmetic and copies ran while one was open for 3% -> 3% of each run, Pallas kernels for 9% -> 11%
where the time goes in v5:
time: 231 us; the launch traced here: 228 us
  waiting for transfers between devices  86.5 us (37%)
  starting transfers between devices  62.5 us (27%)
  Pallas kernels  46 us (20%)
  blocking collectives  18 us (8%)
  other arithmetic  10.2 us (4%)
  local copies, waits for them, and re-layouts  3.24 us (1%)
    ppermute x27, waiting for transfers between devices, shift(): return lax.ppermute(x, MESH, pairs)  64.9 us
    ppermute x27, starting transfers between devices, shift(): return lax.ppermute(x, MESH, pairs)  43.1 us
    pallas_call x4, Pallas kernels, gate_up(): pl.pallas_call(functools.partial(gate_kernel, which, stage), out_shape=ou...  29.9 us
    all_to_all x1, blocking collectives, per_device(): own = lax.all_to_all(spread, ('y', 'xh'), 0, 0, tiled=True)  18 us
    all_to_all x1, waiting for transfers between devices, per_device(): terms = lax.all_to_all(partial, HEAD, 0, 0, tiled=True)  17 us
    ppermute x5, starting transfers between devices, swap_core(): return lax.ppermute(x, 'c', [(0, 1), (1, 0)])  14.4 us
    pallas_call x1, Pallas kernels, attend_project(): pl.pallas_call(attend_kernel, out_shape=jax.ShapeDtypeStruct((blocks, row...  8.88 us
    concatenate x2, other arithmetic, per_device(): jnp.concatenate([k, swap_core(t)], 1)  6.68 us
  transfers between devices with their start and end apart: 33, of which 15 were waited for; matrix products, arithmetic and copies ran while one was open for 3% of the time, Pallas kernels for 11%

profile of v5, /device:TPU:1, one launch (start us, length us, event | category | flops | bytes accessed | tf_op | source)
XLA Modules:
  0.0 227.5 jit_solution(11386531468666899918)
XLA Ops:
  0.6 0.8 pad_maximum_fusion.7
  1.5 18.0 %all_to_all.10.own_ref = bf16[8,128,256]{2,1,0:T(8,128)(2,1)S(1)} all-to-all(bf16[8,128,256]{2,1,0:T(8,128)(2,1)S(1)} %broadcast_in_dim.4), channel_id=1, replica_groups=mesh['y'=4,'xh'=2,'c'=2,'z'=4,'xl'=2] {'y','xh'}, dimensions={0} | all-to-all | bytes 1048576 | tf_op jit(solution)/shard_map/all_to_all | solution.py:429
  19.4 1.8 collective-permute-start
  21.4 1.4 collective-permute-done.oth_ref
  22.8 1.6 copy-done.4
  24.4 8.9 %attend_project.1 = bf16[8,128,1024]{2,1,0:T(8,128)(2,1)} custom-call(s32[2]{0:T(128)S(1)} %pad_add_fusion.1.pos_ref, bf16[128,1024]{1,0:T(8,128)(2,1)S(1)} %copy-done.4, bf16[8,128,256]{2,1,0:T(8,128)(2,1)S(1)} %all_to_all.10.own_ref, bf16[8,128,256]{2,1,0:T(8,128)(2,1)S(1)} %collective-permute-done.oth_ref, bf16[1024,8192]{1,0:T(8,128)(2,1)} %w_hbm.1), custom_call_target="tpu_custom_call" | custom-call | flops 4294967296 | bytes 20971520 | tf_op jit(solution)/shard_map/attend_project/pallas_call | solution.py:111
  33.3 5.7 %prepare.1 = (bf16[2,448,1536]{2,1,0:T(8,128)(2,1)S(1)}, bf16[4,448,256]{2,1,0:T(8,128)(2,1)S(1)}, bf16[2,448,1536]{2,1,0:T(8,128)(2,1)}, bf16[4,448,256]{2,1,0:T(8,128)(2,1)S(1)}) custom-call(s32[4]{0:T(128)S(1)} %pad_add_fusion.pos_ref, bf16[224,8192]{1,0:T(8,128)(2,1)S(1)} %bitcast.17, bf16[224,8192]{1,0:T(8,128)(2,1)S(1)} %bitcast.18, f32[1,8192]{1,0:T(1,128)S(1)} %bitcast.19), custom_call_target="tpu_custom_call" | custom-call | flops 8388608 | bytes 15728640 | tf_op jit(solution)/shard_map/prepare/pallas_call | solution.py:152
  39.0 1.6 copy-done.3
  40.7 5.1 %all-to-all-start.1 = ((bf16[8,128,1024]{2,1,0:T(8,128)(2,1)}), bf16[8,128,1024]{2,1,0:T(8,128)(2,1)}, u32[]{:S(2)}, u32[]{:S(2)}) async-start(bf16[8,128,1024]{2,1,0:T(8,128)(2,1)} %attend_project.1), calls=%async_computation.1 | async-start | bytes 4194304 | tf_op jit(solution)/shard_map/all_to_all | solution.py:436
  46.4 2.2 collective-permute-done.2
  48.6 1.3 pad_maximum_fusion.1.refs_6_.refs_11_
  49.9 5.4 %pad_maximum_fusion.refs_5_.refs_10_ = bf16[2,896,1536]{2,1,0:T(8,128)(2,1)} fusion(bf16[2,448,1536]{2,1,0:T(8,128)(2,1)} %collective-permute-done.1, bf16[2,448,1536]{2,1,0:T(8,128)(2,1)} %copy-done.3), kind=kLoop, calls=%fused_computation | loop fusion | flops 11010048 | bytes 11010048 | tf_op jit(solution)/shard_map/concatenate | solution.py:438
  55.3 17.0 %all-to-all-done.1 = bf16[8,128,1024]{2,1,0:T(8,128)(2,1)} async-done(((bf16[8,128,1024]{2,1,0:T(8,128)(2,1)}), bf16[8,128,1024]{2,1,0:T(8,128)(2,1)}, u32[]{:S(2)}, u32[]{:S(2)}) %all-to-all-start.1) | async-done | bytes 2097184 | tf_op jit(solution)/shard_map/all_to_all | solution.py:436
  72.3 2.0 convert_reduce_fusion
  74.4 1.6 collective-permute-start.3
  76.0 1.0 collective-permute-done.3
  77.2 2.7 %collective-permute-start.5 = (bf16[256,384]{1,0:T(8,128)(2,1)S(1)}, bf16[256,384]{1,0:T(8,128)(2,1)S(1)}, u32[]{:S(2)}, u32[]{:S(2)}) collective-permute-start(bf16[256,384]{1,0:T(8,128)(2,1)S(1)} %slice.20), channel_id=1, source_target_pairs={{0,96},{2,98},{4,100},{6,102},{32,0},{34,2},{36,4},{38,6},{64,32},... | collective-permute-start | bytes 589832 | tf_op jit(solution)/shard_map/ppermute | solution.py:37
  79.8 3.3 %collective-permute-done.4 = bf16[256,384]{1,0:T(8,128)(2,1)S(1)} collective-permute-done((bf16[256,384]{1,0:T(8,128)(2,1)S(1)}, bf16[256,384]{1,0:T(8,128)(2,1)S(1)}, u32[]{:S(2)}, u32[]{:S(2)}) %collective-permute-start.4) | collective-permute-done | bytes 196640 | tf_op jit(solution)/shard_map/ppermute | solution.py:37
  83.2 1.4 collective-permute-done.5
  84.5 1.6 collective-permute-done.6
  87.0 2.6 %collective-permute-start.17 = (bf16[256,128]{1,0:T(8,128)(2,1)S(1)}, bf16[256,128]{1,0:T(8,128)(2,1)S(1)}, u32[]{:S(2)}, u32[]{:S(2)}) collective-permute-start(bf16[256,128]{1,0:T(8,128)(2,1)S(1)} %slice.21), channel_id=1, source_target_pairs={{0,17},{2,19},{4,21},{6,23},{32,49},{34,51},{36,53},{38,55},{64,81... | collective-permute-start | bytes 196616 | tf_op jit(solution)/shard_map/ppermute | solution.py:37
  90.3 10.9 %collective-permute-done.16 = bf16[256,128]{1,0:T(8,128)(2,1)S(1)} collective-permute-done((bf16[256,128]{1,0:T(8,128)(2,1)S(1)}, bf16[256,128]{1,0:T(8,128)(2,1)S(1)}, u32[]{:S(2)}, u32[]{:S(2)}) %collective-permute-start.16) | collective-permute-done | bytes 65568 | tf_op jit(solution)/shard_map/ppermute | solution.py:37
  101.3 2.9 %collective-permute-start.20 = (bf16[4,256,128]{2,1,0:T(8,128)(2,1)S(1)}, bf16[4,256,128]{2,1,0:T(8,128)(2,1)S(1)}, u32[]{:S(2)}, u32[]{:S(2)}) collective-permute-start(bf16[4,256,128]{2,1,0:T(8,128)(2,1)S(1)} %pad_maximum_fusion.6), channel_id=1, source_target_pairs={{0,96},{2,98},{4,100},{6,102},{32,0},{34,2},{36,4},{38,6},{64,32},... | collective-permute-start | bytes 786440 | tf_op jit(solution)/shard_map/ppermute | solution.py:37
  104.3 1.1 collective-permute-start.21
  105.4 5.4 %collective-permute-done.19 = bf16[4,256,128]{2,1,0:T(8,128)(2,1)S(1)} collective-permute-done((bf16[4,256,128]{2,1,0:T(8,128)(2,1)S(1)}, bf16[4,256,128]{2,1,0:T(8,128)(2,1)S(1)}, u32[]{:S(2)}, u32[]{:S(2)}) %collective-permute-start.19) | collective-permute-done | bytes 262176 | tf_op jit(solution)/shard_map/ppermute | solution.py:37
  110.8 2.6 %collective-permute-done.20 = bf16[4,256,128]{2,1,0:T(8,128)(2,1)S(1)} collective-permute-done((bf16[4,256,128]{2,1,0:T(8,128)(2,1)S(1)}, bf16[4,256,128]{2,1,0:T(8,128)(2,1)S(1)}, u32[]{:S(2)}, u32[]{:S(2)}) %collective-permute-start.20) | collective-permute-done | bytes 262176 | tf_op jit(solution)/shard_map/ppermute | solution.py:37
  113.4 0.9 collective-permute-done.21
  115.4 2.5 %collective-permute-start.24 = (bf16[8,256,128]{2,1,0:T(8,128)(2,1)S(1)}, bf16[8,256,128]{2,1,0:T(8,128)(2,1)S(1)}, u32[]{:S(2)}, u32[]{:S(2)}) collective-permute-start(bf16[8,256,128]{2,1,0:T(8,128)(2,1)S(1)} %pad_maximum_fusion.5.refs_4_), channel_id=1, source_target_pairs={{0,6},{2,0},{4,2},{6,4},{32,38},{34,32},{36,34},{38,36},{64,70},{6... | collective-permute-start | bytes 1572872 | tf_op jit(solution)/shard_map/ppermute | solution.py:37
  118.0 11.6 %collective-permute-done.22.refs_6_ = bf16[8,256,128]{2,1,0:T(8,128)(2,1)S(1)} collective-permute-done((bf16[8,256,128]{2,1,0:T(8,128)(2,1)S(1)}, bf16[8,256,128]{2,1,0:T(8,128)(2,1)S(1)}, u32[]{:S(2)}, u32[]{:S(2)}) %collective-permute-start.22) | collective-permute-done | bytes 524320 | tf_op jit(solution)/shard_map/ppermute | solution.py:37
  129.6 0.9 collective-permute-start.13
  130.5 2.6 %collective-permute-start.30 = (bf16[8,256,128]{2,1,0:T(8,128)(2,1)S(1)}, bf16[8,256,128]{2,1,0:T(8,128)(2,1)S(1)}, u32[]{:S(2)}, u32[]{:S(2)}) collective-permute-start(bf16[8,256,128]{2,1,0:T(8,128)(2,1)S(1)} %pad_maximum_fusion.4.refs_3_), channel_id=1, source_target_pairs={{0,6},{2,0},{4,2},{6,4},{32,38},{34,32},{36,34},{38,36},{64,70},{6... | collective-permute-start | bytes 1572872 | tf_op jit(solution)/shard_map/ppermute | solution.py:37
  133.1 2.1 collective-permute-start.11
  135.2 3.7 %collective-permute-done.29.refs_7_ = bf16[8,256,128]{2,1,0:T(8,128)(2,1)S(1)} collective-permute-done((bf16[8,256,128]{2,1,0:T(8,128)(2,1)S(1)}, bf16[8,256,128]{2,1,0:T(8,128)(2,1)S(1)}, u32[]{:S(2)}, u32[]{:S(2)}) %collective-permute-start.29) | collective-permute-done | bytes 524320 | tf_op jit(solution)/shard_map/ppermute | solution.py:37
  138.9 4.0 %collective-permute-start.28 = (bf16[8,256,384]{2,1,0:T(8,128)(2,1)S(1)}, bf16[8,256,384]{2,1,0:T(8,128)(2,1)S(1)}, u32[]{:S(2)}, u32[]{:S(2)}) collective-permute-start(bf16[8,256,384]{2,1,0:T(8,128)(2,1)S(1)} %pad_maximum_fusion.2.refs_0_), channel_id=1, source_target_pairs={{0,17},{2,19},{4,21},{6,23},{32,49},{34,51},{36,53},{38,55},{64,81... | collective-permute-start | bytes 4718600 | tf_op jit(solution)/shard_map/ppermute | solution.py:37
  142.9 2.0 collective-permute-start.14
  145.1 8.3 %collective-permute-start.9 = (bf16[8,256,384]{2,1,0:T(8,128)(2,1)S(1)}, bf16[8,256,384]{2,1,0:T(8,128)(2,1)S(1)}, u32[]{:S(2)}, u32[]{:S(2)}) collective-permute-start(bf16[8,256,384]{2,1,0:T(8,128)(2,1)S(1)} %collective-permute-done.8.refs_0_), channel_id=1, source_target_pairs={{0,1},{2,3},{4,5},{6,7},{32,33},{34,35},{36,37},{38,39},{64,65},{6... | collective-permute-start | bytes 4718600 | tf_op jit(solution)/shard_map/ppermute | solution.py:37
  153.4 1.9 collective-permute-start.27
  155.3 14.2 %collective-permute-done.14.refs_5_ = bf16[4,256,384]{2,1,0:T(8,128)(2,1)S(1)} collective-permute-done((bf16[4,256,384]{2,1,0:T(8,128)(2,1)S(1)}, bf16[4,256,384]{2,1,0:T(8,128)(2,1)S(1)}, u32[]{:S(2)}, u32[]{:S(2)}) %collective-permute-start.14) | collective-permute-done | bytes 786464 | tf_op jit(solution)/shard_map/ppermute | solution.py:37
  169.5 3.3 %collective-permute-start.12 = (bf16[4,256,384]{2,1,0:T(8,128)(2,1)S(1)}, bf16[4,256,384]{2,1,0:T(8,128)(2,1)S(1)}, u32[]{:S(2)}, u32[]{:S(2)}) collective-permute-start(bf16[4,256,384]{2,1,0:T(8,128)(2,1)S(1)} %collective-permute-done.11.refs_4_), channel_id=1, source_target_pairs={{0,17},{2,19},{4,21},{6,23},{32,49},{34,51},{36,53},{38,55},{64,81... | collective-permute-start | bytes 2359304 | tf_op jit(solution)/shard_map/ppermute | solution.py:37
  172.9 7.3 %gate_up.4.refs_12_ = f32[904,2048]{1,0:T(8,128)S(1)} custom-call(s32[4]{0:T(128)S(1)} %pad_add_fusion.pos_ref, bf16[8,256,384]{2,1,0:T(8,128)(2,1)S(1)} %pad_maximum_fusion.2.refs_0_, bf16[4,256,384]{2,1,0:T(8,128)(2,1)S(1)} %collective-permute-done.10.refs_1_, bf16[4,256,384]{2,1,0:T(8,128)(2,1)S(1)} %collective-permute-done.13.refs_2_, ...), custom_call_target="tpu_custom_call" | custom-call | flops 3758096384 | bytes 20971520 | tf_op jit(solution)/shard_map/gate_up/pallas_call | solution.py:311
  180.2 9.2 %collective-permute-done.27.refs_2_ = bf16[4,256,384]{2,1,0:T(8,128)(2,1)S(1)} collective-permute-done((bf16[4,256,384]{2,1,0:T(8,128)(2,1)S(1)}, bf16[4,256,384]{2,1,0:T(8,128)(2,1)S(1)}, u32[]{:S(2)}, u32[]{:S(2)}) %collective-permute-start.27) | collective-permute-done | bytes 786464 | tf_op jit(solution)/shard_map/ppermute | solution.py:37
  189.4 1.7 collective-permute-start.23
  191.1 1.8 collective-permute-start.25
  193.0 12.1 %gate_up.5.refs_7_ = f32[904,2048]{1,0:T(8,128)S(1)} custom-call(s32[4]{0:T(128)S(1)} %pad_add_fusion.pos_ref, bf16[8,256,384]{2,1,0:T(8,128)(2,1)S(1)} %collective-permute-done.8.refs_0_, bf16[4,256,384]{2,1,0:T(8,128)(2,1)S(1)} %collective-permute-done.26.refs_1_, ...), custom_call_target="tpu_custom_call", output_to_operand_aliasing={{}: (13, {})} | custom-call | flops 7516192768 | bytes 20971520 | tf_op jit(solution)/shard_map/gate_up/pallas_call | solution.py:311
  205.1 5.3 %gate_up.7 = (f32[8,2048]{1,0:T(8,128)S(1)}, bf16[464,2048]{1,0:T(8,128)(2,1)S(1)}) custom-call(s32[4]{0:T(128)S(1)} %pad_add_fusion.pos_ref, bf16[8,256,384]{2,1,0:T(8,128)(2,1)S(1)} %collective-permute-done.9.refs_0_, bf16[4,256,384]{2,1,0:T(8,128)(2,1)S(1)} %collective-permute-done.12.refs_1_, bf16[4,256,384]{2,1,0:T(8,128)(2,1)S(1)} %collective-permute-done.15.refs_2_, ...), custom_call_target="tpu_custom_call" | custom-call | flops 3758096384 | bytes 20971520 | tf_op jit(solution)/shard_map/gate_up/pallas_call | solution.py:311
  210.4 10.2 %collective-permute-start.31 = (bf16[464,2048]{1,0:T(8,128)(2,1)S(1)}, bf16[464,2048]{1,0:T(8,128)(2,1)S(1)}, u32[]{:S(2)}, u32[]{:S(2)}) collective-permute-start(bf16[464,2048]{1,0:T(8,128)(2,1)S(1)} %get-tuple-element.45), channel_id=1, source_target_pairs={{0,8},{8,0},{1,9},{9,1},{2,10},{10,2},{3,11},{11,3},{4,12},{12,4},... | collective-permute-start | bytes 5701640 | tf_op jit(solution)/shard_map/ppermute | solution.py:41
  220.6 5.2 %gate_up.6.own_ref = f32[448,2048]{1,0:T(8,128)S(1)} custom-call(s32[4]{0:T(128)S(1)} %pad_add_fusion.pos_ref, bf16[8,256,384]{2,1,0:T(8,128)(2,1)S(1)} %collective-permute-done.9.refs_0_, bf16[4,256,384]{2,1,0:T(8,128)(2,1)S(1)} %collective-permute-done.12.refs_1_, bf16[4,256,384]{2,1,0:T(8,128)(2,1)S(1)} %collective-permute-done.15.refs_2_, ...), custom_call_target="tpu_custom_call" | custom-call | flops 3758096384 | bytes 20971520 | tf_op jit(solution)/shard_map/gate_up/pallas_call | solution.py:311
  225.8 1.6 finish.1
  (59 shorter events, 4.2 us)
Async XLA Ops:
  19.4 3.3 %collective-permute-start = (bf16[8,128,256]{2,1,0:T(8,128)(2,1)S(1)}, bf16[8,128,256]{2,1,0:T(8,128)(2,1)S(1)}, u32[]{:S(2)}, u32[]{:S(2)}) collective-permute-start(bf16[8,128,256]{2,1,0:T(8,128)(2,1)S(1)} %all_to_all.10.own_ref), channel_id=1, source_target_pairs={{0,8},{8,0},{1,9},{9,1},{2,10},{10,2},{3,11},{11,3},{4,12},{12,4},... | collective-permute-start | bytes 1572872 | tf_op jit(solution)/shard_map/ppermute | solution.py:41
  21.4 11.9 %copy-start.1 = (bf16[8192,224]{0,1:T(8,128)(2,1)S(1)}, bf16[8192,224]{0,1:T(8,128)(2,1)}, u32[]{:S(2)}) copy-start(bf16[8192,224]{0,1:T(8,128)(2,1)} %param.14) | copy-start | bytes 11010052
  21.4 11.9 %copy-start.2 = (bf16[8192,224]{0,1:T(8,128)(2,1)S(1)}, bf16[8192,224]{0,1:T(8,128)(2,1)}, u32[]{:S(2)}) copy-start(bf16[8192,224]{0,1:T(8,128)(2,1)} %param.15) | copy-start | bytes 11010052
  22.8 1.6 copy-start.4
  24.4 8.9 %copy-start.5 = (f32[8192]{0:T(1024)S(1)}, f32[8192]{0:T(1024)}, u32[]{:S(2)}) copy-start(f32[8192]{0:T(1024)} %param.13) | copy-start | bytes 98308
  39.0 1.6 copy-start.3
  40.5 9.4 %collective-permute-start.1 = (bf16[2,448,1536]{2,1,0:T(8,128)(2,1)}, bf16[2,448,1536]{2,1,0:T(8,128)(2,1)}, u32[]{:S(2)}, u32[]{:S(2)}) collective-permute-start(bf16[2,448,1536]{2,1,0:T(8,128)(2,1)} %get-tuple-element.28), channel_id=1, source_target_pairs={{0,8},{8,0},{1,9},{9,1},{2,10},{10,2},{3,11},{11,3},{4,12},{12,4},... | collective-permute-start | bytes 8257544 | tf_op jit(solution)/shard_map/ppermute | solution.py:41
  40.7 31.6 %all-to-all-start.1 = ((bf16[8,128,1024]{2,1,0:T(8,128)(2,1)}), bf16[8,128,1024]{2,1,0:T(8,128)(2,1)}, u32[]{:S(2)}, u32[]{:S(2)}) async-start(bf16[8,128,1024]{2,1,0:T(8,128)(2,1)} %attend_project.1), calls=%async_computation.1 | async-start | bytes 4194304 | tf_op jit(solution)/shard_map/all_to_all | solution.py:436
  45.7 2.9 %collective-permute-start.2 = (bf16[4,448,256]{2,1,0:T(8,128)(2,1)S(1)}, bf16[4,448,256]{2,1,0:T(8,128)(2,1)}, u32[]{:S(2)}, u32[]{:S(2)}) collective-permute-start(bf16[4,448,256]{2,1,0:T(8,128)(2,1)S(1)} %get-tuple-element.30), channel_id=1, source_target_pairs={{0,8},{8,0},{1,9},{9,1},{2,10},{10,2},{3,11},{11,3},{4,12},{12,4},... | collective-permute-start | bytes 2752520 | tf_op jit(solution)/shard_map/ppermute | solution.py:41
  55.3 19.0 %copy-start.7 = (bf16[128,1024]{1,0:T(8,128)(2,1)S(1)}, bf16[128,1024]{1,0:T(8,128)(2,1)}, u32[]{:S(2)}) copy-start(bf16[128,1024]{1,0:T(8,128)(2,1)} %param.12) | copy-start | bytes 786436
  74.4 40.0 %copy-start.6 = (bf16[128,1024]{1,0:T(8,128)(2,1)}, bf16[128,1024]{1,0:T(8,128)(2,1)S(1)}, u32[]{:S(2)}) copy-start(bf16[128,1024]{1,0:T(8,128)(2,1)S(1)} %add_convert_fusion) | copy-start | bytes 786436
  74.4 2.6 %collective-permute-start.3 = (bf16[128,512]{1,0:T(8,128)(2,1)S(1)}, bf16[128,512]{1,0:T(8,128)(2,1)S(1)}, u32[]{:S(2)}, u32[]{:S(2)}) collective-permute-start(bf16[128,512]{1,0:T(8,128)(2,1)S(1)} %get-tuple-element.47), channel_id=1, source_target_pairs={{0,8},{8,0},{1,9},{9,1},{2,10},{10,2},{3,11},{11,3},{4,12},{12,4},... | collective-permute-start | bytes 393224 | tf_op jit(solution)/shard_map/ppermute | solution.py:41
  77.1 6.1 %collective-permute-start.4 = (bf16[256,384]{1,0:T(8,128)(2,1)S(1)}, bf16[256,384]{1,0:T(8,128)(2,1)S(1)}, u32[]{:S(2)}, u32[]{:S(2)}) collective-permute-start(bf16[256,384]{1,0:T(8,128)(2,1)S(1)} %slice.20), channel_id=1, source_target_pairs={{0,32},{2,34},{4,36},{6,38},{32,64},{34,66},{36,68},{38,70},{64,96... | collective-permute-start | bytes 589832 | tf_op jit(solution)/shard_map/ppermute | solution.py:37
  77.2 7.4 %collective-permute-start.5 = (bf16[256,384]{1,0:T(8,128)(2,1)S(1)}, bf16[256,384]{1,0:T(8,128)(2,1)S(1)}, u32[]{:S(2)}, u32[]{:S(2)}) collective-permute-start(bf16[256,384]{1,0:T(8,128)(2,1)S(1)} %slice.20), channel_id=1, source_target_pairs={{0,96},{2,98},{4,100},{6,102},{32,0},{34,2},{36,4},{38,6},{64,32},... | collective-permute-start | bytes 589832 | tf_op jit(solution)/shard_map/ppermute | solution.py:37
  79.8 6.3 %collective-permute-start.6 = (bf16[256,384]{1,0:T(8,128)(2,1)S(1)}, bf16[256,384]{1,0:T(8,128)(2,1)S(1)}, u32[]{:S(2)}, u32[]{:S(2)}) collective-permute-start(bf16[256,384]{1,0:T(8,128)(2,1)S(1)} %slice.20), channel_id=1, source_target_pairs={{0,64},{2,66},{4,68},{6,70},{32,96},{34,98},{36,100},{38,102},{64,... | collective-permute-start | bytes 589832 | tf_op jit(solution)/shard_map/ppermute | solution.py:37
  86.3 28.3 %collective-permute-start.7 = (bf16[4,256,384]{2,1,0:T(8,128)(2,1)S(1)}, bf16[4,256,384]{2,1,0:T(8,128)(2,1)S(1)}, u32[]{:S(2)}, u32[]{:S(2)}) collective-permute-start(bf16[4,256,384]{2,1,0:T(8,128)(2,1)S(1)} %pad_maximum_fusion.3), channel_id=1, source_target_pairs={{0,2},{2,4},{4,6},{6,0},{32,34},{34,36},{36,38},{38,32},{64,66},{6... | collective-permute-start | bytes 2359304 | tf_op jit(solution)/shard_map/ppermute | solution.py:37
  86.9 14.3 %collective-permute-start.16 = (bf16[256,128]{1,0:T(8,128)(2,1)S(1)}, bf16[256,128]{1,0:T(8,128)(2,1)S(1)}, u32[]{:S(2)}, u32[]{:S(2)}) collective-permute-start(bf16[256,128]{1,0:T(8,128)(2,1)S(1)} %slice.21), channel_id=1, source_target_pairs={{0,1},{2,3},{4,5},{6,7},{32,33},{34,35},{36,37},{38,39},{64,65},{6... | collective-permute-start | bytes 196616 | tf_op jit(solution)/shard_map/ppermute | solution.py:37
  87.0 14.2 %collective-permute-start.17 = (bf16[256,128]{1,0:T(8,128)(2,1)S(1)}, bf16[256,128]{1,0:T(8,128)(2,1)S(1)}, u32[]{:S(2)}, u32[]{:S(2)}) collective-permute-start(bf16[256,128]{1,0:T(8,128)(2,1)S(1)} %slice.21), channel_id=1, source_target_pairs={{0,17},{2,19},{4,21},{6,23},{32,49},{34,51},{36,53},{38,55},{64,81... | collective-permute-start | bytes 196616 | tf_op jit(solution)/shard_map/ppermute | solution.py:37
  89.6 11.6 %collective-permute-start.18 = (bf16[256,128]{1,0:T(8,128)(2,1)S(1)}, bf16[256,128]{1,0:T(8,128)(2,1)S(1)}, u32[]{:S(2)}, u32[]{:S(2)}) collective-permute-start(bf16[256,128]{1,0:T(8,128)(2,1)S(1)} %slice.21), channel_id=1, source_target_pairs={{0,16},{2,18},{4,20},{6,22},{32,48},{34,50},{36,52},{38,54},{64,80... | collective-permute-start | bytes 196616 | tf_op jit(solution)/shard_map/ppermute | solution.py:37
  101.2 71.7 %copy-start = (bf16[2,896,1536]{2,1,0:T(8,128)(2,1)S(1)}, bf16[2,896,1536]{2,1,0:T(8,128)(2,1)}, u32[]{:S(2)}) copy-start(bf16[2,896,1536]{2,1,0:T(8,128)(2,1)} %pad_maximum_fusion.refs_5_.refs_10_) | copy-start | bytes 16515076
  101.3 9.5 %collective-permute-start.19 = (bf16[4,256,128]{2,1,0:T(8,128)(2,1)S(1)}, bf16[4,256,128]{2,1,0:T(8,128)(2,1)S(1)}, u32[]{:S(2)}, u32[]{:S(2)}) collective-permute-start(bf16[4,256,128]{2,1,0:T(8,128)(2,1)S(1)} %pad_maximum_fusion.6), channel_id=1, source_target_pairs={{0,32},{2,34},{4,36},{6,38},{32,64},{34,66},{36,68},{38,70},{64,96... | collective-permute-start | bytes 786440 | tf_op jit(solution)/shard_map/ppermute | solution.py:37
  101.3 12.1 %collective-permute-start.20 = (bf16[4,256,128]{2,1,0:T(8,128)(2,1)S(1)}, bf16[4,256,128]{2,1,0:T(8,128)(2,1)S(1)}, u32[]{:S(2)}, u32[]{:S(2)}) collective-permute-start(bf16[4,256,128]{2,1,0:T(8,128)(2,1)S(1)} %pad_maximum_fusion.6), channel_id=1, source_target_pairs={{0,96},{2,98},{4,100},{6,102},{32,0},{34,2},{36,4},{38,6},{64,32},... | collective-permute-start | bytes 786440 | tf_op jit(solution)/shard_map/ppermute | solution.py:37
  104.3 10.1 %collective-permute-start.21 = (bf16[4,256,128]{2,1,0:T(8,128)(2,1)S(1)}, bf16[4,256,128]{2,1,0:T(8,128)(2,1)S(1)}, u32[]{:S(2)}, u32[]{:S(2)}) collective-permute-start(bf16[4,256,128]{2,1,0:T(8,128)(2,1)S(1)} %pad_maximum_fusion.6), channel_id=1, source_target_pairs={{0,64},{2,66},{4,68},{6,70},{32,96},{34,98},{36,100},{38,102},{64,... | collective-permute-start | bytes 786440 | tf_op jit(solution)/shard_map/ppermute | solution.py:37
  114.4 15.2 %collective-permute-start.22 = (bf16[8,256,128]{2,1,0:T(8,128)(2,1)S(1)}, bf16[8,256,128]{2,1,0:T(8,128)(2,1)S(1)}, u32[]{:S(2)}, u32[]{:S(2)}) collective-permute-start(bf16[8,256,128]{2,1,0:T(8,128)(2,1)S(1)} %pad_maximum_fusion.4.refs_3_), channel_id=1, source_target_pairs={{0,2},{2,4},{4,6},{6,0},{32,34},{34,36},{36,38},{38,32},{64,66},{6... | collective-permute-start | bytes 1572872 | tf_op jit(solution)/shard_map/ppermute | solution.py:37
  114.8 30.3 %collective-permute-start.8 = (bf16[8,256,384]{2,1,0:T(8,128)(2,1)S(1)}, bf16[8,256,384]{2,1,0:T(8,128)(2,1)S(1)}, u32[]{:S(2)}, u32[]{:S(2)}) collective-permute-start(bf16[8,256,384]{2,1,0:T(8,128)(2,1)S(1)} %pad_maximum_fusion.2.refs_0_), channel_id=1, source_target_pairs={{0,1},{2,3},{4,5},{6,7},{32,33},{34,35},{36,37},{38,39},{64,65},{6... | collective-permute-start | bytes 4718600 | tf_op jit(solution)/shard_map/ppermute | solution.py:37
  115.4 17.7 %collective-permute-start.10 = (bf16[4,256,384]{2,1,0:T(8,128)(2,1)S(1)}, bf16[4,256,384]{2,1,0:T(8,128)(2,1)S(1)}, u32[]{:S(2)}, u32[]{:S(2)}) collective-permute-start(bf16[4,256,384]{2,1,0:T(8,128)(2,1)S(1)} %pad_maximum_fusion.3), channel_id=1, source_target_pairs={{0,6},{2,0},{4,2},{6,4},{32,38},{34,32},{36,34},{38,36},{64,70},{6... | collective-permute-start | bytes 2359304 | tf_op jit(solution)/shard_map/ppermute | solution.py:37
  115.4 15.1 %collective-permute-start.24 = (bf16[8,256,128]{2,1,0:T(8,128)(2,1)S(1)}, bf16[8,256,128]{2,1,0:T(8,128)(2,1)S(1)}, u32[]{:S(2)}, u32[]{:S(2)}) collective-permute-start(bf16[8,256,128]{2,1,0:T(8,128)(2,1)S(1)} %pad_maximum_fusion.5.refs_4_), channel_id=1, source_target_pairs={{0,6},{2,0},{4,2},{6,4},{32,38},{34,32},{36,34},{38,36},{64,70},{6... | collective-permute-start | bytes 1572872 | tf_op jit(solution)/shard_map/ppermute | solution.py:37
  118.0 21.0 %collective-permute-start.29 = (bf16[8,256,128]{2,1,0:T(8,128)(2,1)S(1)}, bf16[8,256,128]{2,1,0:T(8,128)(2,1)S(1)}, u32[]{:S(2)}, u32[]{:S(2)}) collective-permute-start(bf16[8,256,128]{2,1,0:T(8,128)(2,1)S(1)} %pad_maximum_fusion.5.refs_4_), channel_id=1, source_target_pairs={{0,2},{2,4},{4,6},{6,0},{32,34},{34,36},{36,38},{38,32},{64,66},{6... | collective-permute-start | bytes 1572872 | tf_op jit(solution)/shard_map/ppermute | solution.py:37
  129.6 13.3 %collective-permute-start.13 = (bf16[4,256,384]{2,1,0:T(8,128)(2,1)S(1)}, bf16[4,256,384]{2,1,0:T(8,128)(2,1)S(1)}, u32[]{:S(2)}, u32[]{:S(2)}) collective-permute-start(bf16[4,256,384]{2,1,0:T(8,128)(2,1)S(1)} %pad_maximum_fusion.3), channel_id=1, source_target_pairs={{0,4},{2,6},{4,0},{6,2},{32,36},{34,38},{36,32},{38,34},{64,68},{6... | collective-permute-start | bytes 2359304 | tf_op jit(solution)/shard_map/ppermute | solution.py:37
  130.5 14.4 %collective-permute-start.30 = (bf16[8,256,128]{2,1,0:T(8,128)(2,1)S(1)}, bf16[8,256,128]{2,1,0:T(8,128)(2,1)S(1)}, u32[]{:S(2)}, u32[]{:S(2)}) collective-permute-start(bf16[8,256,128]{2,1,0:T(8,128)(2,1)S(1)} %pad_maximum_fusion.4.refs_3_), channel_id=1, source_target_pairs={{0,6},{2,0},{4,2},{6,4},{32,38},{34,32},{36,34},{38,36},{64,70},{6... | collective-permute-start | bytes 1572872 | tf_op jit(solution)/shard_map/ppermute | solution.py:37
  133.1 20.3 %collective-permute-start.11 = (bf16[4,256,384]{2,1,0:T(8,128)(2,1)S(1)}, bf16[4,256,384]{2,1,0:T(8,128)(2,1)S(1)}, u32[]{:S(2)}, u32[]{:S(2)}) collective-permute-start(bf16[4,256,384]{2,1,0:T(8,128)(2,1)S(1)} %collective-permute-done.10.refs_1_), channel_id=1, source_target_pairs={{0,17},{2,19},{4,21},{6,23},{32,49},{34,51},{36,53},{38,55},{64,81... | collective-permute-start | bytes 2359304 | tf_op jit(solution)/shard_map/ppermute | solution.py:37
  138.9 52.2 %collective-permute-start.28 = (bf16[8,256,384]{2,1,0:T(8,128)(2,1)S(1)}, bf16[8,256,384]{2,1,0:T(8,128)(2,1)S(1)}, u32[]{:S(2)}, u32[]{:S(2)}) collective-permute-start(bf16[8,256,384]{2,1,0:T(8,128)(2,1)S(1)} %pad_maximum_fusion.2.refs_0_), channel_id=1, source_target_pairs={{0,17},{2,19},{4,21},{6,23},{32,49},{34,51},{36,53},{38,55},{64,81... | collective-permute-start | bytes 4718600 | tf_op jit(solution)/shard_map/ppermute | solution.py:37
  142.9 26.6 %collective-permute-start.14 = (bf16[4,256,384]{2,1,0:T(8,128)(2,1)S(1)}, bf16[4,256,384]{2,1,0:T(8,128)(2,1)S(1)}, u32[]{:S(2)}, u32[]{:S(2)}) collective-permute-start(bf16[4,256,384]{2,1,0:T(8,128)(2,1)S(1)} %collective-permute-done.13.refs_2_), channel_id=1, source_target_pairs={{0,17},{2,19},{4,21},{6,23},{32,49},{34,51},{36,53},{38,55},{64,81... | collective-permute-start | bytes 2359304 | tf_op jit(solution)/shard_map/ppermute | solution.py:37
  144.9 27.9 %collective-permute-start.26 = (bf16[4,256,384]{2,1,0:T(8,128)(2,1)S(1)}, bf16[4,256,384]{2,1,0:T(8,128)(2,1)S(1)}, u32[]{:S(2)}, u32[]{:S(2)}) collective-permute-start(bf16[4,256,384]{2,1,0:T(8,128)(2,1)S(1)} %collective-permute-done.10.refs_1_), channel_id=1, source_target_pairs={{0,1},{2,3},{4,5},{6,7},{32,33},{34,35},{36,37},{38,39},{64,65},{6... | collective-permute-start | bytes 2359304 | tf_op jit(solution)/shard_map/ppermute | solution.py:37
  145.1 60.0 %collective-permute-start.9 = (bf16[8,256,384]{2,1,0:T(8,128)(2,1)S(1)}, bf16[8,256,384]{2,1,0:T(8,128)(2,1)S(1)}, u32[]{:S(2)}, u32[]{:S(2)}) collective-permute-start(bf16[8,256,384]{2,1,0:T(8,128)(2,1)S(1)} %collective-permute-done.8.refs_0_), channel_id=1, source_target_pairs={{0,1},{2,3},{4,5},{6,7},{32,33},{34,35},{36,37},{38,39},{64,65},{6... | collective-permute-start | bytes 4718600 | tf_op jit(solution)/shard_map/ppermute | solution.py:37
  153.4 36.0 %collective-permute-start.27 = (bf16[4,256,384]{2,1,0:T(8,128)(2,1)S(1)}, bf16[4,256,384]{2,1,0:T(8,128)(2,1)S(1)}, u32[]{:S(2)}, u32[]{:S(2)}) collective-permute-start(bf16[4,256,384]{2,1,0:T(8,128)(2,1)S(1)} %collective-permute-done.13.refs_2_), channel_id=1, source_target_pairs={{0,1},{2,3},{4,5},{6,7},{32,33},{34,35},{36,37},{38,39},{64,65},{6... | collective-permute-start | bytes 2359304 | tf_op jit(solution)/shard_map/ppermute | solution.py:37
  169.5 35.5 %collective-permute-start.12 = (bf16[4,256,384]{2,1,0:T(8,128)(2,1)S(1)}, bf16[4,256,384]{2,1,0:T(8,128)(2,1)S(1)}, u32[]{:S(2)}, u32[]{:S(2)}) collective-permute-start(bf16[4,256,384]{2,1,0:T(8,128)(2,1)S(1)} %collective-permute-done.11.refs_4_), channel_id=1, source_target_pairs={{0,17},{2,19},{4,21},{6,23},{32,49},{34,51},{36,53},{38,55},{64,81... | collective-permute-start | bytes 2359304 | tf_op jit(solution)/shard_map/ppermute | solution.py:37
  172.8 32.2 %collective-permute-start.15 = (bf16[4,256,384]{2,1,0:T(8,128)(2,1)S(1)}, bf16[4,256,384]{2,1,0:T(8,128)(2,1)S(1)}, u32[]{:S(2)}, u32[]{:S(2)}) collective-permute-start(bf16[4,256,384]{2,1,0:T(8,128)(2,1)S(1)} %collective-permute-done.14.refs_5_), channel_id=1, source_target_pairs={{0,17},{2,19},{4,21},{6,23},{32,49},{34,51},{36,53},{38,55},{64,81... | collective-permute-start | bytes 2359304 | tf_op jit(solution)/shard_map/ppermute | solution.py:37
  189.4 15.7 %collective-permute-start.23 = (bf16[8,256,128]{2,1,0:T(8,128)(2,1)S(1)}, bf16[8,256,128]{2,1,0:T(8,128)(2,1)S(1)}, u32[]{:S(2)}, u32[]{:S(2)}) collective-permute-start(bf16[8,256,128]{2,1,0:T(8,128)(2,1)S(1)} %collective-permute-done.22.refs_6_), channel_id=1, source_target_pairs={{0,2},{2,4},{4,6},{6,0},{32,34},{34,36},{36,38},{38,32},{64,66},{6... | collective-permute-start | bytes 1572872 | tf_op jit(solution)/shard_map/ppermute | solution.py:37
  191.1 13.9 %collective-permute-start.25 = (bf16[8,256,128]{2,1,0:T(8,128)(2,1)S(1)}, bf16[8,256,128]{2,1,0:T(8,128)(2,1)S(1)}, u32[]{:S(2)}, u32[]{:S(2)}) collective-permute-start(bf16[8,256,128]{2,1,0:T(8,128)(2,1)S(1)} %collective-permute-done.24.refs_9_), channel_id=1, source_target_pairs={{0,6},{2,0},{4,2},{6,4},{32,38},{34,32},{36,34},{38,36},{64,70},{6... | collective-permute-start | bytes 1572872 | tf_op jit(solution)/shard_map/ppermute | solution.py:37
  210.4 15.4 %collective-permute-start.31 = (bf16[464,2048]{1,0:T(8,128)(2,1)S(1)}, bf16[464,2048]{1,0:T(8,128)(2,1)S(1)}, u32[]{:S(2)}, u32[]{:S(2)}) collective-permute-start(bf16[464,2048]{1,0:T(8,128)(2,1)S(1)} %get-tuple-element.45), channel_id=1, source_target_pairs={{0,8},{8,0},{1,9},{9,1},{2,10},{10,2},{3,11},{11,3},{4,12},{12,4},... | collective-permute-start | bytes 5701640 | tf_op jit(solution)/shard_map/ppermute | solution.py:41

commit v6 on v5

--- a/solution.py
+++ b/solution.py
@@ -23,13 +23,18 @@
 F32 = jnp.float32
 
 
-def shift(x, axes, by):
+def move(x, axes, by):
     pairs = []
     for core in range(2):
+        if axes[core] is None:
+            continue
         for n in range(64):
             at = {"x": n // 16, "y": n // 4 % 4, "z": n % 4}
             to = dict(at)
-            to[axes[core]] = (to[axes[core]] + by) % 4
+            if axes[core] == "p":
+                to["x"] ^= 1
+            else:
+                to[axes[core]] = (to[axes[core]] + by[core]) % 4
             pairs.append(tuple(
                 (((p["y"] * 2 + p["x"] // 2) * 2 + core) * 4 + p["z"]) * 2 + p["x"] % 2
                 for p in (at, to)
@@ -37,15 +42,21 @@
     return lax.ppermute(x, MESH, pairs)
 
 
+def shift(x, axes, by):
+    return move(x, axes, (by, by))
+
+
 def swap_core(x):
     return lax.ppermute(x, "c", [(0, 1), (1, 0)])
 
 
-def attend_kernel(pos_ref, q_ref, own_ref, oth_ref, w_hbm, out_ref, w_buf, qs, acc, att, sems):
+def attend_kernel(pos_ref, q_ref, own_ref, oth_ref, w_hbm, *refs):
+    outs, (w_buf, qs, acc, att, sems) = refs[:4], refs[4:]
     blocks = w_buf.shape[0]
     width = w_buf.shape[2]
     for b in range(blocks):
-        pltpu.make_async_copy(w_hbm.at[:, pl.ds(b * width, width)], w_buf.at[b], sems.at[b]).start()
+        at = pl.multiple_of(pos_ref[2 + b] * width, width)
+        pltpu.make_async_copy(w_hbm.at[:, pl.ds(at, width)], w_buf.at[b], sems.at[b]).start()
     heads = q_ref.shape[1] // HD
     rows = q_ref.shape[0]
     cols = heads * rows
@@ -95,12 +106,15 @@
     for h in range(heads):
         att[:, h * HD:(h + 1) * HD] = final[:, h * rows:(h + 1) * rows].T.astype(BF)
 
-    def project(b, _):
-        pltpu.make_async_copy(w_hbm.at[:, pl.ds(0, width)], w_buf.at[b], sems.at[b]).wait()
-        out_ref[b] = jnp.dot(att[...], w_buf[b], preferred_element_type=F32).astype(BF)
-        return 0
-
-    lax.fori_loop(0, blocks, project, 0)
+    for j, out_ref in enumerate(outs):
+
+        def project(i, _, j=j, out_ref=out_ref):
+            b = j * 2 + i
+            pltpu.make_async_copy(w_hbm.at[:, pl.ds(0, width)], w_buf.at[b], sems.at[b]).wait()
+            out_ref[i] = jnp.dot(att[...], w_buf[b], preferred_element_type=F32).astype(BF)
+            return 0
+
+        lax.fori_loop(0, 2, project, 0)
 
 
 def attend_project(pos, q, own, oth, w, blocks):
@@ -110,9 +124,9 @@
     vm = pl.BlockSpec(memory_space=pltpu.VMEM)
     return pl.pallas_call(
         attend_kernel,
-        out_shape=jax.ShapeDtypeStruct((blocks, rows, width), BF),
+        out_shape=[jax.ShapeDtypeStruct((2, rows, width), BF)] * 4,
         in_specs=[pl.BlockSpec(memory_space=pltpu.SMEM), vm, vm, vm, pl.BlockSpec(memory_space=pl.ANY)],
-        out_specs=vm,
+        out_specs=[vm] * 4,
         scratch_shapes=[
             pltpu.VMEM((blocks, depth, width), BF),
             pltpu.VMEM((rows * cols // HD, HD), BF),
@@ -124,6 +138,44 @@
         cost_estimate=pl.CostEstimate(flops=4 << 30, bytes_accessed=20 << 20, transcendentals=2 << 20),
         name="attend_project",
     )(pos, q, own, oth, w)
+
+
+def middle_kernel(pos_ref, third, keep, r1, r2, r3, b1, b2, b3, mine, buf):
+    z_at, xl = pos_ref[2], pos_ref[0] & 1
+
+    @pl.when(pos_ref[3] == 0)
+    def _():
+        for i, (kept, got) in enumerate(((third, r1), (keep, r2))):
+            for j in range(2):
+                buf[2 * i + j] = kept[j].astype(F32) + got[j].astype(F32)
+        for ref, off in ((b1, 1), (b2, 3), (b3, 2)):
+            ref[...] = buf[(z_at + off) & 3].astype(BF)
+        mine[...] = buf[z_at]
+
+    @pl.when(pos_ref[3] != 0)
+    def _():
+        for j in range(2):
+            buf[j] = (
+                keep[j].astype(F32) + r1[j].astype(F32) + r2[j].astype(F32) + r3[j].astype(F32)
+            )
+        b1[...] = buf[1 - xl].astype(BF)
+        mine[...] = buf[xl]
+
+
+def middle(pos, *pieces):
+    rows, cols = pieces[0].shape[1:]
+    vm = pl.BlockSpec(memory_space=pltpu.VMEM)
+    part = jax.ShapeDtypeStruct((rows, cols), BF)
+    return pl.pallas_call(
+        middle_kernel,
+        out_shape=[part, part, part, jax.ShapeDtypeStruct((rows, cols), F32)],
+        in_specs=[pl.BlockSpec(memory_space=pltpu.SMEM)] + [vm] * 5,
+        out_specs=[vm] * 4,
+        scratch_shapes=[pltpu.VMEM((4, rows, cols), F32)],
+        compiler_params=pltpu.CompilerParams(vmem_limit_bytes=16 << 20),
+        cost_estimate=pl.CostEstimate(flops=1 << 20, bytes_accessed=4 << 20, transcendentals=0),
+        name="middle",
+    )(pos, *pieces)
 
 
 def prep_kernel(pos_ref, g_ref, u_ref, gain_ref, km_ref, ks_ref, sm_ref, ss_ref):
@@ -158,7 +210,7 @@
             in_specs=[wspec, wspec, pl.BlockSpec((1, 1024), lambda i, pos: (0, i))],
             out_specs=[mspec, sspec, mspec, sspec],
         ),
-        compiler_params=pltpu.CompilerParams(vmem_limit_bytes=16 << 20),
+        compiler_params=pltpu.CompilerParams(vmem_limit_bytes=58 << 20),
         cost_estimate=pl.CostEstimate(flops=8 << 20, bytes_accessed=15 << 20, transcendentals=0),
         name="prepare",
     )(pos, gate_t, up_t, gain)
@@ -167,21 +219,33 @@
 def gate_kernel(which, stage, pos_ref, *refs):
     count = len(which)
     refs = list(refs)
-    main = {c: tuple(refs.pop(0) for _ in range(3)) for c in which}
-    side = {c: (refs.pop(0), refs.pop(0)) for c in which}
-    wm, ws = refs.pop(0), refs.pop(0)
     first = stage == "first"
     last = stage in ("theirs", "mine")
-    before = None if first else refs.pop(0)
+    if stage != "mine":
+        main = {c: tuple(refs.pop(0) for _ in range(3)) for c in which}
+        side = {c: (refs.pop(0), refs.pop(0)) for c in which}
+    if first:
+        halves = [refs.pop(0) for _ in range(4)]
+        acc, wm, ws = (refs.pop(0) for _ in range(3))
+        wsem = refs.pop()
+        n2 = halves[0].shape[1]
+        for j, src in enumerate(halves):
+            pltpu.make_async_copy(
+                src, (wm, ws)[j // 2].at[:, pl.ds((j % 2) * n2, n2), :], wsem.at[j // 2]
+            ).start()
+    else:
+        wm, ws, before = (refs.pop(0) for _ in range(3))
     if stage == "theirs":
-        own_ss, par_ref = refs.pop(0), refs.pop(0)
+        own_ss, par_ref, hm, hs = (refs.pop(0) for _ in range(4))
     elif stage == "mine":
-        own_ref = refs.pop(0)
-    else:
+        hm, hs, own_ref = (refs.pop(0) for _ in range(3))
+    elif stage == "middle":
         acc = refs.pop(0)
     if last:
         acc = refs.pop()
-    hm, hs, ssq, table, msem, ssem = refs
+    if not last:
+        hm, hs = refs.pop(0), refs.pop(0)
+    ssq, table, msem, ssem = refs
     x_at, y_at, z_at, core = (pos_ref[m] for m in range(4))
     both = wm.shape[1]
     n2 = both // 2
@@ -206,9 +270,11 @@
             y = jnp.where(core == 0, at(y_at, j), at(y_at, c))
             table[2 * u] = y * 2 + x // 2
             table[2 * u + 1] = x & 1
+            if stage == "mine":
+                continue
             pl.when(core == 0)(functools.partial(fetch, u, c, j, 0))
             pl.when(core != 0)(functools.partial(fetch, u, c, j, 1))
-    for m, c in enumerate(which):
+    for m, c in enumerate(which if stage != "mine" else ()):
         for b in range(4):
             for a in range(4):
                 x = at(x_at, a)
@@ -241,7 +307,8 @@
         )
 
     def unit(u, _):
-        pltpu.make_async_copy(hm.at[u], hm.at[u], msem.at[u]).wait()
+        if stage != "mine":
+            pltpu.make_async_copy(hm.at[u], hm.at[u], msem.at[u]).wait()
         cols = pl.ds(pl.multiple_of(table[2 * u] * 256, 256), 256)
         block = hm[u]
         acc[:rows, cols] += lax.dot_general(
@@ -252,8 +319,12 @@
             ssq[cols, :] += squares(block)
         return 0
 
+    if first:
+        pltpu.make_async_copy(wm, wm, wsem.at[0]).wait()
     lax.fori_loop(0, 4 * count, unit, 0)
-    for m in range(count):
+    if first:
+        pltpu.make_async_copy(ws, ws, wsem.at[1]).wait()
+    for m in range(count if stage != "mine" else 0):
         pltpu.make_async_copy(hs.at[m], hs.at[m], ssem.at[m]).wait()
     piece = 512
 
@@ -290,47 +361,59 @@
     lax.fori_loop(0, hs.shape[1] // piece, tail, 0)
 
 
-def gate_up(pos, which, main, side, weights, before, stage):
-    n2 = weights[0].shape[1] // 2
+def gate_up(pos, which, pieces, weights, held, stage):
+    n2 = weights[0].shape[1] // (1 if stage == "first" else 2)
     tokens = 2048
     count = len(which)
-    first = before is None
-    last = stage in ("theirs", "mine")
     any_spec = pl.BlockSpec(memory_space=pl.ANY)
     vm = pl.BlockSpec(memory_space=pltpu.VMEM)
-    pieces = [p for part in (main, side) for c in which for p in part[c]]
-    operands = pieces + list(weights) + ([] if first else [before])
+    loose = list(pieces) + (list(weights) if stage == "first" else [])
+    fixed = ([] if stage == "first" else list(weights)) + list(held)
+    blocks = [
+        jax.ShapeDtypeStruct((4 * count, 256, 4 * MCOLS), BF),
+        jax.ShapeDtypeStruct((count, tokens, 2 * SCOLS), BF),
+    ]
     partial = jax.ShapeDtypeStruct((2 * n2 + 8, tokens), F32)
     out_shape = {
+        "first": [
+            partial,
+            jax.ShapeDtypeStruct((2, 2 * n2, 4 * MCOLS), BF),
+            jax.ShapeDtypeStruct((4, 2 * n2, 2 * SCOLS), BF),
+        ],
+        "middle": [partial],
         "theirs": [
             jax.ShapeDtypeStruct((8, tokens), F32),
             jax.ShapeDtypeStruct((n2 + 16, tokens), BF),
-        ],
-        "mine": jax.ShapeDtypeStruct((n2, tokens), F32),
-    }.get(stage, partial)
+        ] + blocks,
+        "mine": [jax.ShapeDtypeStruct((n2, tokens), F32)],
+    }[stage]
+    last = stage in ("theirs", "mine")
+    scratch = [] if last else [pltpu.VMEM(t.shape, BF) for t in blocks]
+    scratch += [
+        pltpu.VMEM((tokens, 128), F32),
+        pltpu.SMEM((8 * count,), jnp.int32),
+        pltpu.SemaphoreType.DMA((4 * count,)),
+        pltpu.SemaphoreType.DMA((count,)),
+    ]
+    if stage == "first":
+        scratch.append(pltpu.SemaphoreType.DMA((2,)))
+    if last:
+        scratch.append(pltpu.VMEM((n2, tokens), F32))
     return pl.pallas_call(
         functools.partial(gate_kernel, which, stage),
         out_shape=out_shape,
         in_specs=[pl.BlockSpec(memory_space=pltpu.SMEM)]
-        + [any_spec] * len(pieces)
-        + [vm] * (len(operands) - len(pieces)),
-        out_specs=[vm] * 2 if stage == "theirs" else vm,
-        scratch_shapes=[
-            pltpu.VMEM((4 * count, 256, 4 * MCOLS), BF),
-            pltpu.VMEM((count, tokens, 2 * SCOLS), BF),
-            pltpu.VMEM((tokens, 128), F32),
-            pltpu.SMEM((8 * count,), jnp.int32),
-            pltpu.SemaphoreType.DMA((4 * count,)),
-            pltpu.SemaphoreType.DMA((count,)),
-        ]
-        + ([pltpu.VMEM((n2, tokens), F32)] if last else []),
-        input_output_aliases={} if first or last else {len(operands): 0},
+        + [any_spec] * len(loose)
+        + [vm] * len(fixed),
+        out_specs=[vm] * len(out_shape),
+        scratch_shapes=scratch,
+        input_output_aliases={len(loose) + len(fixed): 0} if stage == "middle" else {},
         compiler_params=pltpu.CompilerParams(vmem_limit_bytes=(10 + 8 * count) << 20),
         cost_estimate=pl.CostEstimate(
             flops=count * n2 * tokens * 4096, bytes_accessed=20 << 20, transcendentals=0
         ),
         name="gate_up",
-    )(pos, *operands)
+    )(pos, *loose, *fixed)
 
 
 def finish_kernel(own_ref, ss_ref, got_ref, out_ref, buf, sems, *, depth):
@@ -429,25 +512,45 @@
     own = lax.all_to_all(spread, ("y", "xh"), 0, 0, tiled=True)
     oth = swap_core(own)
 
-    pos = jnp.stack([group, core]).astype(jnp.int32)
-    partial = attend_project(pos, queries, own, oth, out_weight, 8)
     pos2 = jnp.stack([x_at, y_at, z_at, core]).astype(jnp.int32)
-    partial, gate_raw, up_raw = lax.optimization_barrier((partial, gate_weight.T, up_weight.T))
-    terms = lax.all_to_all(partial, HEAD, 0, 0, tiled=True)
+    slots = [
+        jnp.where(core == 0, p * 2 + q, ((z_at + r) & 3) * 2 + t)
+        for p, q, r, t in zip(
+            (0, 1, 2, 3) * 2, [1 - xl] * 4 + [xl] * 4, (1, 1, 3, 3, 2, 2, 0, 0), (0, 1) * 4
+        )
+    ]
+    pos = jnp.stack([group, core] + slots).astype(jnp.int32)
+    first, second, third, keep = attend_project(pos, queries, own, oth, out_weight, 8)
+    first, second, third, keep, gate_raw, up_raw = lax.optimization_barrier(
+        (first, second, third, keep, gate_weight.T, up_weight.T)
+    )
+    r1 = move(first, ("p", "z"), (0, 1))
+    r2 = move(second, ("p", "z"), (0, -1))
+    r3 = move(third, (None, "z"), (0, 2))
     km, ks, sm, ss = prepare(pos2, gate_raw, up_raw, norm_gain[None, :])
-    weights = [jnp.concatenate([k, swap_core(t)], 1) for k, t in ((km, sm), (ks, ss))]
-    terms, weights = lax.optimization_barrier((terms, weights))
-    hidden = (residual.astype(F32) + jnp.sum(terms.astype(F32), axis=0)).astype(BF)
+    b1, b2, b3, mine = middle(pos2, third, keep, r1, r2, r3)
+    terms = [
+        move(b1, ("z", "p"), (1, 0)),
+        move(b2, ("z", None), (-1, 0)),
+        move(b3, ("z", None), (2, 0)),
+    ]
+    terms, gm, gs = lax.optimization_barrier((terms, swap_core(sm), swap_core(ss)))
+    total = mine + sum(t.astype(F32) for t in terms)
+    hidden = (residual.astype(F32) + total).astype(BF)
 
     keep = jnp.where(core == 0, hidden[:, :512], hidden[:, 512:])
     got = swap_core(jnp.where(core == 0, hidden[:, 512:], hidden[:, :512]))
     chip = jnp.where(core == 0, jnp.concatenate([keep, got], 0), jnp.concatenate([got, keep], 0))
     main, side = gather((chip[:, :MCOLS], chip[:, MCOLS:]), (MAIN, SIDE))
-    sums = gate_up(pos2, (0,), main, side, weights, None, "first")
-    sums = gate_up(pos2, (1, 2), main, side, weights, sums, "middle")
-    own_ss, theirs = gate_up(pos2, (3,), main, side, weights, sums, "theirs")
+
+    def pieces(*slots):
+        return [p for part in (main, side) for c in slots for p in part[c]]
+
+    sums, wm, ws = gate_up(pos2, (0,), pieces(0), (km, gm, ks, gs), (), "first")
+    sums, = gate_up(pos2, (1, 2), pieces(1, 2), (wm, ws), (sums,), "middle")
+    own_ss, theirs, hm, hs = gate_up(pos2, (3,), pieces(3), (wm, ws), (sums,), "theirs")
     got = swap_core(theirs)
-    own_sums = gate_up(pos2, (3,), main, side, weights, sums, "mine")
+    own_sums, = gate_up(pos2, (3,), (), (wm, ws), (sums, hm, hs), "mine")
     out = finish(own_sums, own_ss, got, norm_gain.shape[0])
     return out.T, hidden
 

time: 231 us -> 224 us (0.970); the launches traced: 228 us -> 223 us
  other arithmetic: 10.2 us -> 2.12 us
  Pallas kernels: 46 us -> 49.6 us
  waiting for transfers between devices: 86.5 us -> 89.7 us
    ppermute x27 -> x33, waiting for transfers between devices: 64.9 us -> 87.9 us  [move(): return lax.ppermute(x, MESH, pairs)]
    all_to_all x1 -> x0, waiting for transfers between devices: 17 us -> none  [per_device(): terms = lax.all_to_all(partial, HEAD, 0, 0, tiled=True)]
    concatenate x2 -> x0, other arithmetic: 6.68 us -> none  [per_device(): jnp.concatenate([k, swap_core(t)], 1)]
    all_to_all x1 -> x0, starting transfers between devices: 5.06 us -> none  [per_device(): terms = lax.all_to_all(partial, HEAD, 0, 0, tiled=True)]
    ppermute x27 -> x33, starting transfers between devices: 43.1 us -> 47.8 us  [move(): return lax.ppermute(x, MESH, pairs)]
    pallas_call x1, Pallas kernels: 5.66 us -> 9.46 us  [prepare(): pl.pallas_call(prep_kernel, out_shape=[mshape, sshape, mshape, sshape], g...]
    ppermute x5, waiting for transfers between devices: 4.6 us -> 1.82 us  [swap_core(): return lax.ppermute(x, 'c', [(0, 1), (1, 0)])]
    pallas_call x1 -> x2, Pallas kernels: 8.88 us -> 8.48 us  [the longest x1 7.45 us: attend_project(): pl.pallas_call(attend_kernel, out_shape=[jax.ShapeDtypeStruct((2, rows, w...]
  transfers between devices with their start and end apart: 33 -> 38, of which waited for: 15 -> 18; matrix products, arithmetic and copies ran while one was open for 3% -> 0% of each run, Pallas kernels for 11% -> 11%
where the time goes in v6:
time: 224 us; the launch traced here: 223 us
  waiting for transfers between devices  89.7 us (40%)
  starting transfers between devices  61.4 us (27%)
  Pallas kernels  49.6 us (22%)
  blocking collectives  18 us (8%)
    ppermute x33, waiting for transfers between devices, move(): return lax.ppermute(x, MESH, pairs)  87.9 us
    ppermute x33, starting transfers between devices, move(): return lax.ppermute(x, MESH, pairs)  47.8 us
    pallas_call x4, Pallas kernels, gate_up(): pl.pallas_call(functools.partial(gate_kernel, which, stage), out_shape=ou...  30.1 us
    all_to_all x1, blocking collectives, per_device(): own = lax.all_to_all(spread, ('y', 'xh'), 0, 0, tiled=True)  18 us
    ppermute x5, starting transfers between devices, swap_core(): return lax.ppermute(x, 'c', [(0, 1), (1, 0)])  13.6 us
    pallas_call x1, Pallas kernels, prepare(): pl.pallas_call(prep_kernel, out_shape=[mshape, sshape, mshape, sshape], g...  9.46 us
    pallas_call x1, Pallas kernels, attend_project(): pl.pallas_call(attend_kernel, out_shape=[jax.ShapeDtypeStruct((2, rows, w...  7.45 us
  transfers between devices with their start and end apart: 38, of which 18 were waited for; matrix products, arithmetic and copies ran while one was open for 0% of the time, Pallas kernels for 11%

profile of v6, /device:TPU:1, one launch (start us, length us, event | category | flops | bytes accessed | tf_op | source)
XLA Modules:
  0.0 223.1 jit_solution(882800649101040204)
XLA Ops:
  1.5 18.0 %all_to_all.5.own_ref = bf16[8,128,256]{2,1,0:T(8,128)(2,1)S(1)} all-to-all(bf16[8,128,256]{2,1,0:T(8,128)(2,1)S(1)} %broadcast_in_dim.4), channel_id=1, replica_groups=mesh['y'=4,'xh'=2,'c'=2,'z'=4,'xl'=2] {'y','xh'}, dimensions={0} | all-to-all | bytes 1048576 | tf_op jit(solution)/shard_map/all_to_all | solution.py:512
  19.4 1.8 collective-permute-start
  22.8 0.9 copy-done
  23.7 7.5 %attend_project.1 = (bf16[2,128,1024]{2,1,0:T(8,128)(2,1)S(1)}, bf16[2,128,1024]{2,1,0:T(8,128)(2,1)S(1)}, bf16[2,128,1024]{2,1,0:T(8,128)(2,1)S(1)}, bf16[2,128,1024]{2,1,0:T(8,128)(2,1)S(1)}) custom-call(s32[10]{0:T(128)S(1)} %stack.90.pos_ref, bf16[128,1024]{1,0:T(8,128)(2,1)S(1)} %copy-done, bf16[8,128,256]{2,1,0:T(8,128)(2,1)S(1)} %all_to_all.5.own_ref, ...), custom_call_target="tpu_custom_call" | custom-call | flops 4294967296 | bytes 20971520 | tf_op jit(solution)/shard_map/attend_project/pallas_call | solution.py:125
  31.2 9.5 %prepare.1 = (bf16[2,448,1536]{2,1,0:T(8,128)(2,1)}, bf16[4,448,256]{2,1,0:T(8,128)(2,1)}, bf16[2,448,1536]{2,1,0:T(8,128)(2,1)}, bf16[4,448,256]{2,1,0:T(8,128)(2,1)}) custom-call(s32[4]{0:T(128)} %pad_add_fusion.pos_ref, bf16[224,8192]{1,0:T(8,128)(2,1)} %bitcast.25, bf16[224,8192]{1,0:T(8,128)(2,1)} %bitcast.26, f32[1,8192]{1,0:T(1,128)} %bitcast.36), custom_call_target="tpu_custom_call" | custom-call | flops 8388608 | bytes 15728640 | tf_op jit(solution)/shard_map/prepare/pallas_call | solution.py:204
  41.3 1.6 collective-permute-start.1
  42.9 2.1 collective-permute-start.2
  45.0 3.2 %collective-permute-start.3 = (bf16[2,128,1024]{2,1,0:T(8,128)(2,1)S(1)}, bf16[2,128,1024]{2,1,0:T(8,128)(2,1)S(1)}, u32[]{:S(2)}, u32[]{:S(2)}) collective-permute-start(bf16[2,128,1024]{2,1,0:T(8,128)(2,1)S(1)} %get-tuple-element.46.third), channel_id=1, source_target_pairs={{8,12},{10,14},{12,8},{14,10},{40,44},{42,46},{44,40},{46,42},{72,... | collective-permute-start | bytes 1572872 | tf_op jit(solution)/shard_map/ppermute | solution.py:42
  48.2 3.4 %collective-permute-done.1.r1 = bf16[2,128,1024]{2,1,0:T(8,128)(2,1)S(1)} collective-permute-done((bf16[2,128,1024]{2,1,0:T(8,128)(2,1)S(1)}, bf16[2,128,1024]{2,1,0:T(8,128)(2,1)S(1)}, u32[]{:S(2)}, u32[]{:S(2)}) %collective-permute-start.1) | collective-permute-done | bytes 524320 | tf_op jit(solution)/shard_map/ppermute | solution.py:42
  51.6 5.2 %collective-permute-done.2.r2 = bf16[2,128,1024]{2,1,0:T(8,128)(2,1)S(1)} collective-permute-done((bf16[2,128,1024]{2,1,0:T(8,128)(2,1)S(1)}, bf16[2,128,1024]{2,1,0:T(8,128)(2,1)S(1)}, u32[]{:S(2)}, u32[]{:S(2)}) %collective-permute-start.2) | collective-permute-done | bytes 524320 | tf_op jit(solution)/shard_map/ppermute | solution.py:42
  56.8 1.6 collective-permute-done.3.r3
  58.4 1.0 middle.1
  61.2 3.8 %collective-permute-done.4 = bf16[128,1024]{1,0:T(8,128)(2,1)S(1)} collective-permute-done((bf16[128,1024]{1,0:T(8,128)(2,1)S(1)}, bf16[128,1024]{1,0:T(8,128)(2,1)S(1)}, u32[]{:S(2)}, u32[]{:S(2)}) %collective-permute-start.4) | collective-permute-done | bytes 262176 | tf_op jit(solution)/shard_map/ppermute | solution.py:42
  65.3 8.3 %collective-permute-start.9 = (bf16[128,512]{1,0:T(8,128)(2,1)S(1)}, bf16[128,512]{1,0:T(8,128)(2,1)S(1)}, u32[]{:S(2)}, u32[]{:S(2)}) collective-permute-start(bf16[128,512]{1,0:T(8,128)(2,1)S(1)} %get-tuple-element.83), channel_id=1, source_target_pairs={{0,8},{8,0},{1,9},{9,1},{2,10},{10,2},{3,11},{11,3},{4,12},{12,4},... | collective-permute-start | bytes 393224 | tf_op jit(solution)/shard_map/ppermute | solution.py:50
  73.6 1.0 collective-permute-done.9
  74.7 2.7 %collective-permute-start.11 = (bf16[256,384]{1,0:T(8,128)(2,1)S(1)}, bf16[256,384]{1,0:T(8,128)(2,1)S(1)}, u32[]{:S(2)}, u32[]{:S(2)}) collective-permute-start(bf16[256,384]{1,0:T(8,128)(2,1)S(1)} %slice.20), channel_id=1, source_target_pairs={{0,96},{2,98},{4,100},{6,102},{32,0},{34,2},{36,4},{38,6},{64,32},... | collective-permute-start | bytes 589832 | tf_op jit(solution)/shard_map/ppermute | solution.py:42
  77.7 3.0 %collective-permute-done.10 = bf16[256,384]{1,0:T(8,128)(2,1)S(1)} collective-permute-done((bf16[256,384]{1,0:T(8,128)(2,1)S(1)}, bf16[256,384]{1,0:T(8,128)(2,1)S(1)}, u32[]{:S(2)}, u32[]{:S(2)}) %collective-permute-start.10) | collective-permute-done | bytes 196640 | tf_op jit(solution)/shard_map/ppermute | solution.py:42
  80.7 1.4 collective-permute-done.11
  82.1 1.6 collective-permute-done.12
  84.3 2.7 %collective-permute-start.17 = (bf16[256,128]{1,0:T(8,128)(2,1)S(1)}, bf16[256,128]{1,0:T(8,128)(2,1)S(1)}, u32[]{:S(2)}, u32[]{:S(2)}) collective-permute-start(bf16[256,128]{1,0:T(8,128)(2,1)S(1)} %slice.21), channel_id=1, source_target_pairs={{0,17},{2,19},{4,21},{6,23},{32,49},{34,51},{36,53},{38,55},{64,81... | collective-permute-start | bytes 196616 | tf_op jit(solution)/shard_map/ppermute | solution.py:42
  87.9 10.9 %collective-permute-done.16 = bf16[256,128]{1,0:T(8,128)(2,1)S(1)} collective-permute-done((bf16[256,128]{1,0:T(8,128)(2,1)S(1)}, bf16[256,128]{1,0:T(8,128)(2,1)S(1)}, u32[]{:S(2)}, u32[]{:S(2)}) %collective-permute-start.16) | collective-permute-done | bytes 65568 | tf_op jit(solution)/shard_map/ppermute | solution.py:42
  98.9 2.8 %collective-permute-start.20 = (bf16[4,256,128]{2,1,0:T(8,128)(2,1)S(1)}, bf16[4,256,128]{2,1,0:T(8,128)(2,1)S(1)}, u32[]{:S(2)}, u32[]{:S(2)}) collective-permute-start(bf16[4,256,128]{2,1,0:T(8,128)(2,1)S(1)} %pad_maximum_fusion.4), channel_id=1, source_target_pairs={{0,96},{2,98},{4,100},{6,102},{32,0},{34,2},{36,4},{38,6},{64,32},... | collective-permute-start | bytes 786440 | tf_op jit(solution)/shard_map/ppermute | solution.py:42
  101.7 1.1 collective-permute-start.21
  102.8 5.4 %collective-permute-done.19 = bf16[4,256,128]{2,1,0:T(8,128)(2,1)S(1)} collective-permute-done((bf16[4,256,128]{2,1,0:T(8,128)(2,1)S(1)}, bf16[4,256,128]{2,1,0:T(8,128)(2,1)S(1)}, u32[]{:S(2)}, u32[]{:S(2)}) %collective-permute-start.19) | collective-permute-done | bytes 262176 | tf_op jit(solution)/shard_map/ppermute | solution.py:42
  108.3 2.7 %collective-permute-done.20 = bf16[4,256,128]{2,1,0:T(8,128)(2,1)S(1)} collective-permute-done((bf16[4,256,128]{2,1,0:T(8,128)(2,1)S(1)}, bf16[4,256,128]{2,1,0:T(8,128)(2,1)S(1)}, u32[]{:S(2)}, u32[]{:S(2)}) %collective-permute-start.20) | collective-permute-done | bytes 262176 | tf_op jit(solution)/shard_map/ppermute | solution.py:42
  112.8 1.2 collective-permute-start.22
  114.0 1.3 collective-permute-start.29
  115.4 1.3 collective-permute-start.30
  116.7 10.5 %collective-permute-done.28.refs_6_ = bf16[8,256,128]{2,1,0:T(8,128)(2,1)S(1)} collective-permute-done((bf16[8,256,128]{2,1,0:T(8,128)(2,1)S(1)}, bf16[8,256,128]{2,1,0:T(8,128)(2,1)S(1)}, u32[]{:S(2)}, u32[]{:S(2)}) %collective-permute-start.28) | collective-permute-done | bytes 524320 | tf_op jit(solution)/shard_map/ppermute | solution.py:42
  127.5 9.0 %collective-permute-done.29.refs_7_ = bf16[8,256,128]{2,1,0:T(8,128)(2,1)S(1)} collective-permute-done((bf16[8,256,128]{2,1,0:T(8,128)(2,1)S(1)}, bf16[8,256,128]{2,1,0:T(8,128)(2,1)S(1)}, u32[]{:S(2)}, u32[]{:S(2)}) %collective-permute-start.29) | collective-permute-done | bytes 524320 | tf_op jit(solution)/shard_map/ppermute | solution.py:42
  136.5 2.8 %collective-permute-start.31 = (bf16[8,256,128]{2,1,0:T(8,128)(2,1)S(1)}, bf16[8,256,128]{2,1,0:T(8,128)(2,1)S(1)}, u32[]{:S(2)}, u32[]{:S(2)}) collective-permute-start(bf16[8,256,128]{2,1,0:T(8,128)(2,1)S(1)} %pad_maximum_fusion.3.refs_4_), channel_id=1, source_target_pairs={{0,6},{2,0},{4,2},{6,4},{32,38},{34,32},{36,34},{38,36},{64,70},{6... | collective-permute-start | bytes 1572872 | tf_op jit(solution)/shard_map/ppermute | solution.py:42
  139.3 1.1 collective-permute-start.23
  140.4 1.7 collective-permute-start.25
  142.1 13.9 %collective-permute-done.31.refs_9_ = bf16[8,256,128]{2,1,0:T(8,128)(2,1)S(1)} collective-permute-done((bf16[8,256,128]{2,1,0:T(8,128)(2,1)S(1)}, bf16[8,256,128]{2,1,0:T(8,128)(2,1)S(1)}, u32[]{:S(2)}, u32[]{:S(2)}) %collective-permute-start.31) | collective-permute-done | bytes 524320 | tf_op jit(solution)/shard_map/ppermute | solution.py:42
  156.0 1.7 collective-permute-start.26
  157.7 1.4 collective-permute-start.32
  159.2 9.2 %collective-permute-done.26.refs_4_ = bf16[4,256,384]{2,1,0:T(8,128)(2,1)S(1)} collective-permute-done((bf16[4,256,384]{2,1,0:T(8,128)(2,1)S(1)}, bf16[4,256,384]{2,1,0:T(8,128)(2,1)S(1)}, u32[]{:S(2)}, u32[]{:S(2)}) %collective-permute-start.26) | collective-permute-done | bytes 786464 | tf_op jit(solution)/shard_map/ppermute | solution.py:42
  168.4 3.0 %collective-permute-start.33 = (bf16[4,256,384]{2,1,0:T(8,128)(2,1)S(1)}, bf16[4,256,384]{2,1,0:T(8,128)(2,1)S(1)}, u32[]{:S(2)}, u32[]{:S(2)}) collective-permute-start(bf16[4,256,384]{2,1,0:T(8,128)(2,1)S(1)} %collective-permute-done.26.refs_4_), channel_id=1, source_target_pairs={{0,17},{2,19},{4,21},{6,23},{32,49},{34,51},{36,53},{38,55},{64,81... | collective-permute-start | bytes 2359304 | tf_op jit(solution)/shard_map/ppermute | solution.py:42
  171.3 5.5 %collective-permute-done.27.refs_5_ = bf16[4,256,384]{2,1,0:T(8,128)(2,1)S(1)} collective-permute-done((bf16[4,256,384]{2,1,0:T(8,128)(2,1)S(1)}, bf16[4,256,384]{2,1,0:T(8,128)(2,1)S(1)}, u32[]{:S(2)}, u32[]{:S(2)}) %collective-permute-start.27) | collective-permute-done | bytes 786464 | tf_op jit(solution)/shard_map/ppermute | solution.py:42
  176.8 3.0 %collective-permute-start.34 = (bf16[4,256,384]{2,1,0:T(8,128)(2,1)S(1)}, bf16[4,256,384]{2,1,0:T(8,128)(2,1)S(1)}, u32[]{:S(2)}, u32[]{:S(2)}) collective-permute-start(bf16[4,256,384]{2,1,0:T(8,128)(2,1)S(1)} %collective-permute-done.27.refs_5_), channel_id=1, source_target_pairs={{0,17},{2,19},{4,21},{6,23},{32,49},{34,51},{36,53},{38,55},{64,81... | collective-permute-start | bytes 2359304 | tf_op jit(solution)/shard_map/ppermute | solution.py:42
  179.7 8.1 %gate_up.4 = (f32[904,2048]{1,0:T(8,128)S(1)}, bf16[2,896,1536]{2,1,0:T(8,128)(2,1)S(1)}, bf16[4,896,256]{2,1,0:T(8,128)(2,1)S(1)}) custom-call(s32[4]{0:T(128)S(1)} %copy-done.1, bf16[8,256,384]{2,1,0:T(8,128)(2,1)S(1)} %pad_maximum_fusion.refs_0_, bf16[4,256,384]{2,1,0:T(8,128)(2,1)S(1)} %collective-permute-done.14.refs_1_, ...), custom_call_target="tpu_custom_call" | custom-call | flops 3758096384 | bytes 20971520 | tf_op jit(solution)/shard_map/gate_up/pallas_call | solution.py:402
  187.9 5.4 %collective-permute-start.35 = (bf16[8,256,128]{2,1,0:T(8,128)(2,1)S(1)}, bf16[8,256,128]{2,1,0:T(8,128)(2,1)S(1)}, u32[]{:S(2)}, u32[]{:S(2)}) collective-permute-start(bf16[8,256,128]{2,1,0:T(8,128)(2,1)S(1)} %collective-permute-done.28.refs_6_), channel_id=1, source_target_pairs={{0,2},{2,4},{4,6},{6,0},{32,34},{34,36},{36,38},{38,32},{64,66},{6... | collective-permute-start | bytes 1572872 | tf_op jit(solution)/shard_map/ppermute | solution.py:42
  193.2 3.0 %collective-permute-start.36 = (bf16[8,256,128]{2,1,0:T(8,128)(2,1)S(1)}, bf16[8,256,128]{2,1,0:T(8,128)(2,1)S(1)}, u32[]{:S(2)}, u32[]{:S(2)}) collective-permute-start(bf16[8,256,128]{2,1,0:T(8,128)(2,1)S(1)} %collective-permute-done.31.refs_9_), channel_id=1, source_target_pairs={{0,6},{2,0},{4,2},{6,4},{32,38},{34,32},{36,34},{38,36},{64,70},{6... | collective-permute-start | bytes 1572872 | tf_op jit(solution)/shard_map/ppermute | solution.py:42
  196.3 12.1 %gate_up.5.refs_7_.refs_2_ = f32[904,2048]{1,0:T(8,128)S(1)} custom-call(s32[4]{0:T(128)S(1)} %copy-done.1, bf16[8,256,384]{2,1,0:T(8,128)(2,1)S(1)} %collective-permute-done.22.refs_0_, bf16[4,256,384]{2,1,0:T(8,128)(2,1)S(1)} %collective-permute-done.23.refs_1_, ...), custom_call_target="tpu_custom_call", output_to_operand_aliasing={{}: (13, {})} | custom-call | flops 7516192768 | bytes 20971520 | tf_op jit(solution)/shard_map/gate_up/pallas_call | solution.py:402
  208.4 5.6 %gate_up.6 = (f32[8,2048]{1,0:T(8,128)S(1)}, bf16[464,2048]{1,0:T(8,128)(2,1)S(1)}, bf16[4,256,1536]{2,1,0:T(8,128)(2,1)S(1)}, bf16[1,2048,256]{2,1,0:T(8,128)(2,1)S(1)}) custom-call(s32[4]{0:T(128)S(1)} %copy-done.1, bf16[8,256,384]{2,1,0:T(8,128)(2,1)S(1)} %collective-permute-done.32.refs_0_, bf16[4,256,384]{2,1,0:T(8,128)(2,1)S(1)} %collective-permute-done.33.refs_1_, ...), custom_call_target="tpu_custom_call" | custom-call | flops 3758096384 | bytes 20971520 | tf_op jit(solution)/shard_map/gate_up/pallas_call | solution.py:402
  214.0 3.0 %collective-permute-start.37 = (bf16[464,2048]{1,0:T(8,128)(2,1)S(1)}, bf16[464,2048]{1,0:T(8,128)(2,1)S(1)}, u32[]{:S(2)}, u32[]{:S(2)}) collective-permute-start(bf16[464,2048]{1,0:T(8,128)(2,1)S(1)} %get-tuple-element.81), channel_id=1, source_target_pairs={{0,8},{8,0},{1,9},{9,1},{2,10},{10,2},{3,11},{11,3},{4,12},{12,4},... | collective-permute-start | bytes 5701640 | tf_op jit(solution)/shard_map/ppermute | solution.py:50
  217.0 4.3 %gate_up.7.own_ref = f32[448,2048]{1,0:T(8,128)S(1)} custom-call(s32[4]{0:T(128)S(1)} %copy-done.1, bf16[2,896,1536]{2,1,0:T(8,128)(2,1)S(1)} %get-tuple-element.75.refs_10_.refs_5_.refs_0_, bf16[4,896,256]{2,1,0:T(8,128)(2,1)S(1)} %get-tuple-element.76.refs_11_.refs_6_.refs_1_, f32[904,2048]{1,0:T(8,128)S(1)} %gate_up.5.refs_7_.refs_2_, ...), custom_call_target="tpu_custom_call" | custom-call | flops 3758096384 | bytes 20971520 | tf_op jit(solution)/shard_map/gate_up/pallas_call | solution.py:402
  221.3 1.6 finish.1
  (63 shorter events, 9.4 us)
Async XLA Ops:
  19.4 3.3 %collective-permute-start = (bf16[8,128,256]{2,1,0:T(8,128)(2,1)S(1)}, bf16[8,128,256]{2,1,0:T(8,128)(2,1)S(1)}, u32[]{:S(2)}, u32[]{:S(2)}) collective-permute-start(bf16[8,128,256]{2,1,0:T(8,128)(2,1)S(1)} %all_to_all.5.own_ref), channel_id=1, source_target_pairs={{0,8},{8,0},{1,9},{9,1},{2,10},{10,2},{3,11},{11,3},{4,12},{12,4},... | collective-permute-start | bytes 1572872 | tf_op jit(solution)/shard_map/ppermute | solution.py:50
  22.8 0.9 copy-start
  31.2 27.2 %copy-start.1 = (s32[4]{0:T(128)S(1)}, s32[4]{0:T(128)}, u32[]{:S(2)}) copy-start(s32[4]{0:T(128)} %pad_add_fusion.pos_ref) | copy-start | bytes 52
  40.7 24.4 %copy-start.5 = (bf16[128,1024]{1,0:T(8,128)(2,1)S(1)}, bf16[128,1024]{1,0:T(8,128)(2,1)}, u32[]{:S(2)}) copy-start(bf16[128,1024]{1,0:T(8,128)(2,1)} %param.12) | copy-start | bytes 786436
  40.7 24.3 %collective-permute-start.7 = (bf16[2,448,1536]{2,1,0:T(8,128)(2,1)}, bf16[2,448,1536]{2,1,0:T(8,128)(2,1)S(1)}, u32[]{:S(2)}, u32[]{:S(2)}) collective-permute-start(bf16[2,448,1536]{2,1,0:T(8,128)(2,1)} %get-tuple-element.56), channel_id=1, source_target_pairs={{0,8},{8,0},{1,9},{9,1},{2,10},{10,2},{3,11},{11,3},{4,12},{12,4},... | collective-permute-start | bytes 8257544 | tf_op jit(solution)/shard_map/ppermute | solution.py:50
  41.1 23.9 %collective-permute-start.8 = (bf16[4,448,256]{2,1,0:T(8,128)(2,1)}, bf16[4,448,256]{2,1,0:T(8,128)(2,1)S(1)}, u32[]{:S(2)}, u32[]{:S(2)}) collective-permute-start(bf16[4,448,256]{2,1,0:T(8,128)(2,1)} %get-tuple-element.57), channel_id=1, source_target_pairs={{0,8},{8,0},{1,9},{9,1},{2,10},{10,2},{3,11},{11,3},{4,12},{12,4},... | collective-permute-start | bytes 2752520 | tf_op jit(solution)/shard_map/ppermute | solution.py:50
  41.3 10.3 %collective-permute-start.1 = (bf16[2,128,1024]{2,1,0:T(8,128)(2,1)S(1)}, bf16[2,128,1024]{2,1,0:T(8,128)(2,1)S(1)}, u32[]{:S(2)}, u32[]{:S(2)}) collective-permute-start(bf16[2,128,1024]{2,1,0:T(8,128)(2,1)S(1)} %get-tuple-element.48), channel_id=1, source_target_pairs={{0,1},{2,3},{4,5},{6,7},{32,33},{34,35},{36,37},{38,39},{64,65},{6... | collective-permute-start | bytes 1572872 | tf_op jit(solution)/shard_map/ppermute | solution.py:42
  42.9 13.9 %collective-permute-start.2 = (bf16[2,128,1024]{2,1,0:T(8,128)(2,1)S(1)}, bf16[2,128,1024]{2,1,0:T(8,128)(2,1)S(1)}, u32[]{:S(2)}, u32[]{:S(2)}) collective-permute-start(bf16[2,128,1024]{2,1,0:T(8,128)(2,1)S(1)} %get-tuple-element.49), channel_id=1, source_target_pairs={{0,1},{2,3},{4,5},{6,7},{32,33},{34,35},{36,37},{38,39},{64,65},{6... | collective-permute-start | bytes 1572872 | tf_op jit(solution)/shard_map/ppermute | solution.py:42
  45.0 13.4 %collective-permute-start.3 = (bf16[2,128,1024]{2,1,0:T(8,128)(2,1)S(1)}, bf16[2,128,1024]{2,1,0:T(8,128)(2,1)S(1)}, u32[]{:S(2)}, u32[]{:S(2)}) collective-permute-start(bf16[2,128,1024]{2,1,0:T(8,128)(2,1)S(1)} %get-tuple-element.46.third), channel_id=1, source_target_pairs={{8,12},{10,14},{12,8},{14,10},{40,44},{42,46},{44,40},{46,42},{72,... | collective-permute-start | bytes 1572872 | tf_op jit(solution)/shard_map/ppermute | solution.py:42
  59.4 5.6 %collective-permute-start.4 = (bf16[128,1024]{1,0:T(8,128)(2,1)S(1)}, bf16[128,1024]{1,0:T(8,128)(2,1)S(1)}, u32[]{:S(2)}, u32[]{:S(2)}) collective-permute-start(bf16[128,1024]{1,0:T(8,128)(2,1)S(1)} %get-tuple-element.51), channel_id=1, source_target_pairs={{0,2},{2,4},{4,6},{6,0},{32,34},{34,36},{36,38},{38,32},{64,66},{6... | collective-permute-start | bytes 786440 | tf_op jit(solution)/shard_map/ppermute | solution.py:42
  59.8 5.2 %collective-permute-start.5 = (bf16[128,1024]{1,0:T(8,128)(2,1)S(1)}, bf16[128,1024]{1,0:T(8,128)(2,1)S(1)}, u32[]{:S(2)}, u32[]{:S(2)}) collective-permute-start(bf16[128,1024]{1,0:T(8,128)(2,1)S(1)} %get-tuple-element.52), channel_id=1, source_target_pairs={{0,6},{2,0},{4,2},{6,4},{32,38},{34,32},{36,34},{38,36},{64,70},{6... | collective-permute-start | bytes 786440 | tf_op jit(solution)/shard_map/ppermute | solution.py:42
  60.5 4.5 %collective-permute-start.6 = (bf16[128,1024]{1,0:T(8,128)(2,1)S(1)}, bf16[128,1024]{1,0:T(8,128)(2,1)S(1)}, u32[]{:S(2)}, u32[]{:S(2)}) collective-permute-start(bf16[128,1024]{1,0:T(8,128)(2,1)S(1)} %get-tuple-element.53), channel_id=1, source_target_pairs={{0,4},{2,6},{4,0},{6,2},{32,36},{34,38},{36,32},{38,34},{64,68},{6... | collective-permute-start | bytes 786440 | tf_op jit(solution)/shard_map/ppermute | solution.py:42
  65.2 46.7 %copy-start.4 = (bf16[128,1024]{1,0:T(8,128)(2,1)}, bf16[128,1024]{1,0:T(8,128)(2,1)S(1)}, u32[]{:S(2)}) copy-start(bf16[128,1024]{1,0:T(8,128)(2,1)S(1)} %add_convert_fusion) | copy-start | bytes 786436
  65.3 9.3 %collective-permute-start.9 = (bf16[128,512]{1,0:T(8,128)(2,1)S(1)}, bf16[128,512]{1,0:T(8,128)(2,1)S(1)}, u32[]{:S(2)}, u32[]{:S(2)}) collective-permute-start(bf16[128,512]{1,0:T(8,128)(2,1)S(1)} %get-tuple-element.83), channel_id=1, source_target_pairs={{0,8},{8,0},{1,9},{9,1},{2,10},{10,2},{3,11},{11,3},{4,12},{12,4},... | collective-permute-start | bytes 393224 | tf_op jit(solution)/shard_map/ppermute | solution.py:50
  74.6 6.1 %collective-permute-start.10 = (bf16[256,384]{1,0:T(8,128)(2,1)S(1)}, bf16[256,384]{1,0:T(8,128)(2,1)S(1)}, u32[]{:S(2)}, u32[]{:S(2)}) collective-permute-start(bf16[256,384]{1,0:T(8,128)(2,1)S(1)} %slice.20), channel_id=1, source_target_pairs={{0,32},{2,34},{4,36},{6,38},{32,64},{34,66},{36,68},{38,70},{64,96... | collective-permute-start | bytes 589832 | tf_op jit(solution)/shard_map/ppermute | solution.py:42
  74.7 7.4 %collective-permute-start.11 = (bf16[256,384]{1,0:T(8,128)(2,1)S(1)}, bf16[256,384]{1,0:T(8,128)(2,1)S(1)}, u32[]{:S(2)}, u32[]{:S(2)}) collective-permute-start(bf16[256,384]{1,0:T(8,128)(2,1)S(1)} %slice.20), channel_id=1, source_target_pairs={{0,96},{2,98},{4,100},{6,102},{32,0},{34,2},{36,4},{38,6},{64,32},... | collective-permute-start | bytes 589832 | tf_op jit(solution)/shard_map/ppermute | solution.py:42
  77.4 6.3 %collective-permute-start.12 = (bf16[256,384]{1,0:T(8,128)(2,1)S(1)}, bf16[256,384]{1,0:T(8,128)(2,1)S(1)}, u32[]{:S(2)}, u32[]{:S(2)}) collective-permute-start(bf16[256,384]{1,0:T(8,128)(2,1)S(1)} %slice.20), channel_id=1, source_target_pairs={{0,64},{2,66},{4,68},{6,70},{32,96},{34,98},{36,100},{38,102},{64,... | collective-permute-start | bytes 589832 | tf_op jit(solution)/shard_map/ppermute | solution.py:42
  83.8 28.8 %collective-permute-start.13 = (bf16[4,256,384]{2,1,0:T(8,128)(2,1)S(1)}, bf16[4,256,384]{2,1,0:T(8,128)(2,1)S(1)}, u32[]{:S(2)}, u32[]{:S(2)}) collective-permute-start(bf16[4,256,384]{2,1,0:T(8,128)(2,1)S(1)} %pad_maximum_fusion.1), channel_id=1, source_target_pairs={{0,2},{2,4},{4,6},{6,0},{32,34},{34,36},{36,38},{38,32},{64,66},{6... | collective-permute-start | bytes 2359304 | tf_op jit(solution)/shard_map/ppermute | solution.py:42
  84.2 14.5 %collective-permute-start.16 = (bf16[256,128]{1,0:T(8,128)(2,1)S(1)}, bf16[256,128]{1,0:T(8,128)(2,1)S(1)}, u32[]{:S(2)}, u32[]{:S(2)}) collective-permute-start(bf16[256,128]{1,0:T(8,128)(2,1)S(1)} %slice.21), channel_id=1, source_target_pairs={{0,1},{2,3},{4,5},{6,7},{32,33},{34,35},{36,37},{38,39},{64,65},{6... | collective-permute-start | bytes 196616 | tf_op jit(solution)/shard_map/ppermute | solution.py:42
  84.3 14.4 %collective-permute-start.17 = (bf16[256,128]{1,0:T(8,128)(2,1)S(1)}, bf16[256,128]{1,0:T(8,128)(2,1)S(1)}, u32[]{:S(2)}, u32[]{:S(2)}) collective-permute-start(bf16[256,128]{1,0:T(8,128)(2,1)S(1)} %slice.21), channel_id=1, source_target_pairs={{0,17},{2,19},{4,21},{6,23},{32,49},{34,51},{36,53},{38,55},{64,81... | collective-permute-start | bytes 196616 | tf_op jit(solution)/shard_map/ppermute | solution.py:42
  87.0 11.8 %collective-permute-start.18 = (bf16[256,128]{1,0:T(8,128)(2,1)S(1)}, bf16[256,128]{1,0:T(8,128)(2,1)S(1)}, u32[]{:S(2)}, u32[]{:S(2)}) collective-permute-start(bf16[256,128]{1,0:T(8,128)(2,1)S(1)} %slice.21), channel_id=1, source_target_pairs={{0,16},{2,18},{4,20},{6,22},{32,48},{34,50},{36,52},{38,54},{64,80... | collective-permute-start | bytes 196616 | tf_op jit(solution)/shard_map/ppermute | solution.py:42
  98.8 80.9 %copy-start.2 = (bf16[2,448,1536]{2,1,0:T(8,128)(2,1)S(1)}, bf16[2,448,1536]{2,1,0:T(8,128)(2,1)}, u32[]{:S(2)}) copy-start(bf16[2,448,1536]{2,1,0:T(8,128)(2,1)} %get-tuple-element.71.refs_5_) | copy-start | bytes 8257540
  98.8 80.9 %copy-start.3 = (bf16[4,448,256]{2,1,0:T(8,128)(2,1)S(1)}, bf16[4,448,256]{2,1,0:T(8,128)(2,1)}, u32[]{:S(2)}) copy-start(bf16[4,448,256]{2,1,0:T(8,128)(2,1)} %get-tuple-element.73.refs_7_) | copy-start | bytes 2752516
  98.8 9.4 %collective-permute-start.19 = (bf16[4,256,128]{2,1,0:T(8,128)(2,1)S(1)}, bf16[4,256,128]{2,1,0:T(8,128)(2,1)S(1)}, u32[]{:S(2)}, u32[]{:S(2)}) collective-permute-start(bf16[4,256,128]{2,1,0:T(8,128)(2,1)S(1)} %pad_maximum_fusion.4), channel_id=1, source_target_pairs={{0,32},{2,34},{4,36},{6,38},{32,64},{34,66},{36,68},{38,70},{64,96... | collective-permute-start | bytes 786440 | tf_op jit(solution)/shard_map/ppermute | solution.py:42
  98.9 12.1 %collective-permute-start.20 = (bf16[4,256,128]{2,1,0:T(8,128)(2,1)S(1)}, bf16[4,256,128]{2,1,0:T(8,128)(2,1)S(1)}, u32[]{:S(2)}, u32[]{:S(2)}) collective-permute-start(bf16[4,256,128]{2,1,0:T(8,128)(2,1)S(1)} %pad_maximum_fusion.4), channel_id=1, source_target_pairs={{0,96},{2,98},{4,100},{6,102},{32,0},{34,2},{36,4},{38,6},{64,32},... | collective-permute-start | bytes 786440 | tf_op jit(solution)/shard_map/ppermute | solution.py:42
  101.7 10.2 %collective-permute-start.21 = (bf16[4,256,128]{2,1,0:T(8,128)(2,1)S(1)}, bf16[4,256,128]{2,1,0:T(8,128)(2,1)S(1)}, u32[]{:S(2)}, u32[]{:S(2)}) collective-permute-start(bf16[4,256,128]{2,1,0:T(8,128)(2,1)S(1)} %pad_maximum_fusion.4), channel_id=1, source_target_pairs={{0,64},{2,66},{4,68},{6,70},{32,96},{34,98},{36,100},{38,102},{64,... | collective-permute-start | bytes 786440 | tf_op jit(solution)/shard_map/ppermute | solution.py:42
  111.9 15.2 %collective-permute-start.28 = (bf16[8,256,128]{2,1,0:T(8,128)(2,1)S(1)}, bf16[8,256,128]{2,1,0:T(8,128)(2,1)S(1)}, u32[]{:S(2)}, u32[]{:S(2)}) collective-permute-start(bf16[8,256,128]{2,1,0:T(8,128)(2,1)S(1)} %pad_maximum_fusion.2.refs_3_), channel_id=1, source_target_pairs={{0,2},{2,4},{4,6},{6,0},{32,34},{34,36},{36,38},{38,32},{64,66},{6... | collective-permute-start | bytes 1572872 | tf_op jit(solution)/shard_map/ppermute | solution.py:42
  112.8 44.9 %collective-permute-start.22 = (bf16[8,256,384]{2,1,0:T(8,128)(2,1)S(1)}, bf16[8,256,384]{2,1,0:T(8,128)(2,1)S(1)}, u32[]{:S(2)}, u32[]{:S(2)}) collective-permute-start(bf16[8,256,384]{2,1,0:T(8,128)(2,1)S(1)} %pad_maximum_fusion.refs_0_), channel_id=1, source_target_pairs={{0,1},{2,3},{4,5},{6,7},{32,33},{34,35},{36,37},{38,39},{64,65},{6... | collective-permute-start | bytes 4718600 | tf_op jit(solution)/shard_map/ppermute | solution.py:42
  114.0 25.3 %collective-permute-start.14 = (bf16[4,256,384]{2,1,0:T(8,128)(2,1)S(1)}, bf16[4,256,384]{2,1,0:T(8,128)(2,1)S(1)}, u32[]{:S(2)}, u32[]{:S(2)}) collective-permute-start(bf16[4,256,384]{2,1,0:T(8,128)(2,1)S(1)} %pad_maximum_fusion.1), channel_id=1, source_target_pairs={{0,6},{2,0},{4,2},{6,4},{32,38},{34,32},{36,34},{38,36},{64,70},{6... | collective-permute-start | bytes 2359304 | tf_op jit(solution)/shard_map/ppermute | solution.py:42
  114.0 22.5 %collective-permute-start.29 = (bf16[8,256,128]{2,1,0:T(8,128)(2,1)S(1)}, bf16[8,256,128]{2,1,0:T(8,128)(2,1)S(1)}, u32[]{:S(2)}, u32[]{:S(2)}) collective-permute-start(bf16[8,256,128]{2,1,0:T(8,128)(2,1)S(1)} %pad_maximum_fusion.3.refs_4_), channel_id=1, source_target_pairs={{0,2},{2,4},{4,6},{6,0},{32,34},{34,36},{36,38},{38,32},{64,66},{6... | collective-permute-start | bytes 1572872 | tf_op jit(solution)/shard_map/ppermute | solution.py:42
  115.4 25.0 %collective-permute-start.30 = (bf16[8,256,128]{2,1,0:T(8,128)(2,1)S(1)}, bf16[8,256,128]{2,1,0:T(8,128)(2,1)S(1)}, u32[]{:S(2)}, u32[]{:S(2)}) collective-permute-start(bf16[8,256,128]{2,1,0:T(8,128)(2,1)S(1)} %pad_maximum_fusion.2.refs_3_), channel_id=1, source_target_pairs={{0,6},{2,0},{4,2},{6,4},{32,38},{34,32},{36,34},{38,36},{64,70},{6... | collective-permute-start | bytes 1572872 | tf_op jit(solution)/shard_map/ppermute | solution.py:42
  127.1 30.5 %collective-permute-start.15 = (bf16[4,256,384]{2,1,0:T(8,128)(2,1)S(1)}, bf16[4,256,384]{2,1,0:T(8,128)(2,1)S(1)}, u32[]{:S(2)}, u32[]{:S(2)}) collective-permute-start(bf16[4,256,384]{2,1,0:T(8,128)(2,1)S(1)} %pad_maximum_fusion.1), channel_id=1, source_target_pairs={{0,4},{2,6},{4,0},{6,2},{32,36},{34,38},{36,32},{38,34},{64,68},{6... | collective-permute-start | bytes 2359304 | tf_op jit(solution)/shard_map/ppermute | solution.py:42
  136.5 19.5 %collective-permute-start.31 = (bf16[8,256,128]{2,1,0:T(8,128)(2,1)S(1)}, bf16[8,256,128]{2,1,0:T(8,128)(2,1)S(1)}, u32[]{:S(2)}, u32[]{:S(2)}) collective-permute-start(bf16[8,256,128]{2,1,0:T(8,128)(2,1)S(1)} %pad_maximum_fusion.3.refs_4_), channel_id=1, source_target_pairs={{0,6},{2,0},{4,2},{6,4},{32,38},{34,32},{36,34},{38,36},{64,70},{6... | collective-permute-start | bytes 1572872 | tf_op jit(solution)/shard_map/ppermute | solution.py:42
  139.3 19.8 %collective-permute-start.23 = (bf16[4,256,384]{2,1,0:T(8,128)(2,1)S(1)}, bf16[4,256,384]{2,1,0:T(8,128)(2,1)S(1)}, u32[]{:S(2)}, u32[]{:S(2)}) collective-permute-start(bf16[4,256,384]{2,1,0:T(8,128)(2,1)S(1)} %collective-permute-done.14.refs_1_), channel_id=1, source_target_pairs={{0,1},{2,3},{4,5},{6,7},{32,33},{34,35},{36,37},{38,39},{64,65},{6... | collective-permute-start | bytes 2359304 | tf_op jit(solution)/shard_map/ppermute | solution.py:42
  140.4 52.9 %collective-permute-start.25 = (bf16[8,256,384]{2,1,0:T(8,128)(2,1)S(1)}, bf16[8,256,384]{2,1,0:T(8,128)(2,1)S(1)}, u32[]{:S(2)}, u32[]{:S(2)}) collective-permute-start(bf16[8,256,384]{2,1,0:T(8,128)(2,1)S(1)} %pad_maximum_fusion.refs_0_), channel_id=1, source_target_pairs={{0,17},{2,19},{4,21},{6,23},{32,49},{34,51},{36,53},{38,55},{64,81... | collective-permute-start | bytes 4718600 | tf_op jit(solution)/shard_map/ppermute | solution.py:42
  156.0 12.4 %collective-permute-start.26 = (bf16[4,256,384]{2,1,0:T(8,128)(2,1)S(1)}, bf16[4,256,384]{2,1,0:T(8,128)(2,1)S(1)}, u32[]{:S(2)}, u32[]{:S(2)}) collective-permute-start(bf16[4,256,384]{2,1,0:T(8,128)(2,1)S(1)} %collective-permute-done.14.refs_1_), channel_id=1, source_target_pairs={{0,17},{2,19},{4,21},{6,23},{32,49},{34,51},{36,53},{38,55},{64,81... | collective-permute-start | bytes 2359304 | tf_op jit(solution)/shard_map/ppermute | solution.py:42
  157.6 19.1 %collective-permute-start.27 = (bf16[4,256,384]{2,1,0:T(8,128)(2,1)S(1)}, bf16[4,256,384]{2,1,0:T(8,128)(2,1)S(1)}, u32[]{:S(2)}, u32[]{:S(2)}) collective-permute-start(bf16[4,256,384]{2,1,0:T(8,128)(2,1)S(1)} %collective-permute-done.15.refs_2_), channel_id=1, source_target_pairs={{0,17},{2,19},{4,21},{6,23},{32,49},{34,51},{36,53},{38,55},{64,81... | collective-permute-start | bytes 2359304 | tf_op jit(solution)/shard_map/ppermute | solution.py:42
  157.7 50.8 %collective-permute-start.32 = (bf16[8,256,384]{2,1,0:T(8,128)(2,1)S(1)}, bf16[8,256,384]{2,1,0:T(8,128)(2,1)S(1)}, u32[]{:S(2)}, u32[]{:S(2)}) collective-permute-start(bf16[8,256,384]{2,1,0:T(8,128)(2,1)S(1)} %collective-permute-done.22.refs_0_), channel_id=1, source_target_pairs={{0,1},{2,3},{4,5},{6,7},{32,33},{34,35},{36,37},{38,39},{64,65},{6... | collective-permute-start | bytes 4718600 | tf_op jit(solution)/shard_map/ppermute | solution.py:42
  159.1 28.7 %collective-permute-start.24 = (bf16[4,256,384]{2,1,0:T(8,128)(2,1)S(1)}, bf16[4,256,384]{2,1,0:T(8,128)(2,1)S(1)}, u32[]{:S(2)}, u32[]{:S(2)}) collective-permute-start(bf16[4,256,384]{2,1,0:T(8,128)(2,1)S(1)} %collective-permute-done.15.refs_2_), channel_id=1, source_target_pairs={{0,1},{2,3},{4,5},{6,7},{32,33},{34,35},{36,37},{38,39},{64,65},{6... | collective-permute-start | bytes 2359304 | tf_op jit(solution)/shard_map/ppermute | solution.py:42
  168.4 40.1 %collective-permute-start.33 = (bf16[4,256,384]{2,1,0:T(8,128)(2,1)S(1)}, bf16[4,256,384]{2,1,0:T(8,128)(2,1)S(1)}, u32[]{:S(2)}, u32[]{:S(2)}) collective-permute-start(bf16[4,256,384]{2,1,0:T(8,128)(2,1)S(1)} %collective-permute-done.26.refs_4_), channel_id=1, source_target_pairs={{0,17},{2,19},{4,21},{6,23},{32,49},{34,51},{36,53},{38,55},{64,81... | collective-permute-start | bytes 2359304 | tf_op jit(solution)/shard_map/ppermute | solution.py:42
  176.8 31.6 %collective-permute-start.34 = (bf16[4,256,384]{2,1,0:T(8,128)(2,1)S(1)}, bf16[4,256,384]{2,1,0:T(8,128)(2,1)S(1)}, u32[]{:S(2)}, u32[]{:S(2)}) collective-permute-start(bf16[4,256,384]{2,1,0:T(8,128)(2,1)S(1)} %collective-permute-done.27.refs_5_), channel_id=1, source_target_pairs={{0,17},{2,19},{4,21},{6,23},{32,49},{34,51},{36,53},{38,55},{64,81... | collective-permute-start | bytes 2359304 | tf_op jit(solution)/shard_map/ppermute | solution.py:42
  187.9 20.5 %collective-permute-start.35 = (bf16[8,256,128]{2,1,0:T(8,128)(2,1)S(1)}, bf16[8,256,128]{2,1,0:T(8,128)(2,1)S(1)}, u32[]{:S(2)}, u32[]{:S(2)}) collective-permute-start(bf16[8,256,128]{2,1,0:T(8,128)(2,1)S(1)} %collective-permute-done.28.refs_6_), channel_id=1, source_target_pairs={{0,2},{2,4},{4,6},{6,0},{32,34},{34,36},{36,38},{38,32},{64,66},{6... | collective-permute-start | bytes 1572872 | tf_op jit(solution)/shard_map/ppermute | solution.py:42
  193.2 15.2 %collective-permute-start.36 = (bf16[8,256,128]{2,1,0:T(8,128)(2,1)S(1)}, bf16[8,256,128]{2,1,0:T(8,128)(2,1)S(1)}, u32[]{:S(2)}, u32[]{:S(2)}) collective-permute-start(bf16[8,256,128]{2,1,0:T(8,128)(2,1)S(1)} %collective-permute-done.31.refs_9_), channel_id=1, source_target_pairs={{0,6},{2,0},{4,2},{6,4},{32,38},{34,32},{36,34},{38,36},{64,70},{6... | collective-permute-start | bytes 1572872 | tf_op jit(solution)/shard_map/ppermute | solution.py:42
  214.0 7.3 %collective-permute-start.37 = (bf16[464,2048]{1,0:T(8,128)(2,1)S(1)}, bf16[464,2048]{1,0:T(8,128)(2,1)S(1)}, u32[]{:S(2)}, u32[]{:S(2)}) collective-permute-start(bf16[464,2048]{1,0:T(8,128)(2,1)S(1)} %get-tuple-element.81), channel_id=1, source_target_pairs={{0,8},{8,0},{1,9},{9,1},{2,10},{10,2},{3,11},{11,3},{4,12},{12,4},... | collective-permute-start | bytes 5701640 | tf_op jit(solution)/shard_map/ppermute | solution.py:50

commit v7 on v6

--- a/solution.py
+++ b/solution.py
@@ -462,11 +462,13 @@
     main_near = around(blocks[0], axes[0][0])
     side_near = around(blocks[1], axes[1][0])
     main_near = lax.optimization_barrier([blocks[0]] + main_near)
-    cur_main = lax.optimization_barrier(jnp.stack(main_near))
+    cur_main = jnp.stack(main_near)
+    cur_main = lax.optimization_barrier(cur_main)
     ahead = shift(cur_main, axes[0][1], 1)
     third, fourth = (shift(cur_main, axes[0][1], by) for by in (-1, 2))
     side_near = lax.optimization_barrier([blocks[1]] + side_near)
-    cur_side = lax.optimization_barrier(jnp.stack(side_near))
+    cur_side = jnp.stack(side_near)
+    cur_side = lax.optimization_barrier(cur_side)
     side_next = around(cur_side, axes[1][1])
 
     def both_ways(block, a):
@@ -534,7 +536,7 @@
         move(b2, ("z", None), (-1, 0)),
         move(b3, ("z", None), (2, 0)),
     ]
-    terms, gm, gs = lax.optimization_barrier((terms, swap_core(sm), swap_core(ss)))
+    gm, gs = swap_core(sm), swap_core(ss)
     total = mine + sum(t.astype(F32) for t in terms)
     hidden = (residual.astype(F32) + total).astype(BF)
 

time: 224 us -> 226 us (level)
  waiting for transfers between devices: 89.7 us -> 97.3 us
  starting transfers between devices: 61.4 us -> 56 us
    ppermute x33, starting transfers between devices: 47.8 us -> 38.5 us  [move(): return lax.ppermute(x, MESH, pairs)]
    ppermute x33, waiting for transfers between devices: 87.9 us -> 94.8 us  [move(): return lax.ppermute(x, MESH, pairs)]
    ppermute x5, starting transfers between devices: 13.6 us -> 17.5 us  [swap_core(): return lax.ppermute(x, 'c', [(0, 1), (1, 0)])]
  transfers between devices with their start and end apart: 38 -> 38, of which waited for: 18 -> 13; matrix products, arithmetic and copies ran while one was open for 0% -> 0% of each run, Pallas kernels for 11% -> 15%
where the time goes in v7:
time: 226 us; the launch traced here: 225 us
  waiting for transfers between devices  97.3 us (43%)
  starting transfers between devices  56 us (25%)
  Pallas kernels  50.3 us (22%)
  blocking collectives  18 us (8%)
    ppermute x33, waiting for transfers between devices, move(): return lax.ppermute(x, MESH, pairs)  94.8 us
    ppermute x33, starting transfers between devices, move(): return lax.ppermute(x, MESH, pairs)  38.5 us
    pallas_call x4, Pallas kernels, gate_up(): pl.pallas_call(functools.partial(gate_kernel, which, stage), out_shape=ou...  30.5 us
    all_to_all x1, blocking collectives, per_device(): own = lax.all_to_all(spread, ('y', 'xh'), 0, 0, tiled=True)  18 us
    ppermute x5, starting transfers between devices, swap_core(): return lax.ppermute(x, 'c', [(0, 1), (1, 0)])  17.5 us
    pallas_call x1, Pallas kernels, prepare(): pl.pallas_call(prep_kernel, out_shape=[mshape, sshape, mshape, sshape], g...  9.37 us
    pallas_call x1, Pallas kernels, attend_project(): pl.pallas_call(attend_kernel, out_shape=[jax.ShapeDtypeStruct((2, rows, w...  7.81 us
  transfers between devices with their start and end apart: 38, of which 13 were waited for; matrix products, arithmetic and copies ran while one was open for 0% of the time, Pallas kernels for 15%

profile of v7, /device:TPU:1, one launch (start us, length us, event | category | flops | bytes accessed | tf_op | source)
XLA Modules:
  0.0 225.4 jit_solution(10036222103330808838)
XLA Ops:
  0.6 0.8 pad_maximum_fusion.5
  1.5 18.0 %all_to_all.5.own_ref = bf16[8,128,256]{2,1,0:T(8,128)(2,1)S(1)} all-to-all(bf16[8,128,256]{2,1,0:T(8,128)(2,1)S(1)} %broadcast_in_dim.4), channel_id=1, replica_groups=mesh['y'=4,'xh'=2,'c'=2,'z'=4,'xl'=2] {'y','xh'}, dimensions={0} | all-to-all | bytes 1048576 | tf_op jit(solution)/shard_map/all_to_all | solution.py:514
  19.4 1.8 collective-permute-start
  21.3 1.5 collective-permute-done.oth_ref
  22.8 0.9 copy-done
  23.7 7.8 %attend_project.1 = (bf16[2,128,1024]{2,1,0:T(8,128)(2,1)}, bf16[2,128,1024]{2,1,0:T(8,128)(2,1)S(1)}, bf16[2,128,1024]{2,1,0:T(8,128)(2,1)S(1)}, bf16[2,128,1024]{2,1,0:T(8,128)(2,1)S(1)}) custom-call(s32[10]{0:T(128)S(1)} %stack.90.pos_ref, bf16[128,1024]{1,0:T(8,128)(2,1)S(1)} %copy-done, bf16[8,128,256]{2,1,0:T(8,128)(2,1)S(1)} %all_to_all.5.own_ref, ...), custom_call_target="tpu_custom_call" | custom-call | flops 4294967296 | bytes 20971520 | tf_op jit(solution)/shard_map/attend_project/pallas_call | solution.py:125
  31.6 1.7 collective-permute-start.1
  33.3 2.2 collective-permute-start.2
  35.5 3.1 %collective-permute-start.3 = (bf16[2,128,1024]{2,1,0:T(8,128)(2,1)S(1)}, bf16[2,128,1024]{2,1,0:T(8,128)(2,1)S(1)}, u32[]{:S(2)}, u32[]{:S(2)}) collective-permute-start(bf16[2,128,1024]{2,1,0:T(8,128)(2,1)S(1)} %get-tuple-element.41.third), channel_id=1, source_target_pairs={{8,12},{10,14},{12,8},{14,10},{40,44},{42,46},{44,40},{46,42},{72,... | collective-permute-start | bytes 1572872 | tf_op jit(solution)/shard_map/ppermute | solution.py:42
  38.7 3.5 %collective-permute-done.1.r1 = bf16[2,128,1024]{2,1,0:T(8,128)(2,1)S(1)} collective-permute-done((bf16[2,128,1024]{2,1,0:T(8,128)(2,1)}, bf16[2,128,1024]{2,1,0:T(8,128)(2,1)S(1)}, u32[]{:S(2)}, u32[]{:S(2)}) %collective-permute-start.1) | collective-permute-done | bytes 524320 | tf_op jit(solution)/shard_map/ppermute | solution.py:42
  42.2 5.0 %collective-permute-done.2.r2 = bf16[2,128,1024]{2,1,0:T(8,128)(2,1)S(1)} collective-permute-done((bf16[2,128,1024]{2,1,0:T(8,128)(2,1)S(1)}, bf16[2,128,1024]{2,1,0:T(8,128)(2,1)S(1)}, u32[]{:S(2)}, u32[]{:S(2)}) %collective-permute-start.2) | collective-permute-done | bytes 524320 | tf_op jit(solution)/shard_map/ppermute | solution.py:42
  47.2 1.8 collective-permute-done.3.r3
  49.0 1.0 middle.1
  51.7 3.8 %collective-permute-done.4 = bf16[128,1024]{1,0:T(8,128)(2,1)S(1)} collective-permute-done((bf16[128,1024]{1,0:T(8,128)(2,1)S(1)}, bf16[128,1024]{1,0:T(8,128)(2,1)S(1)}, u32[]{:S(2)}, u32[]{:S(2)}) %collective-permute-start.4) | collective-permute-done | bytes 262176 | tf_op jit(solution)/shard_map/ppermute | solution.py:42
  55.8 8.3 %collective-permute-start.7 = (bf16[128,512]{1,0:T(8,128)(2,1)S(1)}, bf16[128,512]{1,0:T(8,128)(2,1)S(1)}, u32[]{:S(2)}, u32[]{:S(2)}) collective-permute-start(bf16[128,512]{1,0:T(8,128)(2,1)S(1)} %get-tuple-element.73), channel_id=1, source_target_pairs={{0,8},{8,0},{1,9},{9,1},{2,10},{10,2},{3,11},{11,3},{4,12},{12,4},... | collective-permute-start | bytes 393224 | tf_op jit(solution)/shard_map/ppermute | solution.py:50
  64.1 1.0 collective-permute-done.7
  65.6 1.6 collective-permute-start.10
  67.3 0.7 collective-permute-start.8
  68.0 1.9 collective-permute-start.9
  69.9 2.4 %collective-permute-start.15 = (bf16[256,128]{1,0:T(8,128)(2,1)S(1)}, bf16[256,128]{1,0:T(8,128)(2,1)S(1)}, u32[]{:S(2)}, u32[]{:S(2)}) collective-permute-start(bf16[256,128]{1,0:T(8,128)(2,1)S(1)} %slice.21), channel_id=1, source_target_pairs={{0,17},{2,19},{4,21},{6,23},{32,49},{34,51},{36,53},{38,55},{64,81... | collective-permute-start | bytes 196616 | tf_op jit(solution)/shard_map/ppermute | solution.py:42
  72.3 9.4 %prepare.1 = (bf16[2,448,1536]{2,1,0:T(8,128)(2,1)}, bf16[4,448,256]{2,1,0:T(8,128)(2,1)}, bf16[2,448,1536]{2,1,0:T(8,128)(2,1)}, bf16[4,448,256]{2,1,0:T(8,128)(2,1)}) custom-call(s32[4]{0:T(128)} %copy-done.1, bf16[224,8192]{1,0:T(8,128)(2,1)} %bitcast.25, bf16[224,8192]{1,0:T(8,128)(2,1)} %bitcast.26, f32[1,8192]{1,0:T(1,128)} %bitcast.36), custom_call_target="tpu_custom_call" | custom-call | flops 8388608 | bytes 15728640 | tf_op jit(solution)/shard_map/prepare/pallas_call | solution.py:204
  81.7 1.8 collective-permute-start.21
  83.5 1.4 collective-permute-start.17
  85.5 1.6 collective-permute-start.18
  87.3 5.8 %collective-permute-done.17 = bf16[4,256,128]{2,1,0:T(8,128)(2,1)S(1)} collective-permute-done((bf16[4,256,128]{2,1,0:T(8,128)(2,1)S(1)}, bf16[4,256,128]{2,1,0:T(8,128)(2,1)S(1)}, u32[]{:S(2)}, u32[]{:S(2)}) %collective-permute-start.17) | collective-permute-done | bytes 262176 | tf_op jit(solution)/shard_map/ppermute | solution.py:42
  93.1 1.4 collective-permute-start.20
  94.5 3.3 %collective-permute-done.19 = bf16[4,256,128]{2,1,0:T(8,128)(2,1)S(1)} collective-permute-done((bf16[4,256,128]{2,1,0:T(8,128)(2,1)S(1)}, bf16[4,256,128]{2,1,0:T(8,128)(2,1)S(1)}, u32[]{:S(2)}, u32[]{:S(2)}) %collective-permute-start.19) | collective-permute-done | bytes 262176 | tf_op jit(solution)/shard_map/ppermute | solution.py:42
  97.9 1.4 collective-permute-start.28
  99.3 1.3 collective-permute-start.29
  100.6 1.8 collective-permute-start.12
  102.4 1.5 collective-permute-start.30
  104.1 8.0 %collective-permute-done.28.refs_6_ = bf16[8,256,128]{2,1,0:T(8,128)(2,1)S(1)} collective-permute-done((bf16[8,256,128]{2,1,0:T(8,128)(2,1)S(1)}, bf16[8,256,128]{2,1,0:T(8,128)(2,1)S(1)}, u32[]{:S(2)}, u32[]{:S(2)}) %collective-permute-start.28) | collective-permute-done | bytes 524320 | tf_op jit(solution)/shard_map/ppermute | solution.py:42
  112.6 10.7 %collective-permute-done.29.refs_7_ = bf16[8,256,128]{2,1,0:T(8,128)(2,1)S(1)} collective-permute-done((bf16[8,256,128]{2,1,0:T(8,128)(2,1)S(1)}, bf16[8,256,128]{2,1,0:T(8,128)(2,1)S(1)}, u32[]{:S(2)}, u32[]{:S(2)}) %collective-permute-start.29) | collective-permute-done | bytes 524320 | tf_op jit(solution)/shard_map/ppermute | solution.py:42
  123.3 5.2 %collective-permute-start.13 = (bf16[4,256,384]{2,1,0:T(8,128)(2,1)S(1)}, bf16[4,256,384]{2,1,0:T(8,128)(2,1)S(1)}, u32[]{:S(2)}, u32[]{:S(2)}) collective-permute-start(bf16[4,256,384]{2,1,0:T(8,128)(2,1)S(1)} %pad_maximum_fusion.1), channel_id=1, source_target_pairs={{0,4},{2,6},{4,0},{6,2},{32,36},{34,38},{36,32},{38,34},{64,68},{6... | collective-permute-start | bytes 2359304 | tf_op jit(solution)/shard_map/ppermute | solution.py:42
  129.0 18.6 %collective-permute-done.31.refs_9_ = bf16[8,256,128]{2,1,0:T(8,128)(2,1)S(1)} collective-permute-done((bf16[8,256,128]{2,1,0:T(8,128)(2,1)S(1)}, bf16[8,256,128]{2,1,0:T(8,128)(2,1)S(1)}, u32[]{:S(2)}, u32[]{:S(2)}) %collective-permute-start.31) | collective-permute-done | bytes 524320 | tf_op jit(solution)/shard_map/ppermute | solution.py:42
  147.7 0.7 collective-permute-start.25
  148.5 1.4 collective-permute-start.32
  149.9 8.9 %collective-permute-done.26.refs_4_ = bf16[4,256,384]{2,1,0:T(8,128)(2,1)S(1)} collective-permute-done((bf16[4,256,384]{2,1,0:T(8,128)(2,1)S(1)}, bf16[4,256,384]{2,1,0:T(8,128)(2,1)S(1)}, u32[]{:S(2)}, u32[]{:S(2)}) %collective-permute-start.26) | collective-permute-done | bytes 786464 | tf_op jit(solution)/shard_map/ppermute | solution.py:42
  158.8 25.3 %collective-permute-done.27.refs_5_ = bf16[4,256,384]{2,1,0:T(8,128)(2,1)S(1)} collective-permute-done((bf16[4,256,384]{2,1,0:T(8,128)(2,1)S(1)}, bf16[4,256,384]{2,1,0:T(8,128)(2,1)S(1)}, u32[]{:S(2)}, u32[]{:S(2)}) %collective-permute-start.27) | collective-permute-done | bytes 786464 | tf_op jit(solution)/shard_map/ppermute | solution.py:42
  184.1 1.2 collective-permute-start.33
  185.3 8.2 %gate_up.4 = (f32[904,2048]{1,0:T(8,128)S(1)}, bf16[2,896,1536]{2,1,0:T(8,128)(2,1)S(1)}, bf16[4,896,256]{2,1,0:T(8,128)(2,1)S(1)}) custom-call(s32[4]{0:T(128)S(1)} %copy-done.2, bf16[8,256,384]{2,1,0:T(8,128)(2,1)S(1)} %pad_maximum_fusion.refs_0_, bf16[4,256,384]{2,1,0:T(8,128)(2,1)S(1)} %collective-permute-done.12.refs_1_, ...), custom_call_target="tpu_custom_call" | custom-call | flops 3758096384 | bytes 20971520 | tf_op jit(solution)/shard_map/gate_up/pallas_call | solution.py:402
  193.5 1.6 collective-permute-start.35
  195.1 1.9 collective-permute-start.36
  197.0 12.3 %gate_up.5.refs_7_.refs_2_ = f32[904,2048]{1,0:T(8,128)S(1)} custom-call(s32[4]{0:T(128)S(1)} %copy-done.2, bf16[8,256,384]{2,1,0:T(8,128)(2,1)S(1)} %collective-permute-done.22.refs_0_, bf16[4,256,384]{2,1,0:T(8,128)(2,1)S(1)} %collective-permute-done.23.refs_1_, ...), custom_call_target="tpu_custom_call", output_to_operand_aliasing={{}: (13, {})} | custom-call | flops 7516192768 | bytes 20971520 | tf_op jit(solution)/shard_map/gate_up/pallas_call | solution.py:402
  209.3 5.6 %gate_up.6 = (f32[8,2048]{1,0:T(8,128)S(1)}, bf16[464,2048]{1,0:T(8,128)(2,1)S(1)}, bf16[4,256,1536]{2,1,0:T(8,128)(2,1)S(1)}, bf16[1,2048,256]{2,1,0:T(8,128)(2,1)S(1)}) custom-call(s32[4]{0:T(128)S(1)} %copy-done.2, bf16[8,256,384]{2,1,0:T(8,128)(2,1)S(1)} %collective-permute-done.32.refs_0_, bf16[4,256,384]{2,1,0:T(8,128)(2,1)S(1)} %collective-permute-done.33.refs_1_, ...), custom_call_target="tpu_custom_call" | custom-call | flops 3758096384 | bytes 20971520 | tf_op jit(solution)/shard_map/gate_up/pallas_call | solution.py:402
  215.0 4.2 %collective-permute-start.37 = (bf16[464,2048]{1,0:T(8,128)(2,1)S(1)}, bf16[464,2048]{1,0:T(8,128)(2,1)S(1)}, u32[]{:S(2)}, u32[]{:S(2)}) collective-permute-start(bf16[464,2048]{1,0:T(8,128)(2,1)S(1)} %get-tuple-element.71), channel_id=1, source_target_pairs={{0,8},{8,0},{1,9},{9,1},{2,10},{10,2},{3,11},{11,3},{4,12},{12,4},... | collective-permute-start | bytes 5701640 | tf_op jit(solution)/shard_map/ppermute | solution.py:50
  219.1 4.4 %gate_up.7.own_ref = f32[448,2048]{1,0:T(8,128)S(1)} custom-call(s32[4]{0:T(128)S(1)} %copy-done.2, bf16[2,896,1536]{2,1,0:T(8,128)(2,1)S(1)} %get-tuple-element.65.refs_10_.refs_5_.refs_0_, bf16[4,896,256]{2,1,0:T(8,128)(2,1)S(1)} %get-tuple-element.66.refs_11_.refs_6_.refs_1_, f32[904,2048]{1,0:T(8,128)S(1)} %gate_up.5.refs_7_.refs_2_, ...), custom_call_target="tpu_custom_call" | custom-call | flops 3758096384 | bytes 20971520 | tf_op jit(solution)/shard_map/gate_up/pallas_call | solution.py:402
  223.6 1.6 finish.1
  (65 shorter events, 4.8 us)
Async XLA Ops:
  19.4 3.3 %collective-permute-start = (bf16[8,128,256]{2,1,0:T(8,128)(2,1)S(1)}, bf16[8,128,256]{2,1,0:T(8,128)(2,1)S(1)}, u32[]{:S(2)}, u32[]{:S(2)}) collective-permute-start(bf16[8,128,256]{2,1,0:T(8,128)(2,1)S(1)} %all_to_all.5.own_ref), channel_id=1, source_target_pairs={{0,8},{8,0},{1,9},{9,1},{2,10},{10,2},{3,11},{11,3},{4,12},{12,4},... | collective-permute-start | bytes 1572872 | tf_op jit(solution)/shard_map/ppermute | solution.py:50
  22.8 0.9 copy-start
  31.6 24.0 %copy-start.6 = (bf16[128,1024]{1,0:T(8,128)(2,1)S(1)}, bf16[128,1024]{1,0:T(8,128)(2,1)}, u32[]{:S(2)}) copy-start(bf16[128,1024]{1,0:T(8,128)(2,1)} %param.12) | copy-start | bytes 786436
  31.6 10.6 %collective-permute-start.1 = (bf16[2,128,1024]{2,1,0:T(8,128)(2,1)}, bf16[2,128,1024]{2,1,0:T(8,128)(2,1)S(1)}, u32[]{:S(2)}, u32[]{:S(2)}) collective-permute-start(bf16[2,128,1024]{2,1,0:T(8,128)(2,1)} %get-tuple-element.43), channel_id=1, source_target_pairs={{0,1},{2,3},{4,5},{6,7},{32,33},{34,35},{36,37},{38,39},{64,65},{6... | collective-permute-start | bytes 1572872 | tf_op jit(solution)/shard_map/ppermute | solution.py:42
  33.3 13.9 %collective-permute-start.2 = (bf16[2,128,1024]{2,1,0:T(8,128)(2,1)S(1)}, bf16[2,128,1024]{2,1,0:T(8,128)(2,1)S(1)}, u32[]{:S(2)}, u32[]{:S(2)}) collective-permute-start(bf16[2,128,1024]{2,1,0:T(8,128)(2,1)S(1)} %get-tuple-element.44), channel_id=1, source_target_pairs={{0,1},{2,3},{4,5},{6,7},{32,33},{34,35},{36,37},{38,39},{64,65},{6... | collective-permute-start | bytes 1572872 | tf_op jit(solution)/shard_map/ppermute | solution.py:42
  35.5 13.5 %collective-permute-start.3 = (bf16[2,128,1024]{2,1,0:T(8,128)(2,1)S(1)}, bf16[2,128,1024]{2,1,0:T(8,128)(2,1)S(1)}, u32[]{:S(2)}, u32[]{:S(2)}) collective-permute-start(bf16[2,128,1024]{2,1,0:T(8,128)(2,1)S(1)} %get-tuple-element.41.third), channel_id=1, source_target_pairs={{8,12},{10,14},{12,8},{14,10},{40,44},{42,46},{44,40},{46,42},{72,... | collective-permute-start | bytes 1572872 | tf_op jit(solution)/shard_map/ppermute | solution.py:42
  38.7 26.5 %copy-start.1 = (s32[4]{0:T(128)}, s32[4]{0:T(128)S(1)}, u32[]{:S(2)}) copy-start(s32[4]{0:T(128)S(1)} %pad_add_fusion.pos_ref) | copy-start | bytes 52
  50.0 5.6 %collective-permute-start.4 = (bf16[128,1024]{1,0:T(8,128)(2,1)S(1)}, bf16[128,1024]{1,0:T(8,128)(2,1)S(1)}, u32[]{:S(2)}, u32[]{:S(2)}) collective-permute-start(bf16[128,1024]{1,0:T(8,128)(2,1)S(1)} %get-tuple-element.46), channel_id=1, source_target_pairs={{0,2},{2,4},{4,6},{6,0},{32,34},{34,36},{36,38},{38,32},{64,66},{6... | collective-permute-start | bytes 786440 | tf_op jit(solution)/shard_map/ppermute | solution.py:42
  50.4 5.2 %collective-permute-start.5 = (bf16[128,1024]{1,0:T(8,128)(2,1)S(1)}, bf16[128,1024]{1,0:T(8,128)(2,1)S(1)}, u32[]{:S(2)}, u32[]{:S(2)}) collective-permute-start(bf16[128,1024]{1,0:T(8,128)(2,1)S(1)} %get-tuple-element.47), channel_id=1, source_target_pairs={{0,6},{2,0},{4,2},{6,4},{32,38},{34,32},{36,34},{38,36},{64,70},{6... | collective-permute-start | bytes 786440 | tf_op jit(solution)/shard_map/ppermute | solution.py:42
  51.0 4.5 %collective-permute-start.6 = (bf16[128,1024]{1,0:T(8,128)(2,1)S(1)}, bf16[128,1024]{1,0:T(8,128)(2,1)S(1)}, u32[]{:S(2)}, u32[]{:S(2)}) collective-permute-start(bf16[128,1024]{1,0:T(8,128)(2,1)S(1)} %get-tuple-element.48), channel_id=1, source_target_pairs={{0,4},{2,6},{4,0},{6,2},{32,36},{34,38},{36,32},{38,34},{64,68},{6... | collective-permute-start | bytes 786440 | tf_op jit(solution)/shard_map/ppermute | solution.py:42
  55.8 25.9 %copy-start.5 = (bf16[128,1024]{1,0:T(8,128)(2,1)}, bf16[128,1024]{1,0:T(8,128)(2,1)S(1)}, u32[]{:S(2)}) copy-start(bf16[128,1024]{1,0:T(8,128)(2,1)S(1)} %add_convert_fusion) | copy-start | bytes 786436
  55.8 9.3 %collective-permute-start.7 = (bf16[128,512]{1,0:T(8,128)(2,1)S(1)}, bf16[128,512]{1,0:T(8,128)(2,1)S(1)}, u32[]{:S(2)}, u32[]{:S(2)}) collective-permute-start(bf16[128,512]{1,0:T(8,128)(2,1)S(1)} %get-tuple-element.73), channel_id=1, source_target_pairs={{0,8},{8,0},{1,9},{9,1},{2,10},{10,2},{3,11},{11,3},{4,12},{12,4},... | collective-permute-start | bytes 393224 | tf_op jit(solution)/shard_map/ppermute | solution.py:50
  65.2 7.1 %collective-permute-start.14 = (bf16[256,128]{1,0:T(8,128)(2,1)S(1)}, bf16[256,128]{1,0:T(8,128)(2,1)S(1)}, u32[]{:S(2)}, u32[]{:S(2)}) collective-permute-start(bf16[256,128]{1,0:T(8,128)(2,1)S(1)} %slice.21), channel_id=1, source_target_pairs={{0,1},{2,3},{4,5},{6,7},{32,33},{34,35},{36,37},{38,39},{64,65},{6... | collective-permute-start | bytes 196616 | tf_op jit(solution)/shard_map/ppermute | solution.py:42
  65.6 19.3 %collective-permute-start.10 = (bf16[256,384]{1,0:T(8,128)(2,1)S(1)}, bf16[256,384]{1,0:T(8,128)(2,1)S(1)}, u32[]{:S(2)}, u32[]{:S(2)}) collective-permute-start(bf16[256,384]{1,0:T(8,128)(2,1)S(1)} %slice.20), channel_id=1, source_target_pairs={{0,64},{2,66},{4,68},{6,70},{32,96},{34,98},{36,100},{38,102},{64,... | collective-permute-start | bytes 589832 | tf_op jit(solution)/shard_map/ppermute | solution.py:42
  67.3 17.7 %collective-permute-start.8 = (bf16[256,384]{1,0:T(8,128)(2,1)S(1)}, bf16[256,384]{1,0:T(8,128)(2,1)S(1)}, u32[]{:S(2)}, u32[]{:S(2)}) collective-permute-start(bf16[256,384]{1,0:T(8,128)(2,1)S(1)} %slice.20), channel_id=1, source_target_pairs={{0,32},{2,34},{4,36},{6,38},{32,64},{34,66},{36,68},{38,70},{64,96... | collective-permute-start | bytes 589832 | tf_op jit(solution)/shard_map/ppermute | solution.py:42
  68.0 16.9 %collective-permute-start.9 = (bf16[256,384]{1,0:T(8,128)(2,1)S(1)}, bf16[256,384]{1,0:T(8,128)(2,1)S(1)}, u32[]{:S(2)}, u32[]{:S(2)}) collective-permute-start(bf16[256,384]{1,0:T(8,128)(2,1)S(1)} %slice.20), channel_id=1, source_target_pairs={{0,96},{2,98},{4,100},{6,102},{32,0},{34,2},{36,4},{38,6},{64,32},... | collective-permute-start | bytes 589832 | tf_op jit(solution)/shard_map/ppermute | solution.py:42
  69.9 11.8 %collective-permute-start.15 = (bf16[256,128]{1,0:T(8,128)(2,1)S(1)}, bf16[256,128]{1,0:T(8,128)(2,1)S(1)}, u32[]{:S(2)}, u32[]{:S(2)}) collective-permute-start(bf16[256,128]{1,0:T(8,128)(2,1)S(1)} %slice.21), channel_id=1, source_target_pairs={{0,17},{2,19},{4,21},{6,23},{32,49},{34,51},{36,53},{38,55},{64,81... | collective-permute-start | bytes 196616 | tf_op jit(solution)/shard_map/ppermute | solution.py:42
  72.3 11.2 %collective-permute-start.16 = (bf16[256,128]{1,0:T(8,128)(2,1)S(1)}, bf16[256,128]{1,0:T(8,128)(2,1)S(1)}, u32[]{:S(2)}, u32[]{:S(2)}) collective-permute-start(bf16[256,128]{1,0:T(8,128)(2,1)S(1)} %slice.21), channel_id=1, source_target_pairs={{0,16},{2,18},{4,20},{6,22},{32,48},{34,50},{36,52},{38,54},{64,80... | collective-permute-start | bytes 196616 | tf_op jit(solution)/shard_map/ppermute | solution.py:42
  81.7 18.9 %collective-permute-start.21 = (bf16[4,448,256]{2,1,0:T(8,128)(2,1)}, bf16[4,448,256]{2,1,0:T(8,128)(2,1)S(1)}, u32[]{:S(2)}, u32[]{:S(2)}) collective-permute-start(bf16[4,448,256]{2,1,0:T(8,128)(2,1)} %get-tuple-element.64), channel_id=1, source_target_pairs={{0,8},{8,0},{1,9},{9,1},{2,10},{10,2},{3,11},{11,3},{4,12},{12,4},... | collective-permute-start | bytes 2752520 | tf_op jit(solution)/shard_map/ppermute | solution.py:50
  83.5 9.6 %collective-permute-start.17 = (bf16[4,256,128]{2,1,0:T(8,128)(2,1)S(1)}, bf16[4,256,128]{2,1,0:T(8,128)(2,1)S(1)}, u32[]{:S(2)}, u32[]{:S(2)}) collective-permute-start(bf16[4,256,128]{2,1,0:T(8,128)(2,1)S(1)} %pad_maximum_fusion.4), channel_id=1, source_target_pairs={{0,32},{2,34},{4,36},{6,38},{32,64},{34,66},{36,68},{38,70},{64,96... | collective-permute-start | bytes 786440 | tf_op jit(solution)/shard_map/ppermute | solution.py:42
  85.1 100.2 %copy-start.2 = (s32[4]{0:T(128)S(1)}, s32[4]{0:T(128)}, u32[]{:S(2)}) copy-start(s32[4]{0:T(128)} %copy-done.1) | copy-start | bytes 52
  85.1 100.2 %copy-start.3 = (bf16[2,448,1536]{2,1,0:T(8,128)(2,1)S(1)}, bf16[2,448,1536]{2,1,0:T(8,128)(2,1)}, u32[]{:S(2)}) copy-start(bf16[2,448,1536]{2,1,0:T(8,128)(2,1)} %get-tuple-element.61.refs_5_) | copy-start | bytes 8257540
  85.1 100.2 %copy-start.4 = (bf16[4,448,256]{2,1,0:T(8,128)(2,1)S(1)}, bf16[4,448,256]{2,1,0:T(8,128)(2,1)}, u32[]{:S(2)}) copy-start(bf16[4,448,256]{2,1,0:T(8,128)(2,1)} %get-tuple-element.63.refs_7_) | copy-start | bytes 2752516
  85.1 17.3 %collective-permute-start.11 = (bf16[4,256,384]{2,1,0:T(8,128)(2,1)S(1)}, bf16[4,256,384]{2,1,0:T(8,128)(2,1)S(1)}, u32[]{:S(2)}, u32[]{:S(2)}) collective-permute-start(bf16[4,256,384]{2,1,0:T(8,128)(2,1)S(1)} %pad_maximum_fusion.1), channel_id=1, source_target_pairs={{0,2},{2,4},{4,6},{6,0},{32,34},{34,36},{36,38},{38,32},{64,66},{6... | collective-permute-start | bytes 2359304 | tf_op jit(solution)/shard_map/ppermute | solution.py:42
  85.5 9.0 %collective-permute-start.18 = (bf16[4,256,128]{2,1,0:T(8,128)(2,1)S(1)}, bf16[4,256,128]{2,1,0:T(8,128)(2,1)S(1)}, u32[]{:S(2)}, u32[]{:S(2)}) collective-permute-start(bf16[4,256,128]{2,1,0:T(8,128)(2,1)S(1)} %pad_maximum_fusion.4), channel_id=1, source_target_pairs={{0,96},{2,98},{4,100},{6,102},{32,0},{34,2},{36,4},{38,6},{64,32},... | collective-permute-start | bytes 786440 | tf_op jit(solution)/shard_map/ppermute | solution.py:42
  87.1 10.7 %collective-permute-start.19 = (bf16[4,256,128]{2,1,0:T(8,128)(2,1)S(1)}, bf16[4,256,128]{2,1,0:T(8,128)(2,1)S(1)}, u32[]{:S(2)}, u32[]{:S(2)}) collective-permute-start(bf16[4,256,128]{2,1,0:T(8,128)(2,1)S(1)} %pad_maximum_fusion.4), channel_id=1, source_target_pairs={{0,64},{2,66},{4,68},{6,70},{32,96},{34,98},{36,100},{38,102},{64,... | collective-permute-start | bytes 786440 | tf_op jit(solution)/shard_map/ppermute | solution.py:42
  93.1 92.2 %collective-permute-start.20 = (bf16[2,448,1536]{2,1,0:T(8,128)(2,1)}, bf16[2,448,1536]{2,1,0:T(8,128)(2,1)S(1)}, u32[]{:S(2)}, u32[]{:S(2)}) collective-permute-start(bf16[2,448,1536]{2,1,0:T(8,128)(2,1)} %get-tuple-element.62), channel_id=1, source_target_pairs={{0,8},{8,0},{1,9},{9,1},{2,10},{10,2},{3,11},{11,3},{4,12},{12,4},... | collective-permute-start | bytes 8257544 | tf_op jit(solution)/shard_map/ppermute | solution.py:50
  97.9 14.2 %collective-permute-start.28 = (bf16[8,256,128]{2,1,0:T(8,128)(2,1)S(1)}, bf16[8,256,128]{2,1,0:T(8,128)(2,1)S(1)}, u32[]{:S(2)}, u32[]{:S(2)}) collective-permute-start(bf16[8,256,128]{2,1,0:T(8,128)(2,1)S(1)} %pad_maximum_fusion.2.refs_3_), channel_id=1, source_target_pairs={{0,2},{2,4},{4,6},{6,0},{32,34},{34,36},{36,38},{38,32},{64,66},{6... | collective-permute-start | bytes 1572872 | tf_op jit(solution)/shard_map/ppermute | solution.py:42
  99.3 24.0 %collective-permute-start.29 = (bf16[8,256,128]{2,1,0:T(8,128)(2,1)S(1)}, bf16[8,256,128]{2,1,0:T(8,128)(2,1)S(1)}, u32[]{:S(2)}, u32[]{:S(2)}) collective-permute-start(bf16[8,256,128]{2,1,0:T(8,128)(2,1)S(1)} %pad_maximum_fusion.3.refs_4_), channel_id=1, source_target_pairs={{0,2},{2,4},{4,6},{6,0},{32,34},{34,36},{36,38},{38,32},{64,66},{6... | collective-permute-start | bytes 1572872 | tf_op jit(solution)/shard_map/ppermute | solution.py:42
  100.6 28.4 %collective-permute-start.12 = (bf16[4,256,384]{2,1,0:T(8,128)(2,1)S(1)}, bf16[4,256,384]{2,1,0:T(8,128)(2,1)S(1)}, u32[]{:S(2)}, u32[]{:S(2)}) collective-permute-start(bf16[4,256,384]{2,1,0:T(8,128)(2,1)S(1)} %pad_maximum_fusion.1), channel_id=1, source_target_pairs={{0,6},{2,0},{4,2},{6,4},{32,38},{34,32},{36,34},{38,36},{64,70},{6... | collective-permute-start | bytes 2359304 | tf_op jit(solution)/shard_map/ppermute | solution.py:42
  102.4 26.2 %collective-permute-start.30 = (bf16[8,256,128]{2,1,0:T(8,128)(2,1)S(1)}, bf16[8,256,128]{2,1,0:T(8,128)(2,1)S(1)}, u32[]{:S(2)}, u32[]{:S(2)}) collective-permute-start(bf16[8,256,128]{2,1,0:T(8,128)(2,1)S(1)} %pad_maximum_fusion.2.refs_3_), channel_id=1, source_target_pairs={{0,6},{2,0},{4,2},{6,4},{32,38},{34,32},{36,34},{38,36},{64,70},{6... | collective-permute-start | bytes 1572872 | tf_op jit(solution)/shard_map/ppermute | solution.py:42
  112.1 36.4 %collective-permute-start.22 = (bf16[8,256,384]{2,1,0:T(8,128)(2,1)S(1)}, bf16[8,256,384]{2,1,0:T(8,128)(2,1)S(1)}, u32[]{:S(2)}, u32[]{:S(2)}) collective-permute-start(bf16[8,256,384]{2,1,0:T(8,128)(2,1)S(1)} %pad_maximum_fusion.refs_0_), channel_id=1, source_target_pairs={{0,1},{2,3},{4,5},{6,7},{32,33},{34,35},{36,37},{38,39},{64,65},{6... | collective-permute-start | bytes 4718600 | tf_op jit(solution)/shard_map/ppermute | solution.py:42
  123.3 24.3 %collective-permute-start.13 = (bf16[4,256,384]{2,1,0:T(8,128)(2,1)S(1)}, bf16[4,256,384]{2,1,0:T(8,128)(2,1)S(1)}, u32[]{:S(2)}, u32[]{:S(2)}) collective-permute-start(bf16[4,256,384]{2,1,0:T(8,128)(2,1)S(1)} %pad_maximum_fusion.1), channel_id=1, source_target_pairs={{0,4},{2,6},{4,0},{6,2},{32,36},{34,38},{36,32},{38,34},{64,68},{6... | collective-permute-start | bytes 2359304 | tf_op jit(solution)/shard_map/ppermute | solution.py:42
  128.5 19.1 %collective-permute-start.31 = (bf16[8,256,128]{2,1,0:T(8,128)(2,1)S(1)}, bf16[8,256,128]{2,1,0:T(8,128)(2,1)S(1)}, u32[]{:S(2)}, u32[]{:S(2)}) collective-permute-start(bf16[8,256,128]{2,1,0:T(8,128)(2,1)S(1)} %pad_maximum_fusion.3.refs_4_), channel_id=1, source_target_pairs={{0,6},{2,0},{4,2},{6,4},{32,38},{34,32},{36,34},{38,36},{64,70},{6... | collective-permute-start | bytes 1572872 | tf_op jit(solution)/shard_map/ppermute | solution.py:42
  129.0 19.3 %collective-permute-start.23 = (bf16[4,256,384]{2,1,0:T(8,128)(2,1)S(1)}, bf16[4,256,384]{2,1,0:T(8,128)(2,1)S(1)}, u32[]{:S(2)}, u32[]{:S(2)}) collective-permute-start(bf16[4,256,384]{2,1,0:T(8,128)(2,1)S(1)} %collective-permute-done.12.refs_1_), channel_id=1, source_target_pairs={{0,1},{2,3},{4,5},{6,7},{32,33},{34,35},{36,37},{38,39},{64,65},{6... | collective-permute-start | bytes 2359304 | tf_op jit(solution)/shard_map/ppermute | solution.py:42
  147.7 11.1 %collective-permute-start.26 = (bf16[4,256,384]{2,1,0:T(8,128)(2,1)S(1)}, bf16[4,256,384]{2,1,0:T(8,128)(2,1)S(1)}, u32[]{:S(2)}, u32[]{:S(2)}) collective-permute-start(bf16[4,256,384]{2,1,0:T(8,128)(2,1)S(1)} %collective-permute-done.12.refs_1_), channel_id=1, source_target_pairs={{0,17},{2,19},{4,21},{6,23},{32,49},{34,51},{36,53},{38,55},{64,81... | collective-permute-start | bytes 2359304 | tf_op jit(solution)/shard_map/ppermute | solution.py:42
  147.7 47.4 %collective-permute-start.25 = (bf16[8,256,384]{2,1,0:T(8,128)(2,1)S(1)}, bf16[8,256,384]{2,1,0:T(8,128)(2,1)S(1)}, u32[]{:S(2)}, u32[]{:S(2)}) collective-permute-start(bf16[8,256,384]{2,1,0:T(8,128)(2,1)S(1)} %pad_maximum_fusion.refs_0_), channel_id=1, source_target_pairs={{0,17},{2,19},{4,21},{6,23},{32,49},{34,51},{36,53},{38,55},{64,81... | collective-permute-start | bytes 4718600 | tf_op jit(solution)/shard_map/ppermute | solution.py:42
  148.4 35.7 %collective-permute-start.27 = (bf16[4,256,384]{2,1,0:T(8,128)(2,1)S(1)}, bf16[4,256,384]{2,1,0:T(8,128)(2,1)S(1)}, u32[]{:S(2)}, u32[]{:S(2)}) collective-permute-start(bf16[4,256,384]{2,1,0:T(8,128)(2,1)S(1)} %collective-permute-done.13.refs_2_), channel_id=1, source_target_pairs={{0,17},{2,19},{4,21},{6,23},{32,49},{34,51},{36,53},{38,55},{64,81... | collective-permute-start | bytes 2359304 | tf_op jit(solution)/shard_map/ppermute | solution.py:42
  148.5 60.9 %collective-permute-start.32 = (bf16[8,256,384]{2,1,0:T(8,128)(2,1)S(1)}, bf16[8,256,384]{2,1,0:T(8,128)(2,1)S(1)}, u32[]{:S(2)}, u32[]{:S(2)}) collective-permute-start(bf16[8,256,384]{2,1,0:T(8,128)(2,1)S(1)} %collective-permute-done.22.refs_0_), channel_id=1, source_target_pairs={{0,1},{2,3},{4,5},{6,7},{32,33},{34,35},{36,37},{38,39},{64,65},{6... | collective-permute-start | bytes 4718600 | tf_op jit(solution)/shard_map/ppermute | solution.py:42
  158.8 34.7 %collective-permute-start.24 = (bf16[4,256,384]{2,1,0:T(8,128)(2,1)S(1)}, bf16[4,256,384]{2,1,0:T(8,128)(2,1)S(1)}, u32[]{:S(2)}, u32[]{:S(2)}) collective-permute-start(bf16[4,256,384]{2,1,0:T(8,128)(2,1)S(1)} %collective-permute-done.13.refs_2_), channel_id=1, source_target_pairs={{0,1},{2,3},{4,5},{6,7},{32,33},{34,35},{36,37},{38,39},{64,65},{6... | collective-permute-start | bytes 2359304 | tf_op jit(solution)/shard_map/ppermute | solution.py:42
  184.1 25.2 %collective-permute-start.33 = (bf16[4,256,384]{2,1,0:T(8,128)(2,1)S(1)}, bf16[4,256,384]{2,1,0:T(8,128)(2,1)S(1)}, u32[]{:S(2)}, u32[]{:S(2)}) collective-permute-start(bf16[4,256,384]{2,1,0:T(8,128)(2,1)S(1)} %collective-permute-done.26.refs_4_), channel_id=1, source_target_pairs={{0,17},{2,19},{4,21},{6,23},{32,49},{34,51},{36,53},{38,55},{64,81... | collective-permute-start | bytes 2359304 | tf_op jit(solution)/shard_map/ppermute | solution.py:42
  185.3 24.0 %collective-permute-start.34 = (bf16[4,256,384]{2,1,0:T(8,128)(2,1)S(1)}, bf16[4,256,384]{2,1,0:T(8,128)(2,1)S(1)}, u32[]{:S(2)}, u32[]{:S(2)}) collective-permute-start(bf16[4,256,384]{2,1,0:T(8,128)(2,1)S(1)} %collective-permute-done.27.refs_5_), channel_id=1, source_target_pairs={{0,17},{2,19},{4,21},{6,23},{32,49},{34,51},{36,53},{38,55},{64,81... | collective-permute-start | bytes 2359304 | tf_op jit(solution)/shard_map/ppermute | solution.py:42
  193.5 15.8 %collective-permute-start.35 = (bf16[8,256,128]{2,1,0:T(8,128)(2,1)S(1)}, bf16[8,256,128]{2,1,0:T(8,128)(2,1)S(1)}, u32[]{:S(2)}, u32[]{:S(2)}) collective-permute-start(bf16[8,256,128]{2,1,0:T(8,128)(2,1)S(1)} %collective-permute-done.28.refs_6_), channel_id=1, source_target_pairs={{0,2},{2,4},{4,6},{6,0},{32,34},{34,36},{36,38},{38,32},{64,66},{6... | collective-permute-start | bytes 1572872 | tf_op jit(solution)/shard_map/ppermute | solution.py:42
  195.1 14.2 %collective-permute-start.36 = (bf16[8,256,128]{2,1,0:T(8,128)(2,1)S(1)}, bf16[8,256,128]{2,1,0:T(8,128)(2,1)S(1)}, u32[]{:S(2)}, u32[]{:S(2)}) collective-permute-start(bf16[8,256,128]{2,1,0:T(8,128)(2,1)S(1)} %collective-permute-done.31.refs_9_), channel_id=1, source_target_pairs={{0,6},{2,0},{4,2},{6,4},{32,38},{34,32},{36,34},{38,36},{64,70},{6... | collective-permute-start | bytes 1572872 | tf_op jit(solution)/shard_map/ppermute | solution.py:42
  215.0 8.6 %collective-permute-start.37 = (bf16[464,2048]{1,0:T(8,128)(2,1)S(1)}, bf16[464,2048]{1,0:T(8,128)(2,1)S(1)}, u32[]{:S(2)}, u32[]{:S(2)}) collective-permute-start(bf16[464,2048]{1,0:T(8,128)(2,1)S(1)} %get-tuple-element.71), channel_id=1, source_target_pairs={{0,8},{8,0},{1,9},{9,1},{2,10},{10,2},{3,11},{11,3},{4,12},{12,4},... | collective-permute-start | bytes 5701640 | tf_op jit(solution)/shard_map/ppermute | solution.py:50

commit v8 on v7

--- a/solution.py
+++ b/solution.py
@@ -465,7 +465,8 @@
     cur_main = jnp.stack(main_near)
     cur_main = lax.optimization_barrier(cur_main)
     ahead = shift(cur_main, axes[0][1], 1)
-    third, fourth = (shift(cur_main, axes[0][1], by) for by in (-1, 2))
+    third = shift(cur_main, axes[0][1], -1)
+    fourth = shift(cur_main, axes[0][1], 2)
     side_near = lax.optimization_barrier([blocks[1]] + side_near)
     cur_side = jnp.stack(side_near)
     cur_side = lax.optimization_barrier(cur_side)
@@ -476,7 +477,9 @@
 
     low = jnp.concatenate([cur_main, ahead], 0)
     low = lax.optimization_barrier(low)
-    lows = both_ways(low, axes[0])
+    low_minus = shift(low, axes[0][2], -1)
+    low_plus = shift(low, axes[0][2], 1)
+    lows = (low_plus, low_minus)
     thirds = both_ways(third, axes[0])
     fourths = both_ways(fourth, axes[0])
     side_low = jnp.concatenate([cur_side, side_next[0]], 0)

time: 226 us -> 226 us (level)
  no operation moved by 1% of the time
where the time goes in v8:
time: 226 us; the launch traced here: 225 us
  waiting for transfers between devices  97.3 us (43%)
  starting transfers between devices  56 us (25%)
  Pallas kernels  50.3 us (22%)
  blocking collectives  18 us (8%)
    ppermute x33, waiting for transfers between devices, move(): return lax.ppermute(x, MESH, pairs)  94.8 us
    ppermute x33, starting transfers between devices, move(): return lax.ppermute(x, MESH, pairs)  38.5 us
    pallas_call x4, Pallas kernels, gate_up(): pl.pallas_call(functools.partial(gate_kernel, which, stage), out_shape=ou...  30.5 us
    all_to_all x1, blocking collectives, per_device(): own = lax.all_to_all(spread, ('y', 'xh'), 0, 0, tiled=True)  18 us
    ppermute x5, starting transfers between devices, swap_core(): return lax.ppermute(x, 'c', [(0, 1), (1, 0)])  17.5 us
    pallas_call x1, Pallas kernels, prepare(): pl.pallas_call(prep_kernel, out_shape=[mshape, sshape, mshape, sshape], g...  9.37 us
    pallas_call x1, Pallas kernels, attend_project(): pl.pallas_call(attend_kernel, out_shape=[jax.ShapeDtypeStruct((2, rows, w...  7.81 us
  transfers between devices with their start and end apart: 38, of which 13 were waited for; matrix products, arithmetic and copies ran while one was open for 0% of the time, Pallas kernels for 15%

profile of v8, /device:TPU:1, one launch (start us, length us, event | category | flops | bytes accessed | tf_op | source)
XLA Modules:
  0.0 225.4 jit_solution(10036222103330808838)
XLA Ops:
  0.6 0.8 pad_maximum_fusion.5
  1.5 18.0 %all_to_all.5.own_ref = bf16[8,128,256]{2,1,0:T(8,128)(2,1)S(1)} all-to-all(bf16[8,128,256]{2,1,0:T(8,128)(2,1)S(1)} %broadcast_in_dim.4), channel_id=1, replica_groups=mesh['y'=4,'xh'=2,'c'=2,'z'=4,'xl'=2] {'y','xh'}, dimensions={0} | all-to-all | bytes 1048576 | tf_op jit(solution)/shard_map/all_to_all | solution.py:517
  19.4 1.8 collective-permute-start
  21.3 1.5 collective-permute-done.oth_ref
  22.8 0.9 copy-done
  23.7 7.8 %attend_project.1 = (bf16[2,128,1024]{2,1,0:T(8,128)(2,1)}, bf16[2,128,1024]{2,1,0:T(8,128)(2,1)S(1)}, bf16[2,128,1024]{2,1,0:T(8,128)(2,1)S(1)}, bf16[2,128,1024]{2,1,0:T(8,128)(2,1)S(1)}) custom-call(s32[10]{0:T(128)S(1)} %stack.90.pos_ref, bf16[128,1024]{1,0:T(8,128)(2,1)S(1)} %copy-done, bf16[8,128,256]{2,1,0:T(8,128)(2,1)S(1)} %all_to_all.5.own_ref, ...), custom_call_target="tpu_custom_call" | custom-call | flops 4294967296 | bytes 20971520 | tf_op jit(solution)/shard_map/attend_project/pallas_call | solution.py:125
  31.6 1.7 collective-permute-start.1
  33.3 2.2 collective-permute-start.2
  35.5 3.1 %collective-permute-start.3 = (bf16[2,128,1024]{2,1,0:T(8,128)(2,1)S(1)}, bf16[2,128,1024]{2,1,0:T(8,128)(2,1)S(1)}, u32[]{:S(2)}, u32[]{:S(2)}) collective-permute-start(bf16[2,128,1024]{2,1,0:T(8,128)(2,1)S(1)} %get-tuple-element.41.third), channel_id=1, source_target_pairs={{8,12},{10,14},{12,8},{14,10},{40,44},{42,46},{44,40},{46,42},{72,... | collective-permute-start | bytes 1572872 | tf_op jit(solution)/shard_map/ppermute | solution.py:42
  38.7 3.5 %collective-permute-done.1.r1 = bf16[2,128,1024]{2,1,0:T(8,128)(2,1)S(1)} collective-permute-done((bf16[2,128,1024]{2,1,0:T(8,128)(2,1)}, bf16[2,128,1024]{2,1,0:T(8,128)(2,1)S(1)}, u32[]{:S(2)}, u32[]{:S(2)}) %collective-permute-start.1) | collective-permute-done | bytes 524320 | tf_op jit(solution)/shard_map/ppermute | solution.py:42
  42.2 5.0 %collective-permute-done.2.r2 = bf16[2,128,1024]{2,1,0:T(8,128)(2,1)S(1)} collective-permute-done((bf16[2,128,1024]{2,1,0:T(8,128)(2,1)S(1)}, bf16[2,128,1024]{2,1,0:T(8,128)(2,1)S(1)}, u32[]{:S(2)}, u32[]{:S(2)}) %collective-permute-start.2) | collective-permute-done | bytes 524320 | tf_op jit(solution)/shard_map/ppermute | solution.py:42
  47.2 1.8 collective-permute-done.3.r3
  49.0 1.0 middle.1
  51.7 3.8 %collective-permute-done.4 = bf16[128,1024]{1,0:T(8,128)(2,1)S(1)} collective-permute-done((bf16[128,1024]{1,0:T(8,128)(2,1)S(1)}, bf16[128,1024]{1,0:T(8,128)(2,1)S(1)}, u32[]{:S(2)}, u32[]{:S(2)}) %collective-permute-start.4) | collective-permute-done | bytes 262176 | tf_op jit(solution)/shard_map/ppermute | solution.py:42
  55.8 8.3 %collective-permute-start.7 = (bf16[128,512]{1,0:T(8,128)(2,1)S(1)}, bf16[128,512]{1,0:T(8,128)(2,1)S(1)}, u32[]{:S(2)}, u32[]{:S(2)}) collective-permute-start(bf16[128,512]{1,0:T(8,128)(2,1)S(1)} %get-tuple-element.73), channel_id=1, source_target_pairs={{0,8},{8,0},{1,9},{9,1},{2,10},{10,2},{3,11},{11,3},{4,12},{12,4},... | collective-permute-start | bytes 393224 | tf_op jit(solution)/shard_map/ppermute | solution.py:50
  64.1 1.0 collective-permute-done.7
  65.6 1.6 collective-permute-start.10
  67.3 0.7 collective-permute-start.8
  68.0 1.9 collective-permute-start.9
  69.9 2.4 %collective-permute-start.15 = (bf16[256,128]{1,0:T(8,128)(2,1)S(1)}, bf16[256,128]{1,0:T(8,128)(2,1)S(1)}, u32[]{:S(2)}, u32[]{:S(2)}) collective-permute-start(bf16[256,128]{1,0:T(8,128)(2,1)S(1)} %slice.21), channel_id=1, source_target_pairs={{0,17},{2,19},{4,21},{6,23},{32,49},{34,51},{36,53},{38,55},{64,81... | collective-permute-start | bytes 196616 | tf_op jit(solution)/shard_map/ppermute | solution.py:42
  72.3 9.4 %prepare.1 = (bf16[2,448,1536]{2,1,0:T(8,128)(2,1)}, bf16[4,448,256]{2,1,0:T(8,128)(2,1)}, bf16[2,448,1536]{2,1,0:T(8,128)(2,1)}, bf16[4,448,256]{2,1,0:T(8,128)(2,1)}) custom-call(s32[4]{0:T(128)} %copy-done.1, bf16[224,8192]{1,0:T(8,128)(2,1)} %bitcast.25, bf16[224,8192]{1,0:T(8,128)(2,1)} %bitcast.26, f32[1,8192]{1,0:T(1,128)} %bitcast.36), custom_call_target="tpu_custom_call" | custom-call | flops 8388608 | bytes 15728640 | tf_op jit(solution)/shard_map/prepare/pallas_call | solution.py:204
  81.7 1.8 collective-permute-start.21
  83.5 1.4 collective-permute-start.17
  85.5 1.6 collective-permute-start.18
  87.3 5.8 %collective-permute-done.17 = bf16[4,256,128]{2,1,0:T(8,128)(2,1)S(1)} collective-permute-done((bf16[4,256,128]{2,1,0:T(8,128)(2,1)S(1)}, bf16[4,256,128]{2,1,0:T(8,128)(2,1)S(1)}, u32[]{:S(2)}, u32[]{:S(2)}) %collective-permute-start.17) | collective-permute-done | bytes 262176 | tf_op jit(solution)/shard_map/ppermute | solution.py:42
  93.1 1.4 collective-permute-start.20
  94.5 3.3 %collective-permute-done.19 = bf16[4,256,128]{2,1,0:T(8,128)(2,1)S(1)} collective-permute-done((bf16[4,256,128]{2,1,0:T(8,128)(2,1)S(1)}, bf16[4,256,128]{2,1,0:T(8,128)(2,1)S(1)}, u32[]{:S(2)}, u32[]{:S(2)}) %collective-permute-start.19) | collective-permute-done | bytes 262176 | tf_op jit(solution)/shard_map/ppermute | solution.py:42
  97.9 1.4 collective-permute-start.28
  99.3 1.3 collective-permute-start.29
  100.6 1.8 collective-permute-start.12
  102.4 1.5 collective-permute-start.30
  104.1 8.0 %collective-permute-done.28.refs_6_ = bf16[8,256,128]{2,1,0:T(8,128)(2,1)S(1)} collective-permute-done((bf16[8,256,128]{2,1,0:T(8,128)(2,1)S(1)}, bf16[8,256,128]{2,1,0:T(8,128)(2,1)S(1)}, u32[]{:S(2)}, u32[]{:S(2)}) %collective-permute-start.28) | collective-permute-done | bytes 524320 | tf_op jit(solution)/shard_map/ppermute | solution.py:42
  112.6 10.7 %collective-permute-done.29.refs_7_ = bf16[8,256,128]{2,1,0:T(8,128)(2,1)S(1)} collective-permute-done((bf16[8,256,128]{2,1,0:T(8,128)(2,1)S(1)}, bf16[8,256,128]{2,1,0:T(8,128)(2,1)S(1)}, u32[]{:S(2)}, u32[]{:S(2)}) %collective-permute-start.29) | collective-permute-done | bytes 524320 | tf_op jit(solution)/shard_map/ppermute | solution.py:42
  123.3 5.2 %collective-permute-start.13 = (bf16[4,256,384]{2,1,0:T(8,128)(2,1)S(1)}, bf16[4,256,384]{2,1,0:T(8,128)(2,1)S(1)}, u32[]{:S(2)}, u32[]{:S(2)}) collective-permute-start(bf16[4,256,384]{2,1,0:T(8,128)(2,1)S(1)} %pad_maximum_fusion.1), channel_id=1, source_target_pairs={{0,4},{2,6},{4,0},{6,2},{32,36},{34,38},{36,32},{38,34},{64,68},{6... | collective-permute-start | bytes 2359304 | tf_op jit(solution)/shard_map/ppermute | solution.py:42
  129.0 18.6 %collective-permute-done.31.refs_9_ = bf16[8,256,128]{2,1,0:T(8,128)(2,1)S(1)} collective-permute-done((bf16[8,256,128]{2,1,0:T(8,128)(2,1)S(1)}, bf16[8,256,128]{2,1,0:T(8,128)(2,1)S(1)}, u32[]{:S(2)}, u32[]{:S(2)}) %collective-permute-start.31) | collective-permute-done | bytes 524320 | tf_op jit(solution)/shard_map/ppermute | solution.py:42
  147.7 0.7 collective-permute-start.25
  148.5 1.4 collective-permute-start.32
  149.9 8.9 %collective-permute-done.26.refs_4_ = bf16[4,256,384]{2,1,0:T(8,128)(2,1)S(1)} collective-permute-done((bf16[4,256,384]{2,1,0:T(8,128)(2,1)S(1)}, bf16[4,256,384]{2,1,0:T(8,128)(2,1)S(1)}, u32[]{:S(2)}, u32[]{:S(2)}) %collective-permute-start.26) | collective-permute-done | bytes 786464 | tf_op jit(solution)/shard_map/ppermute | solution.py:42
  158.8 25.3 %collective-permute-done.27.refs_5_ = bf16[4,256,384]{2,1,0:T(8,128)(2,1)S(1)} collective-permute-done((bf16[4,256,384]{2,1,0:T(8,128)(2,1)S(1)}, bf16[4,256,384]{2,1,0:T(8,128)(2,1)S(1)}, u32[]{:S(2)}, u32[]{:S(2)}) %collective-permute-start.27) | collective-permute-done | bytes 786464 | tf_op jit(solution)/shard_map/ppermute | solution.py:42
  184.1 1.2 collective-permute-start.33
  185.3 8.2 %gate_up.4 = (f32[904,2048]{1,0:T(8,128)S(1)}, bf16[2,896,1536]{2,1,0:T(8,128)(2,1)S(1)}, bf16[4,896,256]{2,1,0:T(8,128)(2,1)S(1)}) custom-call(s32[4]{0:T(128)S(1)} %copy-done.2, bf16[8,256,384]{2,1,0:T(8,128)(2,1)S(1)} %pad_maximum_fusion.refs_0_, bf16[4,256,384]{2,1,0:T(8,128)(2,1)S(1)} %collective-permute-done.12.refs_1_, ...), custom_call_target="tpu_custom_call" | custom-call | flops 3758096384 | bytes 20971520 | tf_op jit(solution)/shard_map/gate_up/pallas_call | solution.py:402
  193.5 1.6 collective-permute-start.35
  195.1 1.9 collective-permute-start.36
  197.0 12.3 %gate_up.5.refs_7_.refs_2_ = f32[904,2048]{1,0:T(8,128)S(1)} custom-call(s32[4]{0:T(128)S(1)} %copy-done.2, bf16[8,256,384]{2,1,0:T(8,128)(2,1)S(1)} %collective-permute-done.22.refs_0_, bf16[4,256,384]{2,1,0:T(8,128)(2,1)S(1)} %collective-permute-done.23.refs_1_, ...), custom_call_target="tpu_custom_call", output_to_operand_aliasing={{}: (13, {})} | custom-call | flops 7516192768 | bytes 20971520 | tf_op jit(solution)/shard_map/gate_up/pallas_call | solution.py:402
  209.3 5.6 %gate_up.6 = (f32[8,2048]{1,0:T(8,128)S(1)}, bf16[464,2048]{1,0:T(8,128)(2,1)S(1)}, bf16[4,256,1536]{2,1,0:T(8,128)(2,1)S(1)}, bf16[1,2048,256]{2,1,0:T(8,128)(2,1)S(1)}) custom-call(s32[4]{0:T(128)S(1)} %copy-done.2, bf16[8,256,384]{2,1,0:T(8,128)(2,1)S(1)} %collective-permute-done.32.refs_0_, bf16[4,256,384]{2,1,0:T(8,128)(2,1)S(1)} %collective-permute-done.33.refs_1_, ...), custom_call_target="tpu_custom_call" | custom-call | flops 3758096384 | bytes 20971520 | tf_op jit(solution)/shard_map/gate_up/pallas_call | solution.py:402
  215.0 4.2 %collective-permute-start.37 = (bf16[464,2048]{1,0:T(8,128)(2,1)S(1)}, bf16[464,2048]{1,0:T(8,128)(2,1)S(1)}, u32[]{:S(2)}, u32[]{:S(2)}) collective-permute-start(bf16[464,2048]{1,0:T(8,128)(2,1)S(1)} %get-tuple-element.71), channel_id=1, source_target_pairs={{0,8},{8,0},{1,9},{9,1},{2,10},{10,2},{3,11},{11,3},{4,12},{12,4},... | collective-permute-start | bytes 5701640 | tf_op jit(solution)/shard_map/ppermute | solution.py:50
  219.1 4.4 %gate_up.7.own_ref = f32[448,2048]{1,0:T(8,128)S(1)} custom-call(s32[4]{0:T(128)S(1)} %copy-done.2, bf16[2,896,1536]{2,1,0:T(8,128)(2,1)S(1)} %get-tuple-element.65.refs_10_.refs_5_.refs_0_, bf16[4,896,256]{2,1,0:T(8,128)(2,1)S(1)} %get-tuple-element.66.refs_11_.refs_6_.refs_1_, f32[904,2048]{1,0:T(8,128)S(1)} %gate_up.5.refs_7_.refs_2_, ...), custom_call_target="tpu_custom_call" | custom-call | flops 3758096384 | bytes 20971520 | tf_op jit(solution)/shard_map/gate_up/pallas_call | solution.py:402
  223.6 1.6 finish.1
  (65 shorter events, 4.8 us)
Async XLA Ops:
  19.4 3.3 %collective-permute-start = (bf16[8,128,256]{2,1,0:T(8,128)(2,1)S(1)}, bf16[8,128,256]{2,1,0:T(8,128)(2,1)S(1)}, u32[]{:S(2)}, u32[]{:S(2)}) collective-permute-start(bf16[8,128,256]{2,1,0:T(8,128)(2,1)S(1)} %all_to_all.5.own_ref), channel_id=1, source_target_pairs={{0,8},{8,0},{1,9},{9,1},{2,10},{10,2},{3,11},{11,3},{4,12},{12,4},... | collective-permute-start | bytes 1572872 | tf_op jit(solution)/shard_map/ppermute | solution.py:50
  22.8 0.9 copy-start
  31.6 24.0 %copy-start.6 = (bf16[128,1024]{1,0:T(8,128)(2,1)S(1)}, bf16[128,1024]{1,0:T(8,128)(2,1)}, u32[]{:S(2)}) copy-start(bf16[128,1024]{1,0:T(8,128)(2,1)} %param.12) | copy-start | bytes 786436
  31.6 10.6 %collective-permute-start.1 = (bf16[2,128,1024]{2,1,0:T(8,128)(2,1)}, bf16[2,128,1024]{2,1,0:T(8,128)(2,1)S(1)}, u32[]{:S(2)}, u32[]{:S(2)}) collective-permute-start(bf16[2,128,1024]{2,1,0:T(8,128)(2,1)} %get-tuple-element.43), channel_id=1, source_target_pairs={{0,1},{2,3},{4,5},{6,7},{32,33},{34,35},{36,37},{38,39},{64,65},{6... | collective-permute-start | bytes 1572872 | tf_op jit(solution)/shard_map/ppermute | solution.py:42
  33.3 13.9 %collective-permute-start.2 = (bf16[2,128,1024]{2,1,0:T(8,128)(2,1)S(1)}, bf16[2,128,1024]{2,1,0:T(8,128)(2,1)S(1)}, u32[]{:S(2)}, u32[]{:S(2)}) collective-permute-start(bf16[2,128,1024]{2,1,0:T(8,128)(2,1)S(1)} %get-tuple-element.44), channel_id=1, source_target_pairs={{0,1},{2,3},{4,5},{6,7},{32,33},{34,35},{36,37},{38,39},{64,65},{6... | collective-permute-start | bytes 1572872 | tf_op jit(solution)/shard_map/ppermute | solution.py:42
  35.5 13.5 %collective-permute-start.3 = (bf16[2,128,1024]{2,1,0:T(8,128)(2,1)S(1)}, bf16[2,128,1024]{2,1,0:T(8,128)(2,1)S(1)}, u32[]{:S(2)}, u32[]{:S(2)}) collective-permute-start(bf16[2,128,1024]{2,1,0:T(8,128)(2,1)S(1)} %get-tuple-element.41.third), channel_id=1, source_target_pairs={{8,12},{10,14},{12,8},{14,10},{40,44},{42,46},{44,40},{46,42},{72,... | collective-permute-start | bytes 1572872 | tf_op jit(solution)/shard_map/ppermute | solution.py:42
  38.7 26.5 %copy-start.1 = (s32[4]{0:T(128)}, s32[4]{0:T(128)S(1)}, u32[]{:S(2)}) copy-start(s32[4]{0:T(128)S(1)} %pad_add_fusion.pos_ref) | copy-start | bytes 52
  50.0 5.6 %collective-permute-start.4 = (bf16[128,1024]{1,0:T(8,128)(2,1)S(1)}, bf16[128,1024]{1,0:T(8,128)(2,1)S(1)}, u32[]{:S(2)}, u32[]{:S(2)}) collective-permute-start(bf16[128,1024]{1,0:T(8,128)(2,1)S(1)} %get-tuple-element.46), channel_id=1, source_target_pairs={{0,2},{2,4},{4,6},{6,0},{32,34},{34,36},{36,38},{38,32},{64,66},{6... | collective-permute-start | bytes 786440 | tf_op jit(solution)/shard_map/ppermute | solution.py:42
  50.4 5.2 %collective-permute-start.5 = (bf16[128,1024]{1,0:T(8,128)(2,1)S(1)}, bf16[128,1024]{1,0:T(8,128)(2,1)S(1)}, u32[]{:S(2)}, u32[]{:S(2)}) collective-permute-start(bf16[128,1024]{1,0:T(8,128)(2,1)S(1)} %get-tuple-element.47), channel_id=1, source_target_pairs={{0,6},{2,0},{4,2},{6,4},{32,38},{34,32},{36,34},{38,36},{64,70},{6... | collective-permute-start | bytes 786440 | tf_op jit(solution)/shard_map/ppermute | solution.py:42
  51.0 4.5 %collective-permute-start.6 = (bf16[128,1024]{1,0:T(8,128)(2,1)S(1)}, bf16[128,1024]{1,0:T(8,128)(2,1)S(1)}, u32[]{:S(2)}, u32[]{:S(2)}) collective-permute-start(bf16[128,1024]{1,0:T(8,128)(2,1)S(1)} %get-tuple-element.48), channel_id=1, source_target_pairs={{0,4},{2,6},{4,0},{6,2},{32,36},{34,38},{36,32},{38,34},{64,68},{6... | collective-permute-start | bytes 786440 | tf_op jit(solution)/shard_map/ppermute | solution.py:42
  55.8 25.9 %copy-start.5 = (bf16[128,1024]{1,0:T(8,128)(2,1)}, bf16[128,1024]{1,0:T(8,128)(2,1)S(1)}, u32[]{:S(2)}) copy-start(bf16[128,1024]{1,0:T(8,128)(2,1)S(1)} %add_convert_fusion) | copy-start | bytes 786436
  55.8 9.3 %collective-permute-start.7 = (bf16[128,512]{1,0:T(8,128)(2,1)S(1)}, bf16[128,512]{1,0:T(8,128)(2,1)S(1)}, u32[]{:S(2)}, u32[]{:S(2)}) collective-permute-start(bf16[128,512]{1,0:T(8,128)(2,1)S(1)} %get-tuple-element.73), channel_id=1, source_target_pairs={{0,8},{8,0},{1,9},{9,1},{2,10},{10,2},{3,11},{11,3},{4,12},{12,4},... | collective-permute-start | bytes 393224 | tf_op jit(solution)/shard_map/ppermute | solution.py:50
  65.2 7.1 %collective-permute-start.14 = (bf16[256,128]{1,0:T(8,128)(2,1)S(1)}, bf16[256,128]{1,0:T(8,128)(2,1)S(1)}, u32[]{:S(2)}, u32[]{:S(2)}) collective-permute-start(bf16[256,128]{1,0:T(8,128)(2,1)S(1)} %slice.21), channel_id=1, source_target_pairs={{0,1},{2,3},{4,5},{6,7},{32,33},{34,35},{36,37},{38,39},{64,65},{6... | collective-permute-start | bytes 196616 | tf_op jit(solution)/shard_map/ppermute | solution.py:42
  65.6 19.3 %collective-permute-start.10 = (bf16[256,384]{1,0:T(8,128)(2,1)S(1)}, bf16[256,384]{1,0:T(8,128)(2,1)S(1)}, u32[]{:S(2)}, u32[]{:S(2)}) collective-permute-start(bf16[256,384]{1,0:T(8,128)(2,1)S(1)} %slice.20), channel_id=1, source_target_pairs={{0,64},{2,66},{4,68},{6,70},{32,96},{34,98},{36,100},{38,102},{64,... | collective-permute-start | bytes 589832 | tf_op jit(solution)/shard_map/ppermute | solution.py:42
  67.3 17.7 %collective-permute-start.8 = (bf16[256,384]{1,0:T(8,128)(2,1)S(1)}, bf16[256,384]{1,0:T(8,128)(2,1)S(1)}, u32[]{:S(2)}, u32[]{:S(2)}) collective-permute-start(bf16[256,384]{1,0:T(8,128)(2,1)S(1)} %slice.20), channel_id=1, source_target_pairs={{0,32},{2,34},{4,36},{6,38},{32,64},{34,66},{36,68},{38,70},{64,96... | collective-permute-start | bytes 589832 | tf_op jit(solution)/shard_map/ppermute | solution.py:42
  68.0 16.9 %collective-permute-start.9 = (bf16[256,384]{1,0:T(8,128)(2,1)S(1)}, bf16[256,384]{1,0:T(8,128)(2,1)S(1)}, u32[]{:S(2)}, u32[]{:S(2)}) collective-permute-start(bf16[256,384]{1,0:T(8,128)(2,1)S(1)} %slice.20), channel_id=1, source_target_pairs={{0,96},{2,98},{4,100},{6,102},{32,0},{34,2},{36,4},{38,6},{64,32},... | collective-permute-start | bytes 589832 | tf_op jit(solution)/shard_map/ppermute | solution.py:42
  69.9 11.8 %collective-permute-start.15 = (bf16[256,128]{1,0:T(8,128)(2,1)S(1)}, bf16[256,128]{1,0:T(8,128)(2,1)S(1)}, u32[]{:S(2)}, u32[]{:S(2)}) collective-permute-start(bf16[256,128]{1,0:T(8,128)(2,1)S(1)} %slice.21), channel_id=1, source_target_pairs={{0,17},{2,19},{4,21},{6,23},{32,49},{34,51},{36,53},{38,55},{64,81... | collective-permute-start | bytes 196616 | tf_op jit(solution)/shard_map/ppermute | solution.py:42
  72.3 11.2 %collective-permute-start.16 = (bf16[256,128]{1,0:T(8,128)(2,1)S(1)}, bf16[256,128]{1,0:T(8,128)(2,1)S(1)}, u32[]{:S(2)}, u32[]{:S(2)}) collective-permute-start(bf16[256,128]{1,0:T(8,128)(2,1)S(1)} %slice.21), channel_id=1, source_target_pairs={{0,16},{2,18},{4,20},{6,22},{32,48},{34,50},{36,52},{38,54},{64,80... | collective-permute-start | bytes 196616 | tf_op jit(solution)/shard_map/ppermute | solution.py:42
  81.7 18.9 %collective-permute-start.21 = (bf16[4,448,256]{2,1,0:T(8,128)(2,1)}, bf16[4,448,256]{2,1,0:T(8,128)(2,1)S(1)}, u32[]{:S(2)}, u32[]{:S(2)}) collective-permute-start(bf16[4,448,256]{2,1,0:T(8,128)(2,1)} %get-tuple-element.64), channel_id=1, source_target_pairs={{0,8},{8,0},{1,9},{9,1},{2,10},{10,2},{3,11},{11,3},{4,12},{12,4},... | collective-permute-start | bytes 2752520 | tf_op jit(solution)/shard_map/ppermute | solution.py:50
  83.5 9.6 %collective-permute-start.17 = (bf16[4,256,128]{2,1,0:T(8,128)(2,1)S(1)}, bf16[4,256,128]{2,1,0:T(8,128)(2,1)S(1)}, u32[]{:S(2)}, u32[]{:S(2)}) collective-permute-start(bf16[4,256,128]{2,1,0:T(8,128)(2,1)S(1)} %pad_maximum_fusion.4), channel_id=1, source_target_pairs={{0,32},{2,34},{4,36},{6,38},{32,64},{34,66},{36,68},{38,70},{64,96... | collective-permute-start | bytes 786440 | tf_op jit(solution)/shard_map/ppermute | solution.py:42
  85.1 100.2 %copy-start.2 = (s32[4]{0:T(128)S(1)}, s32[4]{0:T(128)}, u32[]{:S(2)}) copy-start(s32[4]{0:T(128)} %copy-done.1) | copy-start | bytes 52
  85.1 100.2 %copy-start.3 = (bf16[2,448,1536]{2,1,0:T(8,128)(2,1)S(1)}, bf16[2,448,1536]{2,1,0:T(8,128)(2,1)}, u32[]{:S(2)}) copy-start(bf16[2,448,1536]{2,1,0:T(8,128)(2,1)} %get-tuple-element.61.refs_5_) | copy-start | bytes 8257540
  85.1 100.2 %copy-start.4 = (bf16[4,448,256]{2,1,0:T(8,128)(2,1)S(1)}, bf16[4,448,256]{2,1,0:T(8,128)(2,1)}, u32[]{:S(2)}) copy-start(bf16[4,448,256]{2,1,0:T(8,128)(2,1)} %get-tuple-element.63.refs_7_) | copy-start | bytes 2752516
  85.1 17.3 %collective-permute-start.11 = (bf16[4,256,384]{2,1,0:T(8,128)(2,1)S(1)}, bf16[4,256,384]{2,1,0:T(8,128)(2,1)S(1)}, u32[]{:S(2)}, u32[]{:S(2)}) collective-permute-start(bf16[4,256,384]{2,1,0:T(8,128)(2,1)S(1)} %pad_maximum_fusion.1), channel_id=1, source_target_pairs={{0,2},{2,4},{4,6},{6,0},{32,34},{34,36},{36,38},{38,32},{64,66},{6... | collective-permute-start | bytes 2359304 | tf_op jit(solution)/shard_map/ppermute | solution.py:42
  85.5 9.0 %collective-permute-start.18 = (bf16[4,256,128]{2,1,0:T(8,128)(2,1)S(1)}, bf16[4,256,128]{2,1,0:T(8,128)(2,1)S(1)}, u32[]{:S(2)}, u32[]{:S(2)}) collective-permute-start(bf16[4,256,128]{2,1,0:T(8,128)(2,1)S(1)} %pad_maximum_fusion.4), channel_id=1, source_target_pairs={{0,96},{2,98},{4,100},{6,102},{32,0},{34,2},{36,4},{38,6},{64,32},... | collective-permute-start | bytes 786440 | tf_op jit(solution)/shard_map/ppermute | solution.py:42
  87.1 10.7 %collective-permute-start.19 = (bf16[4,256,128]{2,1,0:T(8,128)(2,1)S(1)}, bf16[4,256,128]{2,1,0:T(8,128)(2,1)S(1)}, u32[]{:S(2)}, u32[]{:S(2)}) collective-permute-start(bf16[4,256,128]{2,1,0:T(8,128)(2,1)S(1)} %pad_maximum_fusion.4), channel_id=1, source_target_pairs={{0,64},{2,66},{4,68},{6,70},{32,96},{34,98},{36,100},{38,102},{64,... | collective-permute-start | bytes 786440 | tf_op jit(solution)/shard_map/ppermute | solution.py:42
  93.1 92.2 %collective-permute-start.20 = (bf16[2,448,1536]{2,1,0:T(8,128)(2,1)}, bf16[2,448,1536]{2,1,0:T(8,128)(2,1)S(1)}, u32[]{:S(2)}, u32[]{:S(2)}) collective-permute-start(bf16[2,448,1536]{2,1,0:T(8,128)(2,1)} %get-tuple-element.62), channel_id=1, source_target_pairs={{0,8},{8,0},{1,9},{9,1},{2,10},{10,2},{3,11},{11,3},{4,12},{12,4},... | collective-permute-start | bytes 8257544 | tf_op jit(solution)/shard_map/ppermute | solution.py:50
  97.9 14.2 %collective-permute-start.28 = (bf16[8,256,128]{2,1,0:T(8,128)(2,1)S(1)}, bf16[8,256,128]{2,1,0:T(8,128)(2,1)S(1)}, u32[]{:S(2)}, u32[]{:S(2)}) collective-permute-start(bf16[8,256,128]{2,1,0:T(8,128)(2,1)S(1)} %pad_maximum_fusion.2.refs_3_), channel_id=1, source_target_pairs={{0,2},{2,4},{4,6},{6,0},{32,34},{34,36},{36,38},{38,32},{64,66},{6... | collective-permute-start | bytes 1572872 | tf_op jit(solution)/shard_map/ppermute | solution.py:42
  99.3 24.0 %collective-permute-start.29 = (bf16[8,256,128]{2,1,0:T(8,128)(2,1)S(1)}, bf16[8,256,128]{2,1,0:T(8,128)(2,1)S(1)}, u32[]{:S(2)}, u32[]{:S(2)}) collective-permute-start(bf16[8,256,128]{2,1,0:T(8,128)(2,1)S(1)} %pad_maximum_fusion.3.refs_4_), channel_id=1, source_target_pairs={{0,2},{2,4},{4,6},{6,0},{32,34},{34,36},{36,38},{38,32},{64,66},{6... | collective-permute-start | bytes 1572872 | tf_op jit(solution)/shard_map/ppermute | solution.py:42
  100.6 28.4 %collective-permute-start.12 = (bf16[4,256,384]{2,1,0:T(8,128)(2,1)S(1)}, bf16[4,256,384]{2,1,0:T(8,128)(2,1)S(1)}, u32[]{:S(2)}, u32[]{:S(2)}) collective-permute-start(bf16[4,256,384]{2,1,0:T(8,128)(2,1)S(1)} %pad_maximum_fusion.1), channel_id=1, source_target_pairs={{0,6},{2,0},{4,2},{6,4},{32,38},{34,32},{36,34},{38,36},{64,70},{6... | collective-permute-start | bytes 2359304 | tf_op jit(solution)/shard_map/ppermute | solution.py:42
  102.4 26.2 %collective-permute-start.30 = (bf16[8,256,128]{2,1,0:T(8,128)(2,1)S(1)}, bf16[8,256,128]{2,1,0:T(8,128)(2,1)S(1)}, u32[]{:S(2)}, u32[]{:S(2)}) collective-permute-start(bf16[8,256,128]{2,1,0:T(8,128)(2,1)S(1)} %pad_maximum_fusion.2.refs_3_), channel_id=1, source_target_pairs={{0,6},{2,0},{4,2},{6,4},{32,38},{34,32},{36,34},{38,36},{64,70},{6... | collective-permute-start | bytes 1572872 | tf_op jit(solution)/shard_map/ppermute | solution.py:42
  112.1 36.4 %collective-permute-start.22 = (bf16[8,256,384]{2,1,0:T(8,128)(2,1)S(1)}, bf16[8,256,384]{2,1,0:T(8,128)(2,1)S(1)}, u32[]{:S(2)}, u32[]{:S(2)}) collective-permute-start(bf16[8,256,384]{2,1,0:T(8,128)(2,1)S(1)} %pad_maximum_fusion.refs_0_), channel_id=1, source_target_pairs={{0,1},{2,3},{4,5},{6,7},{32,33},{34,35},{36,37},{38,39},{64,65},{6... | collective-permute-start | bytes 4718600 | tf_op jit(solution)/shard_map/ppermute | solution.py:42
  123.3 24.3 %collective-permute-start.13 = (bf16[4,256,384]{2,1,0:T(8,128)(2,1)S(1)}, bf16[4,256,384]{2,1,0:T(8,128)(2,1)S(1)}, u32[]{:S(2)}, u32[]{:S(2)}) collective-permute-start(bf16[4,256,384]{2,1,0:T(8,128)(2,1)S(1)} %pad_maximum_fusion.1), channel_id=1, source_target_pairs={{0,4},{2,6},{4,0},{6,2},{32,36},{34,38},{36,32},{38,34},{64,68},{6... | collective-permute-start | bytes 2359304 | tf_op jit(solution)/shard_map/ppermute | solution.py:42
  128.5 19.1 %collective-permute-start.31 = (bf16[8,256,128]{2,1,0:T(8,128)(2,1)S(1)}, bf16[8,256,128]{2,1,0:T(8,128)(2,1)S(1)}, u32[]{:S(2)}, u32[]{:S(2)}) collective-permute-start(bf16[8,256,128]{2,1,0:T(8,128)(2,1)S(1)} %pad_maximum_fusion.3.refs_4_), channel_id=1, source_target_pairs={{0,6},{2,0},{4,2},{6,4},{32,38},{34,32},{36,34},{38,36},{64,70},{6... | collective-permute-start | bytes 1572872 | tf_op jit(solution)/shard_map/ppermute | solution.py:42
  129.0 19.3 %collective-permute-start.23 = (bf16[4,256,384]{2,1,0:T(8,128)(2,1)S(1)}, bf16[4,256,384]{2,1,0:T(8,128)(2,1)S(1)}, u32[]{:S(2)}, u32[]{:S(2)}) collective-permute-start(bf16[4,256,384]{2,1,0:T(8,128)(2,1)S(1)} %collective-permute-done.12.refs_1_), channel_id=1, source_target_pairs={{0,1},{2,3},{4,5},{6,7},{32,33},{34,35},{36,37},{38,39},{64,65},{6... | collective-permute-start | bytes 2359304 | tf_op jit(solution)/shard_map/ppermute | solution.py:42
  147.7 11.1 %collective-permute-start.26 = (bf16[4,256,384]{2,1,0:T(8,128)(2,1)S(1)}, bf16[4,256,384]{2,1,0:T(8,128)(2,1)S(1)}, u32[]{:S(2)}, u32[]{:S(2)}) collective-permute-start(bf16[4,256,384]{2,1,0:T(8,128)(2,1)S(1)} %collective-permute-done.12.refs_1_), channel_id=1, source_target_pairs={{0,17},{2,19},{4,21},{6,23},{32,49},{34,51},{36,53},{38,55},{64,81... | collective-permute-start | bytes 2359304 | tf_op jit(solution)/shard_map/ppermute | solution.py:42
  147.7 47.4 %collective-permute-start.25 = (bf16[8,256,384]{2,1,0:T(8,128)(2,1)S(1)}, bf16[8,256,384]{2,1,0:T(8,128)(2,1)S(1)}, u32[]{:S(2)}, u32[]{:S(2)}) collective-permute-start(bf16[8,256,384]{2,1,0:T(8,128)(2,1)S(1)} %pad_maximum_fusion.refs_0_), channel_id=1, source_target_pairs={{0,17},{2,19},{4,21},{6,23},{32,49},{34,51},{36,53},{38,55},{64,81... | collective-permute-start | bytes 4718600 | tf_op jit(solution)/shard_map/ppermute | solution.py:42
  148.4 35.7 %collective-permute-start.27 = (bf16[4,256,384]{2,1,0:T(8,128)(2,1)S(1)}, bf16[4,256,384]{2,1,0:T(8,128)(2,1)S(1)}, u32[]{:S(2)}, u32[]{:S(2)}) collective-permute-start(bf16[4,256,384]{2,1,0:T(8,128)(2,1)S(1)} %collective-permute-done.13.refs_2_), channel_id=1, source_target_pairs={{0,17},{2,19},{4,21},{6,23},{32,49},{34,51},{36,53},{38,55},{64,81... | collective-permute-start | bytes 2359304 | tf_op jit(solution)/shard_map/ppermute | solution.py:42
  148.5 60.9 %collective-permute-start.32 = (bf16[8,256,384]{2,1,0:T(8,128)(2,1)S(1)}, bf16[8,256,384]{2,1,0:T(8,128)(2,1)S(1)}, u32[]{:S(2)}, u32[]{:S(2)}) collective-permute-start(bf16[8,256,384]{2,1,0:T(8,128)(2,1)S(1)} %collective-permute-done.22.refs_0_), channel_id=1, source_target_pairs={{0,1},{2,3},{4,5},{6,7},{32,33},{34,35},{36,37},{38,39},{64,65},{6... | collective-permute-start | bytes 4718600 | tf_op jit(solution)/shard_map/ppermute | solution.py:42
  158.8 34.7 %collective-permute-start.24 = (bf16[4,256,384]{2,1,0:T(8,128)(2,1)S(1)}, bf16[4,256,384]{2,1,0:T(8,128)(2,1)S(1)}, u32[]{:S(2)}, u32[]{:S(2)}) collective-permute-start(bf16[4,256,384]{2,1,0:T(8,128)(2,1)S(1)} %collective-permute-done.13.refs_2_), channel_id=1, source_target_pairs={{0,1},{2,3},{4,5},{6,7},{32,33},{34,35},{36,37},{38,39},{64,65},{6... | collective-permute-start | bytes 2359304 | tf_op jit(solution)/shard_map/ppermute | solution.py:42
  184.1 25.2 %collective-permute-start.33 = (bf16[4,256,384]{2,1,0:T(8,128)(2,1)S(1)}, bf16[4,256,384]{2,1,0:T(8,128)(2,1)S(1)}, u32[]{:S(2)}, u32[]{:S(2)}) collective-permute-start(bf16[4,256,384]{2,1,0:T(8,128)(2,1)S(1)} %collective-permute-done.26.refs_4_), channel_id=1, source_target_pairs={{0,17},{2,19},{4,21},{6,23},{32,49},{34,51},{36,53},{38,55},{64,81... | collective-permute-start | bytes 2359304 | tf_op jit(solution)/shard_map/ppermute | solution.py:42
  185.3 24.0 %collective-permute-start.34 = (bf16[4,256,384]{2,1,0:T(8,128)(2,1)S(1)}, bf16[4,256,384]{2,1,0:T(8,128)(2,1)S(1)}, u32[]{:S(2)}, u32[]{:S(2)}) collective-permute-start(bf16[4,256,384]{2,1,0:T(8,128)(2,1)S(1)} %collective-permute-done.27.refs_5_), channel_id=1, source_target_pairs={{0,17},{2,19},{4,21},{6,23},{32,49},{34,51},{36,53},{38,55},{64,81... | collective-permute-start | bytes 2359304 | tf_op jit(solution)/shard_map/ppermute | solution.py:42
  193.5 15.8 %collective-permute-start.35 = (bf16[8,256,128]{2,1,0:T(8,128)(2,1)S(1)}, bf16[8,256,128]{2,1,0:T(8,128)(2,1)S(1)}, u32[]{:S(2)}, u32[]{:S(2)}) collective-permute-start(bf16[8,256,128]{2,1,0:T(8,128)(2,1)S(1)} %collective-permute-done.28.refs_6_), channel_id=1, source_target_pairs={{0,2},{2,4},{4,6},{6,0},{32,34},{34,36},{36,38},{38,32},{64,66},{6... | collective-permute-start | bytes 1572872 | tf_op jit(solution)/shard_map/ppermute | solution.py:42
  195.1 14.2 %collective-permute-start.36 = (bf16[8,256,128]{2,1,0:T(8,128)(2,1)S(1)}, bf16[8,256,128]{2,1,0:T(8,128)(2,1)S(1)}, u32[]{:S(2)}, u32[]{:S(2)}) collective-permute-start(bf16[8,256,128]{2,1,0:T(8,128)(2,1)S(1)} %collective-permute-done.31.refs_9_), channel_id=1, source_target_pairs={{0,6},{2,0},{4,2},{6,4},{32,38},{34,32},{36,34},{38,36},{64,70},{6... | collective-permute-start | bytes 1572872 | tf_op jit(solution)/shard_map/ppermute | solution.py:42
  215.0 8.6 %collective-permute-start.37 = (bf16[464,2048]{1,0:T(8,128)(2,1)S(1)}, bf16[464,2048]{1,0:T(8,128)(2,1)S(1)}, u32[]{:S(2)}, u32[]{:S(2)}) collective-permute-start(bf16[464,2048]{1,0:T(8,128)(2,1)S(1)} %get-tuple-element.71), channel_id=1, source_target_pairs={{0,8},{8,0},{1,9},{9,1},{2,10},{10,2},{3,11},{11,3},{4,12},{12,4},... | collective-permute-start | bytes 5701640 | tf_op jit(solution)/shard_map/ppermute | solution.py:50
